TPU v7x, 32 devices: a whole 2x2x4 slice. The times are simulated.
32 devices in a mesh: ctx: 8 (over z, y), fsdp: 4 (over x, core).
Axes of the slice: x: 2, y: 2, z: 4, core: 2. Of those that a mesh axis runs over, the one named last changes fastest.
Arguments:
- tokens: bfloat16 [4, 4096, 768], P('fsdp', 'ctx'), may hold values from -6 to 6
- cotangent: bfloat16 [4, 4096, 768], P('fsdp', 'ctx'), may hold values from -6 to 6
- pair_table: int32 [4, 8, 2], P('fsdp', 'ctx'), may hold values from 0 to 15, as said below
- seq_ids: int32 [4, 16], P('fsdp'), may hold values from 0 to 1, as said below
- first_gain: bfloat16 [768], P('fsdp'), may hold values from 0.5 to 1.5
- first_shift: bfloat16 [768], P('fsdp'), may hold values from -0.59765625 to 0.59765625
- project_weight: bfloat16 [768, 2304], P(None, 'fsdp'), may hold values from -0.21875 to 0.21875
- project_bias: bfloat16 [2304], P('fsdp'), may hold values from -0.059814453 to 0.059814453
- feature_query: bfloat16 [12, 64, 64], P('fsdp'), may hold values from -1.5 to 1.5
- feature_key: bfloat16 [12, 64, 64], P('fsdp'), may hold values from -1.5 to 1.5
- output_weight: bfloat16 [768, 768], P('fsdp'), may hold values from -9 to 9
- output_bias: bfloat16 [768], P('fsdp'), may hold values from -0.59765625 to 0.59765625
- second_gain: bfloat16 [768], P('fsdp'), may hold values from 0.5 to 1.5
- second_shift: bfloat16 [768], P('fsdp'), may hold values from -0.59765625 to 0.59765625
- expand_weight: bfloat16 [768, 3072], P(None, 'fsdp'), may hold values from -0.21875 to 0.21875
- expand_bias: bfloat16 [3072], P('fsdp'), may hold values from -0.59765625 to 0.59765625
- reduce_weight: bfloat16 [3072, 768], P('fsdp'), may hold values from -0.109375 to 0.109375
- reduce_bias: bfloat16 [768], P('fsdp'), may hold values from -0.59765625 to 0.59765625
Outputs:
- layer_output: float32 [4, 4096, 768], P('fsdp', 'ctx')
- input_grad: float32 [4, 4096, 768], P('fsdp', 'ctx')
- grad_first_gain: float32 [768], P('fsdp')
- grad_first_shift: float32 [768], P('fsdp')
- grad_project_weight: float32 [768, 2304], P(None, 'fsdp')
- grad_project_bias: float32 [2304], P('fsdp')
- grad_feature_query: float32 [12, 64, 64], P('fsdp')
- grad_feature_key: float32 [12, 64, 64], P('fsdp')
- grad_output_weight: float32 [768, 768], P('fsdp')
- grad_output_bias: float32 [768], P('fsdp')
- grad_second_gain: float32 [768], P('fsdp')
- grad_second_shift: float32 [768], P('fsdp')
- grad_expand_weight: float32 [768, 3072], P(None, 'fsdp')
- grad_expand_bias: float32 [3072], P('fsdp')
- grad_reduce_weight: float32 [3072, 768], P('fsdp')
- grad_reduce_bias: float32 [768], P('fsdp')
Inputs may be any that keep to these rules, and one draw needn't show every extreme that they name: `pair_table`: at ctx index c of a group, slots 0 and 1 hold blocks c and 15 - c in either order. `seq_ids`: each group's blocks hold 2 sequences, ids 0 then 1 in block order; sequence 0 has 4 to 12 blocks.
All inputs are finite; a program needn't handle non-finite values.
Results may differ from a plain program's by a relative error of at most 0.019.
Values may be sent and summed in bfloat16 or wider, within the bound.
No kernel may reach another device: no remote copies, remote signals or barrier semaphores. Data moves between devices by JAX's collectives and lax.ppermute only.
A program may use at most 256 MiB of HBM per device.

v0:
```python
import jax
import jax.numpy as jnp
from jax import lax
from jax.sharding import PartitionSpec as P

SEQS = 2


EPS = 1e-05


def prefix(x, axis, combine, identity):
    size, position = (lax.axis_size(axis), lax.axis_index(axis))
    everything = jax.tree.map(lambda part: lax.all_gather(part, axis), x)
    start = jax.tree.map(
        lambda part, zero: jnp.broadcast_to(jnp.asarray(zero, part.dtype), part.shape), x, identity
    )

    def lap(k, before):
        reached = k < position
        new = combine(before, jax.tree.map(lambda part: part[k], everything))
        return jax.tree.map(lambda a, b: jnp.where(reached, a, b), new, before)

    return lax.fori_loop(0, size, lap, start)


def layer_norm(rows_in, gains, shift):
    center = rows_in - jnp.mean(rows_in, axis=-1, keepdims=True)
    spread = jnp.mean(center * center, axis=-1, keepdims=True)
    return center * lax.rsqrt(spread + EPS) * gains + shift


def features(logits):
    return jnp.concatenate(
        [jax.nn.softmax(logits, axis=-1), jax.nn.softmax(-logits, axis=-1)], axis=-1
    )


def gelu_tanh(hidden):
    return jax.nn.gelu(hidden, approximate=True)


def contract_rows(left, right):
    return lax.dot_general(
        left, right, (((0,), (0,)), ((), ())), preferred_element_type=jnp.float32
    )


def times_transpose(left, right):
    return lax.dot_general(
        left, right, (((1,), (1,)), ((), ())), preferred_element_type=jnp.float32
    )


def chain(earlier, later):
    mult_first, state_first, norm_first = earlier
    mult_second, state_second, norm_second = later
    return (
        mult_first * mult_second,
        mult_second[:, None, None, None] * state_first + state_second,
        mult_second[:, None, None] * norm_first + norm_second,
    )


def id_lookup(ids, where_at):
    count = ids.shape[0]
    match = jnp.arange(count, dtype=jnp.int32)[None, :] == where_at[:, None]
    return jnp.sum(jnp.where(match, ids[None, :], 0), axis=1)


def to_lanes(stacked, match):
    shaped = match.reshape(match.shape + (1,) * (stacked.ndim - 1))
    return jnp.sum(shaped * stacked[None], axis=1)


def to_slots(lanes, match):
    flipped = jnp.transpose(match)
    shaped = flipped.reshape(flipped.shape + (1,) * (lanes.ndim - 1))
    return jnp.sum(shaped * lanes[None], axis=1)


def lane_seq_totals(lanes, lane_hot):
    shaped = lane_hot.reshape(lane_hot.shape + (1,) * (lanes.ndim - 1))
    return shaped * lanes[:, None]


def lane_select(totals, lane_hot):
    shaped = lane_hot.reshape(
        lane_hot.shape[:1] + (1,) + lane_hot.shape[1:] + (1,) * (totals.ndim - 2)
    )
    return jnp.sum(shaped * totals[None], axis=2)


def weigh_lanes(selected, weights):
    shaped = weights.reshape(weights.shape + (1,) * (selected.ndim - 2))
    return jnp.sum(shaped * selected, axis=1)


def expand_lane(vector, like):
    return vector.reshape(vector.shape + (1,) * (like.ndim - 1))


def body(
    tokens,
    cotangent,
    pair_table,
    seq_ids,
    first_gain,
    first_shift,
    project_weight,
    project_bias,
    feature_query,
    feature_key,
    output_weight,
    output_bias,
    second_gain,
    second_shift,
    expand_weight,
    expand_bias,
    reduce_weight,
    reduce_bias,
):
    (
        gain_one,
        shift_one,
        project_full,
        project_offset,
        query_map,
        key_map,
        output_full,
        output_offset,
        gain_two,
        shift_two,
        expand_full,
        expand_offset,
        reduce_full,
        reduce_offset,
    ) = (
        lax.all_gather(first_gain, "fsdp", axis=0, tiled=True),
        lax.all_gather(first_shift, "fsdp", axis=0, tiled=True),
        lax.all_gather(project_weight, "fsdp", axis=1, tiled=True),
        lax.all_gather(project_bias, "fsdp", axis=0, tiled=True),
        lax.all_gather(feature_query, "fsdp", axis=0, tiled=True),
        lax.all_gather(feature_key, "fsdp", axis=0, tiled=True),
        lax.all_gather(output_weight, "fsdp", axis=0, tiled=True),
        lax.all_gather(output_bias, "fsdp", axis=0, tiled=True),
        lax.all_gather(second_gain, "fsdp", axis=0, tiled=True),
        lax.all_gather(second_shift, "fsdp", axis=0, tiled=True),
        lax.all_gather(expand_weight, "fsdp", axis=1, tiled=True),
        lax.all_gather(expand_bias, "fsdp", axis=0, tiled=True),
        lax.all_gather(reduce_weight, "fsdp", axis=0, tiled=True),
        lax.all_gather(reduce_bias, "fsdp", axis=0, tiled=True),
    )
    rows_in = tokens[0].astype(jnp.float32)
    rows_n, width = rows_in.shape
    heads = query_map.shape[0]
    head_dim = width // heads
    feats = 2 * head_dim
    slots = pair_table.shape[2]
    half_slots = slots // 2
    block_len = rows_n // slots
    normed_one, norm_back_one = jax.vjp(
        layer_norm, rows_in, gain_one.astype(jnp.float32), shift_one.astype(jnp.float32)
    )
    rounded_one = normed_one.astype(jnp.bfloat16)
    project_out = jnp.dot(
        rounded_one, project_full, preferred_element_type=jnp.float32
    ) + project_offset.astype(jnp.float32)
    queries = project_out[:, :width].astype(jnp.bfloat16).reshape(rows_n, heads, head_dim)
    key_rows = (
        project_out[:, width : 2 * width].astype(jnp.bfloat16).reshape(rows_n, heads, head_dim)
    )
    value_rows = project_out[:, 2 * width :].astype(jnp.bfloat16).reshape(rows_n, heads, head_dim)
    query_logits = jnp.einsum(
        "rhd,hde->rhe", queries, query_map, preferred_element_type=jnp.float32
    )
    query_phi, query_back = jax.vjp(features, query_logits)
    query_feats = query_phi.astype(jnp.bfloat16)
    key_logits = jnp.einsum("rhd,hde->rhe", key_rows, key_map, preferred_element_type=jnp.float32)
    key_phi, key_back = jax.vjp(features, key_logits)
    key_feats = key_phi.astype(jnp.bfloat16)
    query_blocks = query_feats.reshape(slots, block_len, heads, feats)
    key_blocks = key_feats.reshape(slots, block_len, heads, feats)
    value_blocks = value_rows.reshape(slots, block_len, heads, head_dim)
    block_states = jnp.einsum(
        "sbhf,sbhd->shfd", key_blocks, value_blocks, preferred_element_type=jnp.float32
    )
    block_norms = jnp.sum(key_blocks, axis=1, dtype=jnp.float32)
    place = lax.axis_index("ctx")
    nctx = lax.axis_size("ctx")
    ids = seq_ids[0]
    blocks = ids.shape[0]
    positions = pair_table[0, 0]
    lane_index = jnp.arange(slots, dtype=jnp.int32)
    targets = jnp.where(
        lane_index < half_slots,
        lane_index * nctx + place,
        blocks - 1 - (slots - 1 - lane_index) * nctx - place,
    )
    lane_match = (targets[:, None] == positions[None, :]).astype(jnp.float32)
    own_ids = id_lookup(ids, positions)
    prev_ids = id_lookup(ids, positions - 1)
    next_ids = id_lookup(ids, positions + 1)
    starts = (positions == 0) | (own_ids != prev_ids)
    keep_mult = 1.0 - starts.astype(jnp.float32)
    next_same = ((positions + 1 < blocks) & (next_ids == own_ids)).astype(jnp.float32)
    seq_hot = (jnp.arange(SEQS, dtype=jnp.int32)[None, :] == own_ids[:, None]).astype(jnp.float32)
    rising = (lane_index < half_slots).astype(jnp.float32)
    lane_mult = rising * to_lanes(keep_mult, lane_match) + (1.0 - rising) * to_lanes(
        next_same, lane_match
    )
    lane_hot = to_lanes(seq_hot, lane_match)
    before_mask = (lane_index[None, :] < lane_index[:, None]).astype(jnp.float32)
    after_mask = (lane_index[None, :] > lane_index[:, None]).astype(jnp.float32)
    same_mask = (lane_index[None, :] == lane_index[:, None]).astype(jnp.float32)
    unit = (
        jnp.ones((slots,), jnp.float32),
        jnp.zeros((slots, heads, feats, head_dim), jnp.float32),
        jnp.zeros((slots, heads, feats), jnp.float32),
    )
    lane_states = to_lanes(block_states, lane_match)
    lane_norms = to_lanes(block_norms, lane_match)
    running = prefix((lane_mult, lane_states, lane_norms), "ctx", chain, unit)
    total_states, total_norms = lax.psum(
        (lane_seq_totals(lane_states, lane_hot), lane_seq_totals(lane_norms, lane_hot)), "ctx"
    )
    picked_states = lane_select(total_states, lane_hot)
    picked_norms = lane_select(total_norms, lane_hot)
    rise_s = expand_lane(rising, lane_states)
    rise_n = expand_lane(rising, lane_norms)
    mult_s = expand_lane(lane_mult, lane_states)
    mult_n = expand_lane(lane_mult, lane_norms)
    incl_lane_states = (
        weigh_lanes(picked_states, before_mask)
        + rise_s * (mult_s * running[1] + lane_states)
        + (1.0 - rise_s) * (weigh_lanes(picked_states, same_mask) - mult_s * running[1])
    )
    incl_lane_norms = (
        weigh_lanes(picked_norms, before_mask)
        + rise_n * (mult_n * running[2] + lane_norms)
        + (1.0 - rise_n) * (weigh_lanes(picked_norms, same_mask) - mult_n * running[2])
    )
    incl_states = to_slots(incl_lane_states, lane_match)
    incl_norms = to_slots(incl_lane_norms, lane_match)
    state_low = incl_states.astype(jnp.bfloat16)
    norm_low = incl_norms.astype(jnp.bfloat16)
    numer = jnp.einsum(
        "sbhf,shfd->sbhd", query_blocks, state_low, preferred_element_type=jnp.float32
    )
    denom = jnp.einsum("sbhf,shf->sbh", query_blocks, norm_low, preferred_element_type=jnp.float32)
    mixed = (numer / denom[..., None]).reshape(rows_n, width).astype(jnp.bfloat16)
    middle = (
        rows_in
        + jnp.dot(mixed, output_full, preferred_element_type=jnp.float32)
        + output_offset.astype(jnp.float32)
    )
    normed_two, norm_back_two = jax.vjp(
        layer_norm, middle, gain_two.astype(jnp.float32), shift_two.astype(jnp.float32)
    )
    rounded_two = normed_two.astype(jnp.bfloat16)
    hidden = jnp.dot(
        rounded_two, expand_full, preferred_element_type=jnp.float32
    ) + expand_offset.astype(jnp.float32)
    active, gelu_back = jax.vjp(gelu_tanh, hidden)
    active_low = active.astype(jnp.bfloat16)
    layer_out = (
        middle
        + jnp.dot(active_low, reduce_full, preferred_element_type=jnp.float32)
        + reduce_offset.astype(jnp.float32)
    )
    grad_out = cotangent[0].astype(jnp.float32)
    grad_reduced = grad_out.astype(jnp.bfloat16)
    g_reduce_full = contract_rows(active_low, grad_reduced)
    g_reduce_offset = jnp.sum(grad_reduced, axis=0, dtype=jnp.float32)
    grad_active = times_transpose(grad_reduced, reduce_full).astype(jnp.bfloat16)
    grad_hidden = gelu_back(grad_active.astype(jnp.float32))[0].astype(jnp.bfloat16)
    g_expand_full = contract_rows(rounded_two, grad_hidden)
    g_expand_offset = jnp.sum(grad_hidden, axis=0, dtype=jnp.float32)
    grad_middle_part, g_gain_two, g_shift_two = norm_back_two(
        times_transpose(grad_hidden, expand_full)
    )
    grad_middle = grad_out + grad_middle_part
    grad_attended = grad_middle.astype(jnp.bfloat16)
    g_output_full = contract_rows(mixed, grad_attended)
    g_output_offset = jnp.sum(grad_attended, axis=0, dtype=jnp.float32)
    grad_mixed = (
        times_transpose(grad_attended, output_full).astype(jnp.bfloat16).astype(jnp.float32)
    )
    grad_mixed = grad_mixed.reshape(slots, block_len, heads, head_dim)
    grad_numer = (grad_mixed / denom[..., None]).astype(jnp.bfloat16)
    grad_denom = (-jnp.sum(grad_mixed * numer, axis=-1) / (denom * denom)).astype(jnp.bfloat16)
    grad_query_feats = (
        jnp.einsum("sbhd,shfd->sbhf", grad_numer, state_low, preferred_element_type=jnp.float32)
        + grad_denom.astype(jnp.float32)[..., None] * norm_low.astype(jnp.float32)[:, None]
    )
    grad_incl_states = jnp.einsum(
        "sbhf,sbhd->shfd", query_blocks, grad_numer, preferred_element_type=jnp.float32
    )
    grad_incl_norms = jnp.einsum(
        "sbhf,sbh->shf", query_blocks, grad_denom, preferred_element_type=jnp.float32
    )
    grad_lane_states = to_lanes(grad_incl_states, lane_match)
    grad_lane_norms = to_lanes(grad_incl_norms, lane_match)
    back_running = prefix((lane_mult, grad_lane_states, grad_lane_norms), "ctx", chain, unit)
    grad_total_states, grad_total_norms = lax.psum(
        (lane_seq_totals(grad_lane_states, lane_hot), lane_seq_totals(grad_lane_norms, lane_hot)),
        "ctx",
    )
    grad_picked_states = lane_select(grad_total_states, lane_hot)
    grad_picked_norms = lane_select(grad_total_norms, lane_hot)
    lane_grad_states = (
        weigh_lanes(grad_picked_states, after_mask)
        + rise_s * (weigh_lanes(grad_picked_states, same_mask) - mult_s * back_running[1])
        + (1.0 - rise_s) * (grad_lane_states + mult_s * back_running[1])
    )
    lane_grad_norms = (
        weigh_lanes(grad_picked_norms, after_mask)
        + rise_n * (weigh_lanes(grad_picked_norms, same_mask) - mult_n * back_running[2])
        + (1.0 - rise_n) * (grad_lane_norms + mult_n * back_running[2])
    )
    block_grad_states = to_slots(lane_grad_states, lane_match)
    block_grad_norms = to_slots(lane_grad_norms, lane_match)
    grad_states_low = block_grad_states.astype(jnp.bfloat16)
    grad_key_feats = (
        jnp.einsum(
            "sbhd,shfd->sbhf", value_blocks, grad_states_low, preferred_element_type=jnp.float32
        )
        + block_grad_norms[:, None]
    )
    grad_values = jnp.einsum(
        "sbhf,shfd->sbhd", key_blocks, grad_states_low, preferred_element_type=jnp.float32
    ).astype(jnp.bfloat16)
    grad_query_logits = query_back(
        grad_query_feats.astype(jnp.bfloat16).astype(jnp.float32).reshape(rows_n, heads, feats)
    )[0].astype(jnp.bfloat16)
    grad_key_logits = key_back(
        grad_key_feats.astype(jnp.bfloat16).astype(jnp.float32).reshape(rows_n, heads, feats)
    )[0].astype(jnp.bfloat16)
    g_query_map = jnp.einsum(
        "rhd,rhe->hde", queries, grad_query_logits, preferred_element_type=jnp.float32
    )
    g_key_map = jnp.einsum(
        "rhd,rhe->hde", key_rows, grad_key_logits, preferred_element_type=jnp.float32
    )
    grad_queries = jnp.einsum(
        "rhe,hde->rhd", grad_query_logits, query_map, preferred_element_type=jnp.float32
    ).astype(jnp.bfloat16)
    grad_keys = jnp.einsum(
        "rhe,hde->rhd", grad_key_logits, key_map, preferred_element_type=jnp.float32
    ).astype(jnp.bfloat16)
    grad_project = jnp.concatenate(
        [
            grad_queries.reshape(rows_n, width),
            grad_keys.reshape(rows_n, width),
            grad_values.reshape(rows_n, width),
        ],
        axis=1,
    )
    g_project_full = contract_rows(rounded_one, grad_project)
    g_project_offset = jnp.sum(grad_project, axis=0, dtype=jnp.float32)
    grad_rows_part, g_gain_one, g_shift_one = norm_back_one(
        times_transpose(grad_project, project_full)
    )
    input_grad = grad_middle + grad_rows_part
    shards = (
        lax.psum_scatter(
            g_gain_one.astype(jnp.bfloat16), "fsdp", scatter_dimension=0, tiled=True
        ).astype(jnp.float32),
        lax.psum_scatter(
            g_shift_one.astype(jnp.bfloat16), "fsdp", scatter_dimension=0, tiled=True
        ).astype(jnp.float32),
        lax.psum_scatter(
            g_project_full.astype(jnp.bfloat16), "fsdp", scatter_dimension=1, tiled=True
        ).astype(jnp.float32),
        lax.psum_scatter(
            g_project_offset.astype(jnp.bfloat16), "fsdp", scatter_dimension=0, tiled=True
        ).astype(jnp.float32),
        lax.psum_scatter(
            g_query_map.astype(jnp.bfloat16), "fsdp", scatter_dimension=0, tiled=True
        ).astype(jnp.float32),
        lax.psum_scatter(
            g_key_map.astype(jnp.bfloat16), "fsdp", scatter_dimension=0, tiled=True
        ).astype(jnp.float32),
        lax.psum_scatter(
            g_output_full.astype(jnp.bfloat16), "fsdp", scatter_dimension=0, tiled=True
        ).astype(jnp.float32),
        lax.psum_scatter(
            g_output_offset.astype(jnp.bfloat16), "fsdp", scatter_dimension=0, tiled=True
        ).astype(jnp.float32),
        lax.psum_scatter(
            g_gain_two.astype(jnp.bfloat16), "fsdp", scatter_dimension=0, tiled=True
        ).astype(jnp.float32),
        lax.psum_scatter(
            g_shift_two.astype(jnp.bfloat16), "fsdp", scatter_dimension=0, tiled=True
        ).astype(jnp.float32),
        lax.psum_scatter(
            g_expand_full.astype(jnp.bfloat16), "fsdp", scatter_dimension=1, tiled=True
        ).astype(jnp.float32),
        lax.psum_scatter(
            g_expand_offset.astype(jnp.bfloat16), "fsdp", scatter_dimension=0, tiled=True
        ).astype(jnp.float32),
        lax.psum_scatter(
            g_reduce_full.astype(jnp.bfloat16), "fsdp", scatter_dimension=0, tiled=True
        ).astype(jnp.float32),
        lax.psum_scatter(
            g_reduce_offset.astype(jnp.bfloat16), "fsdp", scatter_dimension=0, tiled=True
        ).astype(jnp.float32),
    )
    finals = lax.psum(
        (
            shards[0],
            shards[1],
            shards[2],
            shards[3],
            shards[4],
            shards[5],
            shards[6],
            shards[7],
            shards[8],
            shards[9],
            shards[10],
            shards[11],
            shards[12],
            shards[13],
        ),
        "ctx",
    )
    return (
        layer_out.reshape(1, rows_n, width),
        input_grad.reshape(1, rows_n, width),
        finals[0],
        finals[1],
        finals[2],
        finals[3],
        finals[4],
        finals[5],
        finals[6],
        finals[7],
        finals[8],
        finals[9],
        finals[10],
        finals[11],
        finals[12],
        finals[13],
    )


def solution(mesh):
    in_specs = (
        P("fsdp", "ctx", None),
        P("fsdp", "ctx", None),
        P("fsdp", "ctx", None),
        P("fsdp", None),
        P("fsdp"),
        P("fsdp"),
        P(None, "fsdp"),
        P("fsdp"),
        P("fsdp", None, None),
        P("fsdp", None, None),
        P("fsdp", None),
        P("fsdp"),
        P("fsdp"),
        P("fsdp"),
        P(None, "fsdp"),
        P("fsdp"),
        P("fsdp", None),
        P("fsdp"),
    )
    out_specs = (
        P("fsdp", "ctx", None),
        P("fsdp", "ctx", None),
        P("fsdp"),
        P("fsdp"),
        P(None, "fsdp"),
        P("fsdp"),
        P("fsdp", None, None),
        P("fsdp", None, None),
        P("fsdp", None),
        P("fsdp"),
        P("fsdp"),
        P("fsdp"),
        P(None, "fsdp"),
        P("fsdp"),
        P("fsdp", None),
        P("fsdp"),
    )
    return jax.shard_map(body, mesh=mesh, in_specs=in_specs, out_specs=out_specs, check_vma=False)
```

profile of v0, /device:TPU:0, one launch (start us, length us, event | category | flops | bytes accessed | tf_op | source)
XLA Modules:
  0.0 1092.7 jit_solution(5911283561613175749)
XLA Ops:
  15.7 13.8 %all-reduce.17 = (bf16[2304]{0:T(1024)(128)(2,1)S(1)}, bf16[768]{0:T(1024)(128)(2,1)S(1)}, bf16[768]{0:T(1024)(128)(2,1)S(1)}, bf16[768]{0:T(1024)(128)(2,1)}, b...) all-reduce(bf16[2304]{0:T(1024)(128)(2,1)S(1)} %dynamic-update-slice.2, ...), channel_id=1, replica_groups=mesh['ctx'=8,'fsdp'=4] {'fsdp'}, use_global_device_ids=true, to_apply=%add.2 | all-reduce | flops 6144 | bytes 24576
  29.5 6.8 all_gather.76
  39.9 4.4 all-gather.13.cloned.1.call-done
  44.3 4.2 fusion.20
  84.0 21.0 %all-gather.4 = f32[8,1,2]{2,1,0:T(1,128)S(1)} all-gather(f32[1,1,2]{2,1,0:T(1,128)S(1)} %fusion.90), channel_id=1, replica_groups=mesh['ctx'=8,'fsdp'=4] {'ctx'}, dimensions={0}, use_global_device_ids=true | all-gather | bytes 72 | tf_op jit(solution)/shard_map/all_gather | solution.py:14
  105.7 5.8 all_gather.82
  116.0 5.3 all-gather.5
  123.0 32.8 %all-gather.1 = f32[16,12,128]{2,1,0:T(8,128)} all-gather(f32[2,12,128]{2,1,0:T(8,128)S(1)} %multiply_reduce_fusion.26), channel_id=3, replica_groups=mesh['ctx'=8,'fsdp'=4] {'ctx'}, dimensions={0}, use_global_device_ids=true | all-gather | bytes 110592 | tf_op jit(solution)/shard_map/all_gather | solution.py:14
  162.9 34.9 %psum.127 = f32[2,2,12,128]{3,1,2,0:T(2,128)} all-reduce(f32[2,2,12,128]{3,1,2,0:T(2,128)} %broadcast_multiply_fusion.3), channel_id=1, replica_groups=mesh['ctx'=8,'fsdp'=4] {'ctx'}, use_global_device_ids=true, to_apply=%region_26.27 | all-reduce | flops 6144 | bytes 49152 | tf_op jit(solution)/shard_map/psum | solution.py:224
  219.9 49.4 %all-gather.21.cloned.1.call-done = f32[16,12,128,64]{2,3,1,0:T(8,128)} async-done(((f32[2,12,128,64]{2,3,1,0:T(8,128)}), f32[16,12,128,64]{2,3,1,0:T(8,128)}) %all-gather.21.cloned.1.call-update) | async-done | bytes 6291472 | tf_op jit(solution)/shard_map/all_gather | solution.py:14
  269.3 51.8 %while.32 = (s32[]{:T(128)}, f32[2,12,128,64]{3,2,1,0:T(8,128)}, f32[2,12,128]{2,1,0:T(8,128)S(1)}, s32[]{:T(128)}, f32[8,2]{1,0:T(8,128)}, /*index=5*/f32[8,2,1...) while((s32[]{:T(128)}, f32[2,12,128,64]{3,2,1,0:T(8,128)}, ...), condition=%wide.region_19.20_spmd.clone, body=%wide.region_18.19_spmd.clone.sunk | while | flops 798724 | bytes 5542107 | solution.py:24
  334.9 9.0 fusion.98
  343.9 20.4 %all-gather.19.cloned.1.call-done = bf16[3072,768]{1,0:T(8,128)(2,1)} async-done(((bf16[768,768]{1,0:T(8,128)(2,1)}), bf16[3072,768]{1,0:T(8,128)(2,1)}) %all-gather.19.cloned.1.call-update) | async-done | bytes 4718608 | tf_op jit(solution)/shard_map/all_gather | solution.py:151
  364.3 10.0 fusion.111
  374.3 3.5 multiply_reduce_fusion.2
  385.5 3.1 reshape.635
  403.7 3.2 convolution_convert_fusion.4
  407.0 7.5 convolution_convert_fusion.2
  417.8 37.6 %psum.129 = f32[2,2,12,128]{3,1,2,0:T(2,128)S(1)} all-reduce(f32[2,2,12,128]{3,1,2,0:T(2,128)S(1)} %broadcast_multiply_fusion.2), channel_id=1, replica_groups=mesh['ctx'=8,'fsdp'=4] {'ctx'}, use_global_device_ids=true, to_apply=%region_47.48 | all-reduce | flops 6144 | bytes 49152 | tf_op jit(solution)/shard_map/psum | solution.py:305
  455.4 32.8 %all-gather.3 = f32[16,12,128]{2,1,0:T(8,128)} all-gather(f32[2,12,128]{2,1,0:T(8,128)S(1)} %multiply_reduce_fusion.24), channel_id=5, replica_groups=mesh['ctx'=8,'fsdp'=4] {'ctx'}, dimensions={0}, use_global_device_ids=true | all-gather | bytes 110592 | tf_op jit(solution)/shard_map/all_gather | solution.py:14
  491.6 9.1 convolution_convert_fusion.1
  504.8 78.3 %all-gather.23.cloned.1.call-done = f32[16,12,128,64]{2,3,1,0:T(8,128)} async-done(((f32[2,12,128,64]{2,3,1,0:T(8,128)}), f32[16,12,128,64]{2,3,1,0:T(8,128)}) %all-gather.23.cloned.1.call-update) | async-done | bytes 6291472 | tf_op jit(solution)/shard_map/all_gather | solution.py:14
  583.1 46.9 %while.33 = (s32[]{:T(128)}, f32[2,12,128,64]{3,2,1,0:T(8,128)}, f32[2,12,128]{2,1,0:T(8,128)S(1)}, s32[]{:T(128)}, f32[8,2]{1,0:T(8,128)}, /*index=5*/f32[8,2,1...) while((s32[]{:T(128)}, f32[2,12,128,64]{3,2,1,0:T(8,128)}, ...), condition=%wide.region_45.46_spmd.clone, body=%wide.region_44.45_spmd.clone.sunk | while | flops 798724 | bytes 5542047 | solution.py:24
  646.3 4.0 convolution_convert_fusion
  653.8 29.6 %reduce-scatter.15.cloned.1.call-done = bf16[768,768]{1,0:T(8,128)(2,1)} async-done(((bf16[768,3072]{1,0:T(8,128)(2,1)}), bf16[768,768]{1,0:T(8,128)(2,1)}) %reduce-scatter.15.cloned.1.call-update) | async-done | bytes 1179664 | tf_op jit(solution)/shard_map/reduce_scatter | solution.py:396
  683.4 50.3 %reduce-scatter.17.cloned.1.call-done = bf16[768,768]{1,0:T(8,128)(2,1)} async-done(((bf16[3072,768]{1,0:T(8,128)(2,1)}), bf16[768,768]{1,0:T(8,128)(2,1)}) %reduce-scatter.17.cloned.1.call-update) | async-done | bytes 1179664 | tf_op jit(solution)/shard_map/reduce_scatter | solution.py:402
  735.3 4.3 fusion.99
  741.6 10.3 all-reduce.16
  752.5 3.4 add_bitcast_fusion
  755.9 9.4 add_bitcast_fusion.1
  765.3 34.4 %reduce-scatter.7.cloned.1.call-done = bf16[768,576]{0,1:T(8,128)(2,1)} async-done(((bf16[768,2304]{0,1:T(8,128)(2,1)}), bf16[768,576]{0,1:T(8,128)(2,1)}) %reduce-scatter.7.cloned.1.call-update) | async-done | bytes 884752 | tf_op jit(solution)/shard_map/reduce_scatter | solution.py:372
  799.8 286.2 %all-reduce.25 = (f32[192]{0:T(256)}, f32[192]{0:T(256)}, f32[768,576]{0,1:T(8,128)}, f32[576]{0:T(1024)}, f32[3,64,64]{2,1,0:T(8,128)}, /*index=5*/f32[3,64,64]...) all-reduce(f32[192]{0:T(256)S(1)} %dynamic-slice_convert_fusion.7, ...), channel_id=1, replica_groups=mesh['ctx'=8,'fsdp'=4] {'ctx'}, use_global_device_ids=true, to_apply=%region_58.59 | all-reduce | flops 1796544 | bytes 10784256 | tf_op jit(solution)/shard_map/psum | solution.py:409
  (525 shorter events, 248.9 us)
Async XLA Ops:
  7.2 37.1 %all-gather.13.cloned.1.call-start = ((), (), s32[]{:S(2)}) async-start(), calls=%async_computation.6 | async-start | bytes 4423680 | tf_op jit(solution)/shard_map/all_gather | solution.py:141
  7.9 208.8 %all-reduce.22.cloned.1.call-start = ((), (), s32[]{:S(2)}) async-start(), calls=%async_computation.7 | async-start | bytes 3145728 | tf_op jit(solution)/shard_map/psum | solution.py:224
  39.3 37.1 %copy-start.61 = (f32[2,2]{1,0:T(2,128)}, f32[2,2]{1,0:T(2,128)S(1)}, u32[]{:S(2)}) copy-start(f32[2,2]{1,0:T(2,128)S(1)} %multiply_reduce_fusion.27) | copy-start | bytes 52
  60.7 61.2 %copy-start.2 = (bf16[2,256,12,64]{3,1,2,0:T(8,128)(2,1)}, bf16[2,256,12,64]{3,1,2,0:T(8,128)(2,1)S(1)}, u32[]{:S(2)}) copy-start(bf16[2,256,12,64]{3,1,2,0:T(8,128)(2,1)S(1)} %copy.144) | copy-start | bytes 2359300
  67.4 54.5 %copy-start.4 = (bf16[2,256,12,64]{3,1,2,0:T(8,128)(2,1)}, bf16[2,256,12,64]{3,1,2,0:T(8,128)(2,1)S(1)}, u32[]{:S(2)}) copy-start(bf16[2,256,12,64]{3,1,2,0:T(8,128)(2,1)S(1)} %copy.145) | copy-start | bytes 2359300
  79.1 190.3 %all-gather.21.cloned.1.call-start = ((), (), s32[]{:S(2)}) async-start(), calls=%async_computation.18 | async-start | bytes 7077888 | tf_op jit(solution)/shard_map/all_gather | solution.py:14
  79.8 250.9 %all-gather.15.cloned.1.call-start = ((), (), s32[]{:S(2)}) async-start(), calls=%async_computation.8 | async-start | bytes 1474560 | tf_op jit(solution)/shard_map/all_gather | solution.py:145
  80.4 254.6 %all-gather.17.cloned.1.call-start = ((), (), s32[]{:S(2)}) async-start(), calls=%async_computation.9 | async-start | bytes 5898240 | tf_op jit(solution)/shard_map/all_gather | solution.py:149
  81.0 283.3 %all-gather.19.cloned.1.call-start = ((), (), s32[]{:S(2)}) async-start(), calls=%async_computation.10 | async-start | bytes 5898240 | tf_op jit(solution)/shard_map/all_gather | solution.py:151
  81.5 419.5 %all-reduce.24.cloned.1.call-start = ((), (), s32[]{:S(2)}) async-start(), calls=%async_computation.11 | async-start | bytes 3145728 | tf_op jit(solution)/shard_map/psum | solution.py:305
  159.9 41.3 %copy-start.6 = (f32[512,12,64]{0,2,1:T(8,128)}, f32[512,12,64]{0,2,1:T(8,128)S(1)}, u32[]{:S(2)}) copy-start(f32[512,12,64]{0,2,1:T(8,128)S(1)} %get-tuple-element.491) | copy-start | bytes 4718596
  162.9 43.7 %copy-start.11 = (f32[512,12,64]{0,2,1:T(8,128)}, f32[512,12,64]{0,2,1:T(8,128)S(1)}, u32[]{:S(2)}) copy-start(f32[512,12,64]{0,2,1:T(8,128)S(1)} %get-tuple-element.489) | copy-start | bytes 4718596
  392.5 190.6 %all-gather.23.cloned.1.call-start = ((), (), s32[]{:S(2)}) async-start(), calls=%async_computation.19 | async-start | bytes 7077888 | tf_op jit(solution)/shard_map/all_gather | solution.py:14
  393.3 260.5 %reduce-scatter.9.cloned.1.call-start = ((), (), s32[]{:S(2)}) async-start(), calls=%async_computation.13 | async-start | bytes 245760 | tf_op jit(solution)/shard_map/reduce_scatter | solution.py:378
  403.3 250.5 %reduce-scatter.13.cloned.1.call-start = ((), (), s32[]{:S(2)}) async-start(), calls=%async_computation.15 | async-start | bytes 1474560 | tf_op jit(solution)/shard_map/reduce_scatter | solution.py:384
  406.9 276.5 %reduce-scatter.15.cloned.1.call-start = ((), (), s32[]{:S(2)}) async-start(), calls=%async_computation.16 | async-start | bytes 5898240 | tf_op jit(solution)/shard_map/reduce_scatter | solution.py:396
  414.5 319.2 %reduce-scatter.17.cloned.1.call-start = ((), (), s32[]{:S(2)}) async-start(), calls=%async_computation.17 | async-start | bytes 5898240 | tf_op jit(solution)/shard_map/reduce_scatter | solution.py:402
  417.6 74.1 %copy-start.25 = (bf16[1,512,768]{2,1,0:T(8,128)(2,1)S(1)}, bf16[1,512,768]{2,1,0:T(8,128)(2,1)}, u32[]{:S(2)}) copy-start(bf16[1,512,768]{2,1,0:T(8,128)(2,1)} %param.23) | copy-start | bytes 2359300
  417.6 74.1 %copy-start.95 = (f32[4,1,768]{2,1,0:T(1,128)S(1)}, f32[4,1,768]{2,1,0:T(1,128)}, u32[]{:S(2)}) copy-start(f32[4,1,768]{2,1,0:T(1,128)} %convert_element_type.432) | copy-start | bytes 36868
  417.7 83.0 %copy-start.54 = (f32[2,12,128]{2,1,0:T(8,128)}, f32[2,12,128]{2,1,0:T(8,128)S(1)}, u32[]{:S(2)}) copy-start(f32[2,12,128]{2,1,0:T(8,128)S(1)} %multiply_reduce_fusion.24) | copy-start | bytes 36868
  500.8 264.5 %reduce-scatter.11.cloned.1.call-start = ((), (), s32[]{:S(2)}) async-start(), calls=%async_computation.14 | async-start | bytes 245760 | tf_op jit(solution)/shard_map/reduce_scatter | solution.py:381
  583.1 46.9 %copy-start.55 = (f32[2,12,128]{2,1,0:T(8,128)S(1)}, f32[2,12,128]{2,1,0:T(8,128)}, u32[]{:S(2)}) copy-start(f32[2,12,128]{2,1,0:T(8,128)} %copy-done.54) | copy-start | bytes 36868
  583.1 47.0 %copy-start.66 = (f32[2,12,128]{2,1,0:T(8,128)S(1)}, f32[2,12,128]{2,1,0:T(8,128)}, u32[]{:S(2)}) copy-start(f32[2,12,128]{2,1,0:T(8,128)} %get-tuple-element.403) | copy-start | bytes 36868
  583.1 47.0 %copy-start.67 = (f32[2,12,128]{2,1,0:T(8,128)S(1)}, f32[2,12,128]{2,1,0:T(8,128)}, u32[]{:S(2)}) copy-start(f32[2,12,128]{2,1,0:T(8,128)} %get-tuple-element.404) | copy-start | bytes 36868
  583.1 47.0 %copy-start.100 = (f32[2]{0:T(128)S(1)}, f32[2]{0:T(128)}, u32[]{:S(2)}) copy-start(f32[2]{0:T(128)} %multiply_add_fusion.6) | copy-start | bytes 28
  583.1 47.0 %copy-start.102 = (f32[2]{0:T(128)S(1)}, f32[2]{0:T(128)}, u32[]{:S(2)}) copy-start(f32[2]{0:T(128)} %broadcast_subtract_fusion) | copy-start | bytes 28
  583.1 47.0 %copy-start.104 = (f32[2]{0:T(128)S(1)}, f32[2]{0:T(128)}, u32[]{:S(2)}) copy-start(f32[2]{0:T(128)} %fusion.89) | copy-start | bytes 28
  645.9 153.8 %reduce-scatter.7.cloned.1.call-start = ((), (), s32[]{:S(2)}) async-start(), calls=%async_computation.12 | async-start | bytes 4423680 | tf_op jit(solution)/shard_map/reduce_scatter | solution.py:372
  755.9 43.9 %copy-start.40 = (bf16[768,768]{1,0:T(8,128)(2,1)S(1)}, bf16[768,768]{1,0:T(8,128)(2,1)}, u32[]{:S(2)}) copy-start(bf16[768,768]{1,0:T(8,128)(2,1)} %reduce-scatter.15.cloned.1.call-done) | copy-start | bytes 3538948
  755.9 43.9 %copy-start.41 = (bf16[768,768]{1,0:T(8,128)(2,1)S(1)}, bf16[768,768]{1,0:T(8,128)(2,1)}, u32[]{:S(2)}) copy-start(bf16[768,768]{1,0:T(8,128)(2,1)} %reduce-scatter.17.cloned.1.call-done) | copy-start | bytes 3538948
  755.9 43.8 %copy-start.52 = (bf16[192,768]{1,0:T(8,128)(2,1)S(1)}, bf16[192,768]{1,0:T(8,128)(2,1)}, u32[]{:S(2)}) copy-start(bf16[192,768]{1,0:T(8,128)(2,1)} %reduce-scatter.13.cloned.1.call-done) | copy-start | bytes 884740
  755.9 43.8 %copy-start.69 = (bf16[3,64,64]{2,1,0:T(8,128)(2,1)S(1)}, bf16[3,64,64]{2,1,0:T(8,128)(2,1)}, u32[]{:S(2)}) copy-start(bf16[3,64,64]{2,1,0:T(8,128)(2,1)} %reduce-scatter.9.cloned.1.call-done) | copy-start | bytes 73732
  (109 other events, 516.4 us)
Sparse Core Ops, SparseCore 0:
  9.6 34.6 all-gather.12
  79.2 89.3 all-reduce.21
  170.7 98.5 all-gather.20
  270.7 15.6 all-gather.14
  287.8 37.4 all-gather.16
  326.7 37.4 all-gather.18
  392.6 89.7 all-reduce.23
  484.6 98.4 all-gather.22
  586.1 17.9 reduce-scatter.8
  607.1 25.7 reduce-scatter.12
  635.5 47.8 reduce-scatter.14
  685.8 47.8 reduce-scatter.16
  736.9 19.7 reduce-scatter.10
  759.2 40.4 reduce-scatter.6
where the time goes:
time: 1110 us; the launch traced here: 1090 us
  blocking collectives  487 us (44%)
  waiting for transfers between devices  271 us (24%)
  other arithmetic  116 us (10%)
  local copies, waits for them, and re-layouts  109 us (10%)
  matrix products  89.6 us (8%)
  between operations  19 us (2%)
    psum x1, blocking collectives, body(): lax.psum((shards[0], shards[1], shards[2], shards[3], shards[4], shards[5...  286 us
    all_gather x2, waiting for transfers between devices, prefix(): everything = jax.tree.map(lambda part: lax.all_gather(part, axis), x)  128 us
    all_gather x3, blocking collectives, prefix(): everything = jax.tree.map(lambda part: lax.all_gather(part, axis), x)  86.5 us
    select_n x32, other arithmetic, lap(): return jax.tree.map(lambda a, b: jnp.where(reached, a, b), new, before)  56.6 us
    reduce_scatter x1, waiting for transfers between devices, body(): lax.psum_scatter(g_reduce_full.astype(jnp.bfloat16), 'fsdp', scatter_dime...  50.3 us
    psum x1, blocking collectives, body(): lax.psum((lane_seq_totals(grad_lane_states, lane_hot), lane_seq_totals(gr...  37.6 us
    psum x1, blocking collectives, body(): lax.psum((lane_seq_totals(lane_states, lane_hot), lane_seq_totals(lane_no...  34.9 us
    reduce_scatter x1, waiting for transfers between devices, body(): lax.psum_scatter(g_project_full.astype(jnp.bfloat16), 'fsdp', scatter_dim...  34.4 us
  transfers between devices with their start and end apart: 14, of which 7 were waited for; matrix products, arithmetic and copies ran while one was open for 22% of the time, Pallas kernels for 0%

commit v1 on v0

v1 whole, which is shorter than its diff:
```python
import functools

import jax
import jax.numpy as jnp
from jax import lax
from jax.experimental import pallas as pl
from jax.experimental.pallas import tpu as pltpu
from jax.sharding import PartitionSpec as P

EPS = 1e-05
F32 = jnp.float32
BF16 = jnp.bfloat16
AUG = 80
KEEP = 72
NN = (((1,), (0,)), ((), ()))
NT = (((1,), (1,)), ((), ()))
TN = (((0,), (0,)), ((), ()))
CORE = [(i, i ^ 1) for i in range(4)]
CROSS = [(i, i ^ 2) for i in range(4)]
VMEM = pl.BlockSpec(memory_space=pltpu.VMEM)
SMEM = pl.BlockSpec(memory_space=pltpu.SMEM)


def mm(a, b, dims):
    return lax.dot_general(a, b, dims, preferred_element_type=F32)


def call(kernel, outs, kinds, args, flops, name, scratch=(), aliases=None):
    size = sum(a.size * a.dtype.itemsize for a in args)
    size += sum(o.size * o.dtype.itemsize for o in outs)
    return pl.pallas_call(
        kernel,
        out_shape=outs,
        in_specs=[SMEM if k == "s" else VMEM for k in kinds],
        out_specs=[VMEM] * len(outs),
        scratch_shapes=list(scratch),
        input_output_aliases=aliases or {},
        compiler_params=pltpu.CompilerParams(vmem_limit_bytes=40 << 20),
        cost_estimate=pl.CostEstimate(flops=flops, bytes_accessed=size, transcendentals=0),
        name=name,
    )(*args)


def shaped(shape, dtype=F32):
    return jax.ShapeDtypeStruct(shape, dtype)


def norm_parts(v):
    center = v - jnp.mean(v, axis=-1, keepdims=True)
    scale = lax.rsqrt(jnp.mean(center * center, axis=-1, keepdims=True) + EPS)
    return center * scale, scale


def norm_back(gy, normal, scale, gain):
    a = gy * gain
    return (
        a - jnp.mean(a, axis=-1, keepdims=True)
        - normal * jnp.mean(a * normal, axis=-1, keepdims=True)
    ) * scale


def aug_rows(top, row):
    index = lax.broadcasted_iota(jnp.int32, (AUG - top.shape[0], top.shape[1]), 0)
    tail = jnp.where(index == 0, row, 0.0).astype(BF16)
    return jnp.concatenate([top, tail], axis=0)


def spread_states(total_ref, out_ref, parts, rows_per):
    for part in range(parts):
        out_ref[part] = total_ref[:, part * rows_per : (part + 1) * rows_per, :].astype(BF16)


def collect_states(in_ref, total_ref, parts, rows_per):
    for part in range(parts):
        total_ref[:, part * rows_per : (part + 1) * rows_per, :] = in_ref[part].astype(F32)


def project_kernel(meta, x_ref, p_ref, w0, w1, w2, w3, pb_ref, qkv_ref):
    normal, _ = norm_parts(x_ref[...].astype(F32))
    n = (normal * p_ref[0:1] + p_ref[1:2]).astype(BF16)
    cols = w0.shape[1]
    for j, w in enumerate((w0, w1, w2, w3)):
        out = mm(n, w[...], NN) + pb_ref[j : j + 1]
        start = pl.multiple_of(meta[j] * cols, 64)
        qkv_ref[pl.ds(start, cols), :] = out.astype(BF16).T


def phi(rows_ref, base, map_ref, h):
    rows = rows_ref[pl.ds(pl.multiple_of(base + h * 64, 64), 64), :]
    logits = mm(map_ref[h], rows, TN)
    up = jnp.exp(logits - jnp.max(logits, axis=0, keepdims=True))
    down = jnp.exp(jnp.min(logits, axis=0, keepdims=True) - logits)
    p1 = up / jnp.sum(up, axis=0, keepdims=True)
    p2 = down / jnp.sum(down, axis=0, keepdims=True)
    return p1.astype(BF16), p2.astype(BF16)


def key_kernel(heads, slots, parts, meta, qkv_ref, map_ref, fk_ref, s_ref, total):
    width = heads * 64
    cols = qkv_ref.shape[1] // slots
    rows_per = s_ref.shape[2]
    total[...] = jnp.zeros_like(total)

    def head(h, carry):
        p1, p2 = phi(qkv_ref, width, map_ref, h)
        at = pl.multiple_of(h * 128, 128)
        fk_ref[pl.ds(at, 64), :] = p1
        fk_ref[pl.ds(pl.multiple_of(at + 64, 64), 64), :] = p2
        v = qkv_ref[pl.ds(pl.multiple_of(2 * width + h * 64, 64), 64), :]
        va = aug_rows(v, 1.0)
        fk = jnp.concatenate([p1, p2], axis=0)
        for s in range(slots):
            part = slice(s * cols, (s + 1) * cols)
            state = mm(va[:, part], fk[:, part], NT)
            total[s ^ meta[4], pl.ds(pl.multiple_of(h * KEEP, 8), KEEP), :] = state[:KEEP]
        return carry

    lax.fori_loop(0, heads, head, 0)
    spread_states(total, s_ref, parts, rows_per)


def query_kernel(heads, qkv_ref, map_ref, fq_ref):
    def head(h, carry):
        p1, p2 = phi(qkv_ref, 0, map_ref, h)
        at = pl.multiple_of(h * 128, 128)
        fq_ref[pl.ds(at, 64), :] = p1
        fq_ref[pl.ds(pl.multiple_of(at + 64, 64), 64), :] = p2
        return carry

    lax.fori_loop(0, heads, head, 0)


def scan_kernel(nctx, backward, keep, in_ref, out_ref):
    blocks = 2 * nctx
    order = [(b, 0) if b < nctx else (blocks - 1 - b, 1) for b in range(blocks)]
    acc = jnp.zeros(in_ref.shape[2:], F32)
    for b in reversed(range(blocks)) if backward else range(blocks):
        c, lane = order[b]
        acc = acc * keep[b] + in_ref[c, lane].astype(F32)
        out_ref[c, lane] = acc.astype(BF16)


def fill_output(meta, wo_refs, wo):
    rows = wo_refs[0].shape[0]
    for j, ref in enumerate(wo_refs):
        wo[pl.ds(pl.multiple_of(meta[j] * rows, 64), rows), :] = ref[...]


def attend_kernel(
    heads, slots, parts, meta, c_ref, fq_ref, x_ref, w0, w1, w2, w3, p_ref,
    mixed_ref, den_ref, middle_ref, n2_ref, n2t_ref, total, wo,
):
    cols = fq_ref.shape[1] // slots
    collect_states(c_ref, total, parts, c_ref.shape[2])
    fill_output(meta, (w0, w1, w2, w3), wo)

    def head(h, carry):
        fq = fq_ref[pl.ds(pl.multiple_of(h * 128, 128), 128), :]
        for s in range(slots):
            part = slice(s * cols, (s + 1) * cols)
            c = total[s ^ meta[4], pl.ds(pl.multiple_of(h * KEEP, 8), AUG), :].astype(BF16)
            both = mm(c, fq[:, part], NN)
            den = both[64:65]
            mixed_ref[pl.ds(pl.multiple_of(h * 64, 64), 64), part] = (both[:64] / den).astype(BF16)
            den_ref[pl.ds(pl.multiple_of(h * 8, 8), 8), part] = jnp.broadcast_to(den, (8, cols))
        return carry

    lax.fori_loop(0, heads, head, 0)
    middle = x_ref[...].astype(F32) + mm(mixed_ref[...], wo[...], TN) + p_ref[4:5]
    middle_ref[...] = middle
    normal, _ = norm_parts(middle)
    n2 = (normal * p_ref[2:3] + p_ref[3:4]).astype(BF16)
    n2_ref[...] = n2
    n2t_ref[...] = n2.T


def mlp_kernel(
    tile, n2_ref, n2t_ref, cot_ref, base_ref, back_ref, eb_ref, wea, wra, web, wrb,
    out_ref, dn_ref, gea, gra, geb, grb, gb_ref,
):
    out_ref[...] = base_ref[...]
    dn_ref[...] = back_ref[...]
    for j, (we, wr, ge, gr) in enumerate(((wea, wra, gea, gra), (web, wrb, geb, grb))):

        def step(t, carry):
            at = pl.ds(pl.multiple_of(t * tile, tile), tile)
            w_in = we[:, at]
            w_out = wr[at, :]
            cot = cot_ref[...]
            hidden = mm(n2_ref[...], w_in, NN) + eb_ref[j : j + 1, at]
            square = hidden * hidden
            inner = 0.7978845608028654 * hidden * (1.0 + 0.044715 * square)
            tanh = jnp.tanh(inner)
            half = 0.5 * (1.0 + tanh)
            active = (hidden * half).astype(BF16)
            slope = half + 0.5 * hidden * (1.0 - tanh * tanh) * (
                0.7978845608028654 * (1.0 + 0.134145 * square)
            )
            r_active = mm(cot, w_out, NT).astype(BF16).astype(F32)
            r_hidden32 = (r_active * slope).astype(BF16)
            out_ref[...] += mm(active, w_out, NN)
            dn_ref[...] += mm(r_hidden32, w_in, NT)
            gr[at, :] = mm(active, cot, TN).astype(BF16)
            ge[:, at] = mm(n2t_ref[...], r_hidden32, NN).astype(BF16)
            gb_ref[8 * j : 8 * j + 8, at] = jnp.broadcast_to(
                jnp.sum(r_hidden32.astype(F32), axis=0, keepdims=True), (8, tile)
            )
            return carry

        lax.fori_loop(0, we.shape[1] // tile, step, 0)


def middle_kernel(
    heads, slots, parts, meta, dn_ref, middle_ref, cot_ref, p_ref, mixed_ref, den_ref, fq_ref,
    w0, w1, w2, w3, gm_ref, ratt_ref, raug_ref, g_ref, small_ref, total, wo, rmix,
):
    cols = fq_ref.shape[1] // slots
    fill_output(meta, (w0, w1, w2, w3), wo)
    normal, scale = norm_parts(middle_ref[...])
    gy = dn_ref[...]
    cot = cot_ref[...].astype(F32)
    g_middle = cot + norm_back(gy, normal, scale, p_ref[2:3])
    gm_ref[...] = g_middle
    r_att = g_middle.astype(BF16)
    ratt_ref[...] = r_att
    small_ref[...] = jnp.concatenate(
        [
            jnp.sum(gy * normal, axis=0, keepdims=True),
            jnp.sum(gy, axis=0, keepdims=True),
            jnp.sum(r_att.astype(F32), axis=0, keepdims=True),
            jnp.sum(cot, axis=0, keepdims=True),
            jnp.zeros((4, gy.shape[1]), F32),
        ],
        axis=0,
    )
    rmix[...] = mm(wo[...], r_att, NT).astype(BF16)
    total[...] = jnp.zeros_like(total)

    def head(h, carry):
        rows = pl.ds(pl.multiple_of(h * 64, 64), 64)
        rm = rmix[rows, :].astype(F32)
        inverse = 1.0 / den_ref[pl.ds(pl.multiple_of(h * 8, 8), 8), :][0:1]
        rn = (rm * inverse).astype(BF16)
        rd = -jnp.sum(rm * mixed_ref[rows, :].astype(F32), axis=0, keepdims=True) * inverse
        ra = aug_rows(rn, rd)
        raug_ref[pl.ds(pl.multiple_of(h * AUG, 16), AUG), :] = ra
        fq = fq_ref[pl.ds(pl.multiple_of(h * 128, 128), 128), :]
        for s in range(slots):
            part = slice(s * cols, (s + 1) * cols)
            state = mm(ra[:, part], fq[:, part], NT)
            total[s ^ meta[4], pl.ds(pl.multiple_of(h * KEEP, 8), KEEP), :] = state[:KEEP]
        return carry

    lax.fori_loop(0, heads, head, 0)
    spread_states(total, g_ref, parts, g_ref.shape[2])


def logits_back(p_both, g_both):
    p1, p2 = p_both[:64].astype(F32), p_both[64:].astype(F32)
    g1, g2 = g_both[:64], g_both[64:]
    s1 = jnp.sum(p1 * g1, axis=0, keepdims=True)
    s2 = jnp.sum(p2 * g2, axis=0, keepdims=True)
    return (p1 * (g1 - s1) - p2 * (g2 - s2)).astype(BF16)


def query_back_kernel(
    heads, slots, parts, meta, c_ref, raug_ref, fq_ref, qkv_ref, map_ref, mixed_ref, ratt_ref,
    rq_ref, gmap_ref, g0, g1, g2, g3, total,
):
    cols = fq_ref.shape[1] // slots
    collect_states(c_ref, total, parts, c_ref.shape[2])

    def head(h, carry):
        ra = raug_ref[pl.ds(pl.multiple_of(h * AUG, 16), AUG), :]
        fq = fq_ref[pl.ds(pl.multiple_of(h * 128, 128), 128), :]
        pieces = []
        for s in range(slots):
            part = slice(s * cols, (s + 1) * cols)
            c = total[s ^ meta[4], pl.ds(pl.multiple_of(h * KEEP, 8), AUG), :].astype(BF16)
            pieces.append(mm(c, ra[:, part], TN))
        r_fq = jnp.concatenate(pieces, axis=1).astype(BF16).astype(F32)
        r_l = logits_back(fq, r_fq)
        rows = pl.ds(pl.multiple_of(h * 64, 64), 64)
        rq_ref[rows, :] = mm(map_ref[h], r_l, NN).astype(BF16)
        gmap_ref[h] = mm(qkv_ref[rows, :], r_l, NT)
        return carry

    lax.fori_loop(0, heads, head, 0)
    rows = g0.shape[0]
    for j, g in enumerate((g0, g1, g2, g3)):
        mixed = mixed_ref[pl.ds(pl.multiple_of(meta[j] * rows, 64), rows), :]
        g[...] = mm(mixed, ratt_ref[...], NN).astype(BF16)


def key_back_kernel(
    heads, slots, parts, meta, d_ref, fk_ref, qkv_ref, map_ref, rq_ref, x_ref, p_ref,
    rp_ref, gmap_ref, g0, g1, g2, g3, gpb_ref, total,
):
    width = heads * 64
    cols = fk_ref.shape[1] // slots
    collect_states(d_ref, total, parts, d_ref.shape[2])
    rp_ref[0:width, :] = rq_ref[...]

    def head(h, carry):
        fk = fk_ref[pl.ds(pl.multiple_of(h * 128, 128), 128), :]
        v = qkv_ref[pl.ds(pl.multiple_of(2 * width + h * 64, 64), 64), :]
        va = aug_rows(v, 1.0)
        pieces = []
        for s in range(slots):
            part = slice(s * cols, (s + 1) * cols)
            d = total[s ^ meta[4], pl.ds(pl.multiple_of(h * KEEP, 8), AUG), :].astype(BF16)
            pieces.append(mm(d, va[:, part], TN))
            rv = mm(d[:64], fk[:, part], NN).astype(BF16)
            rp_ref[pl.ds(pl.multiple_of(2 * width + h * 64, 64), 64), part] = rv
        r_fk = jnp.concatenate(pieces, axis=1).astype(BF16).astype(F32)
        r_l = logits_back(fk, r_fk)
        rows = pl.ds(pl.multiple_of(width + h * 64, 64), 64)
        rp_ref[rows, :] = mm(map_ref[h], r_l, NN).astype(BF16)
        gmap_ref[h] = mm(qkv_ref[rows, :], r_l, NT)
        return carry

    lax.fori_loop(0, heads, head, 0)
    normal, _ = norm_parts(x_ref[...].astype(F32))
    nt = (normal * p_ref[0:1] + p_ref[1:2]).astype(BF16).T
    span = g0.shape[1]
    ones = jnp.ones((8, x_ref.shape[0]), BF16)
    for j, g in enumerate((g0, g1, g2, g3)):
        rp = rp_ref[pl.ds(pl.multiple_of(meta[j] * span, 64), span), :]
        g[...] = mm(nt, rp, NT).astype(BF16)
        gpb_ref[8 * j : 8 * j + 8, :] = mm(ones, rp, NT)


def input_kernel(meta, rp_ref, x_ref, p_ref, gm_ref, w0, w1, w2, w3, dx_ref, small_ref):
    span = w0.shape[1]
    back = None
    for j, w in enumerate((w0, w1, w2, w3)):
        rp = rp_ref[pl.ds(pl.multiple_of(meta[j] * span, 64), span), :]
        part = mm(w[...], rp, NN)
        back = part if back is None else back + part
    gy = back.T
    normal, scale = norm_parts(x_ref[...].astype(F32))
    dx_ref[...] = gm_ref[...] + norm_back(gy, normal, scale, p_ref[0:1])
    small_ref[...] = jnp.concatenate(
        [
            jnp.sum(gy * normal, axis=0, keepdims=True),
            jnp.sum(gy, axis=0, keepdims=True),
            jnp.zeros((6, gy.shape[1]), F32),
        ],
        axis=0,
    )


def core_swap(a):
    return lax.ppermute(a, "fsdp", CORE)


def cross_swap(a):
    return lax.ppermute(a, "fsdp", CROSS)


def gather(shard):
    cross = cross_swap(shard)
    return [shard, core_swap(shard), cross, core_swap(cross)]


def add(a, b):
    return (a.astype(F32) + b.astype(F32)).astype(BF16)


def scatter_group(own, core, cross, far):
    far_in = core_swap(far)
    core_in = core_swap(core)
    cross_in = cross_swap(add(cross, far_in))
    return add(add(own, core_in), cross_in)


def sum_ctx(a, nctx, place):
    bits = nctx.bit_length() - 1
    cur = a
    for bit in range(bits):
        half = cur.shape[0] // 2
        mine = (place >> bit) & 1
        pairs = [(i, i ^ (1 << bit)) for i in range(nctx)]
        sent = lax.dynamic_slice_in_dim(cur, (1 - mine) * half, half, 0)
        kept = lax.dynamic_slice_in_dim(cur, mine * half, half, 0)
        cur = add(kept, lax.ppermute(sent, "ctx", pairs))
    for bit in reversed(range(bits)):
        mine = (place >> bit) & 1
        pairs = [(i, i ^ (1 << bit)) for i in range(nctx)]
        other = lax.ppermute(cur, "ctx", pairs)
        first = mine == 0
        cur = jnp.concatenate([jnp.where(first, cur, other), jnp.where(first, other, cur)], axis=0)
    return cur


def exchange(a):
    return lax.all_to_all(a, "ctx", 0, 0, tiled=True)


def straighten(parts, mine):
    a, b, c, d = parts
    odd = (mine & 1) == 1
    upper = (mine & 2) == 2
    a, b = jnp.where(odd, b, a), jnp.where(odd, a, b)
    c, d = jnp.where(odd, d, c), jnp.where(odd, c, d)
    return [
        jnp.where(upper, c, a), jnp.where(upper, d, b),
        jnp.where(upper, a, c), jnp.where(upper, b, d),
    ]


def body(
    tokens, cotangent, pair_table, seq_ids, first_gain, first_shift, project_weight, project_bias,
    feature_query, feature_key, output_weight, output_bias, second_gain, second_shift,
    expand_weight, expand_bias, reduce_weight, reduce_bias,
):
    x = tokens[0]
    cot = cotangent[0]
    rows_n, width = x.shape
    heads = width // feature_query.shape[1]
    own_heads = feature_query.shape[0]
    slots = pair_table.shape[2]
    nctx = lax.axis_size("ctx")
    place = lax.axis_index("ctx")
    mine = lax.axis_index("fsdp")
    span = project_weight.shape[1]
    hidden_own = expand_weight.shape[1]
    shard = width // 4
    wide = heads * 128

    vector = jnp.concatenate(
        [first_gain, first_shift, second_gain, second_shift, output_bias, reduce_bias,
         project_bias, expand_bias]
    )
    pack = jnp.concatenate(
        [feature_query.reshape(-1, 64), feature_key.reshape(-1, 64), vector.reshape(-1, 64)]
    )
    packs = gather(pack)
    projects = gather(project_weight)
    held = lax.optimization_barrier(
        (output_weight, expand_weight, reduce_weight, projects[2])
    )
    outputs = gather(held[0])
    expands = gather(held[1])
    held = lax.optimization_barrier((held[2], expands[2]))
    reduces = gather(held[0])

    map_rows = own_heads * 64
    vectors = [p[2 * map_rows :].reshape(-1) for p in packs]
    ordered = straighten(packs, mine)
    query_map = jnp.concatenate([p[:map_rows] for p in ordered]).reshape(heads, 64, 64)
    key_map = jnp.concatenate([p[map_rows : 2 * map_rows] for p in ordered]).reshape(heads, 64, 64)
    lines = jnp.stack([p[2 * map_rows :].reshape(-1)[: 6 * shard] for p in ordered])
    params = lines.reshape(4, 6, shard).transpose(1, 0, 2).reshape(6, width).astype(F32)
    params = jnp.concatenate([params, jnp.zeros((2, width), F32)])
    project_line = jnp.stack([v[6 * shard : 6 * shard + span] for v in vectors]).astype(F32)
    expand_line = jnp.stack([v[6 * shard + span :] for v in vectors]).astype(F32)

    positions = pair_table[0, 0]
    swap = (positions[0] > positions[1]).astype(jnp.int32)
    meta = jnp.stack([mine, mine ^ 1, mine ^ 2, mine ^ 3, swap]).astype(jnp.int32)
    ids = seq_ids[0]
    same = (ids[1:] == ids[:-1]).astype(F32)
    none = jnp.zeros((1,), F32)
    keep = jnp.concatenate([none, same])
    keep_next = jnp.concatenate([same, none])

    rows_per = -(-(heads * KEEP) // (nctx * 16)) * 16
    state_shape = shaped((nctx, slots, rows_per, 128), BF16)
    total = pltpu.VMEM((slots, nctx * rows_per, 128), F32)
    wo_scratch = pltpu.VMEM((width, width), BF16)
    dense = 2 * rows_n * width * width

    (qkv,) = call(
        project_kernel, [shaped((3 * width, rows_n), BF16)], "svvvvvvv",
        [meta, x, params, *projects, project_line], 3 * dense, "project",
    )
    fk, states = call(
        functools.partial(key_kernel, heads, slots, nctx),
        [shaped((wide, rows_n), BF16), state_shape], "svv", [meta, qkv, key_map], dense // 4, "keys",
        [total],
    )
    arrived = exchange(states)
    (fq,) = call(
        functools.partial(query_kernel, heads), [shaped((wide, rows_n), BF16)], "vv",
        [qkv, query_map], dense // 4, "queries",
    )
    (running,) = call(
        functools.partial(scan_kernel, nctx, False), [state_shape], "sv", [keep, arrived], 0, "scan",
    )
    carried = exchange(running)
    mixed, den, middle, n2, n2t = call(
        functools.partial(attend_kernel, heads, slots, nctx),
        [shaped((width, rows_n), BF16), shaped((heads * 8, rows_n)), shaped((rows_n, width)),
         shaped((rows_n, width), BF16), shaped((width, rows_n), BF16)],
        "svvvvvvvv", [meta, carried, fq, x, *outputs, params], dense * 2, "attend",
        [total, wo_scratch],
    )

    def mlp(base, back, a, b, name):
        lines = jnp.concatenate([expand_line[a : a + 1], expand_line[b : b + 1]])
        grad = shaped((width, hidden_own), BF16)
        grad_t = shaped((hidden_own, width), BF16)
        return call(
            functools.partial(mlp_kernel, 256),
            [shaped((rows_n, width)), shaped((rows_n, width)), grad, grad_t, grad, grad_t,
             shaped((16, hidden_own))],
            "vvvvvvvvvv",
            [n2, n2t, cot, base, back, lines, expands[a], reduces[a], expands[b], reduces[b]],
            12 * dense, name,
        )

    base = middle + params[5:6]
    out1, dn1, ge2, gr2, ge3, gr3, gb23 = mlp(base, jnp.zeros_like(base), 2, 3, "mlp_far")
    layer_out, dn2, ge0, gr0, ge1, gr1, gb01 = mlp(out1, dn1, 0, 1, "mlp_near")

    g_middle, r_att, raug, g_states, small_two = call(
        functools.partial(middle_kernel, heads, slots, nctx),
        [shaped((rows_n, width)), shaped((rows_n, width), BF16), shaped((heads * AUG, rows_n), BF16),
         state_shape, shaped((8, width))],
        "svvvvvvvvvvv", [meta, dn2, middle, cot, params, mixed, den, fq, *outputs], dense * 2, "middle",
        [total, wo_scratch, pltpu.VMEM((width, rows_n), BF16)],
    )
    g_arrived = exchange(g_states)
    rq, g_query_map, go0, go1, go2, go3 = call(
        functools.partial(query_back_kernel, heads, slots, nctx),
        [shaped((width, rows_n), BF16), shaped((heads, 64, 64))] + [shaped((shard, width), BF16)] * 4,
        "svvvvvvv", [meta, carried, raug, fq, qkv, query_map, mixed, r_att], dense * 2, "query_back",
        [total],
    )
    (g_running,) = call(
        functools.partial(scan_kernel, nctx, True), [state_shape], "sv", [keep_next, g_arrived], 0,
        "scan_back",
    )
    g_carried = exchange(g_running)
    rp, g_key_map, gp0, gp1, gp2, gp3, gpb = call(
        functools.partial(key_back_kernel, heads, slots, nctx),
        [shaped((3 * width, rows_n), BF16), shaped((heads, 64, 64))]
        + [shaped((width, span), BF16)] * 4 + [shaped((32, span))],
        "svvvvvvv", [meta, g_carried, fk, qkv, key_map, rq, x, params], dense * 4, "key_back",
        [total],
    )
    dx, small_one = call(
        input_kernel, [shaped((rows_n, width)), shaped((8, width))], "svvvvvvvv",
        [meta, rp, x, params, g_middle, *projects], dense * 3, "input",
    )

    g_expand = sum_ctx(scatter_group(ge0, ge1, ge2, ge3), nctx, place)
    g_reduce = sum_ctx(scatter_group(gr0, gr1, gr2, gr3), nctx, place)
    g_project = sum_ctx(scatter_group(gp0, gp1, gp2, gp3), nctx, place)

    lines = jnp.concatenate([small_one[:2], small_two[:4]]).reshape(6, 4, shard)
    lines = lines.transpose(1, 0, 2).reshape(4, 6 * shard)
    maps = jnp.concatenate(
        [g_query_map.reshape(4, -1), g_key_map.reshape(4, -1)], axis=1
    )
    tail = jnp.concatenate([lines, maps], axis=1)
    tail = straighten([tail[i] for i in range(4)], mine)
    bias_e = [gb01[0], gb01[8], gb23[0], gb23[8]]
    block_rows = 256
    blocks = []
    for j, go in enumerate((go0, go1, go2, go3)):
        flat = jnp.concatenate([tail[j], gpb[8 * j], bias_e[j]]).astype(BF16)
        room = (block_rows - shard) * width - flat.shape[0]
        flat = jnp.concatenate([flat, jnp.zeros((room,), BF16)]).reshape(-1, width)
        blocks.append(jnp.concatenate([go, flat]))
    rest = sum_ctx(scatter_group(*blocks), nctx, place)
    g_output = rest[:shard]
    flat = rest[shard:].reshape(-1).astype(F32)
    pieces = []
    at = 0
    for size in (shard,) * 6 + (own_heads * 4096,) * 2 + (span, hidden_own):
        pieces.append(flat[at : at + size])
        at += size
    g1, s1, g2, s2, bo, br, mq, mk, pb, eb = pieces
    return (
        layer_out[None], dx[None], g1, s1, g_project.astype(F32), pb,
        mq.reshape(own_heads, 64, 64), mk.reshape(own_heads, 64, 64), g_output.astype(F32), bo,
        g2, s2, g_expand.astype(F32), eb, g_reduce.astype(F32), br,
    )


def solution(mesh):
    row = P("fsdp", "ctx", None)
    vec = P("fsdp")
    maps = P("fsdp", None, None)
    in_specs = (
        row, row, row, P("fsdp", None), vec, vec, P(None, "fsdp"), vec, maps, maps,
        P("fsdp", None), vec, vec, vec, P(None, "fsdp"), vec, P("fsdp", None), vec,
    )
    out_specs = (
        row, row, vec, vec, P(None, "fsdp"), vec, maps, maps, P("fsdp", None), vec, vec, vec,
        P(None, "fsdp"), vec, P("fsdp", None), vec,
    )
    return jax.shard_map(body, mesh=mesh, in_specs=in_specs, out_specs=out_specs, check_vma=False)
```

time: 1110 us -> 451 us (0.41)
  blocking collectives: 487 us -> 19.7 us
  waiting for transfers between devices: 271 us -> 152 us
  matrix products: 89.6 us -> 0 us
  other arithmetic: 116 us -> 37.4 us
  Pallas kernels: 0 us -> 76.2 us
  starting transfers between devices: 1.35 us -> 53.3 us
  between operations: 19 us -> 3.61 us
    psum x3 -> x0, blocking collectives: 359 us -> none  [the longest x1 286 us: body(): lax.psum((shards[0], shards[1], shards[2], shards[3], shards[4], shards[5...]
    all_gather x6 -> x0, waiting for transfers between devices: 152 us -> none  [the longest x2 128 us: prefix(): everything = jax.tree.map(lambda part: lax.all_gather(part, axis), x)]
    ppermute x0 -> x51, waiting for transfers between devices: none -> 139 us  [the longest x9 75.5 us: cross_swap(): return lax.ppermute(a, 'fsdp', CROSS)]
    reduce_scatter x6 -> x0, waiting for transfers between devices: 114 us -> none  [the longest x1 50.3 us: body(): lax.psum_scatter(g_reduce_full.astype(jnp.bfloat16), 'fsdp', scatter_dime...]
    all_gather x6 -> x0, blocking collectives: 104 us -> none  [the longest x3 86.5 us: prefix(): everything = jax.tree.map(lambda part: lax.all_gather(part, axis), x)]
    dot_general x24 -> x0, matrix products: 82.4 us -> none  [the longest x4 23.8 us: contract_rows(): lax.dot_general(left, right, (((0,), (0,)), ((), ())), preferred_element_...]
    pallas_call x0 -> x12, Pallas kernels: none -> 76.2 us  [call(): pl.pallas_call(kernel, out_shape=outs, in_specs=[SMEM if k == 's' else VM...]
    select_n x33 -> x13, other arithmetic: 56.6 us -> 3.16 us  [the longest x12 2.02 us: sum_ctx(): jnp.where(first, cur, other)]
  transfers between devices with their start and end apart: 14 -> 54, of which waited for: 7 -> 20; matrix products, arithmetic and copies ran while one was open for 22% -> 20% of each run, Pallas kernels for 0% -> 13%
where the time goes in v1:
time: 451 us; the launch traced here: 444 us
  waiting for transfers between devices  152 us (34%)
  local copies, waits for them, and re-layouts  102 us (23%)
  Pallas kernels  76.2 us (17%)
  starting transfers between devices  53.3 us (12%)
  other arithmetic  37.4 us (8%)
  blocking collectives  19.7 us (4%)
    pallas_call x12, Pallas kernels, call(): pl.pallas_call(kernel, out_shape=outs, in_specs=[SMEM if k == 's' else VM...  76.2 us
    ppermute x9, waiting for transfers between devices, cross_swap(): return lax.ppermute(a, 'fsdp', CROSS)  75.5 us
    unnamed x196, local copies, waits for them, and re-layouts  50.7 us
    ppermute x12, waiting for transfers between devices, sum_ctx(): cur = add(kept, lax.ppermute(sent, 'ctx', pairs))  37 us
    ppermute x12, waiting for transfers between devices, sum_ctx(): other = lax.ppermute(cur, 'ctx', pairs)  26 us
    convert_element_type x20, other arithmetic, add(): return (a.astype(F32) + b.astype(F32)).astype(BF16)  20.7 us
    all_to_all x1, blocking collectives, exchange(): return lax.all_to_all(a, 'ctx', 0, 0, tiled=True)  19.7 us
    ppermute x12, starting transfers between devices, sum_ctx(): cur = add(kept, lax.ppermute(sent, 'ctx', pairs))  16.9 us
  transfers between devices with their start and end apart: 54, of which 20 were waited for; matrix products, arithmetic and copies ran while one was open for 20% of the time, Pallas kernels for 13%

profile of v1, /device:TPU:0, one launch (start us, length us, event | category | flops | bytes accessed | tf_op | source)
XLA Modules:
  0.0 443.6 jit_solution(10927491371106737636)
XLA Ops:
  0.7 3.0 collective-permute-start.4
  3.7 19.9 %collective-permute-done.4 = bf16[768,576]{0,1:T(8,128)(2,1)S(1)} collective-permute-done((bf16[768,576]{0,1:T(8,128)(2,1)}, bf16[768,576]{0,1:T(8,128)(2,1)S(1)}, u32[]{:S(2)}, u32[]{:S(2)}) %collective-permute-start.4) | collective-permute-done | bytes 884768 | tf_op jit(solution)/shard_map/ppermute | solution.py:358
  25.3 5.5 %concatenate.111 = bf16[2496]{0:T(1024)(128)(2,1)S(1)} concatenate(bf16[192]{0:T(256)(128)(2,1)} %param.22, bf16[192]{0:T(256)(128)(2,1)} %param.23, bf16[192]{0:T(256)(128)(2,1)} %param.30, bf16[192]{0:T(256)(128)(2,1)} %param.31, bf16[192]{0:T(256)(128)(2,1)} %param.29, bf16[192]{0:T(256)(128)(2,1)} %param.35, bf16[576]{0:T(1024)(128)(2,1)} %param.25, bf16[768]{0:T(1024)(128)(2,1)} %param.33), dimensions={0} | concatenate | bytes 9984 | tf_op jit(solution)/shard_map/concatenate | solution.py:431
  32.5 20.7 %collective-permute-done = bf16[423,64]{1,0:T(8,128)(2,1)S(1)} collective-permute-done((bf16[423,64]{1,0:T(8,128)(2,1)S(1)}, bf16[423,64]{1,0:T(8,128)(2,1)S(1)}, u32[]{:S(2)}, u32[]{:S(2)}) %collective-permute-start) | collective-permute-done | bytes 54176 | tf_op jit(solution)/shard_map/ppermute | solution.py:358
  79.9 3.6 project.1.qkv_ref
  83.5 5.8 %keys.1 = (bf16[1536,512]{1,0:T(8,128)(2,1)S(1)}, bf16[8,2,112,128]{3,2,1,0:T(8,128)(2,1)S(1)}) custom-call(s32[5]{0:T(128)S(1)} %stack.72.meta, bf16[2304,512]{1,0:T(8,128)(2,1)S(1)} %project.1.qkv_ref, bf16[12,64,64]{2,1,0:T(8,128)(2,1)S(1)} %bitcast.29), custom_call_target="tpu_custom_call" | custom-call | flops 150994944 | bytes 4489236 | tf_op jit(solution)/shard_map/keys/pallas_call | solution.py:31
  91.2 6.0 %all-to-all-start = ((bf16[8,2,112,128]{3,2,1,0:T(8,128)(2,1)}), bf16[8,2,112,128]{3,2,1,0:T(8,128)(2,1)}, u32[]{:S(2)}, u32[]{:S(2)}) async-start(bf16[8,2,112,128]{3,2,1,0:T(8,128)(2,1)} %copy-done.42), calls=%async_computation | async-start | bytes 917504 | tf_op jit(solution)/shard_map/all_to_all | solution.py:397
  97.4 12.9 %all-to-all-done.in_ref = bf16[8,2,112,128]{3,2,1,0:T(8,128)(2,1)} async-done(((bf16[8,2,112,128]{3,2,1,0:T(8,128)(2,1)}), bf16[8,2,112,128]{3,2,1,0:T(8,128)(2,1)}, u32[]{:S(2)}, u32[]{:S(2)}) %all-to-all-start) | async-done | bytes 458784 | tf_op jit(solution)/shard_map/all_to_all | solution.py:397
  112.2 4.3 all-to-all-start.1
  121.5 4.9 %collective-permute-done.7.w2 = bf16[192,768]{1,0:T(8,128)(2,1)} collective-permute-done((bf16[192,768]{1,0:T(8,128)(2,1)}, bf16[192,768]{1,0:T(8,128)(2,1)}, u32[]{:S(2)}, u32[]{:S(2)}) %collective-permute-start.7) | collective-permute-done | bytes 294944 | tf_op jit(solution)/shard_map/ppermute | solution.py:358
  129.2 3.2 queries.1.fq_ref
  140.5 4.7 %attend.1 = (bf16[768,512]{1,0:T(8,128)(2,1)S(1)}, f32[96,512]{1,0:T(8,128)S(1)}, f32[512,768]{1,0:T(8,128)S(1)}, bf16[512,768]{1,0:T(8,128)(2,1)S(1)}, bf16[768,512]{1,0:T(8,128)(2,1)S(1)}) custom-call(s32[5]{0:T(128)S(1)} %stack.72.meta, bf16[8,2,112,128]{3,2,1,0:T(8,128)(2,1)} %all-to-all-done.1.c_ref, bf16[1536,512]{1,0:T(8,128)(2,1)S(1)} %copy-done.1, ...), custom_call_target="tpu_custom_call" | custom-call | flops 1207959552 | bytes 8151060 | tf_op jit(solution)/shard_map/attend/pallas_call | solution.py:31
  148.3 14.7 %mlp_far.1 = (f32[512,768]{1,0:T(8,128)S(1)}, f32[512,768]{1,0:T(8,128)}, bf16[768,768]{1,0:T(8,128)(2,1)S(1)}, bf16[768,768]{1,0:T(8,128)(2,1)S(1)}, bf16[768,7...) custom-call(bf16[512,768]{1,0:T(8,128)(2,1)S(1)} %get-tuple-element.63.n2_ref, ...), custom_call_target="tpu_custom_call" | custom-call | flops 7247757312 | bytes 18143232 | tf_op jit(solution)/shard_map/mlp_far/pallas_call | solution.py:31
  171.2 14.8 %mlp_near.1 = (f32[512,768]{1,0:T(8,128)}, f32[512,768]{1,0:T(8,128)S(1)}, bf16[768,768]{1,0:T(8,128)(2,1)S(1)}, bf16[768,768]{1,0:T(8,128)(2,1)S(1)}, bf16[768,...) custom-call(bf16[512,768]{1,0:T(8,128)(2,1)S(1)} %copy-done.82, ...), custom_call_target="tpu_custom_call" | custom-call | flops 7247757312 | bytes 18143232 | tf_op jit(solution)/shard_map/mlp_near/pallas_call | solution.py:31
  189.0 5.3 %middle.1 = (f32[512,768]{1,0:T(8,128)S(1)}, bf16[512,768]{1,0:T(8,128)(2,1)S(1)}, bf16[960,512]{1,0:T(8,128)(2,1)S(1)}, bf16[8,2,112,128]{3,2,1,0:T(8,128)(2,1)S(1)}, f32[8,768]{1,0:T(8,128)S(1)}) custom-call(s32[5]{0:T(128)S(1)} %stack.72.meta, f32[512,768]{1,0:T(8,128)S(1)} %get-tuple-element.72.dn_ref, f32[512,768]{1,0:T(8,128)S(1)} %get-tuple-element.65.middle_ref, ...), custom_call_target="tpu_custom_call" | custom-call | flops 1207959552 | bytes 11517972 | tf_op jit(solution)/shard_map/middle/pallas_call | solution.py:31
  196.5 19.7 %all_to_all.20.in_ref = bf16[8,2,112,128]{3,2,1,0:T(8,128)(2,1)S(1)} all-to-all(bf16[8,2,112,128]{3,2,1,0:T(8,128)(2,1)S(1)} %get-tuple-element.75), channel_id=1, replica_groups=mesh['ctx'=8,'fsdp'=4] {'ctx'}, dimensions={0} | all-to-all | bytes 917504 | tf_op jit(solution)/shard_map/all_to_all | solution.py:397
  217.6 4.1 all-to-all-start.3
  228.6 6.9 %query_back.1 = (bf16[768,512]{1,0:T(8,128)(2,1)S(1)}, f32[12,64,64]{2,1,0:T(8,128)S(1)}, bf16[192,768]{1,0:T(8,128)(2,1)S(1)}, bf16[192,768]{1,0:T(8,128)(2,1)S...) custom-call(s32[5]{0:T(128)S(1)} %stack.72.meta, bf16[8,2,112,128]{3,2,1,0:T(8,128)(2,1)} %all-to-all-done.1.c_ref, ...), custom_call_target="tpu_custom_call" | custom-call | flops 1207959552 | bytes 9207828 | tf_op jit(solution)/shard_map/query_back/pallas_call | solution.py:31
  249.4 10.3 %key_back.1 = (bf16[2304,512]{1,0:T(8,128)(2,1)S(1)}, f32[12,64,64]{2,1,0:T(8,128)S(1)}, bf16[768,576]{1,0:T(8,128)(2,1)S(1)}, bf16[768,576]{1,0:T(8,128)(2,1)S(...) custom-call(s32[5]{0:T(128)S(1)} %stack.72.meta, ...), custom_call_target="tpu_custom_call" | custom-call | flops 2415919104 | bytes 12255252 | tf_op jit(solution)/shard_map/key_back/pallas_call | solution.py:31
  260.7 5.2 %input.1 = (f32[512,768]{1,0:T(8,128)}, f32[8,768]{1,0:T(8,128)S(1)}) custom-call(s32[5]{0:T(128)S(1)} %stack.72.meta, bf16[2304,512]{1,0:T(8,128)(2,1)S(1)} %get-tuple-element.80.rp_ref, bf16[512,768]{1,0:T(8,128)(2,1)S(1)} %bitcast.23, f32[8,768]{1,0:T(8,128)S(1)} %copy-done.48, f32[512,768]{1,0:T(8,128)S(1)} %copy-done.18, bf16[768,576]{1,0:T(8,128)(2,1)S(1)} %copy.48.w0, ...), custom_call_target="tpu_custom_call" | custom-call | flops 1811939328 | bytes 9879572 | tf_op jit(solution)/shard_map/input/pallas_call | solution.py:31
  286.7 23.6 %collective-permute-done.17 = bf16[256,768]{1,0:T(8,128)(2,1)} collective-permute-done((bf16[256,768]{1,0:T(8,128)(2,1)}, bf16[256,768]{1,0:T(8,128)(2,1)}, u32[]{:S(2)}, u32[]{:S(2)}) %collective-permute-start.17) | collective-permute-done | bytes 393248 | tf_op jit(solution)/shard_map/ppermute | solution.py:358
  316.2 3.0 collective-permute-done.18
  328.3 6.4 %collective-permute-done.35 = bf16[768,768]{1,0:T(8,128)(2,1)S(1)} collective-permute-done((bf16[768,768]{1,0:T(8,128)(2,1)}, bf16[768,768]{1,0:T(8,128)(2,1)S(1)}, u32[]{:S(2)}, u32[]{:S(2)}) %collective-permute-start.35) | collective-permute-done | bytes 1179680 | tf_op jit(solution)/shard_map/ppermute | solution.py:358
  336.5 2.8 collective-permute-start.21
  376.1 8.8 %collective-permute-done.47 = bf16[96,768]{1,0:T(8,128)(2,1)} collective-permute-done((bf16[96,768]{1,0:T(8,128)(2,1)}, bf16[96,768]{1,0:T(8,128)(2,1)}, u32[]{:S(2)}, u32[]{:S(2)}) %collective-permute-start.47) | collective-permute-done | bytes 147488 | tf_op jit(solution)/shard_map/ppermute | solution.py:386
  392.3 3.3 collective-permute-done.39
  398.0 4.3 collective-permute-done.49
  403.1 7.5 %collective-permute-done.28 = bf16[192,576]{1,0:T(8,128)(2,1)S(1)} collective-permute-done((bf16[192,576]{1,0:T(8,128)(2,1)S(1)}, bf16[192,576]{1,0:T(8,128)(2,1)S(1)}, u32[]{:S(2)}, u32[]{:S(2)}) %collective-permute-start.28) | collective-permute-done | bytes 221216 | tf_op jit(solution)/shard_map/ppermute | solution.py:386
  410.9 8.9 %collective-permute-done.29 = bf16[96,576]{1,0:T(8,128)(2,1)S(1)} collective-permute-done((bf16[96,576]{1,0:T(8,128)(2,1)S(1)}, bf16[96,576]{1,0:T(8,128)(2,1)S(1)}, u32[]{:S(2)}, u32[]{:S(2)}) %collective-permute-start.29) | collective-permute-done | bytes 110624 | tf_op jit(solution)/shard_map/ppermute | solution.py:386
  420.5 5.2 %collective-permute-done.30 = bf16[96,576]{1,0:T(8,128)(2,1)S(1)} collective-permute-done((bf16[96,576]{1,0:T(8,128)(2,1)S(1)}, bf16[96,576]{1,0:T(8,128)(2,1)S(1)}, u32[]{:S(2)}, u32[]{:S(2)}) %collective-permute-start.30) | collective-permute-done | bytes 110624 | tf_op jit(solution)/shard_map/ppermute | solution.py:390
  426.1 5.9 %collective-permute-done.31 = bf16[192,576]{1,0:T(8,128)(2,1)S(1)} collective-permute-done((bf16[192,576]{1,0:T(8,128)(2,1)S(1)}, bf16[192,576]{1,0:T(8,128)(2,1)S(1)}, u32[]{:S(2)}, u32[]{:S(2)}) %collective-permute-start.31) | collective-permute-done | bytes 221216 | tf_op jit(solution)/shard_map/ppermute | solution.py:390
  436.2 4.9 %collective-permute-done.32 = bf16[384,576]{1,0:T(8,128)(2,1)S(1)} collective-permute-done((bf16[384,576]{1,0:T(8,128)(2,1)S(1)}, bf16[384,576]{1,0:T(8,128)(2,1)S(1)}, u32[]{:S(2)}, u32[]{:S(2)}) %collective-permute-start.32) | collective-permute-done | bytes 442400 | tf_op jit(solution)/shard_map/ppermute | solution.py:390
  (433 shorter events, 180.0 us)
Async XLA Ops:
  0.7 22.9 %collective-permute-start.4 = (bf16[768,576]{0,1:T(8,128)(2,1)}, bf16[768,576]{0,1:T(8,128)(2,1)S(1)}, u32[]{:S(2)}, u32[]{:S(2)}) collective-permute-start(bf16[768,576]{0,1:T(8,128)(2,1)} %param.24), channel_id=1, source_target_pairs={{0,2},{1,3},{2,0},{3,1},{4,6},{5,7},{6,4},{7,5},{8,10},{9,11},{10,... | collective-permute-start | bytes 2654216 | tf_op jit(solution)/shard_map/ppermute | solution.py:358
  23.5 41.3 %collective-permute-start.9 = (bf16[768,768]{1,0:T(8,128)(2,1)}, bf16[768,768]{1,0:T(8,128)(2,1)S(1)}, u32[]{:S(2)}, u32[]{:S(2)}) collective-permute-start(bf16[768,768]{1,0:T(8,128)(2,1)} %wea), channel_id=1, source_target_pairs={{0,2},{1,3},{2,0},{3,1},{4,6},{5,7},{6,4},{7,5},{8,10},{9,11},{10,... | collective-permute-start | bytes 3538952 | tf_op jit(solution)/shard_map/ppermute | solution.py:358
  31.7 21.6 %collective-permute-start = (bf16[423,64]{1,0:T(8,128)(2,1)S(1)}, bf16[423,64]{1,0:T(8,128)(2,1)S(1)}, u32[]{:S(2)}, u32[]{:S(2)}) collective-permute-start(bf16[423,64]{1,0:T(8,128)(2,1)S(1)} %pad_maximum_fusion.12), channel_id=1, source_target_pairs={{0,2},{1,3},{2,0},{3,1},{4,6},{5,7},{6,4},{7,5},{8,10},{9,11},{10,... | collective-permute-start | bytes 162440 | tf_op jit(solution)/shard_map/ppermute | solution.py:358
  32.0 27.4 %collective-permute-start.2 = (bf16[423,64]{1,0:T(8,128)(2,1)S(1)}, bf16[423,64]{1,0:T(8,128)(2,1)S(1)}, u32[]{:S(2)}, u32[]{:S(2)}) collective-permute-start(bf16[423,64]{1,0:T(8,128)(2,1)S(1)} %pad_maximum_fusion.12), channel_id=1, source_target_pairs={{0,1},{1,0},{2,3},{3,2},{4,5},{5,4},{6,7},{7,6},{8,9},{9,8},{10,11... | collective-permute-start | bytes 162440 | tf_op jit(solution)/shard_map/ppermute | solution.py:354
  32.0 38.0 %collective-permute-start.3 = (bf16[768,576]{0,1:T(8,128)(2,1)}, bf16[768,576]{0,1:T(8,128)(2,1)}, u32[]{:S(2)}, u32[]{:S(2)}) collective-permute-start(bf16[768,576]{0,1:T(8,128)(2,1)} %param.24), channel_id=1, source_target_pairs={{0,1},{1,0},{2,3},{3,2},{4,5},{5,4},{6,7},{7,6},{8,9},{9,8},{10,11... | collective-permute-start | bytes 2654216 | tf_op jit(solution)/shard_map/ppermute | solution.py:354
  64.9 51.7 %collective-permute-start.10 = (bf16[768,768]{1,0:T(8,128)(2,1)}, bf16[768,768]{1,0:T(8,128)(2,1)}, u32[]{:S(2)}, u32[]{:S(2)}) collective-permute-start(bf16[768,768]{1,0:T(8,128)(2,1)} %wra), channel_id=1, source_target_pairs={{0,2},{1,3},{2,0},{3,1},{4,6},{5,7},{6,4},{7,5},{8,10},{9,11},{10,... | collective-permute-start | bytes 3538952 | tf_op jit(solution)/shard_map/ppermute | solution.py:358
  91.2 19.1 %all-to-all-start = ((bf16[8,2,112,128]{3,2,1,0:T(8,128)(2,1)}), bf16[8,2,112,128]{3,2,1,0:T(8,128)(2,1)}, u32[]{:S(2)}, u32[]{:S(2)}) async-start(bf16[8,2,112,128]{3,2,1,0:T(8,128)(2,1)} %copy-done.42), calls=%async_computation | async-start | bytes 917504 | tf_op jit(solution)/shard_map/all_to_all | solution.py:397
  112.2 22.1 %all-to-all-start.1 = ((bf16[8,2,112,128]{3,2,1,0:T(8,128)(2,1)}), bf16[8,2,112,128]{3,2,1,0:T(8,128)(2,1)}, u32[]{:S(2)}, u32[]{:S(2)}) async-start(bf16[8,2,112,128]{3,2,1,0:T(8,128)(2,1)} %copy-done.15), calls=%async_computation.1 | async-start | bytes 917504 | tf_op jit(solution)/shard_map/all_to_all | solution.py:397
  116.5 30.0 %collective-permute-start.11 = (bf16[768,768]{1,0:T(8,128)(2,1)}, bf16[768,768]{1,0:T(8,128)(2,1)}, u32[]{:S(2)}, u32[]{:S(2)}) collective-permute-start(bf16[768,768]{1,0:T(8,128)(2,1)} %copy-done.76), channel_id=1, source_target_pairs={{0,1},{1,0},{2,3},{3,2},{4,5},{5,4},{6,7},{7,6},{8,9},{9,8},{10,11... | collective-permute-start | bytes 3538952 | tf_op jit(solution)/shard_map/ppermute | solution.py:354
  116.6 29.9 %collective-permute-start.12 = (bf16[768,768]{1,0:T(8,128)(2,1)}, bf16[768,768]{1,0:T(8,128)(2,1)}, u32[]{:S(2)}, u32[]{:S(2)}) collective-permute-start(bf16[768,768]{1,0:T(8,128)(2,1)} %collective-permute-done.10.wra), channel_id=1, source_target_pairs={{0,1},{1,0},{2,3},{3,2},{4,5},{5,4},{6,7},{7,6},{8,9},{9,8},{10,11... | collective-permute-start | bytes 3538952 | tf_op jit(solution)/shard_map/ppermute | solution.py:354
  127.0 41.9 %collective-permute-start.13 = (bf16[768,768]{1,0:T(8,128)(2,1)}, bf16[768,768]{1,0:T(8,128)(2,1)}, u32[]{:S(2)}, u32[]{:S(2)}) collective-permute-start(bf16[768,768]{1,0:T(8,128)(2,1)} %wea), channel_id=1, source_target_pairs={{0,1},{1,0},{2,3},{3,2},{4,5},{5,4},{6,7},{7,6},{8,9},{9,8},{10,11... | collective-permute-start | bytes 3538952 | tf_op jit(solution)/shard_map/ppermute | solution.py:354
  128.3 40.6 %collective-permute-start.14 = (bf16[768,768]{1,0:T(8,128)(2,1)}, bf16[768,768]{1,0:T(8,128)(2,1)}, u32[]{:S(2)}, u32[]{:S(2)}) collective-permute-start(bf16[768,768]{1,0:T(8,128)(2,1)} %wra), channel_id=1, source_target_pairs={{0,1},{1,0},{2,3},{3,2},{4,5},{5,4},{6,7},{7,6},{8,9},{9,8},{10,11... | collective-permute-start | bytes 3538952 | tf_op jit(solution)/shard_map/ppermute | solution.py:354
  217.6 26.4 %all-to-all-start.3 = ((bf16[8,2,112,128]{3,2,1,0:T(8,128)(2,1)}), bf16[8,2,112,128]{3,2,1,0:T(8,128)(2,1)}, u32[]{:S(2)}, u32[]{:S(2)}) async-start(bf16[8,2,112,128]{3,2,1,0:T(8,128)(2,1)} %copy-done.16), calls=%async_computation.3 | async-start | bytes 917504 | tf_op jit(solution)/shard_map/all_to_all | solution.py:397
  221.8 48.4 %collective-permute-start.43 = (bf16[768,768]{1,0:T(8,128)(2,1)}, bf16[768,768]{1,0:T(8,128)(2,1)}, u32[]{:S(2)}, u32[]{:S(2)}) collective-permute-start(bf16[768,768]{1,0:T(8,128)(2,1)} %copy-done.78), channel_id=1, source_target_pairs={{0,1},{1,0},{2,3},{3,2},{4,5},{5,4},{6,7},{7,6},{8,9},{9,8},{10,11... | collective-permute-start | bytes 3538952 | tf_op jit(solution)/shard_map/ppermute | solution.py:354
  221.9 89.8 %collective-permute-start.42 = (bf16[768,768]{1,0:T(8,128)(2,1)}, bf16[768,768]{1,0:T(8,128)(2,1)}, u32[]{:S(2)}, u32[]{:S(2)}) collective-permute-start(bf16[768,768]{1,0:T(8,128)(2,1)} %copy-done.74), channel_id=1, source_target_pairs={{0,1},{1,0},{2,3},{3,2},{4,5},{5,4},{6,7},{7,6},{8,9},{9,8},{10,11... | collective-permute-start | bytes 3538952 | tf_op jit(solution)/shard_map/ppermute | solution.py:354
  222.4 57.8 %collective-permute-start.34 = (bf16[768,768]{1,0:T(8,128)(2,1)}, bf16[768,768]{1,0:T(8,128)(2,1)}, u32[]{:S(2)}, u32[]{:S(2)}) collective-permute-start(bf16[768,768]{1,0:T(8,128)(2,1)} %copy-done.75), channel_id=1, source_target_pairs={{0,1},{1,0},{2,3},{3,2},{4,5},{5,4},{6,7},{7,6},{8,9},{9,8},{10,11... | collective-permute-start | bytes 3538952 | tf_op jit(solution)/shard_map/ppermute | solution.py:354
  272.8 39.4 %collective-permute-start.44 = (bf16[768,768]{1,0:T(8,128)(2,1)}, bf16[768,768]{1,0:T(8,128)(2,1)}, u32[]{:S(2)}, u32[]{:S(2)}) collective-permute-start(bf16[768,768]{1,0:T(8,128)(2,1)} %add_convert_fusion.1), channel_id=1, source_target_pairs={{0,2},{1,3},{2,0},{3,1},{4,6},{5,7},{6,4},{7,5},{8,10},{9,11},{10,... | collective-permute-start | bytes 3538952 | tf_op jit(solution)/shard_map/ppermute | solution.py:358
  278.7 31.6 %collective-permute-start.17 = (bf16[256,768]{1,0:T(8,128)(2,1)}, bf16[256,768]{1,0:T(8,128)(2,1)}, u32[]{:S(2)}, u32[]{:S(2)}) collective-permute-start(bf16[256,768]{1,0:T(8,128)(2,1)} %add_convert_fusion.13), channel_id=1, source_target_pairs={{0,2},{1,3},{2,0},{3,1},{4,6},{5,7},{6,4},{7,5},{8,10},{9,11},{10,... | collective-permute-start | bytes 1179656 | tf_op jit(solution)/shard_map/ppermute | solution.py:358
  280.1 45.6 %collective-permute-start.33 = (bf16[768,768]{1,0:T(8,128)(2,1)S(1)}, bf16[768,768]{1,0:T(8,128)(2,1)}, u32[]{:S(2)}, u32[]{:S(2)}) collective-permute-start(bf16[768,768]{1,0:T(8,128)(2,1)S(1)} %copy-done.73), channel_id=1, source_target_pairs={{0,1},{1,0},{2,3},{3,2},{4,5},{5,4},{6,7},{7,6},{8,9},{9,8},{10,11... | collective-permute-start | bytes 3538952 | tf_op jit(solution)/shard_map/ppermute | solution.py:354
  286.1 48.6 %collective-permute-start.35 = (bf16[768,768]{1,0:T(8,128)(2,1)}, bf16[768,768]{1,0:T(8,128)(2,1)S(1)}, u32[]{:S(2)}, u32[]{:S(2)}) collective-permute-start(bf16[768,768]{1,0:T(8,128)(2,1)} %add_convert_fusion.4), channel_id=1, source_target_pairs={{0,2},{1,3},{2,0},{3,1},{4,6},{5,7},{6,4},{7,5},{8,10},{9,11},{10,... | collective-permute-start | bytes 3538952 | tf_op jit(solution)/shard_map/ppermute | solution.py:358
  310.4 31.2 %collective-permute-start.25 = (bf16[768,576]{0,1:T(8,128)(2,1)}, bf16[768,576]{0,1:T(8,128)(2,1)}, u32[]{:S(2)}, u32[]{:S(2)}) collective-permute-start(bf16[768,576]{0,1:T(8,128)(2,1)} %copy.59), channel_id=1, source_target_pairs={{0,1},{1,0},{2,3},{3,2},{4,5},{5,4},{6,7},{7,6},{8,9},{9,8},{10,11... | collective-permute-start | bytes 2654216 | tf_op jit(solution)/shard_map/ppermute | solution.py:354
  311.7 38.9 %collective-permute-start.24 = (bf16[768,576]{0,1:T(8,128)(2,1)}, bf16[768,576]{0,1:T(8,128)(2,1)}, u32[]{:S(2)}, u32[]{:S(2)}) collective-permute-start(bf16[768,576]{0,1:T(8,128)(2,1)} %copy.57), channel_id=1, source_target_pairs={{0,1},{1,0},{2,3},{3,2},{4,5},{5,4},{6,7},{7,6},{8,9},{9,8},{10,11... | collective-permute-start | bytes 2654216 | tf_op jit(solution)/shard_map/ppermute | solution.py:354
  324.0 30.4 %collective-permute-start.45 = (bf16[384,768]{1,0:T(8,128)(2,1)}, bf16[384,768]{1,0:T(8,128)(2,1)}, u32[]{:S(2)}, u32[]{:S(2)}) collective-permute-start(bf16[384,768]{1,0:T(8,128)(2,1)} %constant_dynamic-slice_fusion.2), channel_id=1, source_target_pairs={{0,4},{4,0},{8,12},{12,8},{16,20},{20,16},{24,28},{28,24},{1,5},{5... | collective-permute-start | bytes 1769480 | tf_op jit(solution)/shard_map/ppermute | solution.py:386
  340.1 16.8 %collective-permute-start.36 = (bf16[384,768]{1,0:T(8,128)(2,1)}, bf16[384,768]{1,0:T(8,128)(2,1)}, u32[]{:S(2)}, u32[]{:S(2)}) collective-permute-start(bf16[384,768]{1,0:T(8,128)(2,1)} %constant_dynamic-slice_fusion.5), channel_id=1, source_target_pairs={{0,4},{4,0},{8,12},{12,8},{16,20},{20,16},{24,28},{28,24},{1,5},{5... | collective-permute-start | bytes 1769480 | tf_op jit(solution)/shard_map/ppermute | solution.py:386
  350.0 23.9 %collective-permute-start.26 = (bf16[768,576]{0,1:T(8,128)(2,1)}, bf16[768,576]{0,1:T(8,128)(2,1)}, u32[]{:S(2)}, u32[]{:S(2)}) collective-permute-start(bf16[768,576]{0,1:T(8,128)(2,1)} %copy.61), channel_id=1, source_target_pairs={{0,2},{1,3},{2,0},{3,1},{4,6},{5,7},{6,4},{7,5},{8,10},{9,11},{10,... | collective-permute-start | bytes 2654216 | tf_op jit(solution)/shard_map/ppermute | solution.py:358
  368.3 16.5 %collective-permute-start.47 = (bf16[96,768]{1,0:T(8,128)(2,1)}, bf16[96,768]{1,0:T(8,128)(2,1)}, u32[]{:S(2)}, u32[]{:S(2)}) collective-permute-start(bf16[96,768]{1,0:T(8,128)(2,1)} %constant_dynamic-slice_fusion), channel_id=1, source_target_pairs={{0,16},{4,20},{8,24},{12,28},{16,0},{20,4},{24,8},{28,12},{1,17},{... | collective-permute-start | bytes 442376 | tf_op jit(solution)/shard_map/ppermute | solution.py:386
  372.1 16.4 %collective-permute-start.38 = (bf16[96,768]{1,0:T(8,128)(2,1)}, bf16[96,768]{1,0:T(8,128)(2,1)}, u32[]{:S(2)}, u32[]{:S(2)}) collective-permute-start(bf16[96,768]{1,0:T(8,128)(2,1)} %constant_dynamic-slice_fusion.3), channel_id=1, source_target_pairs={{0,16},{4,20},{8,24},{12,28},{16,0},{20,4},{24,8},{28,12},{1,17},{... | collective-permute-start | bytes 442376 | tf_op jit(solution)/shard_map/ppermute | solution.py:386
  375.9 19.8 %collective-permute-start.27 = (bf16[384,576]{1,0:T(8,128)(2,1)S(1)}, bf16[384,576]{1,0:T(8,128)(2,1)S(1)}, u32[]{:S(2)}, u32[]{:S(2)}) collective-permute-start(bf16[384,576]{1,0:T(8,128)(2,1)S(1)} %constant_dynamic-slice_fusion.8), channel_id=1, source_target_pairs={{0,4},{4,0},{8,12},{12,8},{16,20},{20,16},{24,28},{28,24},{1,5},{5... | collective-permute-start | bytes 1327112 | tf_op jit(solution)/shard_map/ppermute | solution.py:386
  395.6 15.1 %collective-permute-start.40 = (bf16[192,768]{1,0:T(8,128)(2,1)S(1)}, bf16[192,768]{1,0:T(8,128)(2,1)S(1)}, u32[]{:S(2)}, u32[]{:S(2)}) collective-permute-start(bf16[192,768]{1,0:T(8,128)(2,1)S(1)} %pad_maximum_fusion.6), channel_id=1, source_target_pairs={{0,8},{4,12},{8,0},{12,4},{16,24},{20,28},{24,16},{28,20},{1,9},{5... | collective-permute-start | bytes 884744 | tf_op jit(solution)/shard_map/ppermute | solution.py:390
  395.9 14.7 %collective-permute-start.28 = (bf16[192,576]{1,0:T(8,128)(2,1)S(1)}, bf16[192,576]{1,0:T(8,128)(2,1)S(1)}, u32[]{:S(2)}, u32[]{:S(2)}) collective-permute-start(bf16[192,576]{1,0:T(8,128)(2,1)S(1)} %constant_dynamic-slice_fusion.7), channel_id=1, source_target_pairs={{0,8},{4,12},{8,0},{12,4},{16,24},{20,28},{24,16},{28,20},{1,9},{5... | collective-permute-start | bytes 663560 | tf_op jit(solution)/shard_map/ppermute | solution.py:386
  402.4 23.5 %collective-permute-start.50 = (bf16[384,768]{1,0:T(8,128)(2,1)S(1)}, bf16[384,768]{1,0:T(8,128)(2,1)S(1)}, u32[]{:S(2)}, u32[]{:S(2)}) collective-permute-start(bf16[384,768]{1,0:T(8,128)(2,1)S(1)} %pad_maximum_fusion.1), channel_id=1, source_target_pairs={{0,4},{4,0},{8,12},{12,8},{16,20},{20,16},{24,28},{28,24},{1,5},{5... | collective-permute-start | bytes 1769480 | tf_op jit(solution)/shard_map/ppermute | solution.py:390
  419.9 14.5 %collective-permute-start.41 = (bf16[384,768]{1,0:T(8,128)(2,1)S(1)}, bf16[384,768]{1,0:T(8,128)(2,1)S(1)}, u32[]{:S(2)}, u32[]{:S(2)}) collective-permute-start(bf16[384,768]{1,0:T(8,128)(2,1)S(1)} %pad_maximum_fusion), channel_id=1, source_target_pairs={{0,4},{4,0},{8,12},{12,8},{16,20},{20,16},{24,28},{28,24},{1,5},{5... | collective-permute-start | bytes 1769480 | tf_op jit(solution)/shard_map/ppermute | solution.py:390
  (118 other events, 772.0 us)

commit v2 on v1

v2 whole, which is shorter than its diff:
```python
import functools

import jax
import jax.numpy as jnp
from jax import lax
from jax.experimental import pallas as pl
from jax.experimental.pallas import tpu as pltpu
from jax.sharding import PartitionSpec as P

EPS = 1e-05
F32 = jnp.float32
BF16 = jnp.bfloat16
AUG = 80
KEEP = 72
NN = (((1,), (0,)), ((), ()))
NT = (((1,), (1,)), ((), ()))
TN = (((0,), (0,)), ((), ()))
CORE = [(i, i ^ 1) for i in range(4)]
CROSS = [(i, i ^ 2) for i in range(4)]
VMEM = pl.BlockSpec(memory_space=pltpu.VMEM)
SMEM = pl.BlockSpec(memory_space=pltpu.SMEM)
FAR = pl.BlockSpec(memory_space=pltpu.HBM)
ANYWHERE = pl.BlockSpec(memory_space=pl.ANY)
SPECS = {"v": VMEM, "s": SMEM, "h": FAR, "a": ANYWHERE}


def mm(a, b, dims):
    return lax.dot_general(a, b, dims, preferred_element_type=F32)


class Staged:
    def __init__(self, far, near, sem, out):
        self.near, self.state = near, "out" if out else "in"
        self.copy = pltpu.make_async_copy(*((near, far) if out else (far, near)), sem)
        self.shape, self.dtype = near.shape, near.dtype
        if not out:
            self.copy.start()

    def ready(self):
        if self.state == "in":
            self.copy.wait()
            self.state = "ready"

    def flush(self):
        if self.state == "out":
            self.copy.start()
            self.state = "flushed"

    def finish(self):
        self.ready()
        self.flush()
        if self.state == "flushed":
            self.copy.wait()
            self.state = "done"

    def __getitem__(self, index):
        assert self.state in ("ready", "out", "flushed")
        return self.near[index]

    def __setitem__(self, index, value):
        assert self.state == "out"
        self.near[index] = value


def ready(*refs):
    for ref in refs:
        if isinstance(ref, Staged):
            ref.ready()


def flush(*refs):
    for ref in refs:
        if isinstance(ref, Staged):
            ref.flush()


def call(kernel, outs, kinds, args, name, scratch=(), out_kinds=None, limit=32):
    out_kinds = out_kinds or "v" * len(outs)
    both = kinds + out_kinds
    spans = [a[1:] if isinstance(a, tuple) else (0, a.shape[0]) for a in [*args, *outs]]
    args = [a[0] if isinstance(a, tuple) else a for a in args]
    staged = [
        pltpu.VMEM((size, *a.shape[1:]), a.dtype)
        for a, k, (_, size) in zip([*args, *outs], both, spans) if k in "ha"
    ]

    def run(*refs):
        count = len(both)
        extra = len(staged)
        near = refs[count : count + extra]
        sems = refs[count + extra] if extra else None
        rest = refs[count + extra + (1 if extra else 0) :]
        use, at = [], 0
        for i, kind in enumerate(both):
            if kind in "ha":
                start, size = spans[i]
                far = refs[i] if refs[i].shape[0] == size else refs[i].at[pl.ds(start, size)]
                use.append(Staged(far, near[at], sems.at[at], i >= len(kinds)))
                at += 1
            else:
                use.append(refs[i])
        kernel(*use, *rest)
        for ref in use:
            if isinstance(ref, Staged):
                ref.finish()

    sems = [pltpu.SemaphoreType.DMA((len(staged),))] if staged else []
    return pl.pallas_call(
        run,
        out_shape=[
            pltpu.HBM(o.shape, o.dtype) if k == "h" else o for o, k in zip(outs, out_kinds)
        ],
        in_specs=[SPECS[k] for k in kinds],
        out_specs=[SPECS[k] for k in out_kinds],
        scratch_shapes=[*staged, *sems, *scratch],
        compiler_params=pltpu.CompilerParams(vmem_limit_bytes=limit << 20),
        cost_estimate=pl.CostEstimate(flops=1, bytes_accessed=1, transcendentals=0),
        name=name,
    )(*[
        pltpu.with_memory_space_constraint(a, pltpu.HBM) if k == "h" else a
        for a, k in zip(args, kinds)
    ])


def shaped(shape, dtype=F32):
    return jax.ShapeDtypeStruct(shape, dtype)


def norm_parts(v):
    center = v - jnp.mean(v, axis=-1, keepdims=True)
    scale = lax.rsqrt(jnp.mean(center * center, axis=-1, keepdims=True) + EPS)
    return center * scale, scale


def norm_back(gy, normal, scale, gain):
    a = gy * gain
    return (
        a - jnp.mean(a, axis=-1, keepdims=True)
        - normal * jnp.mean(a * normal, axis=-1, keepdims=True)
    ) * scale


def aug_rows(top, row):
    index = lax.broadcasted_iota(jnp.int32, (AUG - top.shape[0], top.shape[1]), 0)
    tail = jnp.where(index == 0, row, 0.0).astype(BF16)
    return jnp.concatenate([top, tail], axis=0)


def spread_states(total_ref, out_ref, parts, rows_per):
    for part in range(parts):
        out_ref[part] = total_ref[:, part * rows_per : (part + 1) * rows_per, :].astype(BF16)


def collect_states(in_ref, total_ref, parts, rows_per):
    for part in range(parts):
        total_ref[:, part * rows_per : (part + 1) * rows_per, :] = in_ref[part].astype(F32)


def project_rows(meta, j, w, n, pb_ref):
    line = jnp.broadcast_to(pb_ref[pl.ds(meta[j], 1), :], (128, w.shape[0])).T
    bias = jnp.concatenate([line] * (n.shape[0] // 128), axis=1)
    return (mm(w[...], n, NT) + bias).astype(BF16)


def near_kernel(meta, x_ref, p_ref, w0, w1, pb_ref, n_ref, half_ref):
    ready(x_ref)
    normal, _ = norm_parts(x_ref[...].astype(F32))
    n = (normal * p_ref[0:1] + p_ref[1:2]).astype(BF16)
    n_ref[...] = n
    flush(n_ref)
    span = w0.shape[0]
    for j, w in enumerate((w0, w1)):
        ready(w)
        start = pl.multiple_of((meta[j] & 1) * span, 64)
        half_ref[pl.ds(start, span), :] = project_rows(meta, j, w, n, pb_ref)


def far_kernel(meta, n_ref, near_ref, w2, w3, pb_ref, qkv_ref):
    span = w2.shape[0]
    ready(n_ref)
    start = pl.multiple_of((meta[0] >> 1) * 2 * span, 64)
    qkv_ref[pl.ds(start, 2 * span), :] = near_ref[...]
    for j, w in ((2, w2), (3, w3)):
        ready(w)
        start = pl.multiple_of(meta[j] * span, 64)
        qkv_ref[pl.ds(start, span), :] = project_rows(meta, j, w, n_ref[...], pb_ref)


def phi(rows_ref, base, map_ref, h):
    rows = rows_ref[pl.ds(pl.multiple_of(base + h * 64, 64), 64), :]
    logits = mm(map_ref[h], rows, TN)
    up = jnp.exp(logits - jnp.max(logits, axis=0, keepdims=True))
    down = jnp.exp(jnp.min(logits, axis=0, keepdims=True) - logits)
    p1 = up / jnp.sum(up, axis=0, keepdims=True)
    p2 = down / jnp.sum(down, axis=0, keepdims=True)
    return p1.astype(BF16), p2.astype(BF16)


def key_kernel(heads, slots, parts, meta, qkv_ref, map_ref, fk_ref, s_ref, total):
    width = heads * 64
    cols = qkv_ref.shape[1] // slots
    rows_per = s_ref.shape[2]
    total[...] = jnp.zeros_like(total)

    def head(h, carry):
        p1, p2 = phi(qkv_ref, width, map_ref, h)
        at = pl.multiple_of(h * 128, 128)
        fk_ref[pl.ds(at, 64), :] = p1
        fk_ref[pl.ds(pl.multiple_of(at + 64, 64), 64), :] = p2
        v = qkv_ref[pl.ds(pl.multiple_of(2 * width + h * 64, 64), 64), :]
        va = aug_rows(v, 1.0)
        fk = jnp.concatenate([p1, p2], axis=0)
        for s in range(slots):
            part = slice(s * cols, (s + 1) * cols)
            state = mm(va[:, part], fk[:, part], NT)
            total[s ^ meta[4], pl.ds(pl.multiple_of(h * KEEP, 8), KEEP), :] = state[:KEEP]
        return carry

    lax.fori_loop(0, heads, head, 0)
    flush(fk_ref)
    spread_states(total, s_ref, parts, rows_per)


def query_kernel(heads, qkv_ref, map_ref, fq_ref):
    def head(h, carry):
        p1, p2 = phi(qkv_ref, 0, map_ref, h)
        at = pl.multiple_of(h * 128, 128)
        fq_ref[pl.ds(at, 64), :] = p1
        fq_ref[pl.ds(pl.multiple_of(at + 64, 64), 64), :] = p2
        return carry

    lax.fori_loop(0, heads, head, 0)


def scan_kernel(nctx, backward, keep, in_ref, out_ref):
    blocks = 2 * nctx
    order = [(b, 0) if b < nctx else (blocks - 1 - b, 1) for b in range(blocks)]
    acc = jnp.zeros(in_ref.shape[2:], F32)
    for b in reversed(range(blocks)) if backward else range(blocks):
        c, lane = order[b]
        acc = acc * keep[b] + in_ref[c, lane].astype(F32)
        out_ref[c, lane] = acc.astype(BF16)


def fill_output(meta, wo_refs, wo):
    rows = wo_refs[0].shape[0]
    for j, ref in enumerate(wo_refs):
        wo[pl.ds(pl.multiple_of(meta[j] * rows, 64), rows), :] = ref[...]


def attend_kernel(
    heads, slots, parts, meta, c_ref, fq_ref, x_ref, w0, w1, w2, w3, p_ref,
    mixed_ref, den_ref, middle_ref, n2_ref, total, wo,
):
    cols = fq_ref.shape[1] // slots
    collect_states(c_ref, total, parts, c_ref.shape[2])
    ready(fq_ref)

    def head(h, carry):
        fq = fq_ref[pl.ds(pl.multiple_of(h * 128, 128), 128), :]
        for s in range(slots):
            part = slice(s * cols, (s + 1) * cols)
            c = total[s ^ meta[4], pl.ds(pl.multiple_of(h * KEEP, 8), AUG), :].astype(BF16)
            both = mm(c, fq[:, part], NN)
            den = both[64:65]
            mixed_ref[pl.ds(pl.multiple_of(h * 64, 64), 64), part] = (both[:64] / den).astype(BF16)
            den_ref[pl.ds(pl.multiple_of(h * 8, 8), 8), part] = jnp.broadcast_to(den, (8, cols))
        return carry

    lax.fori_loop(0, heads, head, 0)
    flush(mixed_ref, den_ref)
    ready(x_ref, w0, w1, w2, w3)
    fill_output(meta, (w0, w1, w2, w3), wo)
    middle = x_ref[...].astype(F32) + mm(mixed_ref[...], wo[...], TN) + p_ref[4:5]
    middle_ref[...] = middle
    flush(middle_ref)
    normal, _ = norm_parts(middle)
    n2 = (normal * p_ref[2:3] + p_ref[3:4]).astype(BF16)
    n2_ref[...] = n2


def mlp_kernel(tile, first, meta, n2_ref, n2o_ref, cot_ref, coto_ref, base_ref, eb_ref, we, wr, *refs):
    if first:
        out_ref, dn_ref, outo_ref, dno_ref, ge, gr, gb_ref, n2t, acc = refs
        dn_ref[...] = jnp.zeros_like(dn_ref)
        acc[...] = jnp.zeros_like(acc)
    else:
        back_ref, baseo_ref, backo_ref = refs[:3]
        out_ref, dn_ref, outo_ref, dno_ref, ge, gr, gb_ref, n2t, acc = refs[3:]
        dn_ref[...] = back_ref[...]
        acc[0] = baseo_ref[...].astype(F32)
        acc[1] = backo_ref[...].astype(F32)
    ready(base_ref)
    out_ref[...] = base_ref[...]
    rows_n = n2_ref.shape[0]
    line = meta[2] if first else meta[0]
    ready(n2_ref, n2o_ref)
    for half, ref in enumerate((n2_ref, n2o_ref)):
        n2t[:, half * rows_n : (half + 1) * rows_n] = ref[...].T
    ready(we, wr, cot_ref, coto_ref)

    def step(t, carry):
        at = pl.ds(pl.multiple_of(t * tile, tile), tile)
        w_in = we[:, at]
        w_out = wr[at, :]
        bias = eb_ref[pl.ds(line, 1), at]
        actives, hiddens, sums = [], [], None
        for half, (n_ref, c_ref) in enumerate(((n2_ref, cot_ref), (n2o_ref, coto_ref))):
            hidden = mm(n_ref[...], w_in, NN) + bias
            square = hidden * hidden
            inner = 0.7978845608028654 * hidden * (1.0 + 0.044715 * square)
            tanh = jnp.tanh(inner)
            part = 0.5 * (1.0 + tanh)
            active = (hidden * part).astype(BF16)
            slope = part + 0.5 * hidden * (1.0 - tanh * tanh) * (
                0.7978845608028654 * (1.0 + 0.134145 * square)
            )
            r_active = mm(c_ref[...], w_out, NT).astype(BF16).astype(F32)
            r_hidden = (r_active * slope).astype(BF16)
            if half == 0:
                out_ref[...] += mm(active, w_out, NN)
                dn_ref[...] += mm(r_hidden, w_in, NT)
            else:
                acc[0] += mm(active, w_out, NN)
                acc[1] += mm(r_hidden, w_in, NT)
            actives.append(active)
            hiddens.append(r_hidden)
            total = jnp.sum(r_hidden.astype(F32), axis=0, keepdims=True)
            sums = total if sums is None else sums + total
        gr[at, :] = (
            mm(actives[0], cot_ref[...], TN) + mm(actives[1], coto_ref[...], TN)
        ).astype(BF16)
        ge[:, at] = (
            mm(n2t[:, :rows_n], hiddens[0], NN) + mm(n2t[:, rows_n:], hiddens[1], NN)
        ).astype(BF16)
        gb_ref[:, at] = jnp.broadcast_to(sums, (8, tile))
        return carry

    lax.fori_loop(0, we.shape[1] // tile, step, 0)
    flush(ge, gr)
    outo_ref[...] = acc[0].astype(BF16)
    dno_ref[...] = acc[1].astype(BF16)


def middle_kernel(
    heads, slots, parts, meta, dn_ref, dnin_ref, middle_ref, cot_ref, p_ref, mixed_ref, den_ref, fq_ref,
    w0, w1, w2, w3, gm_ref, ratt_ref, raug_ref, g_ref, small_ref, total, wo, rmix,
):
    cols = fq_ref.shape[1] // slots
    ready(middle_ref, dnin_ref, cot_ref)
    normal, scale = norm_parts(middle_ref[...])
    gy = dn_ref[...] + dnin_ref[...].astype(F32)
    cot = cot_ref[...].astype(F32)
    g_middle = cot + norm_back(gy, normal, scale, p_ref[2:3])
    gm_ref[...] = g_middle
    r_att = g_middle.astype(BF16)
    ratt_ref[...] = r_att
    flush(gm_ref, ratt_ref)
    small_ref[...] = jnp.concatenate(
        [
            jnp.sum(gy * normal, axis=0, keepdims=True),
            jnp.sum(gy, axis=0, keepdims=True),
            jnp.sum(r_att.astype(F32), axis=0, keepdims=True),
            jnp.sum(cot, axis=0, keepdims=True),
            jnp.zeros((4, gy.shape[1]), F32),
        ],
        axis=0,
    )
    ready(w0, w1, w2, w3)
    fill_output(meta, (w0, w1, w2, w3), wo)
    rmix[...] = mm(wo[...], r_att, NT).astype(BF16)
    total[...] = jnp.zeros_like(total)
    ready(mixed_ref, den_ref, fq_ref)

    def head(h, carry):
        rows = pl.ds(pl.multiple_of(h * 64, 64), 64)
        rm = rmix[rows, :].astype(F32)
        inverse = 1.0 / den_ref[pl.ds(pl.multiple_of(h * 8, 8), 8), :][0:1]
        rn = (rm * inverse).astype(BF16)
        rd = -jnp.sum(rm * mixed_ref[rows, :].astype(F32), axis=0, keepdims=True) * inverse
        ra = aug_rows(rn, rd)
        raug_ref[pl.ds(pl.multiple_of(h * AUG, 16), AUG), :] = ra
        fq = fq_ref[pl.ds(pl.multiple_of(h * 128, 128), 128), :]
        for s in range(slots):
            part = slice(s * cols, (s + 1) * cols)
            state = mm(ra[:, part], fq[:, part], NT)
            total[s ^ meta[4], pl.ds(pl.multiple_of(h * KEEP, 8), KEEP), :] = state[:KEEP]
        return carry

    lax.fori_loop(0, heads, head, 0)
    spread_states(total, g_ref, parts, g_ref.shape[2])
    flush(g_ref, raug_ref)


def logits_back(p_both, g_both):
    p1, p2 = p_both[:64].astype(F32), p_both[64:].astype(F32)
    g1, g2 = g_both[:64], g_both[64:]
    s1 = jnp.sum(p1 * g1, axis=0, keepdims=True)
    s2 = jnp.sum(p2 * g2, axis=0, keepdims=True)
    return (p1 * (g1 - s1) - p2 * (g2 - s2)).astype(BF16)


def query_back_kernel(
    heads, slots, parts, meta, c_ref, raug_ref, fq_ref, qkv_ref, map_ref, mixed_ref, ratt_ref,
    rq_ref, gmap_ref, g0, g1, g2, g3, total,
):
    cols = fq_ref.shape[1] // slots
    ready(c_ref)
    collect_states(c_ref, total, parts, c_ref.shape[2])
    ready(raug_ref, fq_ref, qkv_ref)

    def head(h, carry):
        ra = raug_ref[pl.ds(pl.multiple_of(h * AUG, 16), AUG), :]
        fq = fq_ref[pl.ds(pl.multiple_of(h * 128, 128), 128), :]
        pieces = []
        for s in range(slots):
            part = slice(s * cols, (s + 1) * cols)
            c = total[s ^ meta[4], pl.ds(pl.multiple_of(h * KEEP, 8), AUG), :].astype(BF16)
            pieces.append(mm(c, ra[:, part], TN))
        r_fq = jnp.concatenate(pieces, axis=1).astype(BF16).astype(F32)
        r_l = logits_back(fq, r_fq)
        rows = pl.ds(pl.multiple_of(h * 64, 64), 64)
        rq_ref[rows, :] = mm(map_ref[h], r_l, NN).astype(BF16)
        gmap_ref[h] = mm(qkv_ref[rows, :], r_l, NT)
        return carry

    lax.fori_loop(0, heads, head, 0)
    flush(rq_ref, gmap_ref)
    ready(mixed_ref, ratt_ref)
    rows = g0.shape[0]
    for j, g in enumerate((g0, g1, g2, g3)):
        mixed = mixed_ref[pl.ds(pl.multiple_of(meta[j] * rows, 64), rows), :]
        g[...] = mm(mixed, ratt_ref[...], NN).astype(BF16)
        flush(g)


def key_back_kernel(
    heads, slots, parts, meta, d_ref, fk_ref, qkv_ref, map_ref, rq_ref, n_ref,
    rp_ref, gmap_ref, g1, g3, total,
):
    width = heads * 64
    cols = fk_ref.shape[1] // slots
    collect_states(d_ref, total, parts, d_ref.shape[2])
    ready(fk_ref, qkv_ref, rq_ref)
    rp_ref[0:width, :] = rq_ref[...]

    def head(h, carry):
        fk = fk_ref[pl.ds(pl.multiple_of(h * 128, 128), 128), :]
        v = qkv_ref[pl.ds(pl.multiple_of(2 * width + h * 64, 64), 64), :]
        va = aug_rows(v, 1.0)
        pieces = []
        for s in range(slots):
            part = slice(s * cols, (s + 1) * cols)
            d = total[s ^ meta[4], pl.ds(pl.multiple_of(h * KEEP, 8), AUG), :].astype(BF16)
            pieces.append(mm(d, va[:, part], TN))
            rv = mm(d[:64], fk[:, part], NN).astype(BF16)
            rp_ref[pl.ds(pl.multiple_of(2 * width + h * 64, 64), 64), part] = rv
        r_fk = jnp.concatenate(pieces, axis=1).astype(BF16).astype(F32)
        r_l = logits_back(fk, r_fk)
        rows = pl.ds(pl.multiple_of(width + h * 64, 64), 64)
        rp_ref[rows, :] = mm(map_ref[h], r_l, NN).astype(BF16)
        gmap_ref[h] = mm(qkv_ref[rows, :], r_l, NT)
        return carry

    lax.fori_loop(0, heads, head, 0)
    flush(gmap_ref)
    ready(n_ref)
    span = g1.shape[0]
    for j, g in ((1, g1), (3, g3)):
        rp = rp_ref[pl.ds(pl.multiple_of(meta[j] * span, 64), span), :]
        g[...] = mm(rp, n_ref[...], NN).astype(BF16)
        flush(g)


def project_grad_kernel(meta, rp_ref, n_ref, in0, in2, g0, g2):
    span = g0.shape[0]
    ready(n_ref, in0, in2)
    for j, more, g in ((2, in2, g2), (0, in0, g0)):
        rp = rp_ref[pl.ds(pl.multiple_of(meta[j] * span, 64), span), :]
        g[...] = (mm(rp, n_ref[...], NN) + more[...].astype(F32)).astype(BF16)
        flush(g)


def input_kernel(
    heads, meta, rp_ref, x_ref, p_ref, gm_ref, out_ref, outin_ref, two_ref, ebo_ref, ebc_ref,
    mq_ref, mk_ref, w0, w1, w2, w3, dx_ref, full_ref, b0, b1, b2, b3, pack,
):
    ready(out_ref, outin_ref)
    full_ref[...] = out_ref[...] + outin_ref[...].astype(F32) + p_ref[5:6]
    flush(full_ref)
    span, width = w0.shape
    shard = width // 4
    own_heads = heads // 4
    ones = jnp.ones((8, x_ref.shape[0]), BF16)
    pack[...] = jnp.zeros_like(pack)
    gy = None
    ready(w0, w1, w2, w3, x_ref, gm_ref)
    for j, w in enumerate((w0, w1, w2, w3)):
        rp = rp_ref[pl.ds(pl.multiple_of(meta[j] * span, 64), span), :]
        part = mm(rp, w[...], TN)
        gy = part if gy is None else gy + part
        pack[meta[j], 8:16, :span] = mm(ones, rp, NT)
    pack[meta[0], 16:24, :] = ebo_ref[...]
    pack[meta[2], 16:24, :] = ebc_ref[...]
    normal, scale = norm_parts(x_ref[...].astype(F32))
    dx_ref[...] = gm_ref[...] + norm_back(gy, normal, scale, p_ref[0:1])
    flush(dx_ref)
    ready(mq_ref, mk_ref)
    lines = [
        jnp.sum(gy * normal, axis=0, keepdims=True),
        jnp.sum(gy, axis=0, keepdims=True),
        two_ref[0:1], two_ref[1:2], two_ref[2:3], two_ref[3:4],
    ]
    for i in range(4):
        cut = slice(i * shard, (i + 1) * shard)
        for k, line in enumerate(lines):
            pack[i, k : k + 1, :shard] = line[:, cut]
        for base, ref in ((24, mq_ref), (40, mk_ref)):
            for k in range(4):
                for h in range(own_heads):
                    at = k * shard + h * 64
                    pack[i, base : base + 16, at : at + 64] = ref[
                        i * own_heads + h, 16 * k : 16 * k + 16, :
                    ]
    for j, b in enumerate((b0, b1, b2, b3)):
        b[...] = pack[meta[j]].astype(BF16)


def unpack_kernel(rest_ref, g1, s1, g2, s2, bo, br, pb, eb, mq, mk):
    shard = g1.shape[1]
    own_heads = mq.shape[0]
    for k, ref in enumerate((g1, s1, g2, s2, bo, br)):
        ref[...] = rest_ref[k : k + 1, :shard]
    pb[...] = rest_ref[8:9, : pb.shape[1]]
    eb[...] = rest_ref[16:17, :]
    for base, ref in ((24, mq), (40, mk)):
        for k in range(4):
            for h in range(own_heads):
                at = k * shard + h * 64
                ref[h, 16 * k : 16 * k + 16, :] = rest_ref[base : base + 16, at : at + 64]


def core_swap(a):
    return lax.ppermute(a, "fsdp", CORE)


def cross_swap(a):
    return lax.ppermute(a, "fsdp", CROSS)


def after(value, *others):
    return lax.optimization_barrier((value, *others))[0]


def spread(shard, cross):
    return [shard, core_swap(shard), cross, core_swap(cross)]


def add(a, b):
    return (a.astype(F32) + b.astype(F32)).astype(BF16)


def ctx_pairs(nctx, bit):
    return [(i, i ^ (1 << bit)) for i in range(nctx)]


def rows_sum(parts, start, size):
    out = None
    for offset, part in parts:
        piece = lax.dynamic_slice_in_dim(part, start + offset, size, 0).astype(F32)
        out = piece if out is None else out + piece
    return out.astype(BF16)


class Reduction:
    def __init__(self, parts, nctx, place):
        self.parts = [(0, part) for part in parts]
        self.rows, self.nctx, self.place = parts[0].shape[0], nctx, place
        self.bits = nctx.bit_length() - 1

    def halve(self, bit):
        half = self.rows // 2
        mine = (self.place >> bit) & 1
        sent = rows_sum(self.parts, (1 - mine) * half, half)
        got = lax.ppermute(sent, "ctx", ctx_pairs(self.nctx, bit))
        self.parts = [(offset + mine * half, part) for offset, part in self.parts] + [(0, got)]
        self.rows = half
        return got

    def hold(self, *others):
        offset, last = self.parts[-1]
        self.parts[-1] = (offset, after(last, *others))

    def spread(self):
        cur = rows_sum(self.parts, 0, self.rows)
        for bit in reversed(range(self.bits)):
            other = lax.ppermute(cur, "ctx", ctx_pairs(self.nctx, bit))
            first = ((self.place >> bit) & 1) == 0
            cur = jnp.concatenate(
                [jnp.where(first, cur, other), jnp.where(first, other, cur)], axis=0
            )
        return cur

    def total(self, begin=0):
        for bit in range(begin, self.bits):
            self.halve(bit)
        return self.spread()


def small_sum(parts, nctx):
    own, core, cross, far = parts
    far_in, core_in = core_swap(far), core_swap(core)
    cross_in = cross_swap(add(cross, far_in))
    cur = own.astype(F32) + core_in.astype(F32) + cross_in.astype(F32)
    for bit in range(nctx.bit_length() - 1):
        low = cur.astype(BF16)
        cur = low.astype(F32) + lax.ppermute(low, "ctx", ctx_pairs(nctx, bit)).astype(F32)
    return cur


def straighten(parts, mine):
    a, b, c, d = parts
    odd = (mine & 1) == 1
    upper = (mine & 2) == 2
    a, b = jnp.where(odd, b, a), jnp.where(odd, a, b)
    c, d = jnp.where(odd, d, c), jnp.where(odd, c, d)
    return [
        jnp.where(upper, c, a), jnp.where(upper, d, b),
        jnp.where(upper, a, c), jnp.where(upper, b, d),
    ]


def exchange(a):
    return lax.all_to_all(a, "ctx", 0, 0, tiled=True)


def body(
    tokens, cotangent, pair_table, seq_ids, first_gain, first_shift, project_weight, project_bias,
    feature_query, feature_key, output_weight, output_bias, second_gain, second_shift,
    expand_weight, expand_bias, reduce_weight, reduce_bias,
):
    x = tokens[0]
    cot = cotangent[0]
    rows_n, width = x.shape
    heads = width // feature_query.shape[1]
    own_heads = feature_query.shape[0]
    slots = pair_table.shape[2]
    nctx = lax.axis_size("ctx")
    place = lax.axis_index("ctx")
    mine = lax.axis_index("fsdp")
    span = project_weight.shape[1]
    hidden_own = expand_weight.shape[1]
    shard = width // 4
    wide = heads * 128

    project_t = project_weight.T
    cross_project = cross_swap(project_t)
    vector = jnp.concatenate(
        [first_gain, first_shift, second_gain, second_shift, output_bias, reduce_bias,
         project_bias, expand_bias]
    )
    room = -vector.shape[0] % 1024
    vector = jnp.concatenate([vector, jnp.zeros((room,), BF16)]).reshape(-1, 64)
    map_rows = own_heads * 64
    pack = jnp.concatenate(
        [feature_query.reshape(-1, 64), feature_key.reshape(-1, 64), vector]
    )
    packs = spread(pack, cross_swap(pack))
    ordered = straighten(packs, mine)
    query_map = jnp.concatenate([p[:map_rows] for p in ordered]).reshape(heads, 64, 64)
    key_map = jnp.concatenate([p[map_rows : 2 * map_rows] for p in ordered]).reshape(heads, 64, 64)
    vectors = jnp.stack([p[2 * map_rows :] for p in ordered]).reshape(4, -1).astype(F32)
    params = vectors[:, : 6 * shard].reshape(4, 6, shard).transpose(1, 0, 2).reshape(6, width)
    project_line = vectors[:, 6 * shard : 6 * shard + span]
    expand_line = vectors[:, 6 * shard + span : 6 * shard + span + hidden_own]
    project_core = core_swap(project_t)
    project_far = core_swap(cross_project)
    projects = [project_t, project_core, cross_project, project_far]
    near_expand = jnp.concatenate([expand_weight, output_weight])
    cross_expand = cross_swap(after(near_expand, cross_project))
    core_output = core_swap(output_weight)
    far_output = core_swap(cross_expand[width:])
    outputs = [output_weight, core_output, (cross_expand, width, shard), far_output]
    cross_reduce = cross_swap(after(reduce_weight, cross_expand))
    cot_other = core_swap(cot)

    positions = pair_table[0, 0]
    swap = (positions[0] > positions[1]).astype(jnp.int32)
    meta = jnp.stack([mine, mine ^ 1, mine ^ 2, mine ^ 3, swap]).astype(jnp.int32)
    ids = seq_ids[0]
    same = (ids[1:] == ids[:-1]).astype(F32)
    none = jnp.zeros((1,), F32)
    keep = jnp.concatenate([none, same])
    keep_next = jnp.concatenate([same, none])

    rows_per = -(-(heads * KEEP) // (nctx * 16)) * 16
    state_shape = shaped((nctx, slots, rows_per, 128), BF16)
    total = pltpu.VMEM((slots, nctx * rows_per, 128), F32)
    wo_scratch = pltpu.VMEM((width, width), BF16)
    low = shaped((rows_n, width), BF16)
    full = shaped((rows_n, width))
    table = shaped((width, rows_n), BF16)
    square = shaped((heads, 64, 64))

    n1, near = call(
        near_kernel, [low, shaped((2 * span, rows_n), BF16)], "shvaav",
        [meta, x, params, projects[0], projects[1], project_line], "project_near", (), "hv",
    )
    (qkv,) = call(
        far_kernel, [shaped((3 * width, rows_n), BF16)], "shvaav",
        [meta, n1, near, projects[2], projects[3], project_line], "project_far",
    )
    fk, states = call(
        functools.partial(key_kernel, heads, slots, nctx),
        [shaped((wide, rows_n), BF16), state_shape], "svv",
        [meta, qkv, key_map], "keys", [total], "hh",
    )
    arrived = exchange(states)
    (fq,) = call(
        functools.partial(query_kernel, heads), [shaped((wide, rows_n), BF16)], "vv",
        [after(qkv, states), query_map], "queries", (), "h",
    )
    (running,) = call(
        functools.partial(scan_kernel, nctx, False), [state_shape], "sv",
        [keep, after(arrived, fq, cross_expand)], "scan", (), "h",
    )
    carried = exchange(running)
    mixed, den, middle, n2 = call(
        functools.partial(attend_kernel, heads, slots, nctx),
        [table, shaped((heads * 8, rows_n)), full, low],
        "svhhaaaav", [meta, carried, fq, x, *outputs, params], "attend",
        [total, wo_scratch], "hhhh",
    )
    n2_other = core_swap(n2)

    def mlp(first, base, w_in, w_out, more, name):
        return call(
            functools.partial(mlp_kernel, 384, first),
            [full, full, low, low, shaped((width, hidden_own), BF16),
             shaped((hidden_own, width), BF16), shaped((8, hidden_own))],
            "shaaa" + ("h" if first else "v") + "vaa" + "v" * len(more),
            [meta, n2, n2_other, cot, cot_other, base, expand_line, w_in, w_out, *more], name,
            [pltpu.VMEM((width, 2 * rows_n), BF16), pltpu.VMEM((2, rows_n, width), F32)],
            "vvvvhhv" if first else "hvhhhhv", 40,
        )

    out1, dn1, out1_o, dn1_o, ge_cross, gr_cross, gb_cross = mlp(
        True, middle, (cross_expand, 0, width), cross_reduce, [], "mlp_far"
    )
    ge_in = cross_swap(ge_cross)
    out2, dn2, out2_o, dn2_o, ge_own, gr_own, gb_own = mlp(
        False, out1, expand_weight, reduce_weight, [dn1, out1_o, dn1_o], "mlp_near"
    )
    dn2_in = core_swap(dn2_o)

    g_middle, r_att, raug, g_states, small_two = call(
        functools.partial(middle_kernel, heads, slots, nctx),
        [full, low, shaped((heads * AUG, rows_n), BF16), state_shape, shaped((8, width))],
        "svahavhhhaaaa",
        [meta, dn2, dn2_in, middle, cot, params, mixed, den, fq, *outputs], "middle",
        [total, wo_scratch, pltpu.VMEM((width, rows_n), BF16)], "hhhhv",
    )
    g_arrived = exchange(g_states)
    gr_in = cross_swap(after(gr_cross, ge_in))
    out2_in = core_swap(after(out2_o, g_states))
    rq, g_query_map, *go = call(
        functools.partial(query_back_kernel, heads, slots, nctx),
        [table, square] + [shaped((shard, width), BF16)] * 4,
        "sahhavhh", [meta, carried, raug, fq, (qkv, 0, width), query_map, mixed, r_att], "query_back",
        [total], "hhhhhh",
    )
    (g_running,) = call(
        functools.partial(scan_kernel, nctx, True), [state_shape], "sv",
        [keep_next, after(g_arrived, rq, ge_in)], "scan_back", (), "h",
    )
    g_carried = exchange(g_running)
    sum_e = Reduction([ge_own, after(ge_in, g_running)], nctx, place)
    e_half = sum_e.halve(0)
    go_far, go_core = core_swap(after(go[3], g_running)), core_swap(after(go[1], g_running))
    rp, g_key_map, gp1, gp3 = call(
        functools.partial(key_back_kernel, heads, slots, nctx),
        [shaped((3 * width, rows_n), BF16), square] + [shaped((span, width), BF16)] * 2,
        "svhavhh", [meta, after(g_carried, e_half), fk, qkv, key_map, rq, n1],
        "key_back", [total], "vhhh",
    )
    gp3_in, gp1_in = core_swap(gp3), core_swap(gp1)
    gp_own, gp_cross = call(
        project_grad_kernel, [shaped((span, width), BF16)] * 2, "svhaa",
        [meta, rp, n1, gp1_in, gp3_in], "project_grad", (), "hh",
    )
    go_in = cross_swap(after(add(go[2], go_far), gr_in))
    gp_in = cross_swap(after(gp_cross, go_in))
    small = shaped((64, width), BF16)
    dx, layer_out, *blocks = call(
        functools.partial(input_kernel, heads), [full, full, small, small, small, small],
        "svhvhhavvvhhaaaa",
        [meta, rp, after(x, gp_own), params, g_middle, out2, out2_in, small_two, gb_own, gb_cross,
         g_query_map, g_key_map, *projects],
        "input", [pltpu.VMEM((4, 64, width), F32)], "hhvvvv",
    )
    sum_e.hold(gp_own)
    gr_in = after(gr_in, gp_own)
    g_expand = sum_e.total(1)
    g_reduce = Reduction([gr_own, gr_in], nctx, place).total()
    own_go = add(add(go[0], go_core), go_in)
    g_project = Reduction(
        [jnp.concatenate([gp_own, own_go]),
         jnp.concatenate([gp_in, jnp.zeros_like(own_go)])], nctx, place
    ).total()
    rest = small_sum(blocks, nctx)
    line = shaped((1, shard))
    g1, s1, g2, s2, bo, br, pb, eb, mq, mk = call(
        unpack_kernel,
        [line] * 6 + [shaped((1, span)), shaped((1, hidden_own))]
        + [shaped((own_heads, 64, 64))] * 2, "v", [rest], "unpack",
    )
    return (
        layer_out[None], dx[None], g1[0], s1[0], g_project[:span].T.astype(F32), pb[0], mq, mk,
        g_project[span:].astype(F32), bo[0], g2[0], s2[0], g_expand.astype(F32), eb[0],
        g_reduce.astype(F32), br[0],
    )


def solution(mesh):
    row = P("fsdp", "ctx", None)
    vec = P("fsdp")
    maps = P("fsdp", None, None)
    in_specs = (
        row, row, row, P("fsdp", None), vec, vec, P(None, "fsdp"), vec, maps, maps,
        P("fsdp", None), vec, vec, vec, P(None, "fsdp"), vec, P("fsdp", None), vec,
    )
    out_specs = (
        row, row, vec, vec, P(None, "fsdp"), vec, maps, maps, P("fsdp", None), vec, vec, vec,
        P(None, "fsdp"), vec, P("fsdp", None), vec,
    )
    return jax.shard_map(body, mesh=mesh, in_specs=in_specs, out_specs=out_specs, check_vma=False)
```

time: 451 us -> 345 us (0.76); the launches traced: 444 us -> 344 us
  local copies, waits for them, and re-layouts: 102 us -> 17.7 us
  Pallas kernels: 76.2 us -> 100 us
  waiting for transfers between devices: 152 us -> 131 us
  blocking collectives: 19.7 us -> 0 us
  starting transfers between devices: 53.3 us -> 65.8 us
  other arithmetic: 37.4 us -> 26.3 us
    unnamed x196 -> x92, local copies, waits for them, and re-layouts: 50.7 us -> 9.94 us
    ppermute x9, waiting for transfers between devices: 75.5 us -> 46.9 us  [cross_swap(): return lax.ppermute(a, 'fsdp', CROSS)]
    pallas_call x12 -> x15, Pallas kernels: 76.2 us -> 100 us  [call(): pl.pallas_call(run, out_shape=[pltpu.HBM(o.shape, o.dtype) if k == 'h' el...]
    all_to_all x1 -> x0, blocking collectives: 19.7 us -> none  [exchange(): return lax.all_to_all(a, 'ctx', 0, 0, tiled=True)]
    convert_element_type x20 -> x3, other arithmetic: 20.7 us -> 2.1 us  [add(): return (a.astype(F32) + b.astype(F32)).astype(BF16)]
    convert_element_type x6 -> x18, other arithmetic: 1.77 us -> 13.7 us  [the longest x12 11.4 us: rows_sum(): return out.astype(BF16)]
    ppermute x6 -> x0, local copies, waits for them, and re-layouts: 11.8 us -> none  [the longest x4 8.9 us: core_swap(): return lax.ppermute(a, 'fsdp', CORE)]
    ppermute x24 -> x21, waiting for transfers between devices: 63 us -> 71.4 us  [the longest x9 36.6 us: halve(): got = lax.ppermute(sent, 'ctx', ctx_pairs(self.nctx, bit))]
  transfers between devices with their start and end apart: 54 -> 50, of which waited for: 20 -> 25; matrix products, arithmetic and copies ran while one was open for 20% -> 9% of each run, Pallas kernels for 13% -> 19%
where the time goes in v2:
time: 345 us; the launch traced here: 344 us
  waiting for transfers between devices  131 us (38%)
  Pallas kernels  100 us (29%)
  starting transfers between devices  65.8 us (19%)
  other arithmetic  26.3 us (8%)
  local copies, waits for them, and re-layouts  17.7 us (5%)
    pallas_call x15, Pallas kernels, call(): pl.pallas_call(run, out_shape=[pltpu.HBM(o.shape, o.dtype) if k == 'h' el...  100 us
    ppermute x9, waiting for transfers between devices, cross_swap(): return lax.ppermute(a, 'fsdp', CROSS)  46.9 us
    ppermute x9, waiting for transfers between devices, halve(): got = lax.ppermute(sent, 'ctx', ctx_pairs(self.nctx, bit))  36.6 us
    ppermute x9, waiting for transfers between devices, spread(): other = lax.ppermute(cur, 'ctx', ctx_pairs(self.nctx, bit))  32.5 us
    all_to_all x4, starting transfers between devices, exchange(): return lax.all_to_all(a, 'ctx', 0, 0, tiled=True)  22.4 us
    ppermute x9, starting transfers between devices, cross_swap(): return lax.ppermute(a, 'fsdp', CROSS)  13 us
    ppermute x9, starting transfers between devices, halve(): got = lax.ppermute(sent, 'ctx', ctx_pairs(self.nctx, bit))  12.7 us
    convert_element_type x12, other arithmetic, rows_sum(): return out.astype(BF16)  11.4 us
  transfers between devices with their start and end apart: 50, of which 25 were waited for; matrix products, arithmetic and copies ran while one was open for 9% of the time, Pallas kernels for 19%

profile of v2, /device:TPU:0, one launch (start us, length us, event | category | flops | bytes accessed | tf_op | source)
XLA Modules:
  0.0 343.7 jit_solution(4765089021607568559)
XLA Ops:
  3.7 5.5 %concatenate.57 = bf16[3072]{0:T(1024)(128)(2,1)S(1)} concatenate(bf16[192]{0:T(256)(128)(2,1)} %param.22, bf16[192]{0:T(256)(128)(2,1)} %param.23, bf16[192]{0:T(256)(128)(2,1)} %param.30, bf16[192]{0:T(256)(128)(2,1)} %param.31, bf16[192]{0:T(256)(128)(2,1)} %param.29, bf16[192]{0:T(256)(128)(2,1)} %param.35, bf16[576]{0:T(1024)(128)(2,1)} %param.25, bf16[768]{0:T(1024)(128)(2,1)} %param.33, ...), dimensions={0} | concatenate | bytes 12288 | tf_op jit(solution)/shard_map/concatenate | solution.py:663
  13.3 12.6 %collective-permute-done = bf16[432,64]{1,0:T(8,128)(2,1)S(1)} collective-permute-done((bf16[432,64]{1,0:T(8,128)(2,1)S(1)}, bf16[432,64]{1,0:T(8,128)(2,1)S(1)}, u32[]{:S(2)}, u32[]{:S(2)}) %collective-permute-start) | collective-permute-done | bytes 55328 | tf_op jit(solution)/shard_map/ppermute | solution.py:548
  32.8 3.6 %project_near.1 = (bf16[512,768]{1,0:T(8,128)(2,1)}, bf16[1152,512]{1,0:T(8,128)(2,1)S(1)}) custom-call(s32[5]{0:T(128)S(1)} %stack.42.refs_0_, bf16[512,768]{1,0:T(8,128)(2,1)} %bitcast.37, f32[6,768]{1,0:T(8,128)S(1)} %reshape.78.refs_2_.refs_8_.refs_5_.refs_3_, bf16[576,768]{1,0:T(8,128)(2,1)S(1)} %bitcast.31, ...), custom_call_target="tpu_custom_call" | custom-call | flops 1 | bytes 1 | tf_op jit(solution)/shard_map/project_near/pallas_call | solution.py:108
  39.5 7.5 %keys.1 = (bf16[1536,512]{1,0:T(8,128)(2,1)}, bf16[8,2,112,128]{3,2,1,0:T(8,128)(2,1)}) custom-call(s32[5]{0:T(128)S(1)} %stack.42.refs_0_, bf16[2304,512]{1,0:T(8,128)(2,1)S(1)} %project_far.1.refs_1_.refs_0_.refs_4_.refs_3_, bf16[12,64,64]{2,1,0:T(8,128)(2,1)S(1)} %bitcast.35), custom_call_target="tpu_custom_call" | custom-call | flops 1 | bytes 1 | tf_op jit(solution)/shard_map/keys/pallas_call | solution.py:108
  47.0 5.9 %all-to-all-start = ((bf16[8,2,112,128]{3,2,1,0:T(8,128)(2,1)}), bf16[8,2,112,128]{3,2,1,0:T(8,128)(2,1)S(1)}, u32[]{:S(2)}, u32[]{:S(2)}) async-start(bf16[8,2,112,128]{3,2,1,0:T(8,128)(2,1)} %get-tuple-element.89), calls=%async_computation | async-start | bytes 917504 | tf_op jit(solution)/shard_map/all_to_all | solution.py:634
  53.1 4.4 %queries.1.refs_2_.refs_8_.refs_3_ = bf16[1536,512]{1,0:T(8,128)(2,1)} custom-call(bf16[2304,512]{1,0:T(8,128)(2,1)S(1)} %project_far.1.refs_1_.refs_0_.refs_4_.refs_3_, bf16[12,64,64]{2,1,0:T(8,128)(2,1)S(1)} %bitcast.33), custom_call_target="tpu_custom_call" | custom-call | flops 1 | bytes 1 | tf_op jit(solution)/shard_map/queries/pallas_call | solution.py:108
  57.5 7.9 %collective-permute-done.6.refs_6_.refs_7_.refs_11_ = bf16[960,768]{1,0:T(8,128)(2,1)} collective-permute-done((bf16[960,768]{1,0:T(8,128)(2,1)}, bf16[960,768]{1,0:T(8,128)(2,1)}, u32[]{:S(2)}, u32[]{:S(2)}) %collective-permute-start.6) | collective-permute-done | bytes 1474592 | tf_op jit(solution)/shard_map/ppermute | solution.py:548
  69.1 5.6 %all-to-all-start.1 = ((bf16[8,2,112,128]{3,2,1,0:T(8,128)(2,1)}), bf16[8,2,112,128]{3,2,1,0:T(8,128)(2,1)}, u32[]{:S(2)}, u32[]{:S(2)}) async-start(bf16[8,2,112,128]{3,2,1,0:T(8,128)(2,1)} %scan.1), calls=%async_computation.1 | async-start | bytes 917504 | tf_op jit(solution)/shard_map/all_to_all | solution.py:634
  79.8 7.5 %all-to-all-done.1.refs_1_ = bf16[8,2,112,128]{3,2,1,0:T(8,128)(2,1)} async-done(((bf16[8,2,112,128]{3,2,1,0:T(8,128)(2,1)}), bf16[8,2,112,128]{3,2,1,0:T(8,128)(2,1)}, u32[]{:S(2)}, u32[]{:S(2)}) %all-to-all-start.1) | async-done | bytes 458784 | tf_op jit(solution)/shard_map/all_to_all | solution.py:634
  89.2 7.6 %attend.1 = (bf16[768,512]{1,0:T(8,128)(2,1)}, f32[96,512]{1,0:T(8,128)}, f32[512,768]{1,0:T(8,128)}, bf16[512,768]{1,0:T(8,128)(2,1)}) custom-call(s32[5]{0:T(128)S(1)} %stack.42.refs_0_, bf16[8,2,112,128]{3,2,1,0:T(8,128)(2,1)} %all-to-all-done.1.refs_1_, bf16[1536,512]{1,0:T(8,128)(2,1)} %queries.1.refs_2_.refs_8_.refs_3_, bf16[512,768]{1,0:T(8,128)(2,1)} %bitcast.38, ...), custom_call_target="tpu_custom_call" | custom-call | flops 1 | bytes 1 | tf_op jit(solution)/shard_map/attend/pallas_call | solution.py:108
  97.1 4.7 %collective-permute-done.11.refs_8_ = bf16[768,768]{1,0:T(8,128)(2,1)} collective-permute-done((bf16[768,768]{1,0:T(8,128)(2,1)}, bf16[768,768]{1,0:T(8,128)(2,1)}, u32[]{:S(2)}, u32[]{:S(2)}) %collective-permute-start.11) | collective-permute-done | bytes 1179680 | tf_op jit(solution)/shard_map/ppermute | solution.py:548
  101.8 15.4 %mlp_far.1 = (f32[512,768]{1,0:T(8,128)S(1)}, f32[512,768]{1,0:T(8,128)S(1)}, bf16[512,768]{1,0:T(8,128)(2,1)S(1)}, bf16[512,768]{1,0:T(8,128)(2,1)S(1)}, bf16[7...) custom-call(s32[5]{0:T(128)S(1)} %stack.42.refs_0_, ...), custom_call_target="tpu_custom_call" | custom-call | flops 1 | bytes 1 | tf_op jit(solution)/shard_map/mlp_far/pallas_call | solution.py:108
  117.3 16.8 %mlp_near.1 = (f32[512,768]{1,0:T(8,128)}, f32[512,768]{1,0:T(8,128)S(1)}, bf16[512,768]{1,0:T(8,128)(2,1)}, bf16[512,768]{1,0:T(8,128)(2,1)}, bf16[768,768]{1,0...) custom-call(s32[5]{0:T(128)S(1)} %stack.42.refs_0_, bf16[512,768]{1,0:T(8,128)(2,1)} %get-tuple-element.93.refs_1_, ...), custom_call_target="tpu_custom_call" | custom-call | flops 1 | bytes 1 | tf_op jit(solution)/shard_map/mlp_near/pallas_call | solution.py:108
  136.6 7.7 %middle.1 = (f32[512,768]{1,0:T(8,128)}, bf16[512,768]{1,0:T(8,128)(2,1)}, bf16[960,512]{1,0:T(8,128)(2,1)}, bf16[8,2,112,128]{3,2,1,0:T(8,128)(2,1)}, f32[8,768]{1,0:T(8,128)S(1)}) custom-call(s32[5]{0:T(128)S(1)} %stack.42.refs_0_, f32[512,768]{1,0:T(8,128)S(1)} %get-tuple-element.100.refs_1_, bf16[512,768]{1,0:T(8,128)(2,1)S(1)} %collective-permute-done.12.refs_2_, ...), custom_call_target="tpu_custom_call" | custom-call | flops 1 | bytes 1 | tf_op jit(solution)/shard_map/middle/pallas_call | solution.py:108
  144.4 5.7 %all-to-all-start.2 = ((bf16[8,2,112,128]{3,2,1,0:T(8,128)(2,1)}), bf16[8,2,112,128]{3,2,1,0:T(8,128)(2,1)S(1)}, u32[]{:S(2)}, u32[]{:S(2)}) async-start(bf16[8,2,112,128]{3,2,1,0:T(8,128)(2,1)} %get-tuple-element.104), calls=%async_computation.2 | async-start | bytes 917504 | tf_op jit(solution)/shard_map/all_to_all | solution.py:634
  151.0 9.0 %query_back.1 = (bf16[768,512]{1,0:T(8,128)(2,1)}, f32[12,64,64]{2,1,0:T(8,128)}, bf16[192,768]{1,0:T(8,128)(2,1)}, bf16[192,768]{1,0:T(8,128)(2,1)}, bf16[192,7...) custom-call(s32[5]{0:T(128)S(1)} %stack.42.refs_0_, bf16[8,2,112,128]{3,2,1,0:T(8,128)(2,1)} %all-to-all-done.1.refs_1_, ...), custom_call_target="tpu_custom_call" | custom-call | flops 1 | bytes 1 | tf_op jit(solution)/shard_map/query_back/pallas_call | solution.py:108
  164.9 5.2 %all-to-all-start.3 = ((bf16[8,2,112,128]{3,2,1,0:T(8,128)(2,1)}), bf16[8,2,112,128]{3,2,1,0:T(8,128)(2,1)S(1)}, u32[]{:S(2)}, u32[]{:S(2)}) async-start(bf16[8,2,112,128]{3,2,1,0:T(8,128)(2,1)} %scan_back.1), calls=%async_computation.3 | async-start | bytes 917504 | tf_op jit(solution)/shard_map/all_to_all | solution.py:634
  175.1 15.5 %collective-permute-done.14 = bf16[384,768]{1,0:T(8,128)(2,1)} collective-permute-done((bf16[384,768]{1,0:T(8,128)(2,1)S(1)}, bf16[384,768]{1,0:T(8,128)(2,1)}, u32[]{:S(2)}, u32[]{:S(2)}) %collective-permute-start.14) | collective-permute-done | bytes 589856 | tf_op jit(solution)/shard_map/ppermute | solution.py:585
  190.6 9.5 %key_back.1 = (bf16[2304,512]{1,0:T(8,128)(2,1)S(1)}, f32[12,64,64]{2,1,0:T(8,128)}, bf16[576,768]{1,0:T(8,128)(2,1)}, bf16[576,768]{1,0:T(8,128)(2,1)}) custom-call(s32[5]{0:T(128)S(1)} %stack.42.refs_0_, bf16[8,2,112,128]{3,2,1,0:T(8,128)(2,1)S(1)} %all-to-all-done.3.refs_1_, bf16[1536,512]{1,0:T(8,128)(2,1)} %get-tuple-element.113.refs_2_, ...), custom_call_target="tpu_custom_call" | custom-call | flops 1 | bytes 1 | tf_op jit(solution)/shard_map/key_back/pallas_call | solution.py:108
  209.0 4.0 %project_grad.1 = (bf16[576,768]{1,0:T(8,128)(2,1)}, bf16[576,768]{1,0:T(8,128)(2,1)}) custom-call(s32[5]{0:T(128)S(1)} %stack.42.refs_0_, bf16[2304,512]{1,0:T(8,128)(2,1)S(1)} %copy-done.1, bf16[512,768]{1,0:T(8,128)(2,1)} %get-tuple-element.87.refs_1_.refs_6_.refs_2_, bf16[576,768]{1,0:T(8,128)(2,1)S(1)} %collective-permute-done.15.refs_3_, ...), custom_call_target="tpu_custom_call" | custom-call | flops 1 | bytes 1 | tf_op jit(solution)/shard_map/project_grad/pallas_call | solution.py:108
  213.0 8.2 %input.1 = (f32[512,768]{1,0:T(8,128)}, f32[512,768]{1,0:T(8,128)}, bf16[64,768]{1,0:T(8,128)(2,1)S(1)}, bf16[64,768]{1,0:T(8,128)(2,1)S(1)}, bf16[64,768]{1,0:T(8,128)(2,1)S(1)}, /*index=5*/bf16[64,768]{1,0:T(8,128)(2,1)S(1)}) custom-call(s32[5]{0:T(128)S(1)} %stack.42.refs_0_, bf16[2304,512]{1,0:T(8,128)(2,1)S(1)} %copy-done.2, bf16[512,768]{1,0:T(8,128)(2,1)} %bitcast.39, ...), custom_call_target="tpu_custom_call" | custom-call | flops 1 | bytes 1 | tf_op jit(solution)/shard_map/input/pallas_call | solution.py:108
  228.2 18.9 %collective-permute-done.20 = bf16[64,768]{1,0:T(8,128)(2,1)S(1)} collective-permute-done((bf16[64,768]{1,0:T(8,128)(2,1)S(1)}, bf16[64,768]{1,0:T(8,128)(2,1)S(1)}, u32[]{:S(2)}, u32[]{:S(2)}) %collective-permute-start.20) | collective-permute-done | bytes 98336 | tf_op jit(solution)/shard_map/ppermute | solution.py:548
  260.2 4.2 %collective-permute-done.36 = bf16[96,768]{1,0:T(8,128)(2,1)S(1)} collective-permute-done((bf16[96,768]{1,0:T(8,128)(2,1)S(1)}, bf16[96,768]{1,0:T(8,128)(2,1)S(1)}, u32[]{:S(2)}, u32[]{:S(2)}) %collective-permute-start.36) | collective-permute-done | bytes 147488 | tf_op jit(solution)/shard_map/ppermute | solution.py:585
  267.9 3.4 collective-permute-start.37
  282.4 4.1 %collective-permute-done.42 = bf16[96,768]{1,0:T(8,128)(2,1)S(1)} collective-permute-done((bf16[96,768]{1,0:T(8,128)(2,1)S(1)}, bf16[96,768]{1,0:T(8,128)(2,1)S(1)}, u32[]{:S(2)}, u32[]{:S(2)}) %collective-permute-start.42) | collective-permute-done | bytes 147488 | tf_op jit(solution)/shard_map/ppermute | solution.py:585
  291.0 3.7 %collective-permute-done.38 = bf16[192,768]{1,0:T(8,128)(2,1)S(1)} collective-permute-done((bf16[192,768]{1,0:T(8,128)(2,1)S(1)}, bf16[192,768]{1,0:T(8,128)(2,1)S(1)}, u32[]{:S(2)}, u32[]{:S(2)}) %collective-permute-start.38) | collective-permute-done | bytes 294944 | tf_op jit(solution)/shard_map/ppermute | solution.py:597
  294.9 4.4 %collective-permute-done.30 = bf16[192,768]{1,0:T(8,128)(2,1)S(1)} collective-permute-done((bf16[192,768]{1,0:T(8,128)(2,1)S(1)}, bf16[192,768]{1,0:T(8,128)(2,1)S(1)}, u32[]{:S(2)}, u32[]{:S(2)}) %collective-permute-start.30) | collective-permute-done | bytes 294944 | tf_op jit(solution)/shard_map/ppermute | solution.py:585
  302.5 5.1 %collective-permute-done.31 = bf16[96,768]{1,0:T(8,128)(2,1)S(1)} collective-permute-done((bf16[96,768]{1,0:T(8,128)(2,1)S(1)}, bf16[96,768]{1,0:T(8,128)(2,1)S(1)}, u32[]{:S(2)}, u32[]{:S(2)}) %collective-permute-start.31) | collective-permute-done | bytes 147488 | tf_op jit(solution)/shard_map/ppermute | solution.py:585
  308.3 4.6 %collective-permute-done.44 = bf16[192,768]{1,0:T(8,128)(2,1)S(1)} collective-permute-done((bf16[192,768]{1,0:T(8,128)(2,1)S(1)}, bf16[192,768]{1,0:T(8,128)(2,1)S(1)}, u32[]{:S(2)}, u32[]{:S(2)}) %collective-permute-start.44) | collective-permute-done | bytes 294944 | tf_op jit(solution)/shard_map/ppermute | solution.py:597
  317.4 5.1 %collective-permute-done.33 = bf16[192,768]{1,0:T(8,128)(2,1)S(1)} collective-permute-done((bf16[192,768]{1,0:T(8,128)(2,1)S(1)}, bf16[192,768]{1,0:T(8,128)(2,1)S(1)}, u32[]{:S(2)}, u32[]{:S(2)}) %collective-permute-start.33) | collective-permute-done | bytes 294944 | tf_op jit(solution)/shard_map/ppermute | solution.py:597
  324.3 7.8 %collective-permute-done.45 = bf16[384,768]{1,0:T(8,128)(2,1)S(1)} collective-permute-done((bf16[384,768]{1,0:T(8,128)(2,1)S(1)}, bf16[384,768]{1,0:T(8,128)(2,1)S(1)}, u32[]{:S(2)}, u32[]{:S(2)}) %collective-permute-start.45) | collective-permute-done | bytes 589856 | tf_op jit(solution)/shard_map/ppermute | solution.py:597
  333.9 7.4 %collective-permute-done.34 = bf16[384,768]{1,0:T(8,128)(2,1)S(1)} collective-permute-done((bf16[384,768]{1,0:T(8,128)(2,1)S(1)}, bf16[384,768]{1,0:T(8,128)(2,1)S(1)}, u32[]{:S(2)}, u32[]{:S(2)}) %collective-permute-start.34) | collective-permute-done | bytes 589856 | tf_op jit(solution)/shard_map/ppermute | solution.py:597
  (245 shorter events, 102.4 us)
Async XLA Ops:
  0.6 29.4 %collective-permute-start.4 = (bf16[576,768]{1,0:T(8,128)(2,1)}, bf16[576,768]{1,0:T(8,128)(2,1)S(1)}, u32[]{:S(2)}, u32[]{:S(2)}) collective-permute-start(bf16[576,768]{1,0:T(8,128)(2,1)} %bitcast.29), channel_id=1, source_target_pairs={{0,2},{1,3},{2,0},{3,1},{4,6},{5,7},{6,4},{7,5},{8,10},{9,11},{10,... | collective-permute-start | bytes 2654216 | tf_op jit(solution)/shard_map/ppermute | solution.py:548
  10.1 15.8 %collective-permute-start = (bf16[432,64]{1,0:T(8,128)(2,1)S(1)}, bf16[432,64]{1,0:T(8,128)(2,1)S(1)}, u32[]{:S(2)}, u32[]{:S(2)}) collective-permute-start(bf16[432,64]{1,0:T(8,128)(2,1)S(1)} %pad_maximum_fusion.10), channel_id=1, source_target_pairs={{0,2},{1,3},{2,0},{3,1},{4,6},{5,7},{6,4},{7,5},{8,10},{9,11},{10,... | collective-permute-start | bytes 165896 | tf_op jit(solution)/shard_map/ppermute | solution.py:548
  10.2 17.7 %collective-permute-start.2 = (bf16[432,64]{1,0:T(8,128)(2,1)S(1)}, bf16[432,64]{1,0:T(8,128)(2,1)S(1)}, u32[]{:S(2)}, u32[]{:S(2)}) collective-permute-start(bf16[432,64]{1,0:T(8,128)(2,1)S(1)} %pad_maximum_fusion.10), channel_id=1, source_target_pairs={{0,1},{1,0},{2,3},{3,2},{4,5},{5,4},{6,7},{7,6},{8,9},{9,8},{10,11... | collective-permute-start | bytes 165896 | tf_op jit(solution)/shard_map/ppermute | solution.py:544
  10.2 22.5 %collective-permute-start.3 = (bf16[576,768]{1,0:T(8,128)(2,1)}, bf16[576,768]{1,0:T(8,128)(2,1)S(1)}, u32[]{:S(2)}, u32[]{:S(2)}) collective-permute-start(bf16[576,768]{1,0:T(8,128)(2,1)} %bitcast.30), channel_id=1, source_target_pairs={{0,1},{1,0},{2,3},{3,2},{4,5},{5,4},{6,7},{7,6},{8,9},{9,8},{10,11... | collective-permute-start | bytes 2654216 | tf_op jit(solution)/shard_map/ppermute | solution.py:544
  30.8 34.5 %collective-permute-start.6 = (bf16[960,768]{1,0:T(8,128)(2,1)}, bf16[960,768]{1,0:T(8,128)(2,1)}, u32[]{:S(2)}, u32[]{:S(2)}) collective-permute-start(bf16[960,768]{1,0:T(8,128)(2,1)} %pad_maximum_fusion), channel_id=1, source_target_pairs={{0,2},{1,3},{2,0},{3,1},{4,6},{5,7},{6,4},{7,5},{8,10},{9,11},{10,... | collective-permute-start | bytes 4423688 | tf_op jit(solution)/shard_map/ppermute | solution.py:548
  47.0 18.9 %all-to-all-start = ((bf16[8,2,112,128]{3,2,1,0:T(8,128)(2,1)}), bf16[8,2,112,128]{3,2,1,0:T(8,128)(2,1)S(1)}, u32[]{:S(2)}, u32[]{:S(2)}) async-start(bf16[8,2,112,128]{3,2,1,0:T(8,128)(2,1)} %get-tuple-element.89), calls=%async_computation | async-start | bytes 917504 | tf_op jit(solution)/shard_map/all_to_all | solution.py:634
  69.1 18.2 %all-to-all-start.1 = ((bf16[8,2,112,128]{3,2,1,0:T(8,128)(2,1)}), bf16[8,2,112,128]{3,2,1,0:T(8,128)(2,1)}, u32[]{:S(2)}, u32[]{:S(2)}) async-start(bf16[8,2,112,128]{3,2,1,0:T(8,128)(2,1)} %scan.1), calls=%async_computation.1 | async-start | bytes 917504 | tf_op jit(solution)/shard_map/all_to_all | solution.py:634
  74.7 27.1 %collective-permute-start.11 = (bf16[768,768]{1,0:T(8,128)(2,1)}, bf16[768,768]{1,0:T(8,128)(2,1)}, u32[]{:S(2)}, u32[]{:S(2)}) collective-permute-start(bf16[768,768]{1,0:T(8,128)(2,1)} %refs_8_.1), channel_id=1, source_target_pairs={{0,2},{1,3},{2,0},{3,1},{4,6},{5,7},{6,4},{7,5},{8,10},{9,11},{10,... | collective-permute-start | bytes 3538952 | tf_op jit(solution)/shard_map/ppermute | solution.py:548
  77.8 19.2 %collective-permute-start.10 = (bf16[512,768]{1,0:T(8,128)(2,1)S(1)}, bf16[512,768]{1,0:T(8,128)(2,1)}, u32[]{:S(2)}, u32[]{:S(2)}) collective-permute-start(bf16[512,768]{1,0:T(8,128)(2,1)S(1)} %bitcast.25), channel_id=1, source_target_pairs={{0,1},{1,0},{2,3},{3,2},{4,5},{5,4},{6,7},{7,6},{8,9},{9,8},{10,11... | collective-permute-start | bytes 2359304 | tf_op jit(solution)/shard_map/ppermute | solution.py:544
  134.1 28.7 %collective-permute-start.13 = (bf16[768,768]{1,0:T(8,128)(2,1)}, bf16[768,768]{1,0:T(8,128)(2,1)}, u32[]{:S(2)}, u32[]{:S(2)}) collective-permute-start(bf16[768,768]{1,0:T(8,128)(2,1)} %get-tuple-element.108), channel_id=1, source_target_pairs={{0,2},{1,3},{2,0},{3,1},{4,6},{5,7},{6,4},{7,5},{8,10},{9,11},{10,... | collective-permute-start | bytes 3538952 | tf_op jit(solution)/shard_map/ppermute | solution.py:548
  144.4 19.1 %all-to-all-start.2 = ((bf16[8,2,112,128]{3,2,1,0:T(8,128)(2,1)}), bf16[8,2,112,128]{3,2,1,0:T(8,128)(2,1)S(1)}, u32[]{:S(2)}, u32[]{:S(2)}) async-start(bf16[8,2,112,128]{3,2,1,0:T(8,128)(2,1)} %get-tuple-element.104), calls=%async_computation.2 | async-start | bytes 917504 | tf_op jit(solution)/shard_map/all_to_all | solution.py:634
  164.9 25.7 %all-to-all-start.3 = ((bf16[8,2,112,128]{3,2,1,0:T(8,128)(2,1)}), bf16[8,2,112,128]{3,2,1,0:T(8,128)(2,1)S(1)}, u32[]{:S(2)}, u32[]{:S(2)}) async-start(bf16[8,2,112,128]{3,2,1,0:T(8,128)(2,1)} %scan_back.1), calls=%async_computation.3 | async-start | bytes 917504 | tf_op jit(solution)/shard_map/all_to_all | solution.py:634
  171.5 19.1 %collective-permute-start.14 = (bf16[384,768]{1,0:T(8,128)(2,1)S(1)}, bf16[384,768]{1,0:T(8,128)(2,1)}, u32[]{:S(2)}, u32[]{:S(2)}) collective-permute-start(bf16[384,768]{1,0:T(8,128)(2,1)S(1)} %add_convert_fusion.2), channel_id=1, source_target_pairs={{0,4},{4,0},{8,12},{12,8},{16,20},{20,16},{24,28},{28,24},{1,5},{5... | collective-permute-start | bytes 1769480 | tf_op jit(solution)/shard_map/ppermute | solution.py:585
  173.6 32.2 %collective-permute-start.26 = (bf16[768,768]{1,0:T(8,128)(2,1)}, bf16[768,768]{1,0:T(8,128)(2,1)}, u32[]{:S(2)}, u32[]{:S(2)}) collective-permute-start(bf16[768,768]{1,0:T(8,128)(2,1)} %get-tuple-element.143), channel_id=1, source_target_pairs={{0,2},{1,3},{2,0},{3,1},{4,6},{5,7},{6,4},{7,5},{8,10},{9,11},{10,... | collective-permute-start | bytes 3538952 | tf_op jit(solution)/shard_map/ppermute | solution.py:548
  202.1 10.9 %collective-permute-start.17 = (bf16[512,768]{1,0:T(8,128)(2,1)}, bf16[512,768]{1,0:T(8,128)(2,1)S(1)}, u32[]{:S(2)}, u32[]{:S(2)}) collective-permute-start(bf16[512,768]{1,0:T(8,128)(2,1)} %get-tuple-element.122), channel_id=1, source_target_pairs={{0,1},{1,0},{2,3},{3,2},{4,5},{5,4},{6,7},{7,6},{8,9},{9,8},{10,11... | collective-permute-start | bytes 2359304 | tf_op jit(solution)/shard_map/ppermute | solution.py:544
  204.8 16.6 %collective-permute-start.24 = (bf16[192,768]{1,0:T(8,128)(2,1)}, bf16[192,768]{1,0:T(8,128)(2,1)}, u32[]{:S(2)}, u32[]{:S(2)}) collective-permute-start(bf16[192,768]{1,0:T(8,128)(2,1)} %get-tuple-element.138), channel_id=1, source_target_pairs={{0,1},{1,0},{2,3},{3,2},{4,5},{5,4},{6,7},{7,6},{8,9},{9,8},{10,11... | collective-permute-start | bytes 884744 | tf_op jit(solution)/shard_map/ppermute | solution.py:544
  205.8 15.6 %collective-permute-start.27 = (bf16[192,768]{1,0:T(8,128)(2,1)}, bf16[192,768]{1,0:T(8,128)(2,1)}, u32[]{:S(2)}, u32[]{:S(2)}) collective-permute-start(bf16[192,768]{1,0:T(8,128)(2,1)} %add_convert_fusion.7), channel_id=1, source_target_pairs={{0,2},{1,3},{2,0},{3,1},{4,6},{5,7},{6,4},{7,5},{8,10},{9,11},{10,... | collective-permute-start | bytes 884744 | tf_op jit(solution)/shard_map/ppermute | solution.py:548
  223.1 50.2 %collective-permute-start.28 = (bf16[576,768]{1,0:T(8,128)(2,1)}, bf16[576,768]{1,0:T(8,128)(2,1)S(1)}, u32[]{:S(2)}, u32[]{:S(2)}) collective-permute-start(bf16[576,768]{1,0:T(8,128)(2,1)} %get-tuple-element.146), channel_id=1, source_target_pairs={{0,2},{1,3},{2,0},{3,1},{4,6},{5,7},{6,4},{7,5},{8,10},{9,11},{10,... | collective-permute-start | bytes 2654216 | tf_op jit(solution)/shard_map/ppermute | solution.py:548
  223.7 23.5 %collective-permute-start.20 = (bf16[64,768]{1,0:T(8,128)(2,1)S(1)}, bf16[64,768]{1,0:T(8,128)(2,1)S(1)}, u32[]{:S(2)}, u32[]{:S(2)}) collective-permute-start(bf16[64,768]{1,0:T(8,128)(2,1)S(1)} %add_convert_fusion.18), channel_id=1, source_target_pairs={{0,2},{1,3},{2,0},{3,1},{4,6},{5,7},{6,4},{7,5},{8,10},{9,11},{10,... | collective-permute-start | bytes 294920 | tf_op jit(solution)/shard_map/ppermute | solution.py:548
  226.4 28.3 %collective-permute-start.35 = (bf16[192,768]{1,0:T(8,128)(2,1)S(1)}, bf16[192,768]{1,0:T(8,128)(2,1)S(1)}, u32[]{:S(2)}, u32[]{:S(2)}) collective-permute-start(bf16[192,768]{1,0:T(8,128)(2,1)S(1)} %add_convert_fusion.4), channel_id=1, source_target_pairs={{0,8},{4,12},{8,0},{12,4},{16,24},{20,28},{24,16},{28,20},{1,9},{5... | collective-permute-start | bytes 884744 | tf_op jit(solution)/shard_map/ppermute | solution.py:585
  249.0 16.5 %collective-permute-start.40 = (bf16[384,768]{1,0:T(8,128)(2,1)S(1)}, bf16[384,768]{1,0:T(8,128)(2,1)S(1)}, u32[]{:S(2)}, u32[]{:S(2)}) collective-permute-start(bf16[384,768]{1,0:T(8,128)(2,1)S(1)} %add_convert_fusion), channel_id=1, source_target_pairs={{0,4},{4,0},{8,12},{12,8},{16,20},{20,16},{24,28},{28,24},{1,5},{5... | collective-permute-start | bytes 1769480 | tf_op jit(solution)/shard_map/ppermute | solution.py:585
  255.8 8.6 %collective-permute-start.36 = (bf16[96,768]{1,0:T(8,128)(2,1)S(1)}, bf16[96,768]{1,0:T(8,128)(2,1)S(1)}, u32[]{:S(2)}, u32[]{:S(2)}) collective-permute-start(bf16[96,768]{1,0:T(8,128)(2,1)S(1)} %add_convert_fusion.12), channel_id=1, source_target_pairs={{0,16},{4,20},{8,24},{12,28},{16,0},{20,4},{24,8},{28,12},{1,17},{... | collective-permute-start | bytes 442376 | tf_op jit(solution)/shard_map/ppermute | solution.py:585
  258.0 9.9 %collective-permute-start.23 = (bf16[64,768]{1,0:T(8,128)(2,1)S(1)}, bf16[64,768]{1,0:T(8,128)(2,1)S(1)}, u32[]{:S(2)}, u32[]{:S(2)}) collective-permute-start(bf16[64,768]{1,0:T(8,128)(2,1)S(1)} %add_convert_fusion.15), channel_id=1, source_target_pairs={{0,16},{4,20},{8,24},{12,28},{16,0},{20,4},{24,8},{28,12},{1,17},{... | collective-permute-start | bytes 294920 | tf_op jit(solution)/shard_map/ppermute | solution.py:617
  267.5 10.1 %collective-permute-start.41 = (bf16[192,768]{1,0:T(8,128)(2,1)}, bf16[192,768]{1,0:T(8,128)(2,1)}, u32[]{:S(2)}, u32[]{:S(2)}) collective-permute-start(bf16[192,768]{1,0:T(8,128)(2,1)} %add_convert_fusion.3), channel_id=1, source_target_pairs={{0,8},{4,12},{8,0},{12,4},{16,24},{20,28},{24,16},{28,20},{1,9},{5... | collective-permute-start | bytes 884744 | tf_op jit(solution)/shard_map/ppermute | solution.py:585
  267.9 11.8 %collective-permute-start.37 = (bf16[96,768]{1,0:T(8,128)(2,1)S(1)}, bf16[96,768]{1,0:T(8,128)(2,1)S(1)}, u32[]{:S(2)}, u32[]{:S(2)}) collective-permute-start(bf16[96,768]{1,0:T(8,128)(2,1)S(1)} %add_convert_fusion.11), channel_id=1, source_target_pairs={{0,16},{4,20},{8,24},{12,28},{16,0},{20,4},{24,8},{28,12},{1,17},{... | collective-permute-start | bytes 442376 | tf_op jit(solution)/shard_map/ppermute | solution.py:597
  273.9 14.6 %collective-permute-start.29 = (bf16[384,768]{1,0:T(8,128)(2,1)S(1)}, bf16[384,768]{1,0:T(8,128)(2,1)S(1)}, u32[]{:S(2)}, u32[]{:S(2)}) collective-permute-start(bf16[384,768]{1,0:T(8,128)(2,1)S(1)} %add_convert_fusion.1), channel_id=1, source_target_pairs={{0,4},{4,0},{8,12},{12,8},{16,20},{20,16},{24,28},{28,24},{1,5},{5... | collective-permute-start | bytes 1769480 | tf_op jit(solution)/shard_map/ppermute | solution.py:585
  279.8 14.9 %collective-permute-start.38 = (bf16[192,768]{1,0:T(8,128)(2,1)S(1)}, bf16[192,768]{1,0:T(8,128)(2,1)S(1)}, u32[]{:S(2)}, u32[]{:S(2)}) collective-permute-start(bf16[192,768]{1,0:T(8,128)(2,1)S(1)} %pad_maximum_fusion.6), channel_id=1, source_target_pairs={{0,8},{4,12},{8,0},{12,4},{16,24},{20,28},{24,16},{28,20},{1,9},{5... | collective-permute-start | bytes 884744 | tf_op jit(solution)/shard_map/ppermute | solution.py:597
  288.8 10.4 %collective-permute-start.30 = (bf16[192,768]{1,0:T(8,128)(2,1)S(1)}, bf16[192,768]{1,0:T(8,128)(2,1)S(1)}, u32[]{:S(2)}, u32[]{:S(2)}) collective-permute-start(bf16[192,768]{1,0:T(8,128)(2,1)S(1)} %add_convert_fusion.5), channel_id=1, source_target_pairs={{0,8},{4,12},{8,0},{12,4},{16,24},{20,28},{24,16},{28,20},{1,9},{5... | collective-permute-start | bytes 884744 | tf_op jit(solution)/shard_map/ppermute | solution.py:585
  300.5 12.4 %collective-permute-start.44 = (bf16[192,768]{1,0:T(8,128)(2,1)S(1)}, bf16[192,768]{1,0:T(8,128)(2,1)S(1)}, u32[]{:S(2)}, u32[]{:S(2)}) collective-permute-start(bf16[192,768]{1,0:T(8,128)(2,1)S(1)} %pad_maximum_fusion.7), channel_id=1, source_target_pairs={{0,8},{4,12},{8,0},{12,4},{16,24},{20,28},{24,16},{28,20},{1,9},{5... | collective-permute-start | bytes 884744 | tf_op jit(solution)/shard_map/ppermute | solution.py:597
  302.5 14.7 %collective-permute-start.39 = (bf16[384,768]{1,0:T(8,128)(2,1)S(1)}, bf16[384,768]{1,0:T(8,128)(2,1)S(1)}, u32[]{:S(2)}, u32[]{:S(2)}) collective-permute-start(bf16[384,768]{1,0:T(8,128)(2,1)S(1)} %pad_maximum_fusion.3), channel_id=1, source_target_pairs={{0,4},{4,0},{8,12},{12,8},{16,20},{20,16},{24,28},{28,24},{1,5},{5... | collective-permute-start | bytes 1769480 | tf_op jit(solution)/shard_map/ppermute | solution.py:597
  315.8 16.3 %collective-permute-start.45 = (bf16[384,768]{1,0:T(8,128)(2,1)S(1)}, bf16[384,768]{1,0:T(8,128)(2,1)S(1)}, u32[]{:S(2)}, u32[]{:S(2)}) collective-permute-start(bf16[384,768]{1,0:T(8,128)(2,1)S(1)} %pad_maximum_fusion.4), channel_id=1, source_target_pairs={{0,4},{4,0},{8,12},{12,8},{16,20},{20,16},{24,28},{28,24},{1,5},{5... | collective-permute-start | bytes 1769480 | tf_op jit(solution)/shard_map/ppermute | solution.py:597
  322.6 18.7 %collective-permute-start.34 = (bf16[384,768]{1,0:T(8,128)(2,1)S(1)}, bf16[384,768]{1,0:T(8,128)(2,1)S(1)}, u32[]{:S(2)}, u32[]{:S(2)}) collective-permute-start(bf16[384,768]{1,0:T(8,128)(2,1)S(1)} %pad_maximum_fusion.2), channel_id=1, source_target_pairs={{0,4},{4,0},{8,12},{12,8},{16,20},{20,16},{24,28},{28,24},{1,5},{5... | collective-permute-start | bytes 1769480 | tf_op jit(solution)/shard_map/ppermute | solution.py:597
  (64 other events, 516.2 us)

commit v3 on v2

--- a/solution.py
+++ b/solution.py
@@ -12,6 +12,7 @@
 BF16 = jnp.bfloat16
 AUG = 80
 KEEP = 72
+UNROLL = 3
 NN = (((1,), (0,)), ((), ()))
 NT = (((1,), (1,)), ((), ()))
 TN = (((0,), (0,)), ((), ()))
@@ -29,28 +30,41 @@
 
 
 class Staged:
-    def __init__(self, far, near, sem, out):
+    def __init__(self, far, near, sems, out):
         self.near, self.state = near, "out" if out else "in"
-        self.copy = pltpu.make_async_copy(*((near, far) if out else (far, near)), sem)
+        self.copies, at = [], 0
+        for part, sem in zip(far, sems):
+            here = near if len(far) == 1 else near.at[pl.ds(at, part.shape[0])]
+            pair = (here, part) if out else (part, here)
+            self.copies.append(pltpu.make_async_copy(*pair, sem))
+            at += part.shape[0]
         self.shape, self.dtype = near.shape, near.dtype
         if not out:
-            self.copy.start()
+            self.start()
+
+    def start(self):
+        for copy in self.copies:
+            copy.start()
+
+    def wait(self):
+        for copy in self.copies:
+            copy.wait()
 
     def ready(self):
         if self.state == "in":
-            self.copy.wait()
+            self.wait()
             self.state = "ready"
 
     def flush(self):
         if self.state == "out":
-            self.copy.start()
+            self.start()
             self.state = "flushed"
 
     def finish(self):
         self.ready()
         self.flush()
         if self.state == "flushed":
-            self.copy.wait()
+            self.wait()
             self.state = "done"
 
     def __getitem__(self, index):
@@ -77,40 +91,50 @@
 def call(kernel, outs, kinds, args, name, scratch=(), out_kinds=None, limit=32):
     out_kinds = out_kinds or "v" * len(outs)
     both = kinds + out_kinds
-    spans = [a[1:] if isinstance(a, tuple) else (0, a.shape[0]) for a in [*args, *outs]]
-    args = [a[0] if isinstance(a, tuple) else a for a in args]
+    groups = [a if isinstance(a, list) else [a] for a in [*args, *outs]]
+    groups = [
+        [p if isinstance(p, tuple) else (p, 0, p.shape[0]) for p in group] for group in groups
+    ]
+    operands = [(p[0], k) for group, k in zip(groups[: len(kinds)], kinds) for p in group]
+    pieces = sum(len(group) for group, k in zip(groups, both) if k in "ha")
     staged = [
-        pltpu.VMEM((size, *a.shape[1:]), a.dtype)
-        for a, k, (_, size) in zip([*args, *outs], both, spans) if k in "ha"
+        pltpu.VMEM((sum(p[2] for p in group), *group[0][0].shape[1:]), group[0][0].dtype)
+        for group, k in zip(groups, both) if k in "ha"
     ]
 
     def run(*refs):
-        count = len(both)
+        count = sum(len(group) for group in groups)
         extra = len(staged)
         near = refs[count : count + extra]
         sems = refs[count + extra] if extra else None
         rest = refs[count + extra + (1 if extra else 0) :]
-        use, at = [], 0
-        for i, kind in enumerate(both):
+        use, at, ref_at, sem_at = [], 0, 0, 0
+        for i, (kind, group) in enumerate(zip(both, groups)):
+            mine = refs[ref_at : ref_at + len(group)]
+            ref_at += len(group)
             if kind in "ha":
-                start, size = spans[i]
-                far = refs[i] if refs[i].shape[0] == size else refs[i].at[pl.ds(start, size)]
-                use.append(Staged(far, near[at], sems.at[at], i >= len(kinds)))
+                far = [
+                    ref if ref.shape[0] == size else ref.at[pl.ds(start, size)]
+                    for ref, (_, start, size) in zip(mine, group)
+                ]
+                own = [sems.at[sem_at + j] for j in range(len(group))]
+                sem_at += len(group)
+                use.append(Staged(far, near[at], own, i >= len(kinds)))
                 at += 1
             else:
-                use.append(refs[i])
+                use.append(mine[0])
         kernel(*use, *rest)
         for ref in use:
             if isinstance(ref, Staged):
                 ref.finish()
 
-    sems = [pltpu.SemaphoreType.DMA((len(staged),))] if staged else []
+    sems = [pltpu.SemaphoreType.DMA((pieces,))] if staged else []
     return pl.pallas_call(
         run,
         out_shape=[
             pltpu.HBM(o.shape, o.dtype) if k == "h" else o for o, k in zip(outs, out_kinds)
         ],
-        in_specs=[SPECS[k] for k in kinds],
+        in_specs=[SPECS[k] for _, k in operands],
         out_specs=[SPECS[k] for k in out_kinds],
         scratch_shapes=[*staged, *sems, *scratch],
         compiler_params=pltpu.CompilerParams(vmem_limit_bytes=limit << 20),
@@ -118,7 +142,7 @@
         name=name,
     )(*[
         pltpu.with_memory_space_constraint(a, pltpu.HBM) if k == "h" else a
-        for a, k in zip(args, kinds)
+        for a, k in operands
     ])
 
 
@@ -191,8 +215,8 @@
     logits = mm(map_ref[h], rows, TN)
     up = jnp.exp(logits - jnp.max(logits, axis=0, keepdims=True))
     down = jnp.exp(jnp.min(logits, axis=0, keepdims=True) - logits)
-    p1 = up / jnp.sum(up, axis=0, keepdims=True)
-    p2 = down / jnp.sum(down, axis=0, keepdims=True)
+    p1 = up * (1.0 / jnp.sum(up, axis=0, keepdims=True))
+    p2 = down * (1.0 / jnp.sum(down, axis=0, keepdims=True))
     return p1.astype(BF16), p2.astype(BF16)
 
 
@@ -216,7 +240,7 @@
             total[s ^ meta[4], pl.ds(pl.multiple_of(h * KEEP, 8), KEEP), :] = state[:KEEP]
         return carry
 
-    lax.fori_loop(0, heads, head, 0)
+    lax.fori_loop(0, heads, head, 0, unroll=UNROLL)
     flush(fk_ref)
     spread_states(total, s_ref, parts, rows_per)
 
@@ -229,7 +253,7 @@
         fq_ref[pl.ds(pl.multiple_of(at + 64, 64), 64), :] = p2
         return carry
 
-    lax.fori_loop(0, heads, head, 0)
+    lax.fori_loop(0, heads, head, 0, unroll=UNROLL)
 
 
 def scan_kernel(nctx, backward, keep, in_ref, out_ref):
@@ -250,7 +274,7 @@
 
 def attend_kernel(
     heads, slots, parts, meta, c_ref, fq_ref, x_ref, w0, w1, w2, w3, p_ref,
-    mixed_ref, den_ref, middle_ref, n2_ref, total, wo,
+    mixed_ref, den_ref, middle_ref, n2_ref, wo, total,
 ):
     cols = fq_ref.shape[1] // slots
     collect_states(c_ref, total, parts, c_ref.shape[2])
@@ -263,14 +287,16 @@
             c = total[s ^ meta[4], pl.ds(pl.multiple_of(h * KEEP, 8), AUG), :].astype(BF16)
             both = mm(c, fq[:, part], NN)
             den = both[64:65]
-            mixed_ref[pl.ds(pl.multiple_of(h * 64, 64), 64), part] = (both[:64] / den).astype(BF16)
+            mixed = both[:64] * (1.0 / den)
+            mixed_ref[pl.ds(pl.multiple_of(h * 64, 64), 64), part] = mixed.astype(BF16)
             den_ref[pl.ds(pl.multiple_of(h * 8, 8), 8), part] = jnp.broadcast_to(den, (8, cols))
         return carry
 
-    lax.fori_loop(0, heads, head, 0)
+    lax.fori_loop(0, heads, head, 0, unroll=UNROLL)
     flush(mixed_ref, den_ref)
     ready(x_ref, w0, w1, w2, w3)
     fill_output(meta, (w0, w1, w2, w3), wo)
+    flush(wo)
     middle = x_ref[...].astype(F32) + mm(mixed_ref[...], wo[...], TN) + p_ref[4:5]
     middle_ref[...] = middle
     flush(middle_ref)
@@ -279,72 +305,75 @@
     n2_ref[...] = n2
 
 
-def mlp_kernel(tile, first, meta, n2_ref, n2o_ref, cot_ref, coto_ref, base_ref, eb_ref, we, wr, *refs):
+def mlp_kernel(first, meta, n2_ref, we, n2o_ref, cot_ref, wr, coto_ref, base_ref, eb_ref, *refs):
     if first:
-        out_ref, dn_ref, outo_ref, dno_ref, ge, gr, gb_ref, n2t, acc = refs
-        dn_ref[...] = jnp.zeros_like(dn_ref)
-        acc[...] = jnp.zeros_like(acc)
+        out_ref, dn_ref, outo_ref, dno_ref, ge, ge_low, gr, gb_ref, act, hid = refs
     else:
-        back_ref, baseo_ref, backo_ref = refs[:3]
-        out_ref, dn_ref, outo_ref, dno_ref, ge, gr, gb_ref, n2t, acc = refs[3:]
-        dn_ref[...] = back_ref[...]
-        acc[0] = baseo_ref[...].astype(F32)
-        acc[1] = backo_ref[...].astype(F32)
-    ready(base_ref)
-    out_ref[...] = base_ref[...]
-    rows_n = n2_ref.shape[0]
+        back_ref, baseo_ref, backo_ref, out_ref, dn_ref, outo_ref, dno_ref, ge, gr, gb_ref, act, hid = refs
+    rows_n, width = n2_ref.shape
     line = meta[2] if first else meta[0]
-    ready(n2_ref, n2o_ref)
-    for half, ref in enumerate((n2_ref, n2o_ref)):
-        n2t[:, half * rows_n : (half + 1) * rows_n] = ref[...].T
-    ready(we, wr, cot_ref, coto_ref)
+    tile = we.shape[1] // 2
+    ready(n2_ref, we, n2o_ref, cot_ref, wr, coto_ref)
 
     def step(t, carry):
         at = pl.ds(pl.multiple_of(t * tile, tile), tile)
-        w_in = we[:, at]
-        w_out = wr[at, :]
         bias = eb_ref[pl.ds(line, 1), at]
+        pre = [
+            (mm(n[...], we[:, at], NN) + bias, mm(c[...], wr[at, :], NT))
+            for n, c in ((n2_ref, cot_ref), (n2o_ref, coto_ref))
+        ]
         actives, hiddens, sums = [], [], None
-        for half, (n_ref, c_ref) in enumerate(((n2_ref, cot_ref), (n2o_ref, coto_ref))):
-            hidden = mm(n_ref[...], w_in, NN) + bias
+        for k, (hidden, back) in enumerate(pre):
             square = hidden * hidden
-            inner = 0.7978845608028654 * hidden * (1.0 + 0.044715 * square)
-            tanh = jnp.tanh(inner)
-            part = 0.5 * (1.0 + tanh)
-            active = (hidden * part).astype(BF16)
-            slope = part + 0.5 * hidden * (1.0 - tanh * tanh) * (
-                0.7978845608028654 * (1.0 + 0.134145 * square)
+            part = 0.5 + 0.5 * jnp.tanh(
+                hidden * (0.7978845608028654 + 0.035677408136300125 * square)
             )
-            r_active = mm(c_ref[...], w_out, NT).astype(BF16).astype(F32)
-            r_hidden = (r_active * slope).astype(BF16)
-            if half == 0:
-                out_ref[...] += mm(active, w_out, NN)
-                dn_ref[...] += mm(r_hidden, w_in, NT)
-            else:
-                acc[0] += mm(active, w_out, NN)
-                acc[1] += mm(r_hidden, w_in, NT)
-            actives.append(active)
-            hiddens.append(r_hidden)
-            total = jnp.sum(r_hidden.astype(F32), axis=0, keepdims=True)
+            active = hidden * part
+            slope = part + active * (1.0 - part) * (
+                1.5957691216057308 + 0.21406444881780075 * square
+            )
+            r_hidden = back.astype(BF16).astype(F32) * slope
+            actives.append(active.astype(BF16))
+            hiddens.append(r_hidden.astype(BF16))
+            act[k, :, at] = actives[k]
+            hid[k, :, at] = hiddens[k]
+            total = jnp.sum(r_hidden, axis=0, keepdims=True)
             sums = total if sums is None else sums + total
+        gb_ref[:, at] = jnp.broadcast_to(sums, (8, tile))
+        grad = (mm(n2_ref[...], hiddens[0], TN) + mm(n2o_ref[...], hiddens[1], TN)).astype(BF16)
+        if first:
+            ge[:, at] = grad[: width // 2]
+            ge_low[:, at] = grad[width // 2 :]
+        else:
+            ge[:, at] = grad
         gr[at, :] = (
             mm(actives[0], cot_ref[...], TN) + mm(actives[1], coto_ref[...], TN)
         ).astype(BF16)
-        ge[:, at] = (
-            mm(n2t[:, :rows_n], hiddens[0], NN) + mm(n2t[:, rows_n:], hiddens[1], NN)
-        ).astype(BF16)
-        gb_ref[:, at] = jnp.broadcast_to(sums, (8, tile))
         return carry
 
-    lax.fori_loop(0, we.shape[1] // tile, step, 0)
+    lax.fori_loop(0, 2, step, 0)
     flush(ge, gr)
-    outo_ref[...] = acc[0].astype(BF16)
-    dno_ref[...] = acc[1].astype(BF16)
+    if first:
+        flush(ge_low)
+    ready(base_ref)
+    dno = mm(hid[1], we[...], NT)
+    outo = mm(act[1], wr[...], NN)
+    if first:
+        dno_ref[...] = dno.astype(BF16)
+        outo_ref[...] = outo.astype(BF16)
+        dn_ref[...] = mm(hid[0], we[...], NT)
+    else:
+        dno_ref[...] = (backo_ref[...].astype(F32) + dno).astype(BF16)
+        flush(dno_ref)
+        outo_ref[...] = (baseo_ref[...].astype(F32) + outo).astype(BF16)
+        flush(outo_ref)
+        dn_ref[...] = back_ref[...] + mm(hid[0], we[...], NT)
+    out_ref[...] = base_ref[...] + mm(act[0], wr[...], NN)
 
 
 def middle_kernel(
     heads, slots, parts, meta, dn_ref, dnin_ref, middle_ref, cot_ref, p_ref, mixed_ref, den_ref, fq_ref,
-    w0, w1, w2, w3, gm_ref, ratt_ref, raug_ref, g_ref, small_ref, total, wo, rmix,
+    wo, gm_ref, ratt_ref, raug_ref, g_ref, small_ref, total, rmix,
 ):
     cols = fq_ref.shape[1] // slots
     ready(middle_ref, dnin_ref, cot_ref)
@@ -366,8 +395,7 @@
         ],
         axis=0,
     )
-    ready(w0, w1, w2, w3)
-    fill_output(meta, (w0, w1, w2, w3), wo)
+    ready(wo)
     rmix[...] = mm(wo[...], r_att, NT).astype(BF16)
     total[...] = jnp.zeros_like(total)
     ready(mixed_ref, den_ref, fq_ref)
@@ -387,7 +415,7 @@
             total[s ^ meta[4], pl.ds(pl.multiple_of(h * KEEP, 8), KEEP), :] = state[:KEEP]
         return carry
 
-    lax.fori_loop(0, heads, head, 0)
+    lax.fori_loop(0, heads, head, 0, unroll=UNROLL)
     spread_states(total, g_ref, parts, g_ref.shape[2])
     flush(g_ref, raug_ref)
 
@@ -424,7 +452,7 @@
         gmap_ref[h] = mm(qkv_ref[rows, :], r_l, NT)
         return carry
 
-    lax.fori_loop(0, heads, head, 0)
+    lax.fori_loop(0, heads, head, 0, unroll=UNROLL)
     flush(rq_ref, gmap_ref)
     ready(mixed_ref, ratt_ref)
     rows = g0.shape[0]
@@ -446,7 +474,7 @@
 
     def head(h, carry):
         fk = fk_ref[pl.ds(pl.multiple_of(h * 128, 128), 128), :]
-        v = qkv_ref[pl.ds(pl.multiple_of(2 * width + h * 64, 64), 64), :]
+        v = qkv_ref[pl.ds(pl.multiple_of(width + h * 64, 64), 64), :]
         va = aug_rows(v, 1.0)
         pieces = []
         for s in range(slots):
@@ -459,11 +487,12 @@
         r_l = logits_back(fk, r_fk)
         rows = pl.ds(pl.multiple_of(width + h * 64, 64), 64)
         rp_ref[rows, :] = mm(map_ref[h], r_l, NN).astype(BF16)
-        gmap_ref[h] = mm(qkv_ref[rows, :], r_l, NT)
+        keys = qkv_ref[pl.ds(pl.multiple_of(h * 64, 64), 64), :]
+        gmap_ref[h] = mm(keys, r_l, NT)
         return carry
 
-    lax.fori_loop(0, heads, head, 0)
-    flush(gmap_ref)
+    lax.fori_loop(0, heads, head, 0, unroll=UNROLL)
+    flush(rp_ref, gmap_ref)
     ready(n_ref)
     span = g1.shape[0]
     for j, g in ((1, g1), (3, g3)):
@@ -472,13 +501,14 @@
         flush(g)
 
 
-def project_grad_kernel(meta, rp_ref, n_ref, in0, in2, g0, g2):
-    span = g0.shape[0]
-    ready(n_ref, in0, in2)
-    for j, more, g in ((2, in2, g2), (0, in0, g0)):
+def project_grad_kernel(meta, rp_ref, n_ref, in0, in2, go0, go0_in, go2, go2_in, own, cross):
+    span = in0.shape[0]
+    ready(rp_ref, n_ref, in0, in2, go0, go0_in, go2, go2_in)
+    for j, more, go, go_in, out in ((2, in2, go2, go2_in, cross), (0, in0, go0, go0_in, own)):
         rp = rp_ref[pl.ds(pl.multiple_of(meta[j] * span, 64), span), :]
-        g[...] = (mm(rp, n_ref[...], NN) + more[...].astype(F32)).astype(BF16)
-        flush(g)
+        out[:span, :] = (mm(rp, n_ref[...], NN) + more[...].astype(F32)).astype(BF16)
+        out[span:, :] = (go[...].astype(F32) + go_in[...].astype(F32)).astype(BF16)
+        flush(out)
 
 
 def input_kernel(
@@ -494,12 +524,13 @@
     ones = jnp.ones((8, x_ref.shape[0]), BF16)
     pack[...] = jnp.zeros_like(pack)
     gy = None
-    ready(w0, w1, w2, w3, x_ref, gm_ref)
+    ready(rp_ref, w0, w1, w2, w3, x_ref, gm_ref)
     for j, w in enumerate((w0, w1, w2, w3)):
         rp = rp_ref[pl.ds(pl.multiple_of(meta[j] * span, 64), span), :]
         part = mm(rp, w[...], TN)
         gy = part if gy is None else gy + part
         pack[meta[j], 8:16, :span] = mm(ones, rp, NT)
+    ready(ebo_ref, ebc_ref, two_ref)
     pack[meta[0], 16:24, :] = ebo_ref[...]
     pack[meta[2], 16:24, :] = ebc_ref[...]
     normal, scale = norm_parts(x_ref[...].astype(F32))
@@ -540,6 +571,10 @@
                 ref[h, 16 * k : 16 * k + 16, :] = rest_ref[base : base + 16, at : at + 64]
 
 
+def line1(a):
+    return a.reshape(-1)
+
+
 def core_swap(a):
     return lax.ppermute(a, "fsdp", CORE)
 
@@ -558,15 +593,13 @@
 
 def add(a, b):
     return (a.astype(F32) + b.astype(F32)).astype(BF16)
-
-
-def ctx_pairs(nctx, bit):
-    return [(i, i ^ (1 << bit)) for i in range(nctx)]
 
 
 def rows_sum(parts, start, size):
     out = None
     for offset, part in parts:
+        if isinstance(part, tuple):
+            part, offset = jnp.where(start + offset < part[0].shape[0], *part), -start
         piece = lax.dynamic_slice_in_dim(part, start + offset, size, 0).astype(F32)
         out = piece if out is None else out + piece
     return out.astype(BF16)
@@ -576,46 +609,66 @@
     def __init__(self, parts, nctx, place):
         self.parts = [(0, part) for part in parts]
         self.rows, self.nctx, self.place = parts[0].shape[0], nctx, place
-        self.bits = nctx.bit_length() - 1
-
-    def halve(self, bit):
-        half = self.rows // 2
-        mine = (self.place >> bit) & 1
-        sent = rows_sum(self.parts, (1 - mine) * half, half)
-        got = lax.ppermute(sent, "ctx", ctx_pairs(self.nctx, bit))
-        self.parts = [(offset + mine * half, part) for offset, part in self.parts] + [(0, got)]
-        self.rows = half
+        self.groups = [[bit] for bit in range(nctx.bit_length() - 1)]
+
+    def member(self, group):
+        return sum(((self.place >> bit) & 1) << k for k, bit in enumerate(group))
+
+    def send(self, value, group, other):
+        flip = sum(((other >> k) & 1) << bit for k, bit in enumerate(group))
+        return lax.ppermute(value, "ctx", [(i, i ^ flip) for i in range(self.nctx)])
+
+    def scatter(self, level):
+        group = self.groups[level]
+        count = 1 << len(group)
+        mine = self.member(group)
+        self.rows //= count
+        self.sent = [
+            rows_sum(self.parts, (mine ^ d) * self.rows, self.rows) for d in range(1, count)
+        ]
+        got = [self.send(sent, group, d) for d, sent in enumerate(self.sent, 1)]
+        self.parts = [
+            (0, jnp.where(mine == 0, *part)) if isinstance(part, tuple)
+            else (offset + mine * self.rows, part)
+            for offset, part in self.parts
+        ]
+        self.fresh = len(got)
+        self.parts += [(0, g) for g in got]
         return got
 
     def hold(self, *others):
-        offset, last = self.parts[-1]
-        self.parts[-1] = (offset, after(last, *others))
-
-    def spread(self):
-        cur = rows_sum(self.parts, 0, self.rows)
-        for bit in reversed(range(self.bits)):
-            other = lax.ppermute(cur, "ctx", ctx_pairs(self.nctx, bit))
-            first = ((self.place >> bit) & 1) == 0
-            cur = jnp.concatenate(
-                [jnp.where(first, cur, other), jnp.where(first, other, cur)], axis=0
-            )
-        return cur
-
-    def total(self, begin=0):
-        for bit in range(begin, self.bits):
-            self.halve(bit)
-        return self.spread()
-
-
-def small_sum(parts, nctx):
-    own, core, cross, far = parts
-    far_in, core_in = core_swap(far), core_swap(core)
-    cross_in = cross_swap(add(cross, far_in))
-    cur = own.astype(F32) + core_in.astype(F32) + cross_in.astype(F32)
-    for bit in range(nctx.bit_length() - 1):
-        low = cur.astype(BF16)
-        cur = low.astype(F32) + lax.ppermute(low, "ctx", ctx_pairs(nctx, bit)).astype(F32)
-    return cur
+        last = self.parts[-self.fresh :]
+        held = lax.optimization_barrier((tuple(part for _, part in last), others))[0]
+        self.parts[-self.fresh :] = [(at, part) for (at, _), part in zip(last, held)]
+
+    def own(self):
+        self.cur = rows_sum(self.parts, 0, self.rows)
+
+    def spread(self, level):
+        group = self.groups[level]
+        self.others = [self.send(self.cur, group, d) for d in range(1, 1 << len(group))]
+        self.level = level
+        return self.others
+
+    def join(self, *others):
+        group = self.groups[self.level]
+        parts = [self.cur, *self.others]
+        if others:
+            parts = list(lax.optimization_barrier((tuple(parts), others))[0])
+        for k, bit in enumerate(group):
+            swap = ((self.place >> bit) & 1) == 1
+            parts = [
+                jnp.where(swap, parts[j ^ (1 << k)], parts[j]) for j in range(len(parts))
+            ]
+        self.cur = jnp.concatenate(parts, axis=0)
+
+    def deep(self, first):
+        for level in range(first, len(self.groups)):
+            self.scatter(level)
+        self.own()
+        for level in reversed(range(first, len(self.groups))):
+            self.spread(level)
+            self.join()
 
 
 def straighten(parts, mine):
@@ -676,12 +729,10 @@
     project_core = core_swap(project_t)
     project_far = core_swap(cross_project)
     projects = [project_t, project_core, cross_project, project_far]
-    near_expand = jnp.concatenate([expand_weight, output_weight])
-    cross_expand = cross_swap(after(near_expand, cross_project))
+    near_first = jnp.concatenate([expand_weight, output_weight])
+    cross_first = cross_swap(after(near_first, cross_project))
     core_output = core_swap(output_weight)
-    far_output = core_swap(cross_expand[width:])
-    outputs = [output_weight, core_output, (cross_expand, width, shard), far_output]
-    cross_reduce = cross_swap(after(reduce_weight, cross_expand))
+    cross_reduce = cross_swap(after(reduce_weight, cross_first))
     cot_other = core_swap(cot)
 
     positions = pair_table[0, 0]
@@ -722,32 +773,37 @@
     )
     (running,) = call(
         functools.partial(scan_kernel, nctx, False), [state_shape], "sv",
-        [keep, after(arrived, fq, cross_expand)], "scan", (), "h",
+        [keep, after(arrived, fq, cross_first)], "scan", (), "h",
     )
     carried = exchange(running)
-    mixed, den, middle, n2 = call(
+    far_output = core_swap(after(cross_first, running)[width : width + shard])
+    outputs = [output_weight, core_output, (cross_first, width, shard), far_output]
+    mixed, den, middle, n2, wo = call(
         functools.partial(attend_kernel, heads, slots, nctx),
-        [table, shaped((heads * 8, rows_n)), full, low],
+        [table, shaped((heads * 8, rows_n)), full, low, shaped((width, width), BF16)],
         "svhhaaaav", [meta, carried, fq, x, *outputs, params], "attend",
-        [total, wo_scratch], "hhhh",
+        [total], "hhhvh",
     )
     n2_other = core_swap(n2)
 
     def mlp(first, base, w_in, w_out, more, name):
+        half = shaped((width // 2, hidden_own), BF16)
+        grads = [half, half] if first else [shaped((width, hidden_own), BF16)]
         return call(
-            functools.partial(mlp_kernel, 384, first),
-            [full, full, low, low, shaped((width, hidden_own), BF16),
-             shaped((hidden_own, width), BF16), shaped((8, hidden_own))],
-            "shaaa" + ("h" if first else "v") + "vaa" + "v" * len(more),
-            [meta, n2, n2_other, cot, cot_other, base, expand_line, w_in, w_out, *more], name,
-            [pltpu.VMEM((width, 2 * rows_n), BF16), pltpu.VMEM((2, rows_n, width), F32)],
-            "vvvvhhv" if first else "hvhhhhv", 40,
+            functools.partial(mlp_kernel, first),
+            [full, full, low, low, *grads, shaped((hidden_own, width), BF16),
+             shaped((8, hidden_own))],
+            "saaaaaa" + ("h" if first else "v") + "v" + "v" * len(more),
+            [meta, n2, w_in, n2_other, cot, w_out, cot_other, base, expand_line, *more], name,
+            [pltpu.VMEM((2, rows_n, hidden_own), BF16)] * 2,
+            "vvvvhhhv" if first else "hvhhhhv", 48,
         )
 
-    out1, dn1, out1_o, dn1_o, ge_cross, gr_cross, gb_cross = mlp(
-        True, middle, (cross_expand, 0, width), cross_reduce, [], "mlp_far"
-    )
-    ge_in = cross_swap(ge_cross)
+    out1, dn1, out1_o, dn1_o, ge_top, ge_low, gr_cross, gb_cross = mlp(
+        True, middle, (cross_first, 0, width), cross_reduce, [], "mlp_far"
+    )
+    top_in = cross_swap(ge_top)
+    low_in = cross_swap(after(ge_low, top_in))
     out2, dn2, out2_o, dn2_o, ge_own, gr_own, gb_own = mlp(
         False, out1, expand_weight, reduce_weight, [dn1, out1_o, dn1_o], "mlp_near"
     )
@@ -756,12 +812,12 @@
     g_middle, r_att, raug, g_states, small_two = call(
         functools.partial(middle_kernel, heads, slots, nctx),
         [full, low, shaped((heads * AUG, rows_n), BF16), state_shape, shaped((8, width))],
-        "svahavhhhaaaa",
-        [meta, dn2, dn2_in, middle, cot, params, mixed, den, fq, *outputs], "middle",
-        [total, wo_scratch, pltpu.VMEM((width, rows_n), BF16)], "hhhhv",
+        "svahavhhhh",
+        [meta, dn2, dn2_in, middle, cot, params, mixed, den, fq, wo], "middle",
+        [total, pltpu.VMEM((width, rows_n), BF16)], "hhhhv",
     )
     g_arrived = exchange(g_states)
-    gr_in = cross_swap(after(gr_cross, ge_in))
+    gr_in = cross_swap(after(gr_cross, low_in))
     out2_in = core_swap(after(out2_o, g_states))
     rq, g_query_map, *go = call(
         functools.partial(query_back_kernel, heads, slots, nctx),
@@ -771,43 +827,82 @@
     )
     (g_running,) = call(
         functools.partial(scan_kernel, nctx, True), [state_shape], "sv",
-        [keep_next, after(g_arrived, rq, ge_in)], "scan_back", (), "h",
+        [keep_next, after(g_arrived, rq, low_in)], "scan_back", (), "h",
     )
     g_carried = exchange(g_running)
-    sum_e = Reduction([ge_own, after(ge_in, g_running)], nctx, place)
-    e_half = sum_e.halve(0)
+    top_in, low_in = lax.optimization_barrier((top_in, low_in, g_running))[:2]
+    sum_e = Reduction([ge_own, (top_in, low_in)], nctx, place)
+    e_got = sum_e.scatter(0)
+    sum_r = Reduction([gr_own, after(gr_in, g_running)], nctx, place)
+    r_got = sum_r.scatter(0)
     go_far, go_core = core_swap(after(go[3], g_running)), core_swap(after(go[1], g_running))
     rp, g_key_map, gp1, gp3 = call(
         functools.partial(key_back_kernel, heads, slots, nctx),
         [shaped((3 * width, rows_n), BF16), square] + [shaped((span, width), BF16)] * 2,
-        "svhavhh", [meta, after(g_carried, e_half), fk, qkv, key_map, rq, n1],
-        "key_back", [total], "vhhh",
-    )
-    gp3_in, gp1_in = core_swap(gp3), core_swap(gp1)
-    gp_own, gp_cross = call(
-        project_grad_kernel, [shaped((span, width), BF16)] * 2, "svhaa",
-        [meta, rp, n1, gp1_in, gp3_in], "project_grad", (), "hh",
-    )
-    go_in = cross_swap(after(add(go[2], go_far), gr_in))
-    gp_in = cross_swap(after(gp_cross, go_in))
+        "svhavhh", [meta, after(g_carried, sum_e.sent, sum_r.sent), fk, (qkv, width, 2 * width), key_map, rq, n1],
+        "key_back", [total], "hhhh",
+    )
+    gp3_in, gp1_in = core_swap(after(gp3, e_got)), core_swap(after(gp1, e_got))
+    p_own, p_cross = call(
+        project_grad_kernel, [shaped((width, width), BF16)] * 2, "shhaahaha",
+        [meta, rp, n1, gp1_in, gp3_in, go[0], go_core, go[2], go_far], "project_grad", (), "hh",
+    )
+    p_in = cross_swap(p_cross)
+    sum_e.hold(p_own)
+    sum_e.scatter(1)
     small = shaped((64, width), BF16)
-    dx, layer_out, *blocks = call(
+    dx, layer_out, own_s, core_s, cross_s, far_s = call(
         functools.partial(input_kernel, heads), [full, full, small, small, small, small],
-        "svhvhhavvvhhaaaa",
-        [meta, rp, after(x, gp_own), params, g_middle, out2, out2_in, small_two, gb_own, gb_cross,
-         g_query_map, g_key_map, *projects],
+        "shhvhhaaaahhaaaa",
+        [meta, rp, after(x, p_own, sum_e.sent), params, g_middle, out2, out2_in, small_two,
+         gb_own, gb_cross, g_query_map, g_key_map, *projects],
         "input", [pltpu.VMEM((4, 64, width), F32)], "hhvvvv",
     )
-    sum_e.hold(gp_own)
-    gr_in = after(gr_in, gp_own)
-    g_expand = sum_e.total(1)
-    g_reduce = Reduction([gr_own, gr_in], nctx, place).total()
-    own_go = add(add(go[0], go_core), go_in)
-    g_project = Reduction(
-        [jnp.concatenate([gp_own, own_go]),
-         jnp.concatenate([gp_in, jnp.zeros_like(own_go)])], nctx, place
-    ).total()
-    rest = small_sum(blocks, nctx)
+    far_in, core_in = core_swap(far_s), core_swap(core_s)
+    cross_in = cross_swap(add(cross_s, far_in))
+    small_own = add(own_s, core_in)
+    sum_e.hold(far_in, core_in)
+    e_got = sum_e.scatter(2)
+    sum_r.hold(far_in, core_in)
+    r_got = sum_r.scatter(1)
+    sum_p = Reduction([p_own, p_in], nctx, place)
+    p_got = sum_p.scatter(0)
+    sum_e.hold(sum_p.sent)
+    sum_r.hold(sum_p.sent)
+    sum_e.deep(3)
+    e_got = sum_e.spread(2)
+    r_got = sum_r.scatter(2)
+    sum_p.hold(e_got, r_got)
+    sum_p.scatter(1)
+    sum_e.join(sum_p.sent)
+    e_got = sum_e.spread(1)
+    sum_r.hold(sum_p.sent)
+    sum_r.deep(3)
+    r_got = sum_r.spread(2)
+    sum_p.hold(e_got, r_got)
+    sum_p.scatter(2)
+    sum_e.join(sum_p.sent)
+    e_got = sum_e.spread(0)
+    sum_r.join(sum_p.sent)
+    r_got = sum_r.spread(1)
+    sum_p.hold(r_got)
+    sum_p.deep(3)
+    sum_r.join(sum_p.cur)
+    r_got = sum_r.spread(0)
+    sum_p.spread(2)
+    sum_p.join(e_got)
+    sum_p.spread(1)
+    sum_p.join(r_got)
+    sum_p.spread(0)
+    sum_p.join()
+    sum_e.join()
+    sum_r.join()
+    g_expand, g_reduce, g_project = sum_e.cur, sum_r.cur, sum_p.cur
+    rest = small_own.astype(F32) + cross_in.astype(F32)
+    for level in range(len(sum_p.groups)):
+        low_rest = rest.astype(BF16)
+        rest = low_rest.astype(F32) + sum_p.send(low_rest, sum_p.groups[level], 1).astype(F32)
+    g_output = g_project[span : span + shard]
     line = shaped((1, shard))
     g1, s1, g2, s2, bo, br, pb, eb, mq, mk = call(
         unpack_kernel,
@@ -815,9 +910,9 @@
         + [shaped((own_heads, 64, 64))] * 2, "v", [rest], "unpack",
     )
     return (
-        layer_out[None], dx[None], g1[0], s1[0], g_project[:span].T.astype(F32), pb[0], mq, mk,
-        g_project[span:].astype(F32), bo[0], g2[0], s2[0], g_expand.astype(F32), eb[0],
-        g_reduce.astype(F32), br[0],
+        layer_out[None], dx[None], line1(g1), line1(s1), g_project[:span].T.astype(F32), line1(pb), mq, mk,
+        g_output.astype(F32), line1(bo), line1(g2), line1(s2), g_expand.astype(F32), line1(eb),
+        g_reduce.astype(F32), line1(br),
     )
 
 

time: 345 us -> 318 us (0.922)
  waiting for transfers between devices: 131 us -> 113 us
  Pallas kernels: 100 us -> 92.8 us
  starting transfers between devices: 65.8 us -> 59.3 us
    ppermute x21, waiting for transfers between devices: 71.4 us -> 56.7 us  [send(): return lax.ppermute(value, 'ctx', [(i, i ^ flip) for i in range(self.nctx)])]
    ppermute x9, waiting for transfers between devices: 46.9 us -> 35.7 us  [cross_swap(): return lax.ppermute(a, 'fsdp', CROSS)]
    pallas_call x15, Pallas kernels: 100 us -> 92.8 us  [call(): pl.pallas_call(run, out_shape=[pltpu.HBM(o.shape, o.dtype) if k == 'h' el...]
    all_to_all x4, waiting for transfers between devices: 8.68 us -> 14.4 us  [exchange(): return lax.all_to_all(a, 'ctx', 0, 0, tiled=True)]
    convert_element_type x12, other arithmetic: 11.4 us -> 16 us  [rows_sum(): return out.astype(BF16)]
    unnamed x92 -> x94, local copies, waits for them, and re-layouts: 9.94 us -> 9.62 us
  transfers between devices with their start and end apart: 50 -> 50, of which waited for: 25 -> 27; matrix products, arithmetic and copies ran while one was open for 9% -> 11% of each run, Pallas kernels for 19% -> 24%
where the time goes in v3:
time: 318 us; the launch traced here: 316 us
  waiting for transfers between devices  113 us (36%)
  Pallas kernels  92.8 us (29%)
  starting transfers between devices  59.3 us (19%)
  other arithmetic  29.7 us (9%)
  local copies, waits for them, and re-layouts  18 us (6%)
    pallas_call x15, Pallas kernels, call(): pl.pallas_call(run, out_shape=[pltpu.HBM(o.shape, o.dtype) if k == 'h' el...  92.8 us
    ppermute x21, waiting for transfers between devices, send(): return lax.ppermute(value, 'ctx', [(i, i ^ flip) for i in range(self.nctx)])  56.7 us
    ppermute x9, waiting for transfers between devices, cross_swap(): return lax.ppermute(a, 'fsdp', CROSS)  35.7 us
    ppermute x21, starting transfers between devices, send(): return lax.ppermute(value, 'ctx', [(i, i ^ flip) for i in range(self.nctx)])  23.5 us
    all_to_all x4, starting transfers between devices, exchange(): return lax.all_to_all(a, 'ctx', 0, 0, tiled=True)  21.3 us
    convert_element_type x12, other arithmetic, rows_sum(): return out.astype(BF16)  16 us
    all_to_all x4, waiting for transfers between devices, exchange(): return lax.all_to_all(a, 'ctx', 0, 0, tiled=True)  14.4 us
    ppermute x9, starting transfers between devices, cross_swap(): return lax.ppermute(a, 'fsdp', CROSS)  11.2 us
  transfers between devices with their start and end apart: 50, of which 27 were waited for; matrix products, arithmetic and copies ran while one was open for 11% of the time, Pallas kernels for 24%

profile of v3, /device:TPU:0, one launch (start us, length us, event | category | flops | bytes accessed | tf_op | source)
XLA Modules:
  0.0 316.1 jit_solution(2553768287603431263)
XLA Ops:
  0.6 3.0 collective-permute-start.4
  3.7 5.5 %concatenate.51 = bf16[3072]{0:T(1024)(128)(2,1)S(1)} concatenate(bf16[192]{0:T(256)(128)(2,1)} %param.22, bf16[192]{0:T(256)(128)(2,1)} %param.23, bf16[192]{0:T(256)(128)(2,1)} %param.30, bf16[192]{0:T(256)(128)(2,1)} %param.31, bf16[192]{0:T(256)(128)(2,1)} %param.29, bf16[192]{0:T(256)(128)(2,1)} %param.35, bf16[576]{0:T(1024)(128)(2,1)} %param.25, bf16[768]{0:T(1024)(128)(2,1)} %param.33, ...), dimensions={0} | concatenate | bytes 12288 | tf_op jit(solution)/shard_map/concatenate | solution.py:716
  13.3 12.6 %collective-permute-done = bf16[432,64]{1,0:T(8,128)(2,1)S(1)} collective-permute-done((bf16[432,64]{1,0:T(8,128)(2,1)S(1)}, bf16[432,64]{1,0:T(8,128)(2,1)S(1)}, u32[]{:S(2)}, u32[]{:S(2)}) %collective-permute-start) | collective-permute-done | bytes 55328 | tf_op jit(solution)/shard_map/ppermute | solution.py:583
  32.8 3.6 %project_near.1 = (bf16[512,768]{1,0:T(8,128)(2,1)}, bf16[1152,512]{1,0:T(8,128)(2,1)S(1)}) custom-call(s32[5]{0:T(128)S(1)} %stack.42.refs_0_, bf16[512,768]{1,0:T(8,128)(2,1)} %bitcast.37, f32[6,768]{1,0:T(8,128)S(1)} %reshape.102.refs_2_.refs_8_.refs_5_.refs_3_, bf16[576,768]{1,0:T(8,128)(2,1)S(1)} %bitcast.31, ...), custom_call_target="tpu_custom_call" | custom-call | flops 1 | bytes 1 | tf_op jit(solution)/shard_map/project_near/pallas_call | solution.py:132
  36.4 3.1 project_far.1.refs_1_.refs_0_.refs_4_.refs_3_
  39.5 6.3 %keys.1 = (bf16[1536,512]{1,0:T(8,128)(2,1)}, bf16[8,2,112,128]{3,2,1,0:T(8,128)(2,1)}) custom-call(s32[5]{0:T(128)S(1)} %stack.42.refs_0_, bf16[2304,512]{1,0:T(8,128)(2,1)S(1)} %project_far.1.refs_1_.refs_0_.refs_4_.refs_3_, bf16[12,64,64]{2,1,0:T(8,128)(2,1)S(1)} %bitcast.35), custom_call_target="tpu_custom_call" | custom-call | flops 1 | bytes 1 | tf_op jit(solution)/shard_map/keys/pallas_call | solution.py:132
  45.8 5.9 %all-to-all-start = ((bf16[8,2,112,128]{3,2,1,0:T(8,128)(2,1)}), bf16[8,2,112,128]{3,2,1,0:T(8,128)(2,1)S(1)}, u32[]{:S(2)}, u32[]{:S(2)}) async-start(bf16[8,2,112,128]{3,2,1,0:T(8,128)(2,1)} %get-tuple-element.114), calls=%async_computation | async-start | bytes 917504 | tf_op jit(solution)/shard_map/all_to_all | solution.py:687
  54.7 10.0 %collective-permute-done.6.refs_6_.refs_2_ = bf16[960,768]{1,0:T(8,128)(2,1)} collective-permute-done((bf16[960,768]{1,0:T(8,128)(2,1)}, bf16[960,768]{1,0:T(8,128)(2,1)}, u32[]{:S(2)}, u32[]{:S(2)}) %collective-permute-start.6) | collective-permute-done | bytes 1474592 | tf_op jit(solution)/shard_map/ppermute | solution.py:583
  68.0 6.1 %all-to-all-start.1 = ((bf16[8,2,112,128]{3,2,1,0:T(8,128)(2,1)}), bf16[8,2,112,128]{3,2,1,0:T(8,128)(2,1)}, u32[]{:S(2)}, u32[]{:S(2)}) async-start(bf16[8,2,112,128]{3,2,1,0:T(8,128)(2,1)} %scan.1), calls=%async_computation.1 | async-start | bytes 917504 | tf_op jit(solution)/shard_map/all_to_all | solution.py:687
  79.1 7.6 %all-to-all-done.1.refs_1_ = bf16[8,2,112,128]{3,2,1,0:T(8,128)(2,1)} async-done(((bf16[8,2,112,128]{3,2,1,0:T(8,128)(2,1)}), bf16[8,2,112,128]{3,2,1,0:T(8,128)(2,1)}, u32[]{:S(2)}, u32[]{:S(2)}) %all-to-all-start.1) | async-done | bytes 458784 | tf_op jit(solution)/shard_map/all_to_all | solution.py:687
  90.3 6.0 %attend.1 = (bf16[768,512]{1,0:T(8,128)(2,1)}, f32[96,512]{1,0:T(8,128)}, f32[512,768]{1,0:T(8,128)}, bf16[512,768]{1,0:T(8,128)(2,1)S(1)}, bf16[768,768]{1,0:T(8,128)(2,1)}) custom-call(s32[5]{0:T(128)S(1)} %stack.42.refs_0_, bf16[8,2,112,128]{3,2,1,0:T(8,128)(2,1)} %all-to-all-done.1.refs_1_, bf16[1536,512]{1,0:T(8,128)(2,1)} %queries.1.refs_2_.refs_8_.refs_3_, ...), custom_call_target="tpu_custom_call" | custom-call | flops 1 | bytes 1 | tf_op jit(solution)/shard_map/attend/pallas_call | solution.py:132
  96.6 4.6 %collective-permute-done.11.refs_5_ = bf16[768,768]{1,0:T(8,128)(2,1)} collective-permute-done((bf16[768,768]{1,0:T(8,128)(2,1)}, bf16[768,768]{1,0:T(8,128)(2,1)}, u32[]{:S(2)}, u32[]{:S(2)}) %collective-permute-start.11) | collective-permute-done | bytes 1179680 | tf_op jit(solution)/shard_map/ppermute | solution.py:583
  101.2 14.1 %mlp_far.1 = (f32[512,768]{1,0:T(8,128)}, f32[512,768]{1,0:T(8,128)}, bf16[512,768]{1,0:T(8,128)(2,1)S(1)}, bf16[512,768]{1,0:T(8,128)(2,1)S(1)}, bf16[384,768]{...) custom-call(s32[5]{0:T(128)S(1)} %stack.42.refs_0_, ...), custom_call_target="tpu_custom_call" | custom-call | flops 1 | bytes 1 | tf_op jit(solution)/shard_map/mlp_far/pallas_call | solution.py:132
  117.4 16.4 %mlp_near.1 = (f32[512,768]{1,0:T(8,128)}, f32[512,768]{1,0:T(8,128)}, bf16[512,768]{1,0:T(8,128)(2,1)}, bf16[512,768]{1,0:T(8,128)(2,1)}, bf16[768,768]{1,0:T(8...) custom-call(s32[5]{0:T(128)S(1)} %stack.42.refs_0_, bf16[512,768]{1,0:T(8,128)(2,1)S(1)} %get-tuple-element.119.refs_1_, ...), custom_call_target="tpu_custom_call" | custom-call | flops 1 | bytes 1 | tf_op jit(solution)/shard_map/mlp_near/pallas_call | solution.py:132
  137.8 6.6 %middle.1 = (f32[512,768]{1,0:T(8,128)}, bf16[512,768]{1,0:T(8,128)(2,1)}, bf16[960,512]{1,0:T(8,128)(2,1)}, bf16[8,2,112,128]{3,2,1,0:T(8,128)(2,1)}, f32[8,768]{1,0:T(8,128)S(1)}) custom-call(s32[5]{0:T(128)S(1)} %stack.42.refs_0_, f32[512,768]{1,0:T(8,128)S(1)} %copy-done.10, bf16[512,768]{1,0:T(8,128)(2,1)S(1)} %collective-permute-done.12.refs_2_, ...), custom_call_target="tpu_custom_call" | custom-call | flops 1 | bytes 1 | tf_op jit(solution)/shard_map/middle/pallas_call | solution.py:132
  145.0 5.7 %all-to-all-start.2 = ((bf16[8,2,112,128]{3,2,1,0:T(8,128)(2,1)}), bf16[8,2,112,128]{3,2,1,0:T(8,128)(2,1)S(1)}, u32[]{:S(2)}, u32[]{:S(2)}) async-start(bf16[8,2,112,128]{3,2,1,0:T(8,128)(2,1)} %get-tuple-element.131), calls=%async_computation.2 | async-start | bytes 917504 | tf_op jit(solution)/shard_map/all_to_all | solution.py:687
  151.3 7.6 %query_back.1 = (bf16[768,512]{1,0:T(8,128)(2,1)}, f32[12,64,64]{2,1,0:T(8,128)}, bf16[192,768]{1,0:T(8,128)(2,1)}, bf16[192,768]{1,0:T(8,128)(2,1)}, bf16[192,7...) custom-call(s32[5]{0:T(128)S(1)} %stack.42.refs_0_, bf16[8,2,112,128]{3,2,1,0:T(8,128)(2,1)} %all-to-all-done.1.refs_1_, ...), custom_call_target="tpu_custom_call" | custom-call | flops 1 | bytes 1 | tf_op jit(solution)/shard_map/query_back/pallas_call | solution.py:132
  158.9 5.2 %all-to-all-done.2.refs_1_ = bf16[8,2,112,128]{3,2,1,0:T(8,128)(2,1)S(1)} async-done(((bf16[8,2,112,128]{3,2,1,0:T(8,128)(2,1)}), bf16[8,2,112,128]{3,2,1,0:T(8,128)(2,1)S(1)}, u32[]{:S(2)}, u32[]{:S(2)}) %all-to-all-start.2) | async-done | bytes 458784 | tf_op jit(solution)/shard_map/all_to_all | solution.py:687
  165.5 3.6 %all-to-all-start.3 = ((bf16[8,2,112,128]{3,2,1,0:T(8,128)(2,1)}), bf16[8,2,112,128]{3,2,1,0:T(8,128)(2,1)S(1)}, u32[]{:S(2)}, u32[]{:S(2)}) async-start(bf16[8,2,112,128]{3,2,1,0:T(8,128)(2,1)} %scan_back.1), calls=%async_computation.3 | async-start | bytes 917504 | tf_op jit(solution)/shard_map/all_to_all | solution.py:687
  173.6 5.3 %collective-permute-done.15 = bf16[768,768]{1,0:T(8,128)(2,1)} collective-permute-done((bf16[768,768]{1,0:T(8,128)(2,1)}, bf16[768,768]{1,0:T(8,128)(2,1)}, u32[]{:S(2)}, u32[]{:S(2)}) %collective-permute-start.15) | collective-permute-done | bytes 1179680 | tf_op jit(solution)/shard_map/ppermute | solution.py:583
  182.5 8.1 %key_back.1 = (bf16[2304,512]{1,0:T(8,128)(2,1)}, f32[12,64,64]{2,1,0:T(8,128)}, bf16[576,768]{1,0:T(8,128)(2,1)}, bf16[576,768]{1,0:T(8,128)(2,1)}) custom-call(s32[5]{0:T(128)S(1)} %stack.42.refs_0_, bf16[8,2,112,128]{3,2,1,0:T(8,128)(2,1)S(1)} %all-to-all-done.3.refs_1_, bf16[1536,512]{1,0:T(8,128)(2,1)} %get-tuple-element.147.refs_2_, ...), custom_call_target="tpu_custom_call" | custom-call | flops 1 | bytes 1 | tf_op jit(solution)/shard_map/key_back/pallas_call | solution.py:132
  195.4 5.3 %project_grad.1 = (bf16[768,768]{1,0:T(8,128)(2,1)}, bf16[768,768]{1,0:T(8,128)(2,1)}) custom-call(s32[5]{0:T(128)S(1)} %stack.42.refs_0_, bf16[2304,512]{1,0:T(8,128)(2,1)} %get-tuple-element.148.refs_1_, bf16[512,768]{1,0:T(8,128)(2,1)} %get-tuple-element.112.refs_1_.refs_6_.refs_2_, bf16[576,768]{1,0:T(8,128)(2,1)S(1)} %collective-permute-done.17.refs_3_, ...), custom_call_target="tpu_custom_call" | custom-call | flops 1 | bytes 1 | tf_op jit(solution)/shard_map/project_grad/pallas_call | solution.py:132
  204.9 9.4 %input.1 = (f32[512,768]{1,0:T(8,128)}, f32[512,768]{1,0:T(8,128)}, bf16[64,768]{1,0:T(8,128)(2,1)S(1)}, bf16[64,768]{1,0:T(8,128)(2,1)S(1)}, bf16[64,768]{1,0:T(8,128)(2,1)S(1)}, /*index=5*/bf16[64,768]{1,0:T(8,128)(2,1)S(1)}) custom-call(s32[5]{0:T(128)S(1)} %stack.42.refs_0_, bf16[2304,512]{1,0:T(8,128)(2,1)} %get-tuple-element.148.refs_1_, ...), custom_call_target="tpu_custom_call" | custom-call | flops 1 | bytes 1 | tf_op jit(solution)/shard_map/input/pallas_call | solution.py:132
  219.4 5.2 %collective-permute-done.30 = bf16[192,768]{1,0:T(8,128)(2,1)S(1)} collective-permute-done((bf16[192,768]{1,0:T(8,128)(2,1)}, bf16[192,768]{1,0:T(8,128)(2,1)S(1)}, u32[]{:S(2)}, u32[]{:S(2)}) %collective-permute-start.30) | collective-permute-done | bytes 294944 | tf_op jit(solution)/shard_map/ppermute | solution.py:619
  226.7 3.2 %collective-permute-done.28 = bf16[768,768]{1,0:T(8,128)(2,1)} collective-permute-done((bf16[768,768]{1,0:T(8,128)(2,1)}, bf16[768,768]{1,0:T(8,128)(2,1)}, u32[]{:S(2)}, u32[]{:S(2)}) %collective-permute-start.28) | collective-permute-done | bytes 1179680 | tf_op jit(solution)/shard_map/ppermute | solution.py:583
  240.0 7.1 %collective-permute-done.25 = bf16[64,768]{1,0:T(8,128)(2,1)S(1)} collective-permute-done((bf16[64,768]{1,0:T(8,128)(2,1)S(1)}, bf16[64,768]{1,0:T(8,128)(2,1)S(1)}, u32[]{:S(2)}, u32[]{:S(2)}) %collective-permute-start.25) | collective-permute-done | bytes 98336 | tf_op jit(solution)/shard_map/ppermute | solution.py:619
  256.7 10.4 %collective-permute-done.38 = bf16[96,768]{1,0:T(8,128)(2,1)S(1)} collective-permute-done((bf16[96,768]{1,0:T(8,128)(2,1)S(1)}, bf16[96,768]{1,0:T(8,128)(2,1)S(1)}, u32[]{:S(2)}, u32[]{:S(2)}) %collective-permute-start.38) | collective-permute-done | bytes 147488 | tf_op jit(solution)/shard_map/ppermute | solution.py:619
  275.3 3.3 %collective-permute-done.39 = bf16[96,768]{1,0:T(8,128)(2,1)S(1)} collective-permute-done((bf16[96,768]{1,0:T(8,128)(2,1)S(1)}, bf16[96,768]{1,0:T(8,128)(2,1)S(1)}, u32[]{:S(2)}, u32[]{:S(2)}) %collective-permute-start.39) | collective-permute-done | bytes 147488 | tf_op jit(solution)/shard_map/ppermute | solution.py:619
  278.6 3.4 %collective-permute-done.40 = bf16[192,768]{1,0:T(8,128)(2,1)S(1)} collective-permute-done((bf16[192,768]{1,0:T(8,128)(2,1)S(1)}, bf16[192,768]{1,0:T(8,128)(2,1)S(1)}, u32[]{:S(2)}, u32[]{:S(2)}) %collective-permute-start.40) | collective-permute-done | bytes 294944 | tf_op jit(solution)/shard_map/ppermute | solution.py:619
  284.4 6.7 %collective-permute-done.41 = bf16[96,768]{1,0:T(8,128)(2,1)S(1)} collective-permute-done((bf16[96,768]{1,0:T(8,128)(2,1)S(1)}, bf16[96,768]{1,0:T(8,128)(2,1)S(1)}, u32[]{:S(2)}, u32[]{:S(2)}) %collective-permute-start.41) | collective-permute-done | bytes 147488 | tf_op jit(solution)/shard_map/ppermute | solution.py:619
  293.5 5.6 %collective-permute-done.43 = bf16[192,768]{1,0:T(8,128)(2,1)} collective-permute-done((bf16[192,768]{1,0:T(8,128)(2,1)S(1)}, bf16[192,768]{1,0:T(8,128)(2,1)}, u32[]{:S(2)}, u32[]{:S(2)}) %collective-permute-start.43) | collective-permute-done | bytes 294944 | tf_op jit(solution)/shard_map/ppermute | solution.py:619
  304.7 9.0 %collective-permute-done.45 = bf16[384,768]{1,0:T(8,128)(2,1)S(1)} collective-permute-done((bf16[384,768]{1,0:T(8,128)(2,1)S(1)}, bf16[384,768]{1,0:T(8,128)(2,1)S(1)}, u32[]{:S(2)}, u32[]{:S(2)}) %collective-permute-start.45) | collective-permute-done | bytes 589856 | tf_op jit(solution)/shard_map/ppermute | solution.py:619
  (246 shorter events, 97.9 us)
Async XLA Ops:
  0.6 28.7 %collective-permute-start.4 = (bf16[576,768]{1,0:T(8,128)(2,1)}, bf16[576,768]{1,0:T(8,128)(2,1)S(1)}, u32[]{:S(2)}, u32[]{:S(2)}) collective-permute-start(bf16[576,768]{1,0:T(8,128)(2,1)} %bitcast.29), channel_id=1, source_target_pairs={{0,2},{1,3},{2,0},{3,1},{4,6},{5,7},{6,4},{7,5},{8,10},{9,11},{10,... | collective-permute-start | bytes 2654216 | tf_op jit(solution)/shard_map/ppermute | solution.py:583
  10.1 15.8 %collective-permute-start = (bf16[432,64]{1,0:T(8,128)(2,1)S(1)}, bf16[432,64]{1,0:T(8,128)(2,1)S(1)}, u32[]{:S(2)}, u32[]{:S(2)}) collective-permute-start(bf16[432,64]{1,0:T(8,128)(2,1)S(1)} %pad_maximum_fusion.10), channel_id=1, source_target_pairs={{0,2},{1,3},{2,0},{3,1},{4,6},{5,7},{6,4},{7,5},{8,10},{9,11},{10,... | collective-permute-start | bytes 165896 | tf_op jit(solution)/shard_map/ppermute | solution.py:583
  10.2 17.7 %collective-permute-start.2 = (bf16[432,64]{1,0:T(8,128)(2,1)S(1)}, bf16[432,64]{1,0:T(8,128)(2,1)S(1)}, u32[]{:S(2)}, u32[]{:S(2)}) collective-permute-start(bf16[432,64]{1,0:T(8,128)(2,1)S(1)} %pad_maximum_fusion.10), channel_id=1, source_target_pairs={{0,1},{1,0},{2,3},{3,2},{4,5},{5,4},{6,7},{7,6},{8,9},{9,8},{10,11... | collective-permute-start | bytes 165896 | tf_op jit(solution)/shard_map/ppermute | solution.py:579
  10.2 22.5 %collective-permute-start.3 = (bf16[576,768]{1,0:T(8,128)(2,1)}, bf16[576,768]{1,0:T(8,128)(2,1)S(1)}, u32[]{:S(2)}, u32[]{:S(2)}) collective-permute-start(bf16[576,768]{1,0:T(8,128)(2,1)} %bitcast.30), channel_id=1, source_target_pairs={{0,1},{1,0},{2,3},{3,2},{4,5},{5,4},{6,7},{7,6},{8,9},{9,8},{10,11... | collective-permute-start | bytes 2654216 | tf_op jit(solution)/shard_map/ppermute | solution.py:579
  30.2 34.5 %collective-permute-start.6 = (bf16[960,768]{1,0:T(8,128)(2,1)}, bf16[960,768]{1,0:T(8,128)(2,1)}, u32[]{:S(2)}, u32[]{:S(2)}) collective-permute-start(bf16[960,768]{1,0:T(8,128)(2,1)} %pad_maximum_fusion), channel_id=1, source_target_pairs={{0,2},{1,3},{2,0},{3,1},{4,6},{5,7},{6,4},{7,5},{8,10},{9,11},{10,... | collective-permute-start | bytes 4423688 | tf_op jit(solution)/shard_map/ppermute | solution.py:583
  45.8 18.9 %all-to-all-start = ((bf16[8,2,112,128]{3,2,1,0:T(8,128)(2,1)}), bf16[8,2,112,128]{3,2,1,0:T(8,128)(2,1)S(1)}, u32[]{:S(2)}, u32[]{:S(2)}) async-start(bf16[8,2,112,128]{3,2,1,0:T(8,128)(2,1)} %get-tuple-element.114), calls=%async_computation | async-start | bytes 917504 | tf_op jit(solution)/shard_map/all_to_all | solution.py:687
  68.0 18.7 %all-to-all-start.1 = ((bf16[8,2,112,128]{3,2,1,0:T(8,128)(2,1)}), bf16[8,2,112,128]{3,2,1,0:T(8,128)(2,1)}, u32[]{:S(2)}, u32[]{:S(2)}) async-start(bf16[8,2,112,128]{3,2,1,0:T(8,128)(2,1)} %scan.1), calls=%async_computation.1 | async-start | bytes 917504 | tf_op jit(solution)/shard_map/all_to_all | solution.py:687
  74.1 27.1 %collective-permute-start.11 = (bf16[768,768]{1,0:T(8,128)(2,1)}, bf16[768,768]{1,0:T(8,128)(2,1)}, u32[]{:S(2)}, u32[]{:S(2)}) collective-permute-start(bf16[768,768]{1,0:T(8,128)(2,1)} %refs_5_.1), channel_id=1, source_target_pairs={{0,2},{1,3},{2,0},{3,1},{4,6},{5,7},{6,4},{7,5},{8,10},{9,11},{10,... | collective-permute-start | bytes 3538952 | tf_op jit(solution)/shard_map/ppermute | solution.py:583
  77.1 19.4 %collective-permute-start.10 = (bf16[512,768]{1,0:T(8,128)(2,1)S(1)}, bf16[512,768]{1,0:T(8,128)(2,1)}, u32[]{:S(2)}, u32[]{:S(2)}) collective-permute-start(bf16[512,768]{1,0:T(8,128)(2,1)S(1)} %bitcast.25), channel_id=1, source_target_pairs={{0,1},{1,0},{2,3},{3,2},{4,5},{5,4},{6,7},{7,6},{8,9},{9,8},{10,11... | collective-permute-start | bytes 2359304 | tf_op jit(solution)/shard_map/ppermute | solution.py:579
  115.9 18.0 %collective-permute-start.13 = (bf16[384,768]{1,0:T(8,128)(2,1)}, bf16[384,768]{1,0:T(8,128)(2,1)S(1)}, u32[]{:S(2)}, u32[]{:S(2)}) collective-permute-start(bf16[384,768]{1,0:T(8,128)(2,1)} %get-tuple-element.136), channel_id=1, source_target_pairs={{0,2},{1,3},{2,0},{3,1},{4,6},{5,7},{6,4},{7,5},{8,10},{9,11},{10,... | collective-permute-start | bytes 1769480 | tf_op jit(solution)/shard_map/ppermute | solution.py:583
  133.9 16.8 %collective-permute-start.14 = (bf16[384,768]{1,0:T(8,128)(2,1)}, bf16[384,768]{1,0:T(8,128)(2,1)}, u32[]{:S(2)}, u32[]{:S(2)}) collective-permute-start(bf16[384,768]{1,0:T(8,128)(2,1)} %get-tuple-element.137), channel_id=1, source_target_pairs={{0,2},{1,3},{2,0},{3,1},{4,6},{5,7},{6,4},{7,5},{8,10},{9,11},{10,... | collective-permute-start | bytes 1769480 | tf_op jit(solution)/shard_map/ppermute | solution.py:583
  145.0 19.1 %all-to-all-start.2 = ((bf16[8,2,112,128]{3,2,1,0:T(8,128)(2,1)}), bf16[8,2,112,128]{3,2,1,0:T(8,128)(2,1)S(1)}, u32[]{:S(2)}, u32[]{:S(2)}) async-start(bf16[8,2,112,128]{3,2,1,0:T(8,128)(2,1)} %get-tuple-element.131), calls=%async_computation.2 | async-start | bytes 917504 | tf_op jit(solution)/shard_map/all_to_all | solution.py:687
  150.7 28.1 %collective-permute-start.15 = (bf16[768,768]{1,0:T(8,128)(2,1)}, bf16[768,768]{1,0:T(8,128)(2,1)}, u32[]{:S(2)}, u32[]{:S(2)}) collective-permute-start(bf16[768,768]{1,0:T(8,128)(2,1)} %get-tuple-element.144), channel_id=1, source_target_pairs={{0,2},{1,3},{2,0},{3,1},{4,6},{5,7},{6,4},{7,5},{8,10},{9,11},{10,... | collective-permute-start | bytes 3538952 | tf_op jit(solution)/shard_map/ppermute | solution.py:583
  165.5 16.9 %all-to-all-start.3 = ((bf16[8,2,112,128]{3,2,1,0:T(8,128)(2,1)}), bf16[8,2,112,128]{3,2,1,0:T(8,128)(2,1)S(1)}, u32[]{:S(2)}, u32[]{:S(2)}) async-start(bf16[8,2,112,128]{3,2,1,0:T(8,128)(2,1)} %scan_back.1), calls=%async_computation.3 | async-start | bytes 917504 | tf_op jit(solution)/shard_map/all_to_all | solution.py:687
  171.6 19.0 %collective-permute-start.16 = (bf16[384,768]{1,0:T(8,128)(2,1)}, bf16[384,768]{1,0:T(8,128)(2,1)}, u32[]{:S(2)}, u32[]{:S(2)}) collective-permute-start(bf16[384,768]{1,0:T(8,128)(2,1)} %add_convert_fusion.2), channel_id=1, source_target_pairs={{0,4},{4,0},{8,12},{12,8},{16,20},{20,16},{24,28},{28,24},{1,5},{5... | collective-permute-start | bytes 1769480 | tf_op jit(solution)/shard_map/ppermute | solution.py:619
  191.7 13.2 %collective-permute-start.21 = (bf16[512,768]{1,0:T(8,128)(2,1)}, bf16[512,768]{1,0:T(8,128)(2,1)S(1)}, u32[]{:S(2)}, u32[]{:S(2)}) collective-permute-start(bf16[512,768]{1,0:T(8,128)(2,1)} %get-tuple-element.165), channel_id=1, source_target_pairs={{0,1},{1,0},{2,3},{3,2},{4,5},{5,4},{6,7},{7,6},{8,9},{9,8},{10,11... | collective-permute-start | bytes 2359304 | tf_op jit(solution)/shard_map/ppermute | solution.py:579
  200.7 29.2 %collective-permute-start.28 = (bf16[768,768]{1,0:T(8,128)(2,1)}, bf16[768,768]{1,0:T(8,128)(2,1)}, u32[]{:S(2)}, u32[]{:S(2)}) collective-permute-start(bf16[768,768]{1,0:T(8,128)(2,1)} %get-tuple-element.179), channel_id=1, source_target_pairs={{0,2},{1,3},{2,0},{3,1},{4,6},{5,7},{6,4},{7,5},{8,10},{9,11},{10,... | collective-permute-start | bytes 3538952 | tf_op jit(solution)/shard_map/ppermute | solution.py:583
  201.3 15.9 %collective-permute-start.33 = (bf16[384,768]{1,0:T(8,128)(2,1)}, bf16[384,768]{1,0:T(8,128)(2,1)S(1)}, u32[]{:S(2)}, u32[]{:S(2)}) collective-permute-start(bf16[384,768]{1,0:T(8,128)(2,1)} %add_convert_fusion.1), channel_id=1, source_target_pairs={{0,4},{4,0},{8,12},{12,8},{16,20},{20,16},{24,28},{28,24},{1,5},{5... | collective-permute-start | bytes 1769480 | tf_op jit(solution)/shard_map/ppermute | solution.py:619
  215.7 17.1 %collective-permute-start.24 = (bf16[64,768]{1,0:T(8,128)(2,1)S(1)}, bf16[64,768]{1,0:T(8,128)(2,1)S(1)}, u32[]{:S(2)}, u32[]{:S(2)}) collective-permute-start(bf16[64,768]{1,0:T(8,128)(2,1)S(1)} %add_convert_fusion.15), channel_id=1, source_target_pairs={{0,2},{1,3},{2,0},{3,1},{4,6},{5,7},{6,4},{7,5},{8,10},{9,11},{10,... | collective-permute-start | bytes 294920 | tf_op jit(solution)/shard_map/ppermute | solution.py:583
  218.4 17.7 %collective-permute-start.34 = (bf16[192,768]{1,0:T(8,128)(2,1)S(1)}, bf16[192,768]{1,0:T(8,128)(2,1)S(1)}, u32[]{:S(2)}, u32[]{:S(2)}) collective-permute-start(bf16[192,768]{1,0:T(8,128)(2,1)S(1)} %add_convert_fusion.4), channel_id=1, source_target_pairs={{0,8},{4,12},{8,0},{12,4},{16,24},{20,28},{24,16},{28,20},{1,9},{5... | collective-permute-start | bytes 884744 | tf_op jit(solution)/shard_map/ppermute | solution.py:619
  231.3 18.1 %collective-permute-start.29 = (bf16[384,768]{1,0:T(8,128)(2,1)S(1)}, bf16[384,768]{1,0:T(8,128)(2,1)S(1)}, u32[]{:S(2)}, u32[]{:S(2)}) collective-permute-start(bf16[384,768]{1,0:T(8,128)(2,1)S(1)} %add_convert_fusion), channel_id=1, source_target_pairs={{0,4},{4,0},{8,12},{12,8},{16,20},{20,16},{24,28},{28,24},{1,5},{5... | collective-permute-start | bytes 1769480 | tf_op jit(solution)/shard_map/ppermute | solution.py:619
  232.8 14.3 %collective-permute-start.25 = (bf16[64,768]{1,0:T(8,128)(2,1)S(1)}, bf16[64,768]{1,0:T(8,128)(2,1)S(1)}, u32[]{:S(2)}, u32[]{:S(2)}) collective-permute-start(bf16[64,768]{1,0:T(8,128)(2,1)S(1)} %add_convert_fusion.14), channel_id=1, source_target_pairs={{0,4},{4,0},{8,12},{12,8},{16,20},{20,16},{24,28},{28,24},{1,5},{5... | collective-permute-start | bytes 294920 | tf_op jit(solution)/shard_map/ppermute | solution.py:619
  236.0 12.3 %collective-permute-start.32 = (bf16[96,768]{1,0:T(8,128)(2,1)S(1)}, bf16[96,768]{1,0:T(8,128)(2,1)S(1)}, u32[]{:S(2)}, u32[]{:S(2)}) collective-permute-start(bf16[96,768]{1,0:T(8,128)(2,1)S(1)} %add_convert_fusion.10), channel_id=1, source_target_pairs={{0,16},{4,20},{8,24},{12,28},{16,0},{20,4},{24,8},{28,12},{1,17},{... | collective-permute-start | bytes 442376 | tf_op jit(solution)/shard_map/ppermute | solution.py:619
  237.1 12.3 %collective-permute-start.35 = (bf16[96,768]{1,0:T(8,128)(2,1)S(1)}, bf16[96,768]{1,0:T(8,128)(2,1)S(1)}, u32[]{:S(2)}, u32[]{:S(2)}) collective-permute-start(bf16[96,768]{1,0:T(8,128)(2,1)S(1)} %add_convert_fusion.9), channel_id=1, source_target_pairs={{0,16},{4,20},{8,24},{12,28},{16,0},{20,4},{24,8},{28,12},{1,17},{... | collective-permute-start | bytes 442376 | tf_op jit(solution)/shard_map/ppermute | solution.py:619
  250.4 16.7 %collective-permute-start.36 = (bf16[192,768]{1,0:T(8,128)(2,1)S(1)}, bf16[192,768]{1,0:T(8,128)(2,1)S(1)}, u32[]{:S(2)}, u32[]{:S(2)}) collective-permute-start(bf16[192,768]{1,0:T(8,128)(2,1)S(1)} %add_convert_fusion.3), channel_id=1, source_target_pairs={{0,8},{4,12},{8,0},{12,4},{16,24},{20,28},{24,16},{28,20},{1,9},{5... | collective-permute-start | bytes 884744 | tf_op jit(solution)/shard_map/ppermute | solution.py:619
  250.5 19.2 %collective-permute-start.37 = (bf16[192,768]{1,0:T(8,128)(2,1)S(1)}, bf16[192,768]{1,0:T(8,128)(2,1)S(1)}, u32[]{:S(2)}, u32[]{:S(2)}) collective-permute-start(bf16[192,768]{1,0:T(8,128)(2,1)S(1)} %pad_maximum_fusion.5), channel_id=1, source_target_pairs={{0,8},{4,12},{8,0},{12,4},{16,24},{20,28},{24,16},{28,20},{1,9},{5... | collective-permute-start | bytes 884744 | tf_op jit(solution)/shard_map/ppermute | solution.py:619
  253.6 13.5 %collective-permute-start.38 = (bf16[96,768]{1,0:T(8,128)(2,1)S(1)}, bf16[96,768]{1,0:T(8,128)(2,1)S(1)}, u32[]{:S(2)}, u32[]{:S(2)}) collective-permute-start(bf16[96,768]{1,0:T(8,128)(2,1)S(1)} %add_convert_fusion.8), channel_id=1, source_target_pairs={{0,16},{4,20},{8,24},{12,28},{16,0},{20,4},{24,8},{28,12},{1,17},{... | collective-permute-start | bytes 442376 | tf_op jit(solution)/shard_map/ppermute | solution.py:619
  254.7 36.5 %collective-permute-start.27 = (bf16[64,768]{1,0:T(8,128)(2,1)S(1)}, bf16[64,768]{1,0:T(8,128)(2,1)S(1)}, u32[]{:S(2)}, u32[]{:S(2)}) collective-permute-start(bf16[64,768]{1,0:T(8,128)(2,1)S(1)} %add_convert_fusion.12), channel_id=1, source_target_pairs={{0,16},{4,20},{8,24},{12,28},{16,0},{20,4},{24,8},{28,12},{1,17},{... | collective-permute-start | bytes 294920 | tf_op jit(solution)/shard_map/ppermute | solution.py:619
  271.6 10.4 %collective-permute-start.40 = (bf16[192,768]{1,0:T(8,128)(2,1)S(1)}, bf16[192,768]{1,0:T(8,128)(2,1)S(1)}, u32[]{:S(2)}, u32[]{:S(2)}) collective-permute-start(bf16[192,768]{1,0:T(8,128)(2,1)S(1)} %pad_maximum_fusion.6), channel_id=1, source_target_pairs={{0,8},{4,12},{8,0},{12,4},{16,24},{20,28},{24,16},{28,20},{1,9},{5... | collective-permute-start | bytes 884744 | tf_op jit(solution)/shard_map/ppermute | solution.py:619
  274.1 17.0 %collective-permute-start.42 = (bf16[384,768]{1,0:T(8,128)(2,1)S(1)}, bf16[384,768]{1,0:T(8,128)(2,1)S(1)}, u32[]{:S(2)}, u32[]{:S(2)}) collective-permute-start(bf16[384,768]{1,0:T(8,128)(2,1)S(1)} %pad_maximum_fusion.2), channel_id=1, source_target_pairs={{0,4},{4,0},{8,12},{12,8},{16,20},{20,16},{24,28},{28,24},{1,5},{5... | collective-permute-start | bytes 1769480 | tf_op jit(solution)/shard_map/ppermute | solution.py:619
  283.8 16.1 %collective-permute-start.44 = (bf16[384,768]{1,0:T(8,128)(2,1)S(1)}, bf16[384,768]{1,0:T(8,128)(2,1)S(1)}, u32[]{:S(2)}, u32[]{:S(2)}) collective-permute-start(bf16[384,768]{1,0:T(8,128)(2,1)S(1)} %pad_maximum_fusion.3), channel_id=1, source_target_pairs={{0,4},{4,0},{8,12},{12,8},{16,20},{20,16},{24,28},{28,24},{1,5},{5... | collective-permute-start | bytes 1769480 | tf_op jit(solution)/shard_map/ppermute | solution.py:619
  300.9 12.7 %collective-permute-start.45 = (bf16[384,768]{1,0:T(8,128)(2,1)S(1)}, bf16[384,768]{1,0:T(8,128)(2,1)S(1)}, u32[]{:S(2)}, u32[]{:S(2)}) collective-permute-start(bf16[384,768]{1,0:T(8,128)(2,1)S(1)} %pad_maximum_fusion.4), channel_id=1, source_target_pairs={{0,4},{4,0},{8,12},{12,8},{16,20},{20,16},{24,28},{28,24},{1,5},{5... | collective-permute-start | bytes 1769480 | tf_op jit(solution)/shard_map/ppermute | solution.py:619
  (65 other events, 404.4 us)

commit v4 on v3

--- a/solution.py
+++ b/solution.py
@@ -88,7 +88,7 @@
             ref.flush()
 
 
-def call(kernel, outs, kinds, args, name, scratch=(), out_kinds=None, limit=32):
+def call(kernel, outs, kinds, args, name, scratch=(), out_kinds=None, limit=32, flops=1):
     out_kinds = out_kinds or "v" * len(outs)
     both = kinds + out_kinds
     groups = [a if isinstance(a, list) else [a] for a in [*args, *outs]]
@@ -138,7 +138,7 @@
         out_specs=[SPECS[k] for k in out_kinds],
         scratch_shapes=[*staged, *sems, *scratch],
         compiler_params=pltpu.CompilerParams(vmem_limit_bytes=limit << 20),
-        cost_estimate=pl.CostEstimate(flops=1, bytes_accessed=1, transcendentals=0),
+        cost_estimate=pl.CostEstimate(flops=flops, bytes_accessed=1, transcendentals=0),
         name=name,
     )(*[
         pltpu.with_memory_space_constraint(a, pltpu.HBM) if k == "h" else a
@@ -769,11 +769,11 @@
     arrived = exchange(states)
     (fq,) = call(
         functools.partial(query_kernel, heads), [shaped((wide, rows_n), BF16)], "vv",
-        [after(qkv, states), query_map], "queries", (), "h",
+        [after(qkv, states), query_map], "queries", (), "h", flops=10**12,
     )
     (running,) = call(
         functools.partial(scan_kernel, nctx, False), [state_shape], "sv",
-        [keep, after(arrived, fq, cross_first)], "scan", (), "h",
+        [keep, after(arrived, cross_first)], "scan", (), "h",
     )
     carried = exchange(running)
     far_output = core_swap(after(cross_first, running)[width : width + shard])
@@ -781,7 +781,7 @@
     mixed, den, middle, n2, wo = call(
         functools.partial(attend_kernel, heads, slots, nctx),
         [table, shaped((heads * 8, rows_n)), full, low, shaped((width, width), BF16)],
-        "svhhaaaav", [meta, carried, fq, x, *outputs, params], "attend",
+        "svhhhvavv", [meta, carried, fq, x, *outputs, params], "attend",
         [total], "hhhvh",
     )
     n2_other = core_swap(n2)

time: 318 us -> 308 us (0.969)
  local copies, waits for them, and re-layouts: 18 us -> 11.3 us
  waiting for transfers between devices: 113 us -> 108 us
    unnamed x94 -> x64, local copies, waits for them, and re-layouts: 9.62 us -> 1.55 us
  transfers between devices with their start and end apart: 50 -> 50, of which waited for: 27 -> 27; matrix products, arithmetic and copies ran while one was open for 11% -> 13% of each run, Pallas kernels for 24% -> 26%
where the time goes in v4:
time: 308 us; the launch traced here: 306 us
  waiting for transfers between devices  108 us (35%)
  Pallas kernels  95 us (31%)
  starting transfers between devices  58.6 us (19%)
  other arithmetic  31.2 us (10%)
  local copies, waits for them, and re-layouts  11.3 us (4%)
    pallas_call x15, Pallas kernels, call(): pl.pallas_call(run, out_shape=[pltpu.HBM(o.shape, o.dtype) if k == 'h' el...  95 us
    ppermute x21, waiting for transfers between devices, send(): return lax.ppermute(value, 'ctx', [(i, i ^ flip) for i in range(self.nctx)])  55 us
    ppermute x9, waiting for transfers between devices, cross_swap(): return lax.ppermute(a, 'fsdp', CROSS)  32.6 us
    ppermute x21, starting transfers between devices, send(): return lax.ppermute(value, 'ctx', [(i, i ^ flip) for i in range(self.nctx)])  22.8 us
    all_to_all x4, starting transfers between devices, exchange(): return lax.all_to_all(a, 'ctx', 0, 0, tiled=True)  20 us
    convert_element_type x12, other arithmetic, rows_sum(): return out.astype(BF16)  15.7 us
    all_to_all x4, waiting for transfers between devices, exchange(): return lax.all_to_all(a, 'ctx', 0, 0, tiled=True)  12.5 us
    ppermute x9, starting transfers between devices, cross_swap(): return lax.ppermute(a, 'fsdp', CROSS)  12.4 us
  transfers between devices with their start and end apart: 50, of which 27 were waited for; matrix products, arithmetic and copies ran while one was open for 13% of the time, Pallas kernels for 26%

profile of v4, /device:TPU:0, one launch (start us, length us, event | category | flops | bytes accessed | tf_op | source)
XLA Modules:
  0.0 306.4 jit_solution(15418418872314198385)
XLA Ops:
  0.6 3.0 collective-permute-start.4
  3.7 5.5 %concatenate.51 = bf16[3072]{0:T(1024)(128)(2,1)S(1)} concatenate(bf16[192]{0:T(256)(128)(2,1)} %param.22, bf16[192]{0:T(256)(128)(2,1)} %param.23, bf16[192]{0:T(256)(128)(2,1)} %param.30, bf16[192]{0:T(256)(128)(2,1)} %param.31, bf16[192]{0:T(256)(128)(2,1)} %param.29, bf16[192]{0:T(256)(128)(2,1)} %param.35, bf16[576]{0:T(1024)(128)(2,1)} %param.25, bf16[768]{0:T(1024)(128)(2,1)} %param.33, ...), dimensions={0} | concatenate | bytes 12288 | tf_op jit(solution)/shard_map/concatenate | solution.py:716
  13.3 12.6 %collective-permute-done = bf16[432,64]{1,0:T(8,128)(2,1)S(1)} collective-permute-done((bf16[432,64]{1,0:T(8,128)(2,1)S(1)}, bf16[432,64]{1,0:T(8,128)(2,1)S(1)}, u32[]{:S(2)}, u32[]{:S(2)}) %collective-permute-start) | collective-permute-done | bytes 55328 | tf_op jit(solution)/shard_map/ppermute | solution.py:583
  33.4 3.6 %project_near.1 = (bf16[512,768]{1,0:T(8,128)(2,1)}, bf16[1152,512]{1,0:T(8,128)(2,1)S(1)}) custom-call(s32[5]{0:T(128)S(1)} %stack.42.refs_0_, bf16[512,768]{1,0:T(8,128)(2,1)} %bitcast.33, f32[6,768]{1,0:T(8,128)S(1)} %reshape.102.refs_2_.refs_8_.refs_5_.refs_3_, bf16[576,768]{1,0:T(8,128)(2,1)S(1)} %bitcast.27, ...), custom_call_target="tpu_custom_call" | custom-call | flops 1 | bytes 1 | tf_op jit(solution)/shard_map/project_near/pallas_call | solution.py:132
  37.0 3.1 %project_far.1.refs_1_.refs_0_.refs_4_.refs_3_ = bf16[2304,512]{1,0:T(8,128)(2,1)S(1)} custom-call(s32[5]{0:T(128)S(1)} %stack.42.refs_0_, bf16[512,768]{1,0:T(8,128)(2,1)} %get-tuple-element.112.refs_1_.refs_6_.refs_2_, bf16[1152,512]{1,0:T(8,128)(2,1)S(1)} %get-tuple-element.113.refs_2_, bf16[576,768]{1,0:T(8,128)(2,1)S(1)} %collective-permute-done.4.refs_3_.refs_14_, ...), custom_call_target="tpu_custom_call" | custom-call | flops 1 | bytes 1 | tf_op jit(solution)/shard_map/project_far/pallas_call | solution.py:132
  40.2 6.3 %keys.1 = (bf16[1536,512]{1,0:T(8,128)(2,1)}, bf16[8,2,112,128]{3,2,1,0:T(8,128)(2,1)}) custom-call(s32[5]{0:T(128)S(1)} %stack.42.refs_0_, bf16[2304,512]{1,0:T(8,128)(2,1)S(1)} %project_far.1.refs_1_.refs_0_.refs_4_.refs_3_, bf16[12,64,64]{2,1,0:T(8,128)(2,1)S(1)} %bitcast.29), custom_call_target="tpu_custom_call" | custom-call | flops 1 | bytes 1 | tf_op jit(solution)/shard_map/keys/pallas_call | solution.py:132
  46.5 5.8 %all-to-all-start = ((bf16[8,2,112,128]{3,2,1,0:T(8,128)(2,1)}), bf16[8,2,112,128]{3,2,1,0:T(8,128)(2,1)}, u32[]{:S(2)}, u32[]{:S(2)}) async-start(bf16[8,2,112,128]{3,2,1,0:T(8,128)(2,1)} %get-tuple-element.114), calls=%async_computation | async-start | bytes 917504 | tf_op jit(solution)/shard_map/all_to_all | solution.py:687
  53.9 10.9 %collective-permute-done.6.refs_6_.refs_2_ = bf16[960,768]{1,0:T(8,128)(2,1)} collective-permute-done((bf16[960,768]{1,0:T(8,128)(2,1)}, bf16[960,768]{1,0:T(8,128)(2,1)}, u32[]{:S(2)}, u32[]{:S(2)}) %collective-permute-start.6) | collective-permute-done | bytes 1474592 | tf_op jit(solution)/shard_map/ppermute | solution.py:583
  68.4 5.8 %all-to-all-start.1 = ((bf16[8,2,112,128]{3,2,1,0:T(8,128)(2,1)}), bf16[8,2,112,128]{3,2,1,0:T(8,128)(2,1)}, u32[]{:S(2)}, u32[]{:S(2)}) async-start(bf16[8,2,112,128]{3,2,1,0:T(8,128)(2,1)} %scan.1), calls=%async_computation.1 | async-start | bytes 917504 | tf_op jit(solution)/shard_map/all_to_all | solution.py:687
  78.9 7.7 %all-to-all-done.1.refs_1_ = bf16[8,2,112,128]{3,2,1,0:T(8,128)(2,1)} async-done(((bf16[8,2,112,128]{3,2,1,0:T(8,128)(2,1)}), bf16[8,2,112,128]{3,2,1,0:T(8,128)(2,1)}, u32[]{:S(2)}, u32[]{:S(2)}) %all-to-all-start.1) | async-done | bytes 458784 | tf_op jit(solution)/shard_map/all_to_all | solution.py:687
  86.5 6.1 %attend.1 = (bf16[768,512]{1,0:T(8,128)(2,1)}, f32[96,512]{1,0:T(8,128)}, f32[512,768]{1,0:T(8,128)}, bf16[512,768]{1,0:T(8,128)(2,1)S(1)}, bf16[768,768]{1,0:T(8,128)(2,1)}) custom-call(s32[5]{0:T(128)S(1)} %copy-done.11, bf16[8,2,112,128]{3,2,1,0:T(8,128)(2,1)} %all-to-all-done.1.refs_1_, bf16[1536,512]{1,0:T(8,128)(2,1)} %queries.1.refs_2_.refs_8_.refs_3_, ...), custom_call_target="tpu_custom_call" | custom-call | flops 1 | bytes 1 | tf_op jit(solution)/shard_map/attend/pallas_call | solution.py:132
  95.0 14.3 %mlp_far.1 = (f32[512,768]{1,0:T(8,128)}, f32[512,768]{1,0:T(8,128)}, bf16[512,768]{1,0:T(8,128)(2,1)S(1)}, bf16[512,768]{1,0:T(8,128)(2,1)S(1)}, bf16[384,768]{...) custom-call(s32[5]{0:T(128)S(1)} %copy-done.11, ...), custom_call_target="tpu_custom_call" | custom-call | flops 1 | bytes 1 | tf_op jit(solution)/shard_map/mlp_far/pallas_call | solution.py:132
  110.0 16.5 %mlp_near.1 = (f32[512,768]{1,0:T(8,128)}, f32[512,768]{1,0:T(8,128)}, bf16[512,768]{1,0:T(8,128)(2,1)}, bf16[512,768]{1,0:T(8,128)(2,1)}, bf16[768,768]{1,0:T(8...) custom-call(s32[5]{0:T(128)S(1)} %copy-done.11, bf16[512,768]{1,0:T(8,128)(2,1)S(1)} %get-tuple-element.119.refs_1_, ...), custom_call_target="tpu_custom_call" | custom-call | flops 1 | bytes 1 | tf_op jit(solution)/shard_map/mlp_near/pallas_call | solution.py:132
  130.5 6.8 %middle.1 = (f32[512,768]{1,0:T(8,128)}, bf16[512,768]{1,0:T(8,128)(2,1)}, bf16[960,512]{1,0:T(8,128)(2,1)}, bf16[8,2,112,128]{3,2,1,0:T(8,128)(2,1)}, f32[8,768]{1,0:T(8,128)S(1)}) custom-call(s32[5]{0:T(128)S(1)} %copy-done.11, f32[512,768]{1,0:T(8,128)S(1)} %copy-done.7, bf16[512,768]{1,0:T(8,128)(2,1)S(1)} %collective-permute-done.12.refs_2_, ...), custom_call_target="tpu_custom_call" | custom-call | flops 1 | bytes 1 | tf_op jit(solution)/shard_map/middle/pallas_call | solution.py:132
  137.2 4.2 %all-to-all-start.2 = ((bf16[8,2,112,128]{3,2,1,0:T(8,128)(2,1)}), bf16[8,2,112,128]{3,2,1,0:T(8,128)(2,1)}, u32[]{:S(2)}, u32[]{:S(2)}) async-start(bf16[8,2,112,128]{3,2,1,0:T(8,128)(2,1)} %get-tuple-element.131), calls=%async_computation.2 | async-start | bytes 917504 | tf_op jit(solution)/shard_map/all_to_all | solution.py:687
  144.1 7.6 %query_back.1 = (bf16[768,512]{1,0:T(8,128)(2,1)}, f32[12,64,64]{2,1,0:T(8,128)}, bf16[192,768]{1,0:T(8,128)(2,1)}, bf16[192,768]{1,0:T(8,128)(2,1)}, bf16[192,7...) custom-call(s32[5]{0:T(128)S(1)} %copy-done.11, bf16[8,2,112,128]{3,2,1,0:T(8,128)(2,1)} %all-to-all-done.1.refs_1_, ...), custom_call_target="tpu_custom_call" | custom-call | flops 1 | bytes 1 | tf_op jit(solution)/shard_map/query_back/pallas_call | solution.py:132
  151.7 3.3 %all-to-all-done.2.refs_1_ = bf16[8,2,112,128]{3,2,1,0:T(8,128)(2,1)} async-done(((bf16[8,2,112,128]{3,2,1,0:T(8,128)(2,1)}), bf16[8,2,112,128]{3,2,1,0:T(8,128)(2,1)}, u32[]{:S(2)}, u32[]{:S(2)}) %all-to-all-start.2) | async-done | bytes 458784 | tf_op jit(solution)/shard_map/all_to_all | solution.py:687
  156.9 4.1 %all-to-all-start.3 = ((bf16[8,2,112,128]{3,2,1,0:T(8,128)(2,1)}), bf16[8,2,112,128]{3,2,1,0:T(8,128)(2,1)}, u32[]{:S(2)}, u32[]{:S(2)}) async-start(bf16[8,2,112,128]{3,2,1,0:T(8,128)(2,1)} %scan_back.1), calls=%async_computation.3 | async-start | bytes 917504 | tf_op jit(solution)/shard_map/all_to_all | solution.py:687
  165.3 5.1 %collective-permute-done.15 = bf16[768,768]{1,0:T(8,128)(2,1)} collective-permute-done((bf16[768,768]{1,0:T(8,128)(2,1)}, bf16[768,768]{1,0:T(8,128)(2,1)}, u32[]{:S(2)}, u32[]{:S(2)}) %collective-permute-start.15) | collective-permute-done | bytes 1179680 | tf_op jit(solution)/shard_map/ppermute | solution.py:583
  174.0 8.6 %key_back.1 = (bf16[2304,512]{1,0:T(8,128)(2,1)}, f32[12,64,64]{2,1,0:T(8,128)}, bf16[576,768]{1,0:T(8,128)(2,1)}, bf16[576,768]{1,0:T(8,128)(2,1)}) custom-call(s32[5]{0:T(128)S(1)} %copy-done.11, bf16[8,2,112,128]{3,2,1,0:T(8,128)(2,1)} %all-to-all-done.3.refs_1_, bf16[1536,512]{1,0:T(8,128)(2,1)} %get-tuple-element.147.refs_2_, ...), custom_call_target="tpu_custom_call" | custom-call | flops 1 | bytes 1 | tf_op jit(solution)/shard_map/key_back/pallas_call | solution.py:132
  187.5 5.3 %project_grad.1 = (bf16[768,768]{1,0:T(8,128)(2,1)}, bf16[768,768]{1,0:T(8,128)(2,1)}) custom-call(s32[5]{0:T(128)S(1)} %copy-done.11, bf16[2304,512]{1,0:T(8,128)(2,1)} %get-tuple-element.148.refs_1_, bf16[512,768]{1,0:T(8,128)(2,1)} %get-tuple-element.112.refs_1_.refs_6_.refs_2_, bf16[576,768]{1,0:T(8,128)(2,1)S(1)} %collective-permute-done.17.refs_3_, ...), custom_call_target="tpu_custom_call" | custom-call | flops 1 | bytes 1 | tf_op jit(solution)/shard_map/project_grad/pallas_call | solution.py:132
  198.3 9.4 %input.1 = (f32[512,768]{1,0:T(8,128)}, f32[512,768]{1,0:T(8,128)}, bf16[64,768]{1,0:T(8,128)(2,1)S(1)}, bf16[64,768]{1,0:T(8,128)(2,1)S(1)}, bf16[64,768]{1,0:T(8,128)(2,1)S(1)}, /*index=5*/bf16[64,768]{1,0:T(8,128)(2,1)S(1)}) custom-call(s32[5]{0:T(128)S(1)} %copy-done.11, bf16[2304,512]{1,0:T(8,128)(2,1)} %get-tuple-element.148.refs_1_, ...), custom_call_target="tpu_custom_call" | custom-call | flops 1 | bytes 1 | tf_op jit(solution)/shard_map/input/pallas_call | solution.py:132
  212.6 5.2 %collective-permute-done.30 = bf16[192,768]{1,0:T(8,128)(2,1)S(1)} collective-permute-done((bf16[192,768]{1,0:T(8,128)(2,1)S(1)}, bf16[192,768]{1,0:T(8,128)(2,1)S(1)}, u32[]{:S(2)}, u32[]{:S(2)}) %collective-permute-start.30) | collective-permute-done | bytes 294944 | tf_op jit(solution)/shard_map/ppermute | solution.py:619
  230.3 2.9 collective-permute-start.35
  233.2 5.9 %collective-permute-done.25 = bf16[64,768]{1,0:T(8,128)(2,1)S(1)} collective-permute-done((bf16[64,768]{1,0:T(8,128)(2,1)S(1)}, bf16[64,768]{1,0:T(8,128)(2,1)S(1)}, u32[]{:S(2)}, u32[]{:S(2)}) %collective-permute-start.25) | collective-permute-done | bytes 98336 | tf_op jit(solution)/shard_map/ppermute | solution.py:619
  250.1 9.8 %collective-permute-done.38 = bf16[96,768]{1,0:T(8,128)(2,1)S(1)} collective-permute-done((bf16[96,768]{1,0:T(8,128)(2,1)S(1)}, bf16[96,768]{1,0:T(8,128)(2,1)S(1)}, u32[]{:S(2)}, u32[]{:S(2)}) %collective-permute-start.38) | collective-permute-done | bytes 147488 | tf_op jit(solution)/shard_map/ppermute | solution.py:619
  259.8 3.2 %collective-permute-done.37 = bf16[192,768]{1,0:T(8,128)(2,1)S(1)} collective-permute-done((bf16[192,768]{1,0:T(8,128)(2,1)S(1)}, bf16[192,768]{1,0:T(8,128)(2,1)S(1)}, u32[]{:S(2)}, u32[]{:S(2)}) %collective-permute-start.37) | collective-permute-done | bytes 294944 | tf_op jit(solution)/shard_map/ppermute | solution.py:619
  267.4 4.0 %collective-permute-done.39 = bf16[96,768]{1,0:T(8,128)(2,1)S(1)} collective-permute-done((bf16[96,768]{1,0:T(8,128)(2,1)S(1)}, bf16[96,768]{1,0:T(8,128)(2,1)S(1)}, u32[]{:S(2)}, u32[]{:S(2)}) %collective-permute-start.39) | collective-permute-done | bytes 147488 | tf_op jit(solution)/shard_map/ppermute | solution.py:619
  271.3 3.0 collective-permute-done.40
  278.1 4.8 %collective-permute-done.41 = bf16[96,768]{1,0:T(8,128)(2,1)S(1)} collective-permute-done((bf16[96,768]{1,0:T(8,128)(2,1)S(1)}, bf16[96,768]{1,0:T(8,128)(2,1)S(1)}, u32[]{:S(2)}, u32[]{:S(2)}) %collective-permute-start.41) | collective-permute-done | bytes 147488 | tf_op jit(solution)/shard_map/ppermute | solution.py:619
  285.2 5.2 %collective-permute-done.43 = bf16[192,768]{1,0:T(8,128)(2,1)S(1)} collective-permute-done((bf16[192,768]{1,0:T(8,128)(2,1)S(1)}, bf16[192,768]{1,0:T(8,128)(2,1)S(1)}, u32[]{:S(2)}, u32[]{:S(2)}) %collective-permute-start.43) | collective-permute-done | bytes 294944 | tf_op jit(solution)/shard_map/ppermute | solution.py:619
  295.7 8.3 %collective-permute-done.45 = bf16[384,768]{1,0:T(8,128)(2,1)S(1)} collective-permute-done((bf16[384,768]{1,0:T(8,128)(2,1)S(1)}, bf16[384,768]{1,0:T(8,128)(2,1)S(1)}, u32[]{:S(2)}, u32[]{:S(2)}) %collective-permute-start.45) | collective-permute-done | bytes 589856 | tf_op jit(solution)/shard_map/ppermute | solution.py:619
  (216 shorter events, 95.8 us)
Async XLA Ops:
  0.6 28.7 %collective-permute-start.4 = (bf16[576,768]{1,0:T(8,128)(2,1)}, bf16[576,768]{1,0:T(8,128)(2,1)S(1)}, u32[]{:S(2)}, u32[]{:S(2)}) collective-permute-start(bf16[576,768]{1,0:T(8,128)(2,1)} %bitcast.25), channel_id=1, source_target_pairs={{0,2},{1,3},{2,0},{3,1},{4,6},{5,7},{6,4},{7,5},{8,10},{9,11},{10,... | collective-permute-start | bytes 2654216 | tf_op jit(solution)/shard_map/ppermute | solution.py:583
  10.1 15.8 %collective-permute-start = (bf16[432,64]{1,0:T(8,128)(2,1)S(1)}, bf16[432,64]{1,0:T(8,128)(2,1)S(1)}, u32[]{:S(2)}, u32[]{:S(2)}) collective-permute-start(bf16[432,64]{1,0:T(8,128)(2,1)S(1)} %pad_maximum_fusion.10), channel_id=1, source_target_pairs={{0,2},{1,3},{2,0},{3,1},{4,6},{5,7},{6,4},{7,5},{8,10},{9,11},{10,... | collective-permute-start | bytes 165896 | tf_op jit(solution)/shard_map/ppermute | solution.py:583
  10.2 17.7 %collective-permute-start.2 = (bf16[432,64]{1,0:T(8,128)(2,1)S(1)}, bf16[432,64]{1,0:T(8,128)(2,1)S(1)}, u32[]{:S(2)}, u32[]{:S(2)}) collective-permute-start(bf16[432,64]{1,0:T(8,128)(2,1)S(1)} %pad_maximum_fusion.10), channel_id=1, source_target_pairs={{0,1},{1,0},{2,3},{3,2},{4,5},{5,4},{6,7},{7,6},{8,9},{9,8},{10,11... | collective-permute-start | bytes 165896 | tf_op jit(solution)/shard_map/ppermute | solution.py:579
  10.2 23.1 %collective-permute-start.3 = (bf16[576,768]{1,0:T(8,128)(2,1)}, bf16[576,768]{1,0:T(8,128)(2,1)S(1)}, u32[]{:S(2)}, u32[]{:S(2)}) collective-permute-start(bf16[576,768]{1,0:T(8,128)(2,1)} %bitcast.26), channel_id=1, source_target_pairs={{0,1},{1,0},{2,3},{3,2},{4,5},{5,4},{6,7},{7,6},{8,9},{9,8},{10,11... | collective-permute-start | bytes 2654216 | tf_op jit(solution)/shard_map/ppermute | solution.py:579
  30.2 34.5 %collective-permute-start.6 = (bf16[960,768]{1,0:T(8,128)(2,1)}, bf16[960,768]{1,0:T(8,128)(2,1)}, u32[]{:S(2)}, u32[]{:S(2)}) collective-permute-start(bf16[960,768]{1,0:T(8,128)(2,1)} %pad_maximum_fusion), channel_id=1, source_target_pairs={{0,2},{1,3},{2,0},{3,1},{4,6},{5,7},{6,4},{7,5},{8,10},{9,11},{10,... | collective-permute-start | bytes 4423688 | tf_op jit(solution)/shard_map/ppermute | solution.py:583
  46.5 20.0 %all-to-all-start = ((bf16[8,2,112,128]{3,2,1,0:T(8,128)(2,1)}), bf16[8,2,112,128]{3,2,1,0:T(8,128)(2,1)}, u32[]{:S(2)}, u32[]{:S(2)}) async-start(bf16[8,2,112,128]{3,2,1,0:T(8,128)(2,1)} %get-tuple-element.114), calls=%async_computation | async-start | bytes 917504 | tf_op jit(solution)/shard_map/all_to_all | solution.py:687
  52.3 26.5 %collective-permute-start.7 = (bf16[192,768]{1,0:T(8,128)(2,1)}, bf16[192,768]{1,0:T(8,128)(2,1)}, u32[]{:S(2)}, u32[]{:S(2)}) collective-permute-start(bf16[192,768]{1,0:T(8,128)(2,1)} %refs_4_.1), channel_id=1, source_target_pairs={{0,1},{1,0},{2,3},{3,2},{4,5},{5,4},{6,7},{7,6},{8,9},{9,8},{10,11... | collective-permute-start | bytes 884744 | tf_op jit(solution)/shard_map/ppermute | solution.py:579
  52.3 40.6 %collective-permute-start.10 = (bf16[512,768]{1,0:T(8,128)(2,1)}, bf16[512,768]{1,0:T(8,128)(2,1)}, u32[]{:S(2)}, u32[]{:S(2)}) collective-permute-start(bf16[512,768]{1,0:T(8,128)(2,1)} %bitcast.13.refs_4_), channel_id=1, source_target_pairs={{0,1},{1,0},{2,3},{3,2},{4,5},{5,4},{6,7},{7,6},{8,9},{9,8},{10,11... | collective-permute-start | bytes 2359304 | tf_op jit(solution)/shard_map/ppermute | solution.py:579
  64.8 28.1 %collective-permute-start.11 = (bf16[768,768]{1,0:T(8,128)(2,1)}, bf16[768,768]{1,0:T(8,128)(2,1)}, u32[]{:S(2)}, u32[]{:S(2)}) collective-permute-start(bf16[768,768]{1,0:T(8,128)(2,1)} %refs_5_.1), channel_id=1, source_target_pairs={{0,2},{1,3},{2,0},{3,1},{4,6},{5,7},{6,4},{7,5},{8,10},{9,11},{10,... | collective-permute-start | bytes 3538952 | tf_op jit(solution)/shard_map/ppermute | solution.py:583
  68.4 18.1 %all-to-all-start.1 = ((bf16[8,2,112,128]{3,2,1,0:T(8,128)(2,1)}), bf16[8,2,112,128]{3,2,1,0:T(8,128)(2,1)}, u32[]{:S(2)}, u32[]{:S(2)}) async-start(bf16[8,2,112,128]{3,2,1,0:T(8,128)(2,1)} %scan.1), calls=%async_computation.1 | async-start | bytes 917504 | tf_op jit(solution)/shard_map/all_to_all | solution.py:687
  109.4 17.2 %collective-permute-start.13 = (bf16[384,768]{1,0:T(8,128)(2,1)}, bf16[384,768]{1,0:T(8,128)(2,1)S(1)}, u32[]{:S(2)}, u32[]{:S(2)}) collective-permute-start(bf16[384,768]{1,0:T(8,128)(2,1)} %get-tuple-element.136), channel_id=1, source_target_pairs={{0,2},{1,3},{2,0},{3,1},{4,6},{5,7},{6,4},{7,5},{8,10},{9,11},{10,... | collective-permute-start | bytes 1769480 | tf_op jit(solution)/shard_map/ppermute | solution.py:583
  126.6 16.0 %collective-permute-start.14 = (bf16[384,768]{1,0:T(8,128)(2,1)}, bf16[384,768]{1,0:T(8,128)(2,1)}, u32[]{:S(2)}, u32[]{:S(2)}) collective-permute-start(bf16[384,768]{1,0:T(8,128)(2,1)} %get-tuple-element.137), channel_id=1, source_target_pairs={{0,2},{1,3},{2,0},{3,1},{4,6},{5,7},{6,4},{7,5},{8,10},{9,11},{10,... | collective-permute-start | bytes 1769480 | tf_op jit(solution)/shard_map/ppermute | solution.py:583
  137.2 17.8 %all-to-all-start.2 = ((bf16[8,2,112,128]{3,2,1,0:T(8,128)(2,1)}), bf16[8,2,112,128]{3,2,1,0:T(8,128)(2,1)}, u32[]{:S(2)}, u32[]{:S(2)}) async-start(bf16[8,2,112,128]{3,2,1,0:T(8,128)(2,1)} %get-tuple-element.131), calls=%async_computation.2 | async-start | bytes 917504 | tf_op jit(solution)/shard_map/all_to_all | solution.py:687
  142.6 27.8 %collective-permute-start.15 = (bf16[768,768]{1,0:T(8,128)(2,1)}, bf16[768,768]{1,0:T(8,128)(2,1)}, u32[]{:S(2)}, u32[]{:S(2)}) collective-permute-start(bf16[768,768]{1,0:T(8,128)(2,1)} %get-tuple-element.144), channel_id=1, source_target_pairs={{0,2},{1,3},{2,0},{3,1},{4,6},{5,7},{6,4},{7,5},{8,10},{9,11},{10,... | collective-permute-start | bytes 3538952 | tf_op jit(solution)/shard_map/ppermute | solution.py:583
  156.9 17.1 %all-to-all-start.3 = ((bf16[8,2,112,128]{3,2,1,0:T(8,128)(2,1)}), bf16[8,2,112,128]{3,2,1,0:T(8,128)(2,1)}, u32[]{:S(2)}, u32[]{:S(2)}) async-start(bf16[8,2,112,128]{3,2,1,0:T(8,128)(2,1)} %scan_back.1), calls=%async_computation.3 | async-start | bytes 917504 | tf_op jit(solution)/shard_map/all_to_all | solution.py:687
  163.5 19.2 %collective-permute-start.16 = (bf16[384,768]{1,0:T(8,128)(2,1)}, bf16[384,768]{1,0:T(8,128)(2,1)}, u32[]{:S(2)}, u32[]{:S(2)}) collective-permute-start(bf16[384,768]{1,0:T(8,128)(2,1)} %add_convert_fusion.2), channel_id=1, source_target_pairs={{0,4},{4,0},{8,12},{12,8},{16,20},{20,16},{24,28},{28,24},{1,5},{5... | collective-permute-start | bytes 1769480 | tf_op jit(solution)/shard_map/ppermute | solution.py:619
  183.7 14.5 %collective-permute-start.21 = (bf16[512,768]{1,0:T(8,128)(2,1)}, bf16[512,768]{1,0:T(8,128)(2,1)S(1)}, u32[]{:S(2)}, u32[]{:S(2)}) collective-permute-start(bf16[512,768]{1,0:T(8,128)(2,1)} %get-tuple-element.165), channel_id=1, source_target_pairs={{0,1},{1,0},{2,3},{3,2},{4,5},{5,4},{6,7},{7,6},{8,9},{9,8},{10,11... | collective-permute-start | bytes 2359304 | tf_op jit(solution)/shard_map/ppermute | solution.py:579
  192.8 29.2 %collective-permute-start.28 = (bf16[768,768]{1,0:T(8,128)(2,1)}, bf16[768,768]{1,0:T(8,128)(2,1)}, u32[]{:S(2)}, u32[]{:S(2)}) collective-permute-start(bf16[768,768]{1,0:T(8,128)(2,1)} %get-tuple-element.179), channel_id=1, source_target_pairs={{0,2},{1,3},{2,0},{3,1},{4,6},{5,7},{6,4},{7,5},{8,10},{9,11},{10,... | collective-permute-start | bytes 3538952 | tf_op jit(solution)/shard_map/ppermute | solution.py:583
  194.3 15.4 %collective-permute-start.33 = (bf16[384,768]{1,0:T(8,128)(2,1)}, bf16[384,768]{1,0:T(8,128)(2,1)}, u32[]{:S(2)}, u32[]{:S(2)}) collective-permute-start(bf16[384,768]{1,0:T(8,128)(2,1)} %add_convert_fusion.1), channel_id=1, source_target_pairs={{0,4},{4,0},{8,12},{12,8},{16,20},{20,16},{24,28},{28,24},{1,5},{5... | collective-permute-start | bytes 1769480 | tf_op jit(solution)/shard_map/ppermute | solution.py:619
  209.1 15.5 %collective-permute-start.24 = (bf16[64,768]{1,0:T(8,128)(2,1)S(1)}, bf16[64,768]{1,0:T(8,128)(2,1)S(1)}, u32[]{:S(2)}, u32[]{:S(2)}) collective-permute-start(bf16[64,768]{1,0:T(8,128)(2,1)S(1)} %add_convert_fusion.15), channel_id=1, source_target_pairs={{0,2},{1,3},{2,0},{3,1},{4,6},{5,7},{6,4},{7,5},{8,10},{9,11},{10,... | collective-permute-start | bytes 294920 | tf_op jit(solution)/shard_map/ppermute | solution.py:583
  211.0 18.2 %collective-permute-start.34 = (bf16[192,768]{1,0:T(8,128)(2,1)S(1)}, bf16[192,768]{1,0:T(8,128)(2,1)S(1)}, u32[]{:S(2)}, u32[]{:S(2)}) collective-permute-start(bf16[192,768]{1,0:T(8,128)(2,1)S(1)} %add_convert_fusion.4), channel_id=1, source_target_pairs={{0,8},{4,12},{8,0},{12,4},{16,24},{20,28},{24,16},{28,20},{1,9},{5... | collective-permute-start | bytes 884744 | tf_op jit(solution)/shard_map/ppermute | solution.py:619
  223.2 19.3 %collective-permute-start.29 = (bf16[384,768]{1,0:T(8,128)(2,1)S(1)}, bf16[384,768]{1,0:T(8,128)(2,1)S(1)}, u32[]{:S(2)}, u32[]{:S(2)}) collective-permute-start(bf16[384,768]{1,0:T(8,128)(2,1)S(1)} %add_convert_fusion), channel_id=1, source_target_pairs={{0,4},{4,0},{8,12},{12,8},{16,20},{20,16},{24,28},{28,24},{1,5},{5... | collective-permute-start | bytes 1769480 | tf_op jit(solution)/shard_map/ppermute | solution.py:619
  224.7 14.4 %collective-permute-start.25 = (bf16[64,768]{1,0:T(8,128)(2,1)S(1)}, bf16[64,768]{1,0:T(8,128)(2,1)S(1)}, u32[]{:S(2)}, u32[]{:S(2)}) collective-permute-start(bf16[64,768]{1,0:T(8,128)(2,1)S(1)} %add_convert_fusion.14), channel_id=1, source_target_pairs={{0,4},{4,0},{8,12},{12,8},{16,20},{20,16},{24,28},{28,24},{1,5},{5... | collective-permute-start | bytes 294920 | tf_op jit(solution)/shard_map/ppermute | solution.py:619
  229.0 11.5 %collective-permute-start.32 = (bf16[96,768]{1,0:T(8,128)(2,1)S(1)}, bf16[96,768]{1,0:T(8,128)(2,1)S(1)}, u32[]{:S(2)}, u32[]{:S(2)}) collective-permute-start(bf16[96,768]{1,0:T(8,128)(2,1)S(1)} %add_convert_fusion.10), channel_id=1, source_target_pairs={{0,16},{4,20},{8,24},{12,28},{16,0},{20,4},{24,8},{28,12},{1,17},{... | collective-permute-start | bytes 442376 | tf_op jit(solution)/shard_map/ppermute | solution.py:619
  230.3 12.2 %collective-permute-start.35 = (bf16[96,768]{1,0:T(8,128)(2,1)S(1)}, bf16[96,768]{1,0:T(8,128)(2,1)S(1)}, u32[]{:S(2)}, u32[]{:S(2)}) collective-permute-start(bf16[96,768]{1,0:T(8,128)(2,1)S(1)} %add_convert_fusion.9), channel_id=1, source_target_pairs={{0,16},{4,20},{8,24},{12,28},{16,0},{20,4},{24,8},{28,12},{1,17},{... | collective-permute-start | bytes 442376 | tf_op jit(solution)/shard_map/ppermute | solution.py:619
  243.6 16.2 %collective-permute-start.36 = (bf16[192,768]{1,0:T(8,128)(2,1)S(1)}, bf16[192,768]{1,0:T(8,128)(2,1)S(1)}, u32[]{:S(2)}, u32[]{:S(2)}) collective-permute-start(bf16[192,768]{1,0:T(8,128)(2,1)S(1)} %add_convert_fusion.3), channel_id=1, source_target_pairs={{0,8},{4,12},{8,0},{12,4},{16,24},{20,28},{24,16},{28,20},{1,9},{5... | collective-permute-start | bytes 884744 | tf_op jit(solution)/shard_map/ppermute | solution.py:619
  243.7 19.3 %collective-permute-start.37 = (bf16[192,768]{1,0:T(8,128)(2,1)S(1)}, bf16[192,768]{1,0:T(8,128)(2,1)S(1)}, u32[]{:S(2)}, u32[]{:S(2)}) collective-permute-start(bf16[192,768]{1,0:T(8,128)(2,1)S(1)} %pad_maximum_fusion.5), channel_id=1, source_target_pairs={{0,8},{4,12},{8,0},{12,4},{16,24},{20,28},{24,16},{28,20},{1,9},{5... | collective-permute-start | bytes 884744 | tf_op jit(solution)/shard_map/ppermute | solution.py:619
  247.0 12.9 %collective-permute-start.38 = (bf16[96,768]{1,0:T(8,128)(2,1)S(1)}, bf16[96,768]{1,0:T(8,128)(2,1)S(1)}, u32[]{:S(2)}, u32[]{:S(2)}) collective-permute-start(bf16[96,768]{1,0:T(8,128)(2,1)S(1)} %add_convert_fusion.8), channel_id=1, source_target_pairs={{0,16},{4,20},{8,24},{12,28},{16,0},{20,4},{24,8},{28,12},{1,17},{... | collective-permute-start | bytes 442376 | tf_op jit(solution)/shard_map/ppermute | solution.py:619
  247.6 35.4 %collective-permute-start.27 = (bf16[64,768]{1,0:T(8,128)(2,1)S(1)}, bf16[64,768]{1,0:T(8,128)(2,1)S(1)}, u32[]{:S(2)}, u32[]{:S(2)}) collective-permute-start(bf16[64,768]{1,0:T(8,128)(2,1)S(1)} %add_convert_fusion.12), channel_id=1, source_target_pairs={{0,16},{4,20},{8,24},{12,28},{16,0},{20,4},{24,8},{28,12},{1,17},{... | collective-permute-start | bytes 294920 | tf_op jit(solution)/shard_map/ppermute | solution.py:619
  266.3 16.5 %collective-permute-start.42 = (bf16[384,768]{1,0:T(8,128)(2,1)S(1)}, bf16[384,768]{1,0:T(8,128)(2,1)S(1)}, u32[]{:S(2)}, u32[]{:S(2)}) collective-permute-start(bf16[384,768]{1,0:T(8,128)(2,1)S(1)} %pad_maximum_fusion.2), channel_id=1, source_target_pairs={{0,4},{4,0},{8,12},{12,8},{16,20},{20,16},{24,28},{28,24},{1,5},{5... | collective-permute-start | bytes 1769480 | tf_op jit(solution)/shard_map/ppermute | solution.py:619
  277.4 13.8 %collective-permute-start.44 = (bf16[384,768]{1,0:T(8,128)(2,1)}, bf16[384,768]{1,0:T(8,128)(2,1)S(1)}, u32[]{:S(2)}, u32[]{:S(2)}) collective-permute-start(bf16[384,768]{1,0:T(8,128)(2,1)} %pad_maximum_fusion.3), channel_id=1, source_target_pairs={{0,4},{4,0},{8,12},{12,8},{16,20},{20,16},{24,28},{28,24},{1,5},{5... | collective-permute-start | bytes 1769480 | tf_op jit(solution)/shard_map/ppermute | solution.py:619
  291.3 12.7 %collective-permute-start.45 = (bf16[384,768]{1,0:T(8,128)(2,1)S(1)}, bf16[384,768]{1,0:T(8,128)(2,1)S(1)}, u32[]{:S(2)}, u32[]{:S(2)}) collective-permute-start(bf16[384,768]{1,0:T(8,128)(2,1)S(1)} %pad_maximum_fusion.4), channel_id=1, source_target_pairs={{0,4},{4,0},{8,12},{12,8},{16,20},{20,16},{24,28},{28,24},{1,5},{5... | collective-permute-start | bytes 1769480 | tf_op jit(solution)/shard_map/ppermute | solution.py:619
  (50 other events, 394.5 us)

commit v5 on v4

--- a/solution.py
+++ b/solution.py
@@ -356,19 +356,19 @@
     if first:
         flush(ge_low)
     ready(base_ref)
-    dno = mm(hid[1], we[...], NT)
-    outo = mm(act[1], wr[...], NN)
+    out_ref[...] = base_ref[...] + mm(act[0], wr[...], NN)
+    flush(out_ref)
+    dn = mm(hid[0], we[...], NT)
     if first:
-        dno_ref[...] = dno.astype(BF16)
-        outo_ref[...] = outo.astype(BF16)
-        dn_ref[...] = mm(hid[0], we[...], NT)
+        dn_ref[...] = dn
+        outo_ref[...] = mm(act[1], wr[...], NN).astype(BF16)
+        dno_ref[...] = mm(hid[1], we[...], NT).astype(BF16)
     else:
-        dno_ref[...] = (backo_ref[...].astype(F32) + dno).astype(BF16)
-        flush(dno_ref)
-        outo_ref[...] = (baseo_ref[...].astype(F32) + outo).astype(BF16)
+        dn_ref[...] = back_ref[...] + dn
+        flush(dn_ref)
+        outo_ref[...] = (baseo_ref[...].astype(F32) + mm(act[1], wr[...], NN)).astype(BF16)
         flush(outo_ref)
-        dn_ref[...] = back_ref[...] + mm(hid[0], we[...], NT)
-    out_ref[...] = base_ref[...] + mm(act[0], wr[...], NN)
+        dno_ref[...] = (backo_ref[...].astype(F32) + mm(hid[1], we[...], NT)).astype(BF16)
 
 
 def middle_kernel(
@@ -376,7 +376,7 @@
     wo, gm_ref, ratt_ref, raug_ref, g_ref, small_ref, total, rmix,
 ):
     cols = fq_ref.shape[1] // slots
-    ready(middle_ref, dnin_ref, cot_ref)
+    ready(middle_ref, dn_ref, dnin_ref, cot_ref)
     normal, scale = norm_parts(middle_ref[...])
     gy = dn_ref[...] + dnin_ref[...].astype(F32)
     cot = cot_ref[...].astype(F32)
@@ -796,7 +796,7 @@
             "saaaaaa" + ("h" if first else "v") + "v" + "v" * len(more),
             [meta, n2, w_in, n2_other, cot, w_out, cot_other, base, expand_line, *more], name,
             [pltpu.VMEM((2, rows_n, hidden_own), BF16)] * 2,
-            "vvvvhhhv" if first else "hvhhhhv", 48,
+            "vvvvhhhv" if first else "hhhvhhv", 48,
         )
 
     out1, dn1, out1_o, dn1_o, ge_top, ge_low, gr_cross, gb_cross = mlp(
@@ -807,12 +807,12 @@
     out2, dn2, out2_o, dn2_o, ge_own, gr_own, gb_own = mlp(
         False, out1, expand_weight, reduce_weight, [dn1, out1_o, dn1_o], "mlp_near"
     )
-    dn2_in = core_swap(dn2_o)
+    dn2_in = core_swap(after(dn2_o, top_in))
 
     g_middle, r_att, raug, g_states, small_two = call(
         functools.partial(middle_kernel, heads, slots, nctx),
         [full, low, shaped((heads * AUG, rows_n), BF16), state_shape, shaped((8, width))],
-        "svahavhhhh",
+        "shahavhhhh",
         [meta, dn2, dn2_in, middle, cot, params, mixed, den, fq, wo], "middle",
         [total, pltpu.VMEM((width, rows_n), BF16)], "hhhhv",
     )

time: 308 us -> 305 us (level)
  transfers between devices with their start and end apart: 50 -> 50, of which waited for: 27 -> 28; matrix products, arithmetic and copies ran while one was open for 13% -> 13% of each run, Pallas kernels for 26% -> 26%
where the time goes in v5:
time: 305 us; the launch traced here: 303 us
  waiting for transfers between devices  108 us (35%)
  Pallas kernels  93.5 us (31%)
  starting transfers between devices  57.7 us (19%)
  other arithmetic  31.2 us (10%)
  local copies, waits for them, and re-layouts  9.88 us (3%)
    pallas_call x15, Pallas kernels, call(): pl.pallas_call(run, out_shape=[pltpu.HBM(o.shape, o.dtype) if k == 'h' el...  93.5 us
    ppermute x21, waiting for transfers between devices, send(): return lax.ppermute(value, 'ctx', [(i, i ^ flip) for i in range(self.nctx)])  54.7 us
    ppermute x9, waiting for transfers between devices, cross_swap(): return lax.ppermute(a, 'fsdp', CROSS)  35.6 us
    ppermute x21, starting transfers between devices, send(): return lax.ppermute(value, 'ctx', [(i, i ^ flip) for i in range(self.nctx)])  22.6 us
    all_to_all x4, starting transfers between devices, exchange(): return lax.all_to_all(a, 'ctx', 0, 0, tiled=True)  19.9 us
    convert_element_type x12, other arithmetic, rows_sum(): return out.astype(BF16)  15.8 us
    ppermute x9, starting transfers between devices, cross_swap(): return lax.ppermute(a, 'fsdp', CROSS)  11.9 us
    all_to_all x4, waiting for transfers between devices, exchange(): return lax.all_to_all(a, 'ctx', 0, 0, tiled=True)  10.3 us
  transfers between devices with their start and end apart: 50, of which 28 were waited for; matrix products, arithmetic and copies ran while one was open for 13% of the time, Pallas kernels for 26%

profile of v5, /device:TPU:0, one launch (start us, length us, event | category | flops | bytes accessed | tf_op | source)
XLA Modules:
  0.0 303.4 jit_solution(15218401431435256709)
XLA Ops:
  0.6 3.0 collective-permute-start.4
  3.7 5.5 %concatenate.51 = bf16[3072]{0:T(1024)(128)(2,1)S(1)} concatenate(bf16[192]{0:T(256)(128)(2,1)} %param.22, bf16[192]{0:T(256)(128)(2,1)} %param.23, bf16[192]{0:T(256)(128)(2,1)} %param.30, bf16[192]{0:T(256)(128)(2,1)} %param.31, bf16[192]{0:T(256)(128)(2,1)} %param.29, bf16[192]{0:T(256)(128)(2,1)} %param.35, bf16[576]{0:T(1024)(128)(2,1)} %param.25, bf16[768]{0:T(1024)(128)(2,1)} %param.33, ...), dimensions={0} | concatenate | bytes 12288 | tf_op jit(solution)/shard_map/concatenate | solution.py:716
  13.3 12.6 %collective-permute-done = bf16[432,64]{1,0:T(8,128)(2,1)S(1)} collective-permute-done((bf16[432,64]{1,0:T(8,128)(2,1)S(1)}, bf16[432,64]{1,0:T(8,128)(2,1)S(1)}, u32[]{:S(2)}, u32[]{:S(2)}) %collective-permute-start) | collective-permute-done | bytes 55328 | tf_op jit(solution)/shard_map/ppermute | solution.py:583
  33.4 3.6 %project_near.1 = (bf16[512,768]{1,0:T(8,128)(2,1)}, bf16[1152,512]{1,0:T(8,128)(2,1)S(1)}) custom-call(s32[5]{0:T(128)S(1)} %stack.42.refs_0_, bf16[512,768]{1,0:T(8,128)(2,1)} %bitcast.33, f32[6,768]{1,0:T(8,128)S(1)} %reshape.102.refs_2_.refs_8_.refs_5_.refs_3_, bf16[576,768]{1,0:T(8,128)(2,1)S(1)} %bitcast.27, ...), custom_call_target="tpu_custom_call" | custom-call | flops 1 | bytes 1 | tf_op jit(solution)/shard_map/project_near/pallas_call | solution.py:132
  37.0 3.1 %project_far.1.refs_1_.refs_0_.refs_4_.refs_3_ = bf16[2304,512]{1,0:T(8,128)(2,1)S(1)} custom-call(s32[5]{0:T(128)S(1)} %stack.42.refs_0_, bf16[512,768]{1,0:T(8,128)(2,1)} %get-tuple-element.113.refs_1_.refs_6_.refs_2_, bf16[1152,512]{1,0:T(8,128)(2,1)S(1)} %get-tuple-element.114.refs_2_, bf16[576,768]{1,0:T(8,128)(2,1)S(1)} %collective-permute-done.4.refs_3_.refs_14_, ...), custom_call_target="tpu_custom_call" | custom-call | flops 1 | bytes 1 | tf_op jit(solution)/shard_map/project_far/pallas_call | solution.py:132
  40.2 6.3 %keys.1 = (bf16[1536,512]{1,0:T(8,128)(2,1)}, bf16[8,2,112,128]{3,2,1,0:T(8,128)(2,1)}) custom-call(s32[5]{0:T(128)S(1)} %stack.42.refs_0_, bf16[2304,512]{1,0:T(8,128)(2,1)S(1)} %project_far.1.refs_1_.refs_0_.refs_4_.refs_3_, bf16[12,64,64]{2,1,0:T(8,128)(2,1)S(1)} %bitcast.29), custom_call_target="tpu_custom_call" | custom-call | flops 1 | bytes 1 | tf_op jit(solution)/shard_map/keys/pallas_call | solution.py:132
  46.5 5.8 %all-to-all-start = ((bf16[8,2,112,128]{3,2,1,0:T(8,128)(2,1)}), bf16[8,2,112,128]{3,2,1,0:T(8,128)(2,1)}, u32[]{:S(2)}, u32[]{:S(2)}) async-start(bf16[8,2,112,128]{3,2,1,0:T(8,128)(2,1)} %get-tuple-element.115), calls=%async_computation | async-start | bytes 917504 | tf_op jit(solution)/shard_map/all_to_all | solution.py:687
  53.9 10.9 %collective-permute-done.6.refs_6_.refs_2_ = bf16[960,768]{1,0:T(8,128)(2,1)} collective-permute-done((bf16[960,768]{1,0:T(8,128)(2,1)}, bf16[960,768]{1,0:T(8,128)(2,1)}, u32[]{:S(2)}, u32[]{:S(2)}) %collective-permute-start.6) | collective-permute-done | bytes 1474592 | tf_op jit(solution)/shard_map/ppermute | solution.py:583
  68.4 5.8 %all-to-all-start.1 = ((bf16[8,2,112,128]{3,2,1,0:T(8,128)(2,1)}), bf16[8,2,112,128]{3,2,1,0:T(8,128)(2,1)}, u32[]{:S(2)}, u32[]{:S(2)}) async-start(bf16[8,2,112,128]{3,2,1,0:T(8,128)(2,1)} %scan.1), calls=%async_computation.1 | async-start | bytes 917504 | tf_op jit(solution)/shard_map/all_to_all | solution.py:687
  78.9 7.7 %all-to-all-done.1.refs_1_ = bf16[8,2,112,128]{3,2,1,0:T(8,128)(2,1)} async-done(((bf16[8,2,112,128]{3,2,1,0:T(8,128)(2,1)}), bf16[8,2,112,128]{3,2,1,0:T(8,128)(2,1)}, u32[]{:S(2)}, u32[]{:S(2)}) %all-to-all-start.1) | async-done | bytes 458784 | tf_op jit(solution)/shard_map/all_to_all | solution.py:687
  86.5 6.1 %attend.1 = (bf16[768,512]{1,0:T(8,128)(2,1)}, f32[96,512]{1,0:T(8,128)}, f32[512,768]{1,0:T(8,128)}, bf16[512,768]{1,0:T(8,128)(2,1)S(1)}, bf16[768,768]{1,0:T(8,128)(2,1)}) custom-call(s32[5]{0:T(128)S(1)} %copy-done.9, bf16[8,2,112,128]{3,2,1,0:T(8,128)(2,1)} %all-to-all-done.1.refs_1_, bf16[1536,512]{1,0:T(8,128)(2,1)} %queries.1.refs_2_.refs_8_.refs_3_, ...), custom_call_target="tpu_custom_call" | custom-call | flops 1 | bytes 1 | tf_op jit(solution)/shard_map/attend/pallas_call | solution.py:132
  95.0 14.3 %mlp_far.1 = (f32[512,768]{1,0:T(8,128)}, f32[512,768]{1,0:T(8,128)}, bf16[512,768]{1,0:T(8,128)(2,1)S(1)}, bf16[512,768]{1,0:T(8,128)(2,1)S(1)}, bf16[384,768]{...) custom-call(s32[5]{0:T(128)S(1)} %copy-done.9, ...), custom_call_target="tpu_custom_call" | custom-call | flops 1 | bytes 1 | tf_op jit(solution)/shard_map/mlp_far/pallas_call | solution.py:132
  109.9 14.7 %mlp_near.1 = (f32[512,768]{1,0:T(8,128)}, f32[512,768]{1,0:T(8,128)}, bf16[512,768]{1,0:T(8,128)(2,1)}, bf16[512,768]{1,0:T(8,128)(2,1)S(1)}, bf16[768,768]{1,0...) custom-call(s32[5]{0:T(128)S(1)} %copy-done.9, bf16[512,768]{1,0:T(8,128)(2,1)S(1)} %get-tuple-element.120.refs_1_, ...), custom_call_target="tpu_custom_call" | custom-call | flops 1 | bytes 1 | tf_op jit(solution)/shard_map/mlp_near/pallas_call | solution.py:132
  127.3 7.2 %middle.1 = (f32[512,768]{1,0:T(8,128)}, bf16[512,768]{1,0:T(8,128)(2,1)}, bf16[960,512]{1,0:T(8,128)(2,1)}, bf16[8,2,112,128]{3,2,1,0:T(8,128)(2,1)}, f32[8,768]{1,0:T(8,128)S(1)}) custom-call(s32[5]{0:T(128)S(1)} %copy-done.9, f32[512,768]{1,0:T(8,128)} %get-tuple-element.127.refs_1_, bf16[512,768]{1,0:T(8,128)(2,1)S(1)} %collective-permute-done.13.refs_2_, ...), custom_call_target="tpu_custom_call" | custom-call | flops 1 | bytes 1 | tf_op jit(solution)/shard_map/middle/pallas_call | solution.py:132
  134.5 4.1 %all-to-all-start.2 = ((bf16[8,2,112,128]{3,2,1,0:T(8,128)(2,1)}), bf16[8,2,112,128]{3,2,1,0:T(8,128)(2,1)}, u32[]{:S(2)}, u32[]{:S(2)}) async-start(bf16[8,2,112,128]{3,2,1,0:T(8,128)(2,1)} %get-tuple-element.134), calls=%async_computation.2 | async-start | bytes 917504 | tf_op jit(solution)/shard_map/all_to_all | solution.py:687
  142.3 7.5 %query_back.1 = (bf16[768,512]{1,0:T(8,128)(2,1)}, f32[12,64,64]{2,1,0:T(8,128)}, bf16[192,768]{1,0:T(8,128)(2,1)}, bf16[192,768]{1,0:T(8,128)(2,1)}, bf16[192,7...) custom-call(s32[5]{0:T(128)S(1)} %copy-done.9, bf16[8,2,112,128]{3,2,1,0:T(8,128)(2,1)} %all-to-all-done.1.refs_1_, ...), custom_call_target="tpu_custom_call" | custom-call | flops 1 | bytes 1 | tf_op jit(solution)/shard_map/query_back/pallas_call | solution.py:132
  154.2 4.1 %all-to-all-start.3 = ((bf16[8,2,112,128]{3,2,1,0:T(8,128)(2,1)}), bf16[8,2,112,128]{3,2,1,0:T(8,128)(2,1)}, u32[]{:S(2)}, u32[]{:S(2)}) async-start(bf16[8,2,112,128]{3,2,1,0:T(8,128)(2,1)} %scan_back.1), calls=%async_computation.3 | async-start | bytes 917504 | tf_op jit(solution)/shard_map/all_to_all | solution.py:687
  162.6 6.4 %collective-permute-done.15 = bf16[768,768]{1,0:T(8,128)(2,1)} collective-permute-done((bf16[768,768]{1,0:T(8,128)(2,1)}, bf16[768,768]{1,0:T(8,128)(2,1)}, u32[]{:S(2)}, u32[]{:S(2)}) %collective-permute-start.15) | collective-permute-done | bytes 1179680 | tf_op jit(solution)/shard_map/ppermute | solution.py:583
  171.2 8.6 %key_back.1 = (bf16[2304,512]{1,0:T(8,128)(2,1)}, f32[12,64,64]{2,1,0:T(8,128)}, bf16[576,768]{1,0:T(8,128)(2,1)}, bf16[576,768]{1,0:T(8,128)(2,1)}) custom-call(s32[5]{0:T(128)S(1)} %copy-done.9, bf16[8,2,112,128]{3,2,1,0:T(8,128)(2,1)} %all-to-all-done.3.refs_1_, bf16[1536,512]{1,0:T(8,128)(2,1)} %get-tuple-element.149.refs_2_, ...), custom_call_target="tpu_custom_call" | custom-call | flops 1 | bytes 1 | tf_op jit(solution)/shard_map/key_back/pallas_call | solution.py:132
  184.7 5.3 %project_grad.1 = (bf16[768,768]{1,0:T(8,128)(2,1)}, bf16[768,768]{1,0:T(8,128)(2,1)}) custom-call(s32[5]{0:T(128)S(1)} %copy-done.9, bf16[2304,512]{1,0:T(8,128)(2,1)} %get-tuple-element.150.refs_1_, bf16[512,768]{1,0:T(8,128)(2,1)} %get-tuple-element.113.refs_1_.refs_6_.refs_2_, bf16[576,768]{1,0:T(8,128)(2,1)S(1)} %collective-permute-done.17.refs_3_, ...), custom_call_target="tpu_custom_call" | custom-call | flops 1 | bytes 1 | tf_op jit(solution)/shard_map/project_grad/pallas_call | solution.py:132
  195.3 9.4 %input.1 = (f32[512,768]{1,0:T(8,128)}, f32[512,768]{1,0:T(8,128)}, bf16[64,768]{1,0:T(8,128)(2,1)S(1)}, bf16[64,768]{1,0:T(8,128)(2,1)S(1)}, bf16[64,768]{1,0:T(8,128)(2,1)S(1)}, /*index=5*/bf16[64,768]{1,0:T(8,128)(2,1)S(1)}) custom-call(s32[5]{0:T(128)S(1)} %copy-done.9, bf16[2304,512]{1,0:T(8,128)(2,1)} %get-tuple-element.150.refs_1_, ...), custom_call_target="tpu_custom_call" | custom-call | flops 1 | bytes 1 | tf_op jit(solution)/shard_map/input/pallas_call | solution.py:132
  209.6 5.2 %collective-permute-done.30 = bf16[192,768]{1,0:T(8,128)(2,1)S(1)} collective-permute-done((bf16[192,768]{1,0:T(8,128)(2,1)S(1)}, bf16[192,768]{1,0:T(8,128)(2,1)S(1)}, u32[]{:S(2)}, u32[]{:S(2)}) %collective-permute-start.30) | collective-permute-done | bytes 294944 | tf_op jit(solution)/shard_map/ppermute | solution.py:619
  216.2 3.0 collective-permute-done.28
  227.3 2.9 collective-permute-start.35
  230.2 6.2 %collective-permute-done.25 = bf16[64,768]{1,0:T(8,128)(2,1)S(1)} collective-permute-done((bf16[64,768]{1,0:T(8,128)(2,1)S(1)}, bf16[64,768]{1,0:T(8,128)(2,1)S(1)}, u32[]{:S(2)}, u32[]{:S(2)}) %collective-permute-start.25) | collective-permute-done | bytes 98336 | tf_op jit(solution)/shard_map/ppermute | solution.py:619
  247.0 9.8 %collective-permute-done.38 = bf16[96,768]{1,0:T(8,128)(2,1)S(1)} collective-permute-done((bf16[96,768]{1,0:T(8,128)(2,1)S(1)}, bf16[96,768]{1,0:T(8,128)(2,1)S(1)}, u32[]{:S(2)}, u32[]{:S(2)}) %collective-permute-start.38) | collective-permute-done | bytes 147488 | tf_op jit(solution)/shard_map/ppermute | solution.py:619
  256.8 3.2 %collective-permute-done.37 = bf16[192,768]{1,0:T(8,128)(2,1)S(1)} collective-permute-done((bf16[192,768]{1,0:T(8,128)(2,1)S(1)}, bf16[192,768]{1,0:T(8,128)(2,1)S(1)}, u32[]{:S(2)}, u32[]{:S(2)}) %collective-permute-start.37) | collective-permute-done | bytes 294944 | tf_op jit(solution)/shard_map/ppermute | solution.py:619
  264.4 3.9 %collective-permute-done.39 = bf16[96,768]{1,0:T(8,128)(2,1)S(1)} collective-permute-done((bf16[96,768]{1,0:T(8,128)(2,1)S(1)}, bf16[96,768]{1,0:T(8,128)(2,1)S(1)}, u32[]{:S(2)}, u32[]{:S(2)}) %collective-permute-start.39) | collective-permute-done | bytes 147488 | tf_op jit(solution)/shard_map/ppermute | solution.py:619
  268.3 3.0 collective-permute-done.40
  275.0 4.8 %collective-permute-done.41 = bf16[96,768]{1,0:T(8,128)(2,1)S(1)} collective-permute-done((bf16[96,768]{1,0:T(8,128)(2,1)S(1)}, bf16[96,768]{1,0:T(8,128)(2,1)S(1)}, u32[]{:S(2)}, u32[]{:S(2)}) %collective-permute-start.41) | collective-permute-done | bytes 147488 | tf_op jit(solution)/shard_map/ppermute | solution.py:619
  282.2 5.2 %collective-permute-done.43 = bf16[192,768]{1,0:T(8,128)(2,1)S(1)} collective-permute-done((bf16[192,768]{1,0:T(8,128)(2,1)S(1)}, bf16[192,768]{1,0:T(8,128)(2,1)S(1)}, u32[]{:S(2)}, u32[]{:S(2)}) %collective-permute-start.43) | collective-permute-done | bytes 294944 | tf_op jit(solution)/shard_map/ppermute | solution.py:619
  292.7 8.3 %collective-permute-done.45 = bf16[384,768]{1,0:T(8,128)(2,1)S(1)} collective-permute-done((bf16[384,768]{1,0:T(8,128)(2,1)S(1)}, bf16[384,768]{1,0:T(8,128)(2,1)S(1)}, u32[]{:S(2)}, u32[]{:S(2)}) %collective-permute-start.45) | collective-permute-done | bytes 589856 | tf_op jit(solution)/shard_map/ppermute | solution.py:619
  (212 shorter events, 93.1 us)
Async XLA Ops:
  0.6 28.7 %collective-permute-start.4 = (bf16[576,768]{1,0:T(8,128)(2,1)}, bf16[576,768]{1,0:T(8,128)(2,1)S(1)}, u32[]{:S(2)}, u32[]{:S(2)}) collective-permute-start(bf16[576,768]{1,0:T(8,128)(2,1)} %bitcast.25), channel_id=1, source_target_pairs={{0,2},{1,3},{2,0},{3,1},{4,6},{5,7},{6,4},{7,5},{8,10},{9,11},{10,... | collective-permute-start | bytes 2654216 | tf_op jit(solution)/shard_map/ppermute | solution.py:583
  10.1 15.8 %collective-permute-start = (bf16[432,64]{1,0:T(8,128)(2,1)S(1)}, bf16[432,64]{1,0:T(8,128)(2,1)S(1)}, u32[]{:S(2)}, u32[]{:S(2)}) collective-permute-start(bf16[432,64]{1,0:T(8,128)(2,1)S(1)} %pad_maximum_fusion.10), channel_id=1, source_target_pairs={{0,2},{1,3},{2,0},{3,1},{4,6},{5,7},{6,4},{7,5},{8,10},{9,11},{10,... | collective-permute-start | bytes 165896 | tf_op jit(solution)/shard_map/ppermute | solution.py:583
  10.2 17.7 %collective-permute-start.2 = (bf16[432,64]{1,0:T(8,128)(2,1)S(1)}, bf16[432,64]{1,0:T(8,128)(2,1)S(1)}, u32[]{:S(2)}, u32[]{:S(2)}) collective-permute-start(bf16[432,64]{1,0:T(8,128)(2,1)S(1)} %pad_maximum_fusion.10), channel_id=1, source_target_pairs={{0,1},{1,0},{2,3},{3,2},{4,5},{5,4},{6,7},{7,6},{8,9},{9,8},{10,11... | collective-permute-start | bytes 165896 | tf_op jit(solution)/shard_map/ppermute | solution.py:579
  10.2 23.1 %collective-permute-start.3 = (bf16[576,768]{1,0:T(8,128)(2,1)}, bf16[576,768]{1,0:T(8,128)(2,1)S(1)}, u32[]{:S(2)}, u32[]{:S(2)}) collective-permute-start(bf16[576,768]{1,0:T(8,128)(2,1)} %bitcast.26), channel_id=1, source_target_pairs={{0,1},{1,0},{2,3},{3,2},{4,5},{5,4},{6,7},{7,6},{8,9},{9,8},{10,11... | collective-permute-start | bytes 2654216 | tf_op jit(solution)/shard_map/ppermute | solution.py:579
  30.2 34.5 %collective-permute-start.6 = (bf16[960,768]{1,0:T(8,128)(2,1)}, bf16[960,768]{1,0:T(8,128)(2,1)}, u32[]{:S(2)}, u32[]{:S(2)}) collective-permute-start(bf16[960,768]{1,0:T(8,128)(2,1)} %pad_maximum_fusion), channel_id=1, source_target_pairs={{0,2},{1,3},{2,0},{3,1},{4,6},{5,7},{6,4},{7,5},{8,10},{9,11},{10,... | collective-permute-start | bytes 4423688 | tf_op jit(solution)/shard_map/ppermute | solution.py:583
  46.5 20.0 %all-to-all-start = ((bf16[8,2,112,128]{3,2,1,0:T(8,128)(2,1)}), bf16[8,2,112,128]{3,2,1,0:T(8,128)(2,1)}, u32[]{:S(2)}, u32[]{:S(2)}) async-start(bf16[8,2,112,128]{3,2,1,0:T(8,128)(2,1)} %get-tuple-element.115), calls=%async_computation | async-start | bytes 917504 | tf_op jit(solution)/shard_map/all_to_all | solution.py:687
  52.3 26.5 %collective-permute-start.7 = (bf16[192,768]{1,0:T(8,128)(2,1)}, bf16[192,768]{1,0:T(8,128)(2,1)}, u32[]{:S(2)}, u32[]{:S(2)}) collective-permute-start(bf16[192,768]{1,0:T(8,128)(2,1)} %refs_4_.1), channel_id=1, source_target_pairs={{0,1},{1,0},{2,3},{3,2},{4,5},{5,4},{6,7},{7,6},{8,9},{9,8},{10,11... | collective-permute-start | bytes 884744 | tf_op jit(solution)/shard_map/ppermute | solution.py:579
  52.3 40.6 %collective-permute-start.10 = (bf16[512,768]{1,0:T(8,128)(2,1)}, bf16[512,768]{1,0:T(8,128)(2,1)}, u32[]{:S(2)}, u32[]{:S(2)}) collective-permute-start(bf16[512,768]{1,0:T(8,128)(2,1)} %bitcast.13.refs_4_), channel_id=1, source_target_pairs={{0,1},{1,0},{2,3},{3,2},{4,5},{5,4},{6,7},{7,6},{8,9},{9,8},{10,11... | collective-permute-start | bytes 2359304 | tf_op jit(solution)/shard_map/ppermute | solution.py:579
  64.8 28.1 %collective-permute-start.11 = (bf16[768,768]{1,0:T(8,128)(2,1)}, bf16[768,768]{1,0:T(8,128)(2,1)}, u32[]{:S(2)}, u32[]{:S(2)}) collective-permute-start(bf16[768,768]{1,0:T(8,128)(2,1)} %refs_5_.1), channel_id=1, source_target_pairs={{0,2},{1,3},{2,0},{3,1},{4,6},{5,7},{6,4},{7,5},{8,10},{9,11},{10,... | collective-permute-start | bytes 3538952 | tf_op jit(solution)/shard_map/ppermute | solution.py:583
  68.4 18.1 %all-to-all-start.1 = ((bf16[8,2,112,128]{3,2,1,0:T(8,128)(2,1)}), bf16[8,2,112,128]{3,2,1,0:T(8,128)(2,1)}, u32[]{:S(2)}, u32[]{:S(2)}) async-start(bf16[8,2,112,128]{3,2,1,0:T(8,128)(2,1)} %scan.1), calls=%async_computation.1 | async-start | bytes 917504 | tf_op jit(solution)/shard_map/all_to_all | solution.py:687
  109.3 15.6 %collective-permute-start.12 = (bf16[384,768]{1,0:T(8,128)(2,1)}, bf16[384,768]{1,0:T(8,128)(2,1)S(1)}, u32[]{:S(2)}, u32[]{:S(2)}) collective-permute-start(bf16[384,768]{1,0:T(8,128)(2,1)} %get-tuple-element.129), channel_id=1, source_target_pairs={{0,2},{1,3},{2,0},{3,1},{4,6},{5,7},{6,4},{7,5},{8,10},{9,11},{10,... | collective-permute-start | bytes 1769480 | tf_op jit(solution)/shard_map/ppermute | solution.py:583
  125.0 16.1 %collective-permute-start.14 = (bf16[384,768]{1,0:T(8,128)(2,1)}, bf16[384,768]{1,0:T(8,128)(2,1)}, u32[]{:S(2)}, u32[]{:S(2)}) collective-permute-start(bf16[384,768]{1,0:T(8,128)(2,1)} %get-tuple-element.139), channel_id=1, source_target_pairs={{0,2},{1,3},{2,0},{3,1},{4,6},{5,7},{6,4},{7,5},{8,10},{9,11},{10,... | collective-permute-start | bytes 1769480 | tf_op jit(solution)/shard_map/ppermute | solution.py:583
  134.5 17.8 %all-to-all-start.2 = ((bf16[8,2,112,128]{3,2,1,0:T(8,128)(2,1)}), bf16[8,2,112,128]{3,2,1,0:T(8,128)(2,1)}, u32[]{:S(2)}, u32[]{:S(2)}) async-start(bf16[8,2,112,128]{3,2,1,0:T(8,128)(2,1)} %get-tuple-element.134), calls=%async_computation.2 | async-start | bytes 917504 | tf_op jit(solution)/shard_map/all_to_all | solution.py:687
  141.0 27.9 %collective-permute-start.15 = (bf16[768,768]{1,0:T(8,128)(2,1)}, bf16[768,768]{1,0:T(8,128)(2,1)}, u32[]{:S(2)}, u32[]{:S(2)}) collective-permute-start(bf16[768,768]{1,0:T(8,128)(2,1)} %get-tuple-element.146), channel_id=1, source_target_pairs={{0,2},{1,3},{2,0},{3,1},{4,6},{5,7},{6,4},{7,5},{8,10},{9,11},{10,... | collective-permute-start | bytes 3538952 | tf_op jit(solution)/shard_map/ppermute | solution.py:583
  154.2 17.1 %all-to-all-start.3 = ((bf16[8,2,112,128]{3,2,1,0:T(8,128)(2,1)}), bf16[8,2,112,128]{3,2,1,0:T(8,128)(2,1)}, u32[]{:S(2)}, u32[]{:S(2)}) async-start(bf16[8,2,112,128]{3,2,1,0:T(8,128)(2,1)} %scan_back.1), calls=%async_computation.3 | async-start | bytes 917504 | tf_op jit(solution)/shard_map/all_to_all | solution.py:687
  160.7 19.2 %collective-permute-start.16 = (bf16[384,768]{1,0:T(8,128)(2,1)}, bf16[384,768]{1,0:T(8,128)(2,1)}, u32[]{:S(2)}, u32[]{:S(2)}) collective-permute-start(bf16[384,768]{1,0:T(8,128)(2,1)} %add_convert_fusion.2), channel_id=1, source_target_pairs={{0,4},{4,0},{8,12},{12,8},{16,20},{20,16},{24,28},{28,24},{1,5},{5... | collective-permute-start | bytes 1769480 | tf_op jit(solution)/shard_map/ppermute | solution.py:619
  181.0 14.3 %collective-permute-start.21 = (bf16[512,768]{1,0:T(8,128)(2,1)}, bf16[512,768]{1,0:T(8,128)(2,1)S(1)}, u32[]{:S(2)}, u32[]{:S(2)}) collective-permute-start(bf16[512,768]{1,0:T(8,128)(2,1)} %get-tuple-element.167), channel_id=1, source_target_pairs={{0,1},{1,0},{2,3},{3,2},{4,5},{5,4},{6,7},{7,6},{8,9},{9,8},{10,11... | collective-permute-start | bytes 2359304 | tf_op jit(solution)/shard_map/ppermute | solution.py:579
  190.0 29.2 %collective-permute-start.28 = (bf16[768,768]{1,0:T(8,128)(2,1)}, bf16[768,768]{1,0:T(8,128)(2,1)}, u32[]{:S(2)}, u32[]{:S(2)}) collective-permute-start(bf16[768,768]{1,0:T(8,128)(2,1)} %get-tuple-element.181), channel_id=1, source_target_pairs={{0,2},{1,3},{2,0},{3,1},{4,6},{5,7},{6,4},{7,5},{8,10},{9,11},{10,... | collective-permute-start | bytes 3538952 | tf_op jit(solution)/shard_map/ppermute | solution.py:583
  191.3 15.7 %collective-permute-start.33 = (bf16[384,768]{1,0:T(8,128)(2,1)}, bf16[384,768]{1,0:T(8,128)(2,1)}, u32[]{:S(2)}, u32[]{:S(2)}) collective-permute-start(bf16[384,768]{1,0:T(8,128)(2,1)} %add_convert_fusion.1), channel_id=1, source_target_pairs={{0,4},{4,0},{8,12},{12,8},{16,20},{20,16},{24,28},{28,24},{1,5},{5... | collective-permute-start | bytes 1769480 | tf_op jit(solution)/shard_map/ppermute | solution.py:619
  206.1 15.8 %collective-permute-start.24 = (bf16[64,768]{1,0:T(8,128)(2,1)S(1)}, bf16[64,768]{1,0:T(8,128)(2,1)S(1)}, u32[]{:S(2)}, u32[]{:S(2)}) collective-permute-start(bf16[64,768]{1,0:T(8,128)(2,1)S(1)} %add_convert_fusion.15), channel_id=1, source_target_pairs={{0,2},{1,3},{2,0},{3,1},{4,6},{5,7},{6,4},{7,5},{8,10},{9,11},{10,... | collective-permute-start | bytes 294920 | tf_op jit(solution)/shard_map/ppermute | solution.py:583
  208.2 17.9 %collective-permute-start.34 = (bf16[192,768]{1,0:T(8,128)(2,1)S(1)}, bf16[192,768]{1,0:T(8,128)(2,1)S(1)}, u32[]{:S(2)}, u32[]{:S(2)}) collective-permute-start(bf16[192,768]{1,0:T(8,128)(2,1)S(1)} %add_convert_fusion.4), channel_id=1, source_target_pairs={{0,8},{4,12},{8,0},{12,4},{16,24},{20,28},{24,16},{28,20},{1,9},{5... | collective-permute-start | bytes 884744 | tf_op jit(solution)/shard_map/ppermute | solution.py:619
  220.4 19.1 %collective-permute-start.29 = (bf16[384,768]{1,0:T(8,128)(2,1)S(1)}, bf16[384,768]{1,0:T(8,128)(2,1)S(1)}, u32[]{:S(2)}, u32[]{:S(2)}) collective-permute-start(bf16[384,768]{1,0:T(8,128)(2,1)S(1)} %add_convert_fusion), channel_id=1, source_target_pairs={{0,4},{4,0},{8,12},{12,8},{16,20},{20,16},{24,28},{28,24},{1,5},{5... | collective-permute-start | bytes 1769480 | tf_op jit(solution)/shard_map/ppermute | solution.py:619
  222.0 14.4 %collective-permute-start.25 = (bf16[64,768]{1,0:T(8,128)(2,1)S(1)}, bf16[64,768]{1,0:T(8,128)(2,1)S(1)}, u32[]{:S(2)}, u32[]{:S(2)}) collective-permute-start(bf16[64,768]{1,0:T(8,128)(2,1)S(1)} %add_convert_fusion.14), channel_id=1, source_target_pairs={{0,4},{4,0},{8,12},{12,8},{16,20},{20,16},{24,28},{28,24},{1,5},{5... | collective-permute-start | bytes 294920 | tf_op jit(solution)/shard_map/ppermute | solution.py:619
  226.0 11.5 %collective-permute-start.32 = (bf16[96,768]{1,0:T(8,128)(2,1)S(1)}, bf16[96,768]{1,0:T(8,128)(2,1)S(1)}, u32[]{:S(2)}, u32[]{:S(2)}) collective-permute-start(bf16[96,768]{1,0:T(8,128)(2,1)S(1)} %add_convert_fusion.10), channel_id=1, source_target_pairs={{0,16},{4,20},{8,24},{12,28},{16,0},{20,4},{24,8},{28,12},{1,17},{... | collective-permute-start | bytes 442376 | tf_op jit(solution)/shard_map/ppermute | solution.py:619
  227.3 12.2 %collective-permute-start.35 = (bf16[96,768]{1,0:T(8,128)(2,1)S(1)}, bf16[96,768]{1,0:T(8,128)(2,1)S(1)}, u32[]{:S(2)}, u32[]{:S(2)}) collective-permute-start(bf16[96,768]{1,0:T(8,128)(2,1)S(1)} %add_convert_fusion.9), channel_id=1, source_target_pairs={{0,16},{4,20},{8,24},{12,28},{16,0},{20,4},{24,8},{28,12},{1,17},{... | collective-permute-start | bytes 442376 | tf_op jit(solution)/shard_map/ppermute | solution.py:619
  240.6 16.2 %collective-permute-start.36 = (bf16[192,768]{1,0:T(8,128)(2,1)S(1)}, bf16[192,768]{1,0:T(8,128)(2,1)S(1)}, u32[]{:S(2)}, u32[]{:S(2)}) collective-permute-start(bf16[192,768]{1,0:T(8,128)(2,1)S(1)} %add_convert_fusion.3), channel_id=1, source_target_pairs={{0,8},{4,12},{8,0},{12,4},{16,24},{20,28},{24,16},{28,20},{1,9},{5... | collective-permute-start | bytes 884744 | tf_op jit(solution)/shard_map/ppermute | solution.py:619
  240.7 19.3 %collective-permute-start.37 = (bf16[192,768]{1,0:T(8,128)(2,1)S(1)}, bf16[192,768]{1,0:T(8,128)(2,1)S(1)}, u32[]{:S(2)}, u32[]{:S(2)}) collective-permute-start(bf16[192,768]{1,0:T(8,128)(2,1)S(1)} %pad_maximum_fusion.5), channel_id=1, source_target_pairs={{0,8},{4,12},{8,0},{12,4},{16,24},{20,28},{24,16},{28,20},{1,9},{5... | collective-permute-start | bytes 884744 | tf_op jit(solution)/shard_map/ppermute | solution.py:619
  243.9 12.9 %collective-permute-start.38 = (bf16[96,768]{1,0:T(8,128)(2,1)S(1)}, bf16[96,768]{1,0:T(8,128)(2,1)S(1)}, u32[]{:S(2)}, u32[]{:S(2)}) collective-permute-start(bf16[96,768]{1,0:T(8,128)(2,1)S(1)} %add_convert_fusion.8), channel_id=1, source_target_pairs={{0,16},{4,20},{8,24},{12,28},{16,0},{20,4},{24,8},{28,12},{1,17},{... | collective-permute-start | bytes 442376 | tf_op jit(solution)/shard_map/ppermute | solution.py:619
  244.6 35.4 %collective-permute-start.27 = (bf16[64,768]{1,0:T(8,128)(2,1)S(1)}, bf16[64,768]{1,0:T(8,128)(2,1)S(1)}, u32[]{:S(2)}, u32[]{:S(2)}) collective-permute-start(bf16[64,768]{1,0:T(8,128)(2,1)S(1)} %add_convert_fusion.12), channel_id=1, source_target_pairs={{0,16},{4,20},{8,24},{12,28},{16,0},{20,4},{24,8},{28,12},{1,17},{... | collective-permute-start | bytes 294920 | tf_op jit(solution)/shard_map/ppermute | solution.py:619
  263.3 16.5 %collective-permute-start.42 = (bf16[384,768]{1,0:T(8,128)(2,1)S(1)}, bf16[384,768]{1,0:T(8,128)(2,1)S(1)}, u32[]{:S(2)}, u32[]{:S(2)}) collective-permute-start(bf16[384,768]{1,0:T(8,128)(2,1)S(1)} %pad_maximum_fusion.2), channel_id=1, source_target_pairs={{0,4},{4,0},{8,12},{12,8},{16,20},{20,16},{24,28},{28,24},{1,5},{5... | collective-permute-start | bytes 1769480 | tf_op jit(solution)/shard_map/ppermute | solution.py:619
  274.3 13.8 %collective-permute-start.44 = (bf16[384,768]{1,0:T(8,128)(2,1)}, bf16[384,768]{1,0:T(8,128)(2,1)S(1)}, u32[]{:S(2)}, u32[]{:S(2)}) collective-permute-start(bf16[384,768]{1,0:T(8,128)(2,1)} %pad_maximum_fusion.3), channel_id=1, source_target_pairs={{0,4},{4,0},{8,12},{12,8},{16,20},{20,16},{24,28},{28,24},{1,5},{5... | collective-permute-start | bytes 1769480 | tf_op jit(solution)/shard_map/ppermute | solution.py:619
  288.2 12.7 %collective-permute-start.45 = (bf16[384,768]{1,0:T(8,128)(2,1)S(1)}, bf16[384,768]{1,0:T(8,128)(2,1)S(1)}, u32[]{:S(2)}, u32[]{:S(2)}) collective-permute-start(bf16[384,768]{1,0:T(8,128)(2,1)S(1)} %pad_maximum_fusion.4), channel_id=1, source_target_pairs={{0,4},{4,0},{8,12},{12,8},{16,20},{20,16},{24,28},{28,24},{1,5},{5... | collective-permute-start | bytes 1769480 | tf_op jit(solution)/shard_map/ppermute | solution.py:619
  (48 other events, 378.3 us)

commit v6 on v5

--- a/solution.py
+++ b/solution.py
@@ -12,7 +12,7 @@
 BF16 = jnp.bfloat16
 AUG = 80
 KEEP = 72
-UNROLL = 3
+UNROLL = 4
 NN = (((1,), (0,)), ((), ()))
 NT = (((1,), (1,)), ((), ()))
 TN = (((0,), (0,)), ((), ()))
@@ -885,7 +885,6 @@
     e_got = sum_e.spread(0)
     sum_r.join(sum_p.sent)
     r_got = sum_r.spread(1)
-    sum_p.hold(r_got)
     sum_p.deep(3)
     sum_r.join(sum_p.cur)
     r_got = sum_r.spread(0)

time: 305 us -> 305 us (level)
  transfers between devices with their start and end apart: 50 -> 50, of which waited for: 28 -> 29; matrix products, arithmetic and copies ran while one was open for 13% -> 13% of each run, Pallas kernels for 26% -> 26%
where the time goes in v6:
time: 305 us; the launch traced here: 303 us
  waiting for transfers between devices  107 us (35%)
  Pallas kernels  92.4 us (30%)
  starting transfers between devices  59.6 us (20%)
  other arithmetic  31.2 us (10%)
  local copies, waits for them, and re-layouts  9.88 us (3%)
    pallas_call x15, Pallas kernels, call(): pl.pallas_call(run, out_shape=[pltpu.HBM(o.shape, o.dtype) if k == 'h' el...  92.4 us
    ppermute x21, waiting for transfers between devices, send(): return lax.ppermute(value, 'ctx', [(i, i ^ flip) for i in range(self.nctx)])  53.4 us
    ppermute x9, waiting for transfers between devices, cross_swap(): return lax.ppermute(a, 'fsdp', CROSS)  36.1 us
    ppermute x21, starting transfers between devices, send(): return lax.ppermute(value, 'ctx', [(i, i ^ flip) for i in range(self.nctx)])  24.5 us
    all_to_all x4, starting transfers between devices, exchange(): return lax.all_to_all(a, 'ctx', 0, 0, tiled=True)  19.9 us
    convert_element_type x12, other arithmetic, rows_sum(): return out.astype(BF16)  15.8 us
    ppermute x9, starting transfers between devices, cross_swap(): return lax.ppermute(a, 'fsdp', CROSS)  11.9 us
    all_to_all x4, waiting for transfers between devices, exchange(): return lax.all_to_all(a, 'ctx', 0, 0, tiled=True)  10.5 us
  transfers between devices with their start and end apart: 50, of which 29 were waited for; matrix products, arithmetic and copies ran while one was open for 13% of the time, Pallas kernels for 26%

profile of v6, /device:TPU:0, one launch (start us, length us, event | category | flops | bytes accessed | tf_op | source)
XLA Modules:
  0.0 303.4 jit_solution(1833614297398936710)
XLA Ops:
  0.6 3.0 collective-permute-start.4
  3.7 5.5 %concatenate.51 = bf16[3072]{0:T(1024)(128)(2,1)S(1)} concatenate(bf16[192]{0:T(256)(128)(2,1)} %param.22, bf16[192]{0:T(256)(128)(2,1)} %param.23, bf16[192]{0:T(256)(128)(2,1)} %param.30, bf16[192]{0:T(256)(128)(2,1)} %param.31, bf16[192]{0:T(256)(128)(2,1)} %param.29, bf16[192]{0:T(256)(128)(2,1)} %param.35, bf16[576]{0:T(1024)(128)(2,1)} %param.25, bf16[768]{0:T(1024)(128)(2,1)} %param.33, ...), dimensions={0} | concatenate | bytes 12288 | tf_op jit(solution)/shard_map/concatenate | solution.py:716
  13.3 12.6 %collective-permute-done = bf16[432,64]{1,0:T(8,128)(2,1)S(1)} collective-permute-done((bf16[432,64]{1,0:T(8,128)(2,1)S(1)}, bf16[432,64]{1,0:T(8,128)(2,1)S(1)}, u32[]{:S(2)}, u32[]{:S(2)}) %collective-permute-start) | collective-permute-done | bytes 55328 | tf_op jit(solution)/shard_map/ppermute | solution.py:583
  33.4 3.6 %project_near.1 = (bf16[512,768]{1,0:T(8,128)(2,1)}, bf16[1152,512]{1,0:T(8,128)(2,1)S(1)}) custom-call(s32[5]{0:T(128)S(1)} %stack.42.refs_0_, bf16[512,768]{1,0:T(8,128)(2,1)} %bitcast.33, f32[6,768]{1,0:T(8,128)S(1)} %reshape.102.refs_2_.refs_8_.refs_5_.refs_3_, bf16[576,768]{1,0:T(8,128)(2,1)S(1)} %bitcast.27, ...), custom_call_target="tpu_custom_call" | custom-call | flops 1 | bytes 1 | tf_op jit(solution)/shard_map/project_near/pallas_call | solution.py:132
  37.0 3.1 %project_far.1.refs_1_.refs_0_.refs_4_.refs_3_ = bf16[2304,512]{1,0:T(8,128)(2,1)S(1)} custom-call(s32[5]{0:T(128)S(1)} %stack.42.refs_0_, bf16[512,768]{1,0:T(8,128)(2,1)} %get-tuple-element.112.refs_1_.refs_6_.refs_2_, bf16[1152,512]{1,0:T(8,128)(2,1)S(1)} %get-tuple-element.113.refs_2_, bf16[576,768]{1,0:T(8,128)(2,1)S(1)} %collective-permute-done.4.refs_3_.refs_14_, ...), custom_call_target="tpu_custom_call" | custom-call | flops 1 | bytes 1 | tf_op jit(solution)/shard_map/project_far/pallas_call | solution.py:132
  40.2 6.1 %keys.1 = (bf16[1536,512]{1,0:T(8,128)(2,1)}, bf16[8,2,112,128]{3,2,1,0:T(8,128)(2,1)}) custom-call(s32[5]{0:T(128)S(1)} %stack.42.refs_0_, bf16[2304,512]{1,0:T(8,128)(2,1)S(1)} %project_far.1.refs_1_.refs_0_.refs_4_.refs_3_, bf16[12,64,64]{2,1,0:T(8,128)(2,1)S(1)} %bitcast.29), custom_call_target="tpu_custom_call" | custom-call | flops 1 | bytes 1 | tf_op jit(solution)/shard_map/keys/pallas_call | solution.py:132
  46.3 5.8 %all-to-all-start = ((bf16[8,2,112,128]{3,2,1,0:T(8,128)(2,1)}), bf16[8,2,112,128]{3,2,1,0:T(8,128)(2,1)}, u32[]{:S(2)}, u32[]{:S(2)}) async-start(bf16[8,2,112,128]{3,2,1,0:T(8,128)(2,1)} %get-tuple-element.114), calls=%async_computation | async-start | bytes 917504 | tf_op jit(solution)/shard_map/all_to_all | solution.py:687
  53.7 11.1 %collective-permute-done.6.refs_6_.refs_2_ = bf16[960,768]{1,0:T(8,128)(2,1)} collective-permute-done((bf16[960,768]{1,0:T(8,128)(2,1)}, bf16[960,768]{1,0:T(8,128)(2,1)}, u32[]{:S(2)}, u32[]{:S(2)}) %collective-permute-start.6) | collective-permute-done | bytes 1474592 | tf_op jit(solution)/shard_map/ppermute | solution.py:583
  68.4 5.8 %all-to-all-start.1 = ((bf16[8,2,112,128]{3,2,1,0:T(8,128)(2,1)}), bf16[8,2,112,128]{3,2,1,0:T(8,128)(2,1)}, u32[]{:S(2)}, u32[]{:S(2)}) async-start(bf16[8,2,112,128]{3,2,1,0:T(8,128)(2,1)} %scan.1), calls=%async_computation.1 | async-start | bytes 917504 | tf_op jit(solution)/shard_map/all_to_all | solution.py:687
  78.7 7.9 %all-to-all-done.1.refs_1_ = bf16[8,2,112,128]{3,2,1,0:T(8,128)(2,1)} async-done(((bf16[8,2,112,128]{3,2,1,0:T(8,128)(2,1)}), bf16[8,2,112,128]{3,2,1,0:T(8,128)(2,1)}, u32[]{:S(2)}, u32[]{:S(2)}) %all-to-all-start.1) | async-done | bytes 458784 | tf_op jit(solution)/shard_map/all_to_all | solution.py:687
  86.5 6.0 %attend.1 = (bf16[768,512]{1,0:T(8,128)(2,1)}, f32[96,512]{1,0:T(8,128)}, f32[512,768]{1,0:T(8,128)}, bf16[512,768]{1,0:T(8,128)(2,1)S(1)}, bf16[768,768]{1,0:T(8,128)(2,1)}) custom-call(s32[5]{0:T(128)S(1)} %copy-done.9, bf16[8,2,112,128]{3,2,1,0:T(8,128)(2,1)} %all-to-all-done.1.refs_1_, bf16[1536,512]{1,0:T(8,128)(2,1)} %queries.1.refs_2_.refs_8_.refs_3_, ...), custom_call_target="tpu_custom_call" | custom-call | flops 1 | bytes 1 | tf_op jit(solution)/shard_map/attend/pallas_call | solution.py:132
  94.9 14.3 %mlp_far.1 = (f32[512,768]{1,0:T(8,128)}, f32[512,768]{1,0:T(8,128)}, bf16[512,768]{1,0:T(8,128)(2,1)S(1)}, bf16[512,768]{1,0:T(8,128)(2,1)S(1)}, bf16[384,768]{...) custom-call(s32[5]{0:T(128)S(1)} %copy-done.9, ...), custom_call_target="tpu_custom_call" | custom-call | flops 1 | bytes 1 | tf_op jit(solution)/shard_map/mlp_far/pallas_call | solution.py:132
  109.8 14.7 %mlp_near.1 = (f32[512,768]{1,0:T(8,128)}, f32[512,768]{1,0:T(8,128)}, bf16[512,768]{1,0:T(8,128)(2,1)}, bf16[512,768]{1,0:T(8,128)(2,1)S(1)}, bf16[768,768]{1,0...) custom-call(s32[5]{0:T(128)S(1)} %copy-done.9, bf16[512,768]{1,0:T(8,128)(2,1)S(1)} %get-tuple-element.119.refs_1_, ...), custom_call_target="tpu_custom_call" | custom-call | flops 1 | bytes 1 | tf_op jit(solution)/shard_map/mlp_near/pallas_call | solution.py:132
  127.1 7.0 %middle.1 = (f32[512,768]{1,0:T(8,128)}, bf16[512,768]{1,0:T(8,128)(2,1)}, bf16[960,512]{1,0:T(8,128)(2,1)}, bf16[8,2,112,128]{3,2,1,0:T(8,128)(2,1)}, f32[8,768]{1,0:T(8,128)S(1)}) custom-call(s32[5]{0:T(128)S(1)} %copy-done.9, f32[512,768]{1,0:T(8,128)} %get-tuple-element.126.refs_1_, bf16[512,768]{1,0:T(8,128)(2,1)S(1)} %collective-permute-done.13.refs_2_, ...), custom_call_target="tpu_custom_call" | custom-call | flops 1 | bytes 1 | tf_op jit(solution)/shard_map/middle/pallas_call | solution.py:132
  134.2 4.1 %all-to-all-start.2 = ((bf16[8,2,112,128]{3,2,1,0:T(8,128)(2,1)}), bf16[8,2,112,128]{3,2,1,0:T(8,128)(2,1)}, u32[]{:S(2)}, u32[]{:S(2)}) async-start(bf16[8,2,112,128]{3,2,1,0:T(8,128)(2,1)} %get-tuple-element.133), calls=%async_computation.2 | async-start | bytes 917504 | tf_op jit(solution)/shard_map/all_to_all | solution.py:687
  142.1 7.4 %query_back.1 = (bf16[768,512]{1,0:T(8,128)(2,1)}, f32[12,64,64]{2,1,0:T(8,128)}, bf16[192,768]{1,0:T(8,128)(2,1)}, bf16[192,768]{1,0:T(8,128)(2,1)}, bf16[192,7...) custom-call(s32[5]{0:T(128)S(1)} %copy-done.9, bf16[8,2,112,128]{3,2,1,0:T(8,128)(2,1)} %all-to-all-done.1.refs_1_, ...), custom_call_target="tpu_custom_call" | custom-call | flops 1 | bytes 1 | tf_op jit(solution)/shard_map/query_back/pallas_call | solution.py:132
  153.9 4.1 %all-to-all-start.3 = ((bf16[8,2,112,128]{3,2,1,0:T(8,128)(2,1)}), bf16[8,2,112,128]{3,2,1,0:T(8,128)(2,1)}, u32[]{:S(2)}, u32[]{:S(2)}) async-start(bf16[8,2,112,128]{3,2,1,0:T(8,128)(2,1)} %scan_back.1), calls=%async_computation.3 | async-start | bytes 917504 | tf_op jit(solution)/shard_map/all_to_all | solution.py:687
  162.3 6.5 %collective-permute-done.15 = bf16[768,768]{1,0:T(8,128)(2,1)} collective-permute-done((bf16[768,768]{1,0:T(8,128)(2,1)}, bf16[768,768]{1,0:T(8,128)(2,1)}, u32[]{:S(2)}, u32[]{:S(2)}) %collective-permute-start.15) | collective-permute-done | bytes 1179680 | tf_op jit(solution)/shard_map/ppermute | solution.py:583
  170.9 8.4 %key_back.1 = (bf16[2304,512]{1,0:T(8,128)(2,1)}, f32[12,64,64]{2,1,0:T(8,128)}, bf16[576,768]{1,0:T(8,128)(2,1)}, bf16[576,768]{1,0:T(8,128)(2,1)}) custom-call(s32[5]{0:T(128)S(1)} %copy-done.9, bf16[8,2,112,128]{3,2,1,0:T(8,128)(2,1)} %all-to-all-done.3.refs_1_, bf16[1536,512]{1,0:T(8,128)(2,1)} %get-tuple-element.148.refs_2_, ...), custom_call_target="tpu_custom_call" | custom-call | flops 1 | bytes 1 | tf_op jit(solution)/shard_map/key_back/pallas_call | solution.py:132
  184.2 5.3 %project_grad.1 = (bf16[768,768]{1,0:T(8,128)(2,1)}, bf16[768,768]{1,0:T(8,128)(2,1)}) custom-call(s32[5]{0:T(128)S(1)} %copy-done.9, bf16[2304,512]{1,0:T(8,128)(2,1)} %get-tuple-element.149.refs_1_, bf16[512,768]{1,0:T(8,128)(2,1)} %get-tuple-element.112.refs_1_.refs_6_.refs_2_, bf16[576,768]{1,0:T(8,128)(2,1)S(1)} %collective-permute-done.17.refs_3_, ...), custom_call_target="tpu_custom_call" | custom-call | flops 1 | bytes 1 | tf_op jit(solution)/shard_map/project_grad/pallas_call | solution.py:132
  194.8 9.4 %input.1 = (f32[512,768]{1,0:T(8,128)}, f32[512,768]{1,0:T(8,128)}, bf16[64,768]{1,0:T(8,128)(2,1)S(1)}, bf16[64,768]{1,0:T(8,128)(2,1)S(1)}, bf16[64,768]{1,0:T(8,128)(2,1)S(1)}, /*index=5*/bf16[64,768]{1,0:T(8,128)(2,1)S(1)}) custom-call(s32[5]{0:T(128)S(1)} %copy-done.9, bf16[2304,512]{1,0:T(8,128)(2,1)} %get-tuple-element.149.refs_1_, ...), custom_call_target="tpu_custom_call" | custom-call | flops 1 | bytes 1 | tf_op jit(solution)/shard_map/input/pallas_call | solution.py:132
  209.1 5.2 %collective-permute-done.30 = bf16[192,768]{1,0:T(8,128)(2,1)S(1)} collective-permute-done((bf16[192,768]{1,0:T(8,128)(2,1)S(1)}, bf16[192,768]{1,0:T(8,128)(2,1)S(1)}, u32[]{:S(2)}, u32[]{:S(2)}) %collective-permute-start.30) | collective-permute-done | bytes 294944 | tf_op jit(solution)/shard_map/ppermute | solution.py:619
  215.7 3.0 collective-permute-done.28
  226.8 2.9 collective-permute-start.35
  229.7 6.2 %collective-permute-done.25 = bf16[64,768]{1,0:T(8,128)(2,1)S(1)} collective-permute-done((bf16[64,768]{1,0:T(8,128)(2,1)S(1)}, bf16[64,768]{1,0:T(8,128)(2,1)S(1)}, u32[]{:S(2)}, u32[]{:S(2)}) %collective-permute-start.25) | collective-permute-done | bytes 98336 | tf_op jit(solution)/shard_map/ppermute | solution.py:619
  246.5 9.8 %collective-permute-done.38 = bf16[96,768]{1,0:T(8,128)(2,1)S(1)} collective-permute-done((bf16[96,768]{1,0:T(8,128)(2,1)S(1)}, bf16[96,768]{1,0:T(8,128)(2,1)S(1)}, u32[]{:S(2)}, u32[]{:S(2)}) %collective-permute-start.38) | collective-permute-done | bytes 147488 | tf_op jit(solution)/shard_map/ppermute | solution.py:619
  256.3 3.2 %collective-permute-done.37 = bf16[192,768]{1,0:T(8,128)(2,1)S(1)} collective-permute-done((bf16[192,768]{1,0:T(8,128)(2,1)S(1)}, bf16[192,768]{1,0:T(8,128)(2,1)S(1)}, u32[]{:S(2)}, u32[]{:S(2)}) %collective-permute-start.37) | collective-permute-done | bytes 294944 | tf_op jit(solution)/shard_map/ppermute | solution.py:619
  263.8 4.0 %collective-permute-done.39 = bf16[96,768]{1,0:T(8,128)(2,1)S(1)} collective-permute-done((bf16[96,768]{1,0:T(8,128)(2,1)S(1)}, bf16[96,768]{1,0:T(8,128)(2,1)S(1)}, u32[]{:S(2)}, u32[]{:S(2)}) %collective-permute-start.39) | collective-permute-done | bytes 147488 | tf_op jit(solution)/shard_map/ppermute | solution.py:619
  269.5 2.9 collective-permute-done.43
  276.6 2.7 collective-permute-start.42
  284.0 3.6 %collective-permute-done.44 = bf16[384,768]{1,0:T(8,128)(2,1)S(1)} collective-permute-done((bf16[384,768]{1,0:T(8,128)(2,1)}, bf16[384,768]{1,0:T(8,128)(2,1)S(1)}, u32[]{:S(2)}, u32[]{:S(2)}) %collective-permute-start.44) | collective-permute-done | bytes 589856 | tf_op jit(solution)/shard_map/ppermute | solution.py:619
  292.1 8.8 %collective-permute-done.45 = bf16[384,768]{1,0:T(8,128)(2,1)S(1)} collective-permute-done((bf16[384,768]{1,0:T(8,128)(2,1)S(1)}, bf16[384,768]{1,0:T(8,128)(2,1)S(1)}, u32[]{:S(2)}, u32[]{:S(2)}) %collective-permute-start.45) | collective-permute-done | bytes 589856 | tf_op jit(solution)/shard_map/ppermute | solution.py:619
  (212 shorter events, 96.7 us)
Async XLA Ops:
  0.6 28.7 %collective-permute-start.4 = (bf16[576,768]{1,0:T(8,128)(2,1)}, bf16[576,768]{1,0:T(8,128)(2,1)S(1)}, u32[]{:S(2)}, u32[]{:S(2)}) collective-permute-start(bf16[576,768]{1,0:T(8,128)(2,1)} %bitcast.25), channel_id=1, source_target_pairs={{0,2},{1,3},{2,0},{3,1},{4,6},{5,7},{6,4},{7,5},{8,10},{9,11},{10,... | collective-permute-start | bytes 2654216 | tf_op jit(solution)/shard_map/ppermute | solution.py:583
  10.1 15.8 %collective-permute-start = (bf16[432,64]{1,0:T(8,128)(2,1)S(1)}, bf16[432,64]{1,0:T(8,128)(2,1)S(1)}, u32[]{:S(2)}, u32[]{:S(2)}) collective-permute-start(bf16[432,64]{1,0:T(8,128)(2,1)S(1)} %pad_maximum_fusion.10), channel_id=1, source_target_pairs={{0,2},{1,3},{2,0},{3,1},{4,6},{5,7},{6,4},{7,5},{8,10},{9,11},{10,... | collective-permute-start | bytes 165896 | tf_op jit(solution)/shard_map/ppermute | solution.py:583
  10.2 17.7 %collective-permute-start.2 = (bf16[432,64]{1,0:T(8,128)(2,1)S(1)}, bf16[432,64]{1,0:T(8,128)(2,1)S(1)}, u32[]{:S(2)}, u32[]{:S(2)}) collective-permute-start(bf16[432,64]{1,0:T(8,128)(2,1)S(1)} %pad_maximum_fusion.10), channel_id=1, source_target_pairs={{0,1},{1,0},{2,3},{3,2},{4,5},{5,4},{6,7},{7,6},{8,9},{9,8},{10,11... | collective-permute-start | bytes 165896 | tf_op jit(solution)/shard_map/ppermute | solution.py:579
  10.2 23.1 %collective-permute-start.3 = (bf16[576,768]{1,0:T(8,128)(2,1)}, bf16[576,768]{1,0:T(8,128)(2,1)S(1)}, u32[]{:S(2)}, u32[]{:S(2)}) collective-permute-start(bf16[576,768]{1,0:T(8,128)(2,1)} %bitcast.26), channel_id=1, source_target_pairs={{0,1},{1,0},{2,3},{3,2},{4,5},{5,4},{6,7},{7,6},{8,9},{9,8},{10,11... | collective-permute-start | bytes 2654216 | tf_op jit(solution)/shard_map/ppermute | solution.py:579
  30.2 34.5 %collective-permute-start.6 = (bf16[960,768]{1,0:T(8,128)(2,1)}, bf16[960,768]{1,0:T(8,128)(2,1)}, u32[]{:S(2)}, u32[]{:S(2)}) collective-permute-start(bf16[960,768]{1,0:T(8,128)(2,1)} %pad_maximum_fusion), channel_id=1, source_target_pairs={{0,2},{1,3},{2,0},{3,1},{4,6},{5,7},{6,4},{7,5},{8,10},{9,11},{10,... | collective-permute-start | bytes 4423688 | tf_op jit(solution)/shard_map/ppermute | solution.py:583
  46.3 20.2 %all-to-all-start = ((bf16[8,2,112,128]{3,2,1,0:T(8,128)(2,1)}), bf16[8,2,112,128]{3,2,1,0:T(8,128)(2,1)}, u32[]{:S(2)}, u32[]{:S(2)}) async-start(bf16[8,2,112,128]{3,2,1,0:T(8,128)(2,1)} %get-tuple-element.114), calls=%async_computation | async-start | bytes 917504 | tf_op jit(solution)/shard_map/all_to_all | solution.py:687
  52.1 26.5 %collective-permute-start.7 = (bf16[192,768]{1,0:T(8,128)(2,1)}, bf16[192,768]{1,0:T(8,128)(2,1)}, u32[]{:S(2)}, u32[]{:S(2)}) collective-permute-start(bf16[192,768]{1,0:T(8,128)(2,1)} %refs_4_.1), channel_id=1, source_target_pairs={{0,1},{1,0},{2,3},{3,2},{4,5},{5,4},{6,7},{7,6},{8,9},{9,8},{10,11... | collective-permute-start | bytes 884744 | tf_op jit(solution)/shard_map/ppermute | solution.py:579
  52.1 40.6 %collective-permute-start.10 = (bf16[512,768]{1,0:T(8,128)(2,1)}, bf16[512,768]{1,0:T(8,128)(2,1)}, u32[]{:S(2)}, u32[]{:S(2)}) collective-permute-start(bf16[512,768]{1,0:T(8,128)(2,1)} %bitcast.13.refs_4_), channel_id=1, source_target_pairs={{0,1},{1,0},{2,3},{3,2},{4,5},{5,4},{6,7},{7,6},{8,9},{9,8},{10,11... | collective-permute-start | bytes 2359304 | tf_op jit(solution)/shard_map/ppermute | solution.py:579
  64.8 28.0 %collective-permute-start.11 = (bf16[768,768]{1,0:T(8,128)(2,1)}, bf16[768,768]{1,0:T(8,128)(2,1)}, u32[]{:S(2)}, u32[]{:S(2)}) collective-permute-start(bf16[768,768]{1,0:T(8,128)(2,1)} %refs_5_.1), channel_id=1, source_target_pairs={{0,2},{1,3},{2,0},{3,1},{4,6},{5,7},{6,4},{7,5},{8,10},{9,11},{10,... | collective-permute-start | bytes 3538952 | tf_op jit(solution)/shard_map/ppermute | solution.py:583
  68.4 18.1 %all-to-all-start.1 = ((bf16[8,2,112,128]{3,2,1,0:T(8,128)(2,1)}), bf16[8,2,112,128]{3,2,1,0:T(8,128)(2,1)}, u32[]{:S(2)}, u32[]{:S(2)}) async-start(bf16[8,2,112,128]{3,2,1,0:T(8,128)(2,1)} %scan.1), calls=%async_computation.1 | async-start | bytes 917504 | tf_op jit(solution)/shard_map/all_to_all | solution.py:687
  109.2 15.6 %collective-permute-start.12 = (bf16[384,768]{1,0:T(8,128)(2,1)}, bf16[384,768]{1,0:T(8,128)(2,1)S(1)}, u32[]{:S(2)}, u32[]{:S(2)}) collective-permute-start(bf16[384,768]{1,0:T(8,128)(2,1)} %get-tuple-element.128), channel_id=1, source_target_pairs={{0,2},{1,3},{2,0},{3,1},{4,6},{5,7},{6,4},{7,5},{8,10},{9,11},{10,... | collective-permute-start | bytes 1769480 | tf_op jit(solution)/shard_map/ppermute | solution.py:583
  124.8 16.1 %collective-permute-start.14 = (bf16[384,768]{1,0:T(8,128)(2,1)}, bf16[384,768]{1,0:T(8,128)(2,1)}, u32[]{:S(2)}, u32[]{:S(2)}) collective-permute-start(bf16[384,768]{1,0:T(8,128)(2,1)} %get-tuple-element.138), channel_id=1, source_target_pairs={{0,2},{1,3},{2,0},{3,1},{4,6},{5,7},{6,4},{7,5},{8,10},{9,11},{10,... | collective-permute-start | bytes 1769480 | tf_op jit(solution)/shard_map/ppermute | solution.py:583
  134.2 17.8 %all-to-all-start.2 = ((bf16[8,2,112,128]{3,2,1,0:T(8,128)(2,1)}), bf16[8,2,112,128]{3,2,1,0:T(8,128)(2,1)}, u32[]{:S(2)}, u32[]{:S(2)}) async-start(bf16[8,2,112,128]{3,2,1,0:T(8,128)(2,1)} %get-tuple-element.133), calls=%async_computation.2 | async-start | bytes 917504 | tf_op jit(solution)/shard_map/all_to_all | solution.py:687
  140.9 27.9 %collective-permute-start.15 = (bf16[768,768]{1,0:T(8,128)(2,1)}, bf16[768,768]{1,0:T(8,128)(2,1)}, u32[]{:S(2)}, u32[]{:S(2)}) collective-permute-start(bf16[768,768]{1,0:T(8,128)(2,1)} %get-tuple-element.145), channel_id=1, source_target_pairs={{0,2},{1,3},{2,0},{3,1},{4,6},{5,7},{6,4},{7,5},{8,10},{9,11},{10,... | collective-permute-start | bytes 3538952 | tf_op jit(solution)/shard_map/ppermute | solution.py:583
  153.9 17.1 %all-to-all-start.3 = ((bf16[8,2,112,128]{3,2,1,0:T(8,128)(2,1)}), bf16[8,2,112,128]{3,2,1,0:T(8,128)(2,1)}, u32[]{:S(2)}, u32[]{:S(2)}) async-start(bf16[8,2,112,128]{3,2,1,0:T(8,128)(2,1)} %scan_back.1), calls=%async_computation.3 | async-start | bytes 917504 | tf_op jit(solution)/shard_map/all_to_all | solution.py:687
  160.4 19.0 %collective-permute-start.16 = (bf16[384,768]{1,0:T(8,128)(2,1)}, bf16[384,768]{1,0:T(8,128)(2,1)}, u32[]{:S(2)}, u32[]{:S(2)}) collective-permute-start(bf16[384,768]{1,0:T(8,128)(2,1)} %add_convert_fusion.2), channel_id=1, source_target_pairs={{0,4},{4,0},{8,12},{12,8},{16,20},{20,16},{24,28},{28,24},{1,5},{5... | collective-permute-start | bytes 1769480 | tf_op jit(solution)/shard_map/ppermute | solution.py:619
  180.5 14.3 %collective-permute-start.21 = (bf16[512,768]{1,0:T(8,128)(2,1)}, bf16[512,768]{1,0:T(8,128)(2,1)S(1)}, u32[]{:S(2)}, u32[]{:S(2)}) collective-permute-start(bf16[512,768]{1,0:T(8,128)(2,1)} %get-tuple-element.166), channel_id=1, source_target_pairs={{0,1},{1,0},{2,3},{3,2},{4,5},{5,4},{6,7},{7,6},{8,9},{9,8},{10,11... | collective-permute-start | bytes 2359304 | tf_op jit(solution)/shard_map/ppermute | solution.py:579
  189.5 29.2 %collective-permute-start.28 = (bf16[768,768]{1,0:T(8,128)(2,1)}, bf16[768,768]{1,0:T(8,128)(2,1)}, u32[]{:S(2)}, u32[]{:S(2)}) collective-permute-start(bf16[768,768]{1,0:T(8,128)(2,1)} %get-tuple-element.180), channel_id=1, source_target_pairs={{0,2},{1,3},{2,0},{3,1},{4,6},{5,7},{6,4},{7,5},{8,10},{9,11},{10,... | collective-permute-start | bytes 3538952 | tf_op jit(solution)/shard_map/ppermute | solution.py:583
  190.8 15.7 %collective-permute-start.33 = (bf16[384,768]{1,0:T(8,128)(2,1)}, bf16[384,768]{1,0:T(8,128)(2,1)}, u32[]{:S(2)}, u32[]{:S(2)}) collective-permute-start(bf16[384,768]{1,0:T(8,128)(2,1)} %add_convert_fusion.1), channel_id=1, source_target_pairs={{0,4},{4,0},{8,12},{12,8},{16,20},{20,16},{24,28},{28,24},{1,5},{5... | collective-permute-start | bytes 1769480 | tf_op jit(solution)/shard_map/ppermute | solution.py:619
  205.6 15.8 %collective-permute-start.24 = (bf16[64,768]{1,0:T(8,128)(2,1)S(1)}, bf16[64,768]{1,0:T(8,128)(2,1)S(1)}, u32[]{:S(2)}, u32[]{:S(2)}) collective-permute-start(bf16[64,768]{1,0:T(8,128)(2,1)S(1)} %add_convert_fusion.15), channel_id=1, source_target_pairs={{0,2},{1,3},{2,0},{3,1},{4,6},{5,7},{6,4},{7,5},{8,10},{9,11},{10,... | collective-permute-start | bytes 294920 | tf_op jit(solution)/shard_map/ppermute | solution.py:583
  207.7 17.9 %collective-permute-start.34 = (bf16[192,768]{1,0:T(8,128)(2,1)S(1)}, bf16[192,768]{1,0:T(8,128)(2,1)S(1)}, u32[]{:S(2)}, u32[]{:S(2)}) collective-permute-start(bf16[192,768]{1,0:T(8,128)(2,1)S(1)} %add_convert_fusion.4), channel_id=1, source_target_pairs={{0,8},{4,12},{8,0},{12,4},{16,24},{20,28},{24,16},{28,20},{1,9},{5... | collective-permute-start | bytes 884744 | tf_op jit(solution)/shard_map/ppermute | solution.py:619
  219.9 19.1 %collective-permute-start.29 = (bf16[384,768]{1,0:T(8,128)(2,1)S(1)}, bf16[384,768]{1,0:T(8,128)(2,1)S(1)}, u32[]{:S(2)}, u32[]{:S(2)}) collective-permute-start(bf16[384,768]{1,0:T(8,128)(2,1)S(1)} %add_convert_fusion), channel_id=1, source_target_pairs={{0,4},{4,0},{8,12},{12,8},{16,20},{20,16},{24,28},{28,24},{1,5},{5... | collective-permute-start | bytes 1769480 | tf_op jit(solution)/shard_map/ppermute | solution.py:619
  221.4 14.4 %collective-permute-start.25 = (bf16[64,768]{1,0:T(8,128)(2,1)S(1)}, bf16[64,768]{1,0:T(8,128)(2,1)S(1)}, u32[]{:S(2)}, u32[]{:S(2)}) collective-permute-start(bf16[64,768]{1,0:T(8,128)(2,1)S(1)} %add_convert_fusion.14), channel_id=1, source_target_pairs={{0,4},{4,0},{8,12},{12,8},{16,20},{20,16},{24,28},{28,24},{1,5},{5... | collective-permute-start | bytes 294920 | tf_op jit(solution)/shard_map/ppermute | solution.py:619
  226.8 12.2 %collective-permute-start.35 = (bf16[96,768]{1,0:T(8,128)(2,1)S(1)}, bf16[96,768]{1,0:T(8,128)(2,1)S(1)}, u32[]{:S(2)}, u32[]{:S(2)}) collective-permute-start(bf16[96,768]{1,0:T(8,128)(2,1)S(1)} %add_convert_fusion.9), channel_id=1, source_target_pairs={{0,16},{4,20},{8,24},{12,28},{16,0},{20,4},{24,8},{28,12},{1,17},{... | collective-permute-start | bytes 442376 | tf_op jit(solution)/shard_map/ppermute | solution.py:619
  240.1 16.2 %collective-permute-start.36 = (bf16[192,768]{1,0:T(8,128)(2,1)S(1)}, bf16[192,768]{1,0:T(8,128)(2,1)S(1)}, u32[]{:S(2)}, u32[]{:S(2)}) collective-permute-start(bf16[192,768]{1,0:T(8,128)(2,1)S(1)} %add_convert_fusion.3), channel_id=1, source_target_pairs={{0,8},{4,12},{8,0},{12,4},{16,24},{20,28},{24,16},{28,20},{1,9},{5... | collective-permute-start | bytes 884744 | tf_op jit(solution)/shard_map/ppermute | solution.py:619
  240.2 19.3 %collective-permute-start.37 = (bf16[192,768]{1,0:T(8,128)(2,1)S(1)}, bf16[192,768]{1,0:T(8,128)(2,1)S(1)}, u32[]{:S(2)}, u32[]{:S(2)}) collective-permute-start(bf16[192,768]{1,0:T(8,128)(2,1)S(1)} %pad_maximum_fusion.5), channel_id=1, source_target_pairs={{0,8},{4,12},{8,0},{12,4},{16,24},{20,28},{24,16},{28,20},{1,9},{5... | collective-permute-start | bytes 884744 | tf_op jit(solution)/shard_map/ppermute | solution.py:619
  243.4 12.9 %collective-permute-start.38 = (bf16[96,768]{1,0:T(8,128)(2,1)S(1)}, bf16[96,768]{1,0:T(8,128)(2,1)S(1)}, u32[]{:S(2)}, u32[]{:S(2)}) collective-permute-start(bf16[96,768]{1,0:T(8,128)(2,1)S(1)} %add_convert_fusion.8), channel_id=1, source_target_pairs={{0,16},{4,20},{8,24},{12,28},{16,0},{20,4},{24,8},{28,12},{1,17},{... | collective-permute-start | bytes 442376 | tf_op jit(solution)/shard_map/ppermute | solution.py:619
  244.1 35.2 %collective-permute-start.27 = (bf16[64,768]{1,0:T(8,128)(2,1)S(1)}, bf16[64,768]{1,0:T(8,128)(2,1)S(1)}, u32[]{:S(2)}, u32[]{:S(2)}) collective-permute-start(bf16[64,768]{1,0:T(8,128)(2,1)S(1)} %add_convert_fusion.12), channel_id=1, source_target_pairs={{0,16},{4,20},{8,24},{12,28},{16,0},{20,4},{24,8},{28,12},{1,17},{... | collective-permute-start | bytes 294920 | tf_op jit(solution)/shard_map/ppermute | solution.py:619
  260.8 11.6 %collective-permute-start.43 = (bf16[192,768]{1,0:T(8,128)(2,1)S(1)}, bf16[192,768]{1,0:T(8,128)(2,1)S(1)}, u32[]{:S(2)}, u32[]{:S(2)}) collective-permute-start(bf16[192,768]{1,0:T(8,128)(2,1)S(1)} %pad_maximum_fusion.7), channel_id=1, source_target_pairs={{0,8},{4,12},{8,0},{12,4},{16,24},{20,28},{24,16},{28,20},{1,9},{5... | collective-permute-start | bytes 884744 | tf_op jit(solution)/shard_map/ppermute | solution.py:619
  262.8 13.7 %collective-permute-start.41 = (bf16[384,768]{1,0:T(8,128)(2,1)S(1)}, bf16[384,768]{1,0:T(8,128)(2,1)S(1)}, u32[]{:S(2)}, u32[]{:S(2)}) collective-permute-start(bf16[384,768]{1,0:T(8,128)(2,1)S(1)} %pad_maximum_fusion.2), channel_id=1, source_target_pairs={{0,4},{4,0},{8,12},{12,8},{16,20},{20,16},{24,28},{28,24},{1,5},{5... | collective-permute-start | bytes 1769480 | tf_op jit(solution)/shard_map/ppermute | solution.py:619
  273.3 14.3 %collective-permute-start.44 = (bf16[384,768]{1,0:T(8,128)(2,1)}, bf16[384,768]{1,0:T(8,128)(2,1)S(1)}, u32[]{:S(2)}, u32[]{:S(2)}) collective-permute-start(bf16[384,768]{1,0:T(8,128)(2,1)} %pad_maximum_fusion.3), channel_id=1, source_target_pairs={{0,4},{4,0},{8,12},{12,8},{16,20},{20,16},{24,28},{28,24},{1,5},{5... | collective-permute-start | bytes 1769480 | tf_op jit(solution)/shard_map/ppermute | solution.py:619
  287.7 13.3 %collective-permute-start.45 = (bf16[384,768]{1,0:T(8,128)(2,1)S(1)}, bf16[384,768]{1,0:T(8,128)(2,1)S(1)}, u32[]{:S(2)}, u32[]{:S(2)}) collective-permute-start(bf16[384,768]{1,0:T(8,128)(2,1)S(1)} %pad_maximum_fusion.4), channel_id=1, source_target_pairs={{0,4},{4,0},{8,12},{12,8},{16,20},{20,16},{24,28},{28,24},{1,5},{5... | collective-permute-start | bytes 1769480 | tf_op jit(solution)/shard_map/ppermute | solution.py:619
  (48 other events, 378.5 us)

commit v7 on v6

--- a/solution.py
+++ b/solution.py
@@ -12,7 +12,7 @@
 BF16 = jnp.bfloat16
 AUG = 80
 KEEP = 72
-UNROLL = 4
+UNROLL = 6
 NN = (((1,), (0,)), ((), ()))
 NT = (((1,), (1,)), ((), ()))
 TN = (((0,), (0,)), ((), ()))

time: 305 us -> 309 us (1.013); the launches traced: 303 us -> 304 us
  transfers between devices with their start and end apart: 50 -> 50, of which waited for: 29 -> 28; matrix products, arithmetic and copies ran while one was open for 13% -> 13% of each run, Pallas kernels for 26% -> 25%
where the time goes in v7:
time: 309 us; the launch traced here: 304 us
  waiting for transfers between devices  108 us (35%)
  Pallas kernels  91.4 us (30%)
  starting transfers between devices  59.7 us (19%)
  other arithmetic  31.2 us (10%)
  local copies, waits for them, and re-layouts  9.88 us (3%)
  between operations  3.19 us (1%)
    pallas_call x15, Pallas kernels, call(): pl.pallas_call(run, out_shape=[pltpu.HBM(o.shape, o.dtype) if k == 'h' el...  91.4 us
    ppermute x21, waiting for transfers between devices, send(): return lax.ppermute(value, 'ctx', [(i, i ^ flip) for i in range(self.nctx)])  53.5 us
    ppermute x9, waiting for transfers between devices, cross_swap(): return lax.ppermute(a, 'fsdp', CROSS)  36.5 us
    ppermute x21, starting transfers between devices, send(): return lax.ppermute(value, 'ctx', [(i, i ^ flip) for i in range(self.nctx)])  24.4 us
    all_to_all x4, starting transfers between devices, exchange(): return lax.all_to_all(a, 'ctx', 0, 0, tiled=True)  20.2 us
    convert_element_type x12, other arithmetic, rows_sum(): return out.astype(BF16)  15.8 us
    ppermute x9, starting transfers between devices, cross_swap(): return lax.ppermute(a, 'fsdp', CROSS)  11.9 us
    all_to_all x4, waiting for transfers between devices, exchange(): return lax.all_to_all(a, 'ctx', 0, 0, tiled=True)  10.6 us
  transfers between devices with their start and end apart: 50, of which 28 were waited for; matrix products, arithmetic and copies ran while one was open for 13% of the time, Pallas kernels for 25%

profile of v7, /device:TPU:0, one launch (start us, length us, event | category | flops | bytes accessed | tf_op | source)
XLA Modules:
  0.0 303.6 jit_solution(11323284520935138429)
XLA Ops:
  0.6 3.0 collective-permute-start.4
  3.7 5.5 %concatenate.51 = bf16[3072]{0:T(1024)(128)(2,1)S(1)} concatenate(bf16[192]{0:T(256)(128)(2,1)} %param.22, bf16[192]{0:T(256)(128)(2,1)} %param.23, bf16[192]{0:T(256)(128)(2,1)} %param.30, bf16[192]{0:T(256)(128)(2,1)} %param.31, bf16[192]{0:T(256)(128)(2,1)} %param.29, bf16[192]{0:T(256)(128)(2,1)} %param.35, bf16[576]{0:T(1024)(128)(2,1)} %param.25, bf16[768]{0:T(1024)(128)(2,1)} %param.33, ...), dimensions={0} | concatenate | bytes 12288 | tf_op jit(solution)/shard_map/concatenate | solution.py:716
  13.3 12.6 %collective-permute-done = bf16[432,64]{1,0:T(8,128)(2,1)S(1)} collective-permute-done((bf16[432,64]{1,0:T(8,128)(2,1)S(1)}, bf16[432,64]{1,0:T(8,128)(2,1)S(1)}, u32[]{:S(2)}, u32[]{:S(2)}) %collective-permute-start) | collective-permute-done | bytes 55328 | tf_op jit(solution)/shard_map/ppermute | solution.py:583
  33.4 3.6 %project_near.1 = (bf16[512,768]{1,0:T(8,128)(2,1)}, bf16[1152,512]{1,0:T(8,128)(2,1)S(1)}) custom-call(s32[5]{0:T(128)S(1)} %stack.42.refs_0_, bf16[512,768]{1,0:T(8,128)(2,1)} %bitcast.33, f32[6,768]{1,0:T(8,128)S(1)} %reshape.102.refs_2_.refs_8_.refs_5_.refs_3_, bf16[576,768]{1,0:T(8,128)(2,1)S(1)} %bitcast.27, ...), custom_call_target="tpu_custom_call" | custom-call | flops 1 | bytes 1 | tf_op jit(solution)/shard_map/project_near/pallas_call | solution.py:132
  37.0 3.1 %project_far.1.refs_1_.refs_0_.refs_4_.refs_3_ = bf16[2304,512]{1,0:T(8,128)(2,1)S(1)} custom-call(s32[5]{0:T(128)S(1)} %stack.42.refs_0_, bf16[512,768]{1,0:T(8,128)(2,1)} %get-tuple-element.112.refs_1_.refs_6_.refs_2_, bf16[1152,512]{1,0:T(8,128)(2,1)S(1)} %get-tuple-element.113.refs_2_, bf16[576,768]{1,0:T(8,128)(2,1)S(1)} %collective-permute-done.4.refs_3_.refs_14_, ...), custom_call_target="tpu_custom_call" | custom-call | flops 1 | bytes 1 | tf_op jit(solution)/shard_map/project_far/pallas_call | solution.py:132
  40.2 6.0 %keys.1 = (bf16[1536,512]{1,0:T(8,128)(2,1)}, bf16[8,2,112,128]{3,2,1,0:T(8,128)(2,1)}) custom-call(s32[5]{0:T(128)S(1)} %stack.42.refs_0_, bf16[2304,512]{1,0:T(8,128)(2,1)S(1)} %project_far.1.refs_1_.refs_0_.refs_4_.refs_3_, bf16[12,64,64]{2,1,0:T(8,128)(2,1)S(1)} %bitcast.29), custom_call_target="tpu_custom_call" | custom-call | flops 1 | bytes 1 | tf_op jit(solution)/shard_map/keys/pallas_call | solution.py:132
  46.1 5.8 %all-to-all-start = ((bf16[8,2,112,128]{3,2,1,0:T(8,128)(2,1)}), bf16[8,2,112,128]{3,2,1,0:T(8,128)(2,1)}, u32[]{:S(2)}, u32[]{:S(2)}) async-start(bf16[8,2,112,128]{3,2,1,0:T(8,128)(2,1)} %get-tuple-element.114), calls=%async_computation | async-start | bytes 917504 | tf_op jit(solution)/shard_map/all_to_all | solution.py:687
  53.6 11.2 %collective-permute-done.6.refs_6_.refs_2_ = bf16[960,768]{1,0:T(8,128)(2,1)} collective-permute-done((bf16[960,768]{1,0:T(8,128)(2,1)}, bf16[960,768]{1,0:T(8,128)(2,1)}, u32[]{:S(2)}, u32[]{:S(2)}) %collective-permute-start.6) | collective-permute-done | bytes 1474592 | tf_op jit(solution)/shard_map/ppermute | solution.py:583
  68.4 6.1 %all-to-all-start.1 = ((bf16[8,2,112,128]{3,2,1,0:T(8,128)(2,1)}), bf16[8,2,112,128]{3,2,1,0:T(8,128)(2,1)}, u32[]{:S(2)}, u32[]{:S(2)}) async-start(bf16[8,2,112,128]{3,2,1,0:T(8,128)(2,1)} %scan.1), calls=%async_computation.1 | async-start | bytes 917504 | tf_op jit(solution)/shard_map/all_to_all | solution.py:687
  78.7 8.0 %all-to-all-done.1.refs_1_ = bf16[8,2,112,128]{3,2,1,0:T(8,128)(2,1)} async-done(((bf16[8,2,112,128]{3,2,1,0:T(8,128)(2,1)}), bf16[8,2,112,128]{3,2,1,0:T(8,128)(2,1)}, u32[]{:S(2)}, u32[]{:S(2)}) %all-to-all-start.1) | async-done | bytes 458784 | tf_op jit(solution)/shard_map/all_to_all | solution.py:687
  86.7 5.8 %attend.1 = (bf16[768,512]{1,0:T(8,128)(2,1)}, f32[96,512]{1,0:T(8,128)}, f32[512,768]{1,0:T(8,128)}, bf16[512,768]{1,0:T(8,128)(2,1)S(1)}, bf16[768,768]{1,0:T(8,128)(2,1)}) custom-call(s32[5]{0:T(128)S(1)} %copy-done.9, bf16[8,2,112,128]{3,2,1,0:T(8,128)(2,1)} %all-to-all-done.1.refs_1_, bf16[1536,512]{1,0:T(8,128)(2,1)} %queries.1.refs_2_.refs_8_.refs_3_, ...), custom_call_target="tpu_custom_call" | custom-call | flops 1 | bytes 1 | tf_op jit(solution)/shard_map/attend/pallas_call | solution.py:132
  94.9 14.3 %mlp_far.1 = (f32[512,768]{1,0:T(8,128)}, f32[512,768]{1,0:T(8,128)}, bf16[512,768]{1,0:T(8,128)(2,1)S(1)}, bf16[512,768]{1,0:T(8,128)(2,1)S(1)}, bf16[384,768]{...) custom-call(s32[5]{0:T(128)S(1)} %copy-done.9, ...), custom_call_target="tpu_custom_call" | custom-call | flops 1 | bytes 1 | tf_op jit(solution)/shard_map/mlp_far/pallas_call | solution.py:132
  109.8 14.7 %mlp_near.1 = (f32[512,768]{1,0:T(8,128)}, f32[512,768]{1,0:T(8,128)}, bf16[512,768]{1,0:T(8,128)(2,1)}, bf16[512,768]{1,0:T(8,128)(2,1)S(1)}, bf16[768,768]{1,0...) custom-call(s32[5]{0:T(128)S(1)} %copy-done.9, bf16[512,768]{1,0:T(8,128)(2,1)S(1)} %get-tuple-element.119.refs_1_, ...), custom_call_target="tpu_custom_call" | custom-call | flops 1 | bytes 1 | tf_op jit(solution)/shard_map/mlp_near/pallas_call | solution.py:132
  127.1 6.9 %middle.1 = (f32[512,768]{1,0:T(8,128)}, bf16[512,768]{1,0:T(8,128)(2,1)}, bf16[960,512]{1,0:T(8,128)(2,1)}, bf16[8,2,112,128]{3,2,1,0:T(8,128)(2,1)}, f32[8,768]{1,0:T(8,128)S(1)}) custom-call(s32[5]{0:T(128)S(1)} %copy-done.9, f32[512,768]{1,0:T(8,128)} %get-tuple-element.126.refs_1_, bf16[512,768]{1,0:T(8,128)(2,1)S(1)} %collective-permute-done.13.refs_2_, ...), custom_call_target="tpu_custom_call" | custom-call | flops 1 | bytes 1 | tf_op jit(solution)/shard_map/middle/pallas_call | solution.py:132
  134.1 4.1 %all-to-all-start.2 = ((bf16[8,2,112,128]{3,2,1,0:T(8,128)(2,1)}), bf16[8,2,112,128]{3,2,1,0:T(8,128)(2,1)}, u32[]{:S(2)}, u32[]{:S(2)}) async-start(bf16[8,2,112,128]{3,2,1,0:T(8,128)(2,1)} %get-tuple-element.133), calls=%async_computation.2 | async-start | bytes 917504 | tf_op jit(solution)/shard_map/all_to_all | solution.py:687
  142.1 7.1 %query_back.1 = (bf16[768,512]{1,0:T(8,128)(2,1)}, f32[12,64,64]{2,1,0:T(8,128)}, bf16[192,768]{1,0:T(8,128)(2,1)}, bf16[192,768]{1,0:T(8,128)(2,1)}, bf16[192,7...) custom-call(s32[5]{0:T(128)S(1)} %copy-done.9, bf16[8,2,112,128]{3,2,1,0:T(8,128)(2,1)} %all-to-all-done.1.refs_1_, ...), custom_call_target="tpu_custom_call" | custom-call | flops 1 | bytes 1 | tf_op jit(solution)/shard_map/query_back/pallas_call | solution.py:132
  153.8 4.1 %all-to-all-start.3 = ((bf16[8,2,112,128]{3,2,1,0:T(8,128)(2,1)}), bf16[8,2,112,128]{3,2,1,0:T(8,128)(2,1)}, u32[]{:S(2)}, u32[]{:S(2)}) async-start(bf16[8,2,112,128]{3,2,1,0:T(8,128)(2,1)} %scan_back.1), calls=%async_computation.3 | async-start | bytes 917504 | tf_op jit(solution)/shard_map/all_to_all | solution.py:687
  162.2 6.6 %collective-permute-done.15 = bf16[768,768]{1,0:T(8,128)(2,1)} collective-permute-done((bf16[768,768]{1,0:T(8,128)(2,1)}, bf16[768,768]{1,0:T(8,128)(2,1)}, u32[]{:S(2)}, u32[]{:S(2)}) %collective-permute-start.15) | collective-permute-done | bytes 1179680 | tf_op jit(solution)/shard_map/ppermute | solution.py:583
  170.8 8.2 %key_back.1 = (bf16[2304,512]{1,0:T(8,128)(2,1)}, f32[12,64,64]{2,1,0:T(8,128)}, bf16[576,768]{1,0:T(8,128)(2,1)}, bf16[576,768]{1,0:T(8,128)(2,1)}) custom-call(s32[5]{0:T(128)S(1)} %copy-done.9, bf16[8,2,112,128]{3,2,1,0:T(8,128)(2,1)} %all-to-all-done.3.refs_1_, bf16[1536,512]{1,0:T(8,128)(2,1)} %get-tuple-element.148.refs_2_, ...), custom_call_target="tpu_custom_call" | custom-call | flops 1 | bytes 1 | tf_op jit(solution)/shard_map/key_back/pallas_call | solution.py:132
  183.9 5.3 %project_grad.1 = (bf16[768,768]{1,0:T(8,128)(2,1)}, bf16[768,768]{1,0:T(8,128)(2,1)}) custom-call(s32[5]{0:T(128)S(1)} %copy-done.9, bf16[2304,512]{1,0:T(8,128)(2,1)} %get-tuple-element.149.refs_1_, bf16[512,768]{1,0:T(8,128)(2,1)} %get-tuple-element.112.refs_1_.refs_6_.refs_2_, bf16[576,768]{1,0:T(8,128)(2,1)S(1)} %collective-permute-done.17.refs_3_, ...), custom_call_target="tpu_custom_call" | custom-call | flops 1 | bytes 1 | tf_op jit(solution)/shard_map/project_grad/pallas_call | solution.py:132
  194.5 9.4 %input.1 = (f32[512,768]{1,0:T(8,128)}, f32[512,768]{1,0:T(8,128)}, bf16[64,768]{1,0:T(8,128)(2,1)S(1)}, bf16[64,768]{1,0:T(8,128)(2,1)S(1)}, bf16[64,768]{1,0:T(8,128)(2,1)S(1)}, /*index=5*/bf16[64,768]{1,0:T(8,128)(2,1)S(1)}) custom-call(s32[5]{0:T(128)S(1)} %copy-done.9, bf16[2304,512]{1,0:T(8,128)(2,1)} %get-tuple-element.149.refs_1_, ...), custom_call_target="tpu_custom_call" | custom-call | flops 1 | bytes 1 | tf_op jit(solution)/shard_map/input/pallas_call | solution.py:132
  208.8 5.2 %collective-permute-done.30 = bf16[192,768]{1,0:T(8,128)(2,1)S(1)} collective-permute-done((bf16[192,768]{1,0:T(8,128)(2,1)S(1)}, bf16[192,768]{1,0:T(8,128)(2,1)S(1)}, u32[]{:S(2)}, u32[]{:S(2)}) %collective-permute-start.30) | collective-permute-done | bytes 294944 | tf_op jit(solution)/shard_map/ppermute | solution.py:619
  215.4 3.0 collective-permute-done.28
  226.5 2.9 collective-permute-start.35
  229.4 6.2 %collective-permute-done.25 = bf16[64,768]{1,0:T(8,128)(2,1)S(1)} collective-permute-done((bf16[64,768]{1,0:T(8,128)(2,1)S(1)}, bf16[64,768]{1,0:T(8,128)(2,1)S(1)}, u32[]{:S(2)}, u32[]{:S(2)}) %collective-permute-start.25) | collective-permute-done | bytes 98336 | tf_op jit(solution)/shard_map/ppermute | solution.py:619
  246.2 9.8 %collective-permute-done.38 = bf16[96,768]{1,0:T(8,128)(2,1)S(1)} collective-permute-done((bf16[96,768]{1,0:T(8,128)(2,1)S(1)}, bf16[96,768]{1,0:T(8,128)(2,1)S(1)}, u32[]{:S(2)}, u32[]{:S(2)}) %collective-permute-start.38) | collective-permute-done | bytes 147488 | tf_op jit(solution)/shard_map/ppermute | solution.py:619
  256.0 3.2 %collective-permute-done.37 = bf16[192,768]{1,0:T(8,128)(2,1)S(1)} collective-permute-done((bf16[192,768]{1,0:T(8,128)(2,1)S(1)}, bf16[192,768]{1,0:T(8,128)(2,1)S(1)}, u32[]{:S(2)}, u32[]{:S(2)}) %collective-permute-start.37) | collective-permute-done | bytes 294944 | tf_op jit(solution)/shard_map/ppermute | solution.py:619
  263.5 4.0 %collective-permute-done.39 = bf16[96,768]{1,0:T(8,128)(2,1)S(1)} collective-permute-done((bf16[96,768]{1,0:T(8,128)(2,1)S(1)}, bf16[96,768]{1,0:T(8,128)(2,1)S(1)}, u32[]{:S(2)}, u32[]{:S(2)}) %collective-permute-start.39) | collective-permute-done | bytes 147488 | tf_op jit(solution)/shard_map/ppermute | solution.py:619
  269.2 2.9 collective-permute-done.43
  276.3 2.7 collective-permute-start.42
  283.7 3.6 %collective-permute-done.44 = bf16[384,768]{1,0:T(8,128)(2,1)S(1)} collective-permute-done((bf16[384,768]{1,0:T(8,128)(2,1)}, bf16[384,768]{1,0:T(8,128)(2,1)S(1)}, u32[]{:S(2)}, u32[]{:S(2)}) %collective-permute-start.44) | collective-permute-done | bytes 589856 | tf_op jit(solution)/shard_map/ppermute | solution.py:619
  291.8 8.9 %collective-permute-done.45 = bf16[384,768]{1,0:T(8,128)(2,1)S(1)} collective-permute-done((bf16[384,768]{1,0:T(8,128)(2,1)S(1)}, bf16[384,768]{1,0:T(8,128)(2,1)S(1)}, u32[]{:S(2)}, u32[]{:S(2)}) %collective-permute-start.45) | collective-permute-done | bytes 589856 | tf_op jit(solution)/shard_map/ppermute | solution.py:619
  (212 shorter events, 96.6 us)
Async XLA Ops:
  0.6 28.7 %collective-permute-start.4 = (bf16[576,768]{1,0:T(8,128)(2,1)}, bf16[576,768]{1,0:T(8,128)(2,1)S(1)}, u32[]{:S(2)}, u32[]{:S(2)}) collective-permute-start(bf16[576,768]{1,0:T(8,128)(2,1)} %bitcast.25), channel_id=1, source_target_pairs={{0,2},{1,3},{2,0},{3,1},{4,6},{5,7},{6,4},{7,5},{8,10},{9,11},{10,... | collective-permute-start | bytes 2654216 | tf_op jit(solution)/shard_map/ppermute | solution.py:583
  10.1 15.8 %collective-permute-start = (bf16[432,64]{1,0:T(8,128)(2,1)S(1)}, bf16[432,64]{1,0:T(8,128)(2,1)S(1)}, u32[]{:S(2)}, u32[]{:S(2)}) collective-permute-start(bf16[432,64]{1,0:T(8,128)(2,1)S(1)} %pad_maximum_fusion.10), channel_id=1, source_target_pairs={{0,2},{1,3},{2,0},{3,1},{4,6},{5,7},{6,4},{7,5},{8,10},{9,11},{10,... | collective-permute-start | bytes 165896 | tf_op jit(solution)/shard_map/ppermute | solution.py:583
  10.2 17.7 %collective-permute-start.2 = (bf16[432,64]{1,0:T(8,128)(2,1)S(1)}, bf16[432,64]{1,0:T(8,128)(2,1)S(1)}, u32[]{:S(2)}, u32[]{:S(2)}) collective-permute-start(bf16[432,64]{1,0:T(8,128)(2,1)S(1)} %pad_maximum_fusion.10), channel_id=1, source_target_pairs={{0,1},{1,0},{2,3},{3,2},{4,5},{5,4},{6,7},{7,6},{8,9},{9,8},{10,11... | collective-permute-start | bytes 165896 | tf_op jit(solution)/shard_map/ppermute | solution.py:579
  10.2 23.1 %collective-permute-start.3 = (bf16[576,768]{1,0:T(8,128)(2,1)}, bf16[576,768]{1,0:T(8,128)(2,1)S(1)}, u32[]{:S(2)}, u32[]{:S(2)}) collective-permute-start(bf16[576,768]{1,0:T(8,128)(2,1)} %bitcast.26), channel_id=1, source_target_pairs={{0,1},{1,0},{2,3},{3,2},{4,5},{5,4},{6,7},{7,6},{8,9},{9,8},{10,11... | collective-permute-start | bytes 2654216 | tf_op jit(solution)/shard_map/ppermute | solution.py:579
  30.2 34.5 %collective-permute-start.6 = (bf16[960,768]{1,0:T(8,128)(2,1)}, bf16[960,768]{1,0:T(8,128)(2,1)}, u32[]{:S(2)}, u32[]{:S(2)}) collective-permute-start(bf16[960,768]{1,0:T(8,128)(2,1)} %pad_maximum_fusion), channel_id=1, source_target_pairs={{0,2},{1,3},{2,0},{3,1},{4,6},{5,7},{6,4},{7,5},{8,10},{9,11},{10,... | collective-permute-start | bytes 4423688 | tf_op jit(solution)/shard_map/ppermute | solution.py:583
  46.1 20.4 %all-to-all-start = ((bf16[8,2,112,128]{3,2,1,0:T(8,128)(2,1)}), bf16[8,2,112,128]{3,2,1,0:T(8,128)(2,1)}, u32[]{:S(2)}, u32[]{:S(2)}) async-start(bf16[8,2,112,128]{3,2,1,0:T(8,128)(2,1)} %get-tuple-element.114), calls=%async_computation | async-start | bytes 917504 | tf_op jit(solution)/shard_map/all_to_all | solution.py:687
  52.0 26.7 %collective-permute-start.7 = (bf16[192,768]{1,0:T(8,128)(2,1)}, bf16[192,768]{1,0:T(8,128)(2,1)}, u32[]{:S(2)}, u32[]{:S(2)}) collective-permute-start(bf16[192,768]{1,0:T(8,128)(2,1)} %refs_4_.1), channel_id=1, source_target_pairs={{0,1},{1,0},{2,3},{3,2},{4,5},{5,4},{6,7},{7,6},{8,9},{9,8},{10,11... | collective-permute-start | bytes 884744 | tf_op jit(solution)/shard_map/ppermute | solution.py:579
  52.0 40.7 %collective-permute-start.10 = (bf16[512,768]{1,0:T(8,128)(2,1)}, bf16[512,768]{1,0:T(8,128)(2,1)}, u32[]{:S(2)}, u32[]{:S(2)}) collective-permute-start(bf16[512,768]{1,0:T(8,128)(2,1)} %bitcast.13.refs_4_), channel_id=1, source_target_pairs={{0,1},{1,0},{2,3},{3,2},{4,5},{5,4},{6,7},{7,6},{8,9},{9,8},{10,11... | collective-permute-start | bytes 2359304 | tf_op jit(solution)/shard_map/ppermute | solution.py:579
  64.8 28.0 %collective-permute-start.11 = (bf16[768,768]{1,0:T(8,128)(2,1)}, bf16[768,768]{1,0:T(8,128)(2,1)}, u32[]{:S(2)}, u32[]{:S(2)}) collective-permute-start(bf16[768,768]{1,0:T(8,128)(2,1)} %refs_5_.1), channel_id=1, source_target_pairs={{0,2},{1,3},{2,0},{3,1},{4,6},{5,7},{6,4},{7,5},{8,10},{9,11},{10,... | collective-permute-start | bytes 3538952 | tf_op jit(solution)/shard_map/ppermute | solution.py:583
  68.4 18.2 %all-to-all-start.1 = ((bf16[8,2,112,128]{3,2,1,0:T(8,128)(2,1)}), bf16[8,2,112,128]{3,2,1,0:T(8,128)(2,1)}, u32[]{:S(2)}, u32[]{:S(2)}) async-start(bf16[8,2,112,128]{3,2,1,0:T(8,128)(2,1)} %scan.1), calls=%async_computation.1 | async-start | bytes 917504 | tf_op jit(solution)/shard_map/all_to_all | solution.py:687
  109.2 15.6 %collective-permute-start.12 = (bf16[384,768]{1,0:T(8,128)(2,1)}, bf16[384,768]{1,0:T(8,128)(2,1)S(1)}, u32[]{:S(2)}, u32[]{:S(2)}) collective-permute-start(bf16[384,768]{1,0:T(8,128)(2,1)} %get-tuple-element.128), channel_id=1, source_target_pairs={{0,2},{1,3},{2,0},{3,1},{4,6},{5,7},{6,4},{7,5},{8,10},{9,11},{10,... | collective-permute-start | bytes 1769480 | tf_op jit(solution)/shard_map/ppermute | solution.py:583
  124.8 16.1 %collective-permute-start.14 = (bf16[384,768]{1,0:T(8,128)(2,1)}, bf16[384,768]{1,0:T(8,128)(2,1)}, u32[]{:S(2)}, u32[]{:S(2)}) collective-permute-start(bf16[384,768]{1,0:T(8,128)(2,1)} %get-tuple-element.138), channel_id=1, source_target_pairs={{0,2},{1,3},{2,0},{3,1},{4,6},{5,7},{6,4},{7,5},{8,10},{9,11},{10,... | collective-permute-start | bytes 1769480 | tf_op jit(solution)/shard_map/ppermute | solution.py:583
  134.1 17.8 %all-to-all-start.2 = ((bf16[8,2,112,128]{3,2,1,0:T(8,128)(2,1)}), bf16[8,2,112,128]{3,2,1,0:T(8,128)(2,1)}, u32[]{:S(2)}, u32[]{:S(2)}) async-start(bf16[8,2,112,128]{3,2,1,0:T(8,128)(2,1)} %get-tuple-element.133), calls=%async_computation.2 | async-start | bytes 917504 | tf_op jit(solution)/shard_map/all_to_all | solution.py:687
  140.9 27.9 %collective-permute-start.15 = (bf16[768,768]{1,0:T(8,128)(2,1)}, bf16[768,768]{1,0:T(8,128)(2,1)}, u32[]{:S(2)}, u32[]{:S(2)}) collective-permute-start(bf16[768,768]{1,0:T(8,128)(2,1)} %get-tuple-element.145), channel_id=1, source_target_pairs={{0,2},{1,3},{2,0},{3,1},{4,6},{5,7},{6,4},{7,5},{8,10},{9,11},{10,... | collective-permute-start | bytes 3538952 | tf_op jit(solution)/shard_map/ppermute | solution.py:583
  153.8 17.1 %all-to-all-start.3 = ((bf16[8,2,112,128]{3,2,1,0:T(8,128)(2,1)}), bf16[8,2,112,128]{3,2,1,0:T(8,128)(2,1)}, u32[]{:S(2)}, u32[]{:S(2)}) async-start(bf16[8,2,112,128]{3,2,1,0:T(8,128)(2,1)} %scan_back.1), calls=%async_computation.3 | async-start | bytes 917504 | tf_op jit(solution)/shard_map/all_to_all | solution.py:687
  160.3 18.8 %collective-permute-start.16 = (bf16[384,768]{1,0:T(8,128)(2,1)}, bf16[384,768]{1,0:T(8,128)(2,1)}, u32[]{:S(2)}, u32[]{:S(2)}) collective-permute-start(bf16[384,768]{1,0:T(8,128)(2,1)} %add_convert_fusion.2), channel_id=1, source_target_pairs={{0,4},{4,0},{8,12},{12,8},{16,20},{20,16},{24,28},{28,24},{1,5},{5... | collective-permute-start | bytes 1769480 | tf_op jit(solution)/shard_map/ppermute | solution.py:619
  180.2 14.3 %collective-permute-start.21 = (bf16[512,768]{1,0:T(8,128)(2,1)}, bf16[512,768]{1,0:T(8,128)(2,1)S(1)}, u32[]{:S(2)}, u32[]{:S(2)}) collective-permute-start(bf16[512,768]{1,0:T(8,128)(2,1)} %get-tuple-element.166), channel_id=1, source_target_pairs={{0,1},{1,0},{2,3},{3,2},{4,5},{5,4},{6,7},{7,6},{8,9},{9,8},{10,11... | collective-permute-start | bytes 2359304 | tf_op jit(solution)/shard_map/ppermute | solution.py:579
  189.2 29.2 %collective-permute-start.28 = (bf16[768,768]{1,0:T(8,128)(2,1)}, bf16[768,768]{1,0:T(8,128)(2,1)}, u32[]{:S(2)}, u32[]{:S(2)}) collective-permute-start(bf16[768,768]{1,0:T(8,128)(2,1)} %get-tuple-element.180), channel_id=1, source_target_pairs={{0,2},{1,3},{2,0},{3,1},{4,6},{5,7},{6,4},{7,5},{8,10},{9,11},{10,... | collective-permute-start | bytes 3538952 | tf_op jit(solution)/shard_map/ppermute | solution.py:583
  190.5 15.8 %collective-permute-start.33 = (bf16[384,768]{1,0:T(8,128)(2,1)}, bf16[384,768]{1,0:T(8,128)(2,1)}, u32[]{:S(2)}, u32[]{:S(2)}) collective-permute-start(bf16[384,768]{1,0:T(8,128)(2,1)} %add_convert_fusion.1), channel_id=1, source_target_pairs={{0,4},{4,0},{8,12},{12,8},{16,20},{20,16},{24,28},{28,24},{1,5},{5... | collective-permute-start | bytes 1769480 | tf_op jit(solution)/shard_map/ppermute | solution.py:619
  205.3 15.9 %collective-permute-start.24 = (bf16[64,768]{1,0:T(8,128)(2,1)S(1)}, bf16[64,768]{1,0:T(8,128)(2,1)S(1)}, u32[]{:S(2)}, u32[]{:S(2)}) collective-permute-start(bf16[64,768]{1,0:T(8,128)(2,1)S(1)} %add_convert_fusion.15), channel_id=1, source_target_pairs={{0,2},{1,3},{2,0},{3,1},{4,6},{5,7},{6,4},{7,5},{8,10},{9,11},{10,... | collective-permute-start | bytes 294920 | tf_op jit(solution)/shard_map/ppermute | solution.py:583
  207.5 17.8 %collective-permute-start.34 = (bf16[192,768]{1,0:T(8,128)(2,1)S(1)}, bf16[192,768]{1,0:T(8,128)(2,1)S(1)}, u32[]{:S(2)}, u32[]{:S(2)}) collective-permute-start(bf16[192,768]{1,0:T(8,128)(2,1)S(1)} %add_convert_fusion.4), channel_id=1, source_target_pairs={{0,8},{4,12},{8,0},{12,4},{16,24},{20,28},{24,16},{28,20},{1,9},{5... | collective-permute-start | bytes 884744 | tf_op jit(solution)/shard_map/ppermute | solution.py:619
  219.6 19.1 %collective-permute-start.29 = (bf16[384,768]{1,0:T(8,128)(2,1)S(1)}, bf16[384,768]{1,0:T(8,128)(2,1)S(1)}, u32[]{:S(2)}, u32[]{:S(2)}) collective-permute-start(bf16[384,768]{1,0:T(8,128)(2,1)S(1)} %add_convert_fusion), channel_id=1, source_target_pairs={{0,4},{4,0},{8,12},{12,8},{16,20},{20,16},{24,28},{28,24},{1,5},{5... | collective-permute-start | bytes 1769480 | tf_op jit(solution)/shard_map/ppermute | solution.py:619
  221.2 14.3 %collective-permute-start.25 = (bf16[64,768]{1,0:T(8,128)(2,1)S(1)}, bf16[64,768]{1,0:T(8,128)(2,1)S(1)}, u32[]{:S(2)}, u32[]{:S(2)}) collective-permute-start(bf16[64,768]{1,0:T(8,128)(2,1)S(1)} %add_convert_fusion.14), channel_id=1, source_target_pairs={{0,4},{4,0},{8,12},{12,8},{16,20},{20,16},{24,28},{28,24},{1,5},{5... | collective-permute-start | bytes 294920 | tf_op jit(solution)/shard_map/ppermute | solution.py:619
  226.5 12.2 %collective-permute-start.35 = (bf16[96,768]{1,0:T(8,128)(2,1)S(1)}, bf16[96,768]{1,0:T(8,128)(2,1)S(1)}, u32[]{:S(2)}, u32[]{:S(2)}) collective-permute-start(bf16[96,768]{1,0:T(8,128)(2,1)S(1)} %add_convert_fusion.9), channel_id=1, source_target_pairs={{0,16},{4,20},{8,24},{12,28},{16,0},{20,4},{24,8},{28,12},{1,17},{... | collective-permute-start | bytes 442376 | tf_op jit(solution)/shard_map/ppermute | solution.py:619
  239.8 16.2 %collective-permute-start.36 = (bf16[192,768]{1,0:T(8,128)(2,1)S(1)}, bf16[192,768]{1,0:T(8,128)(2,1)S(1)}, u32[]{:S(2)}, u32[]{:S(2)}) collective-permute-start(bf16[192,768]{1,0:T(8,128)(2,1)S(1)} %add_convert_fusion.3), channel_id=1, source_target_pairs={{0,8},{4,12},{8,0},{12,4},{16,24},{20,28},{24,16},{28,20},{1,9},{5... | collective-permute-start | bytes 884744 | tf_op jit(solution)/shard_map/ppermute | solution.py:619
  239.9 19.3 %collective-permute-start.37 = (bf16[192,768]{1,0:T(8,128)(2,1)S(1)}, bf16[192,768]{1,0:T(8,128)(2,1)S(1)}, u32[]{:S(2)}, u32[]{:S(2)}) collective-permute-start(bf16[192,768]{1,0:T(8,128)(2,1)S(1)} %pad_maximum_fusion.5), channel_id=1, source_target_pairs={{0,8},{4,12},{8,0},{12,4},{16,24},{20,28},{24,16},{28,20},{1,9},{5... | collective-permute-start | bytes 884744 | tf_op jit(solution)/shard_map/ppermute | solution.py:619
  243.1 12.9 %collective-permute-start.38 = (bf16[96,768]{1,0:T(8,128)(2,1)S(1)}, bf16[96,768]{1,0:T(8,128)(2,1)S(1)}, u32[]{:S(2)}, u32[]{:S(2)}) collective-permute-start(bf16[96,768]{1,0:T(8,128)(2,1)S(1)} %add_convert_fusion.8), channel_id=1, source_target_pairs={{0,16},{4,20},{8,24},{12,28},{16,0},{20,4},{24,8},{28,12},{1,17},{... | collective-permute-start | bytes 442376 | tf_op jit(solution)/shard_map/ppermute | solution.py:619
  243.8 35.2 %collective-permute-start.27 = (bf16[64,768]{1,0:T(8,128)(2,1)S(1)}, bf16[64,768]{1,0:T(8,128)(2,1)S(1)}, u32[]{:S(2)}, u32[]{:S(2)}) collective-permute-start(bf16[64,768]{1,0:T(8,128)(2,1)S(1)} %add_convert_fusion.12), channel_id=1, source_target_pairs={{0,16},{4,20},{8,24},{12,28},{16,0},{20,4},{24,8},{28,12},{1,17},{... | collective-permute-start | bytes 294920 | tf_op jit(solution)/shard_map/ppermute | solution.py:619
  260.5 11.6 %collective-permute-start.43 = (bf16[192,768]{1,0:T(8,128)(2,1)S(1)}, bf16[192,768]{1,0:T(8,128)(2,1)S(1)}, u32[]{:S(2)}, u32[]{:S(2)}) collective-permute-start(bf16[192,768]{1,0:T(8,128)(2,1)S(1)} %pad_maximum_fusion.7), channel_id=1, source_target_pairs={{0,8},{4,12},{8,0},{12,4},{16,24},{20,28},{24,16},{28,20},{1,9},{5... | collective-permute-start | bytes 884744 | tf_op jit(solution)/shard_map/ppermute | solution.py:619
  262.5 13.7 %collective-permute-start.41 = (bf16[384,768]{1,0:T(8,128)(2,1)S(1)}, bf16[384,768]{1,0:T(8,128)(2,1)S(1)}, u32[]{:S(2)}, u32[]{:S(2)}) collective-permute-start(bf16[384,768]{1,0:T(8,128)(2,1)S(1)} %pad_maximum_fusion.2), channel_id=1, source_target_pairs={{0,4},{4,0},{8,12},{12,8},{16,20},{20,16},{24,28},{28,24},{1,5},{5... | collective-permute-start | bytes 1769480 | tf_op jit(solution)/shard_map/ppermute | solution.py:619
  273.0 14.3 %collective-permute-start.44 = (bf16[384,768]{1,0:T(8,128)(2,1)}, bf16[384,768]{1,0:T(8,128)(2,1)S(1)}, u32[]{:S(2)}, u32[]{:S(2)}) collective-permute-start(bf16[384,768]{1,0:T(8,128)(2,1)} %pad_maximum_fusion.3), channel_id=1, source_target_pairs={{0,4},{4,0},{8,12},{12,8},{16,20},{20,16},{24,28},{28,24},{1,5},{5... | collective-permute-start | bytes 1769480 | tf_op jit(solution)/shard_map/ppermute | solution.py:619
  287.4 13.3 %collective-permute-start.45 = (bf16[384,768]{1,0:T(8,128)(2,1)S(1)}, bf16[384,768]{1,0:T(8,128)(2,1)S(1)}, u32[]{:S(2)}, u32[]{:S(2)}) collective-permute-start(bf16[384,768]{1,0:T(8,128)(2,1)S(1)} %pad_maximum_fusion.4), channel_id=1, source_target_pairs={{0,4},{4,0},{8,12},{12,8},{16,20},{20,16},{24,28},{28,24},{1,5},{5... | collective-permute-start | bytes 1769480 | tf_op jit(solution)/shard_map/ppermute | solution.py:619
  (48 other events, 377.5 us)
